TPU v7x, 32 devices: a whole 2x2x4 slice. The times are simulated.
32 devices in a mesh: uly: 4 (over y, core), blk: 8 (over z, x).
Axes of the slice: x: 2, y: 2, z: 4, core: 2. Of those that a mesh axis runs over, the one named last changes fastest.
Arguments:
- hidden: bfloat16 [2, 2048, 1280], P(None, ('uly', 'blk')), may hold values from -0.15625 to 0.15625
- positions: int32 [2, 2048], P(None, ('uly', 'blk')), may hold values from 0 to 2047, as said below
- w_query: bfloat16 [1280, 1280], P(('uly', 'blk')), may hold values from -0.15625 to 0.15625
- w_key: bfloat16 [1280, 1280], P(('uly', 'blk')), may hold values from -0.15625 to 0.15625
- w_value: bfloat16 [1280, 1280], P(('uly', 'blk')), may hold values from -0.15625 to 0.15625
- w_out: bfloat16 [1280, 1280], P(('uly', 'blk')), may hold values from -0.15625 to 0.15625
- w_up: bfloat16 [5120, 1280], P(('uly', 'blk')), may hold values from -0.15625 to 0.15625
- w_gate: bfloat16 [5120, 1280], P(('uly', 'blk')), may hold values from -0.15625 to 0.15625
- w_down: bfloat16 [1280, 5120], P(('uly', 'blk')), may hold values from -0.078125 to 0.078125
- qk_scale: bfloat16 [1280], P(('uly', 'blk')), may hold values from 0.8984375 to 1.59375
- alpha_attn: bfloat16 [1280], P(('uly', 'blk')), may hold values from 0.099609375 to 0.59765625
- alpha_mlp: bfloat16 [1280], P(('uly', 'blk')), may hold values from 0.099609375 to 0.59765625
- up_scale: bfloat16 [5120], P(('uly', 'blk')), may hold values from 0.5 to 2
- gate_scale: bfloat16 [5120], P(('uly', 'blk')), may hold values from 0.5 to 2
- cotangent: bfloat16 [2, 2048, 1280], P(None, ('uly', 'blk')), may hold values from -12 to 12
Outputs:
- layer_out: bfloat16 [2, 2048, 1280], P(None, ('uly', 'blk'))
- grad_hidden: float32 [2, 2048, 1280], P(None, ('uly', 'blk'))
- grad_query: float32 [1280, 1280], P(('uly', 'blk'))
- grad_key: float32 [1280, 1280], P(('uly', 'blk'))
- grad_value: float32 [1280, 1280], P(('uly', 'blk'))
- grad_out: float32 [1280, 1280], P(('uly', 'blk'))
- grad_up: float32 [5120, 1280], P(('uly', 'blk'))
- grad_gate: float32 [5120, 1280], P(('uly', 'blk'))
- down_weight_gradient: float32 [1280, 5120], P(('uly', 'blk'))
- grad_qk_scale: float32 [1280], P(('uly', 'blk'))
- grad_alpha_attn: float32 [1280], P(('uly', 'blk'))
- grad_alpha_mlp: float32 [1280], P(('uly', 'blk'))
- grad_up_scale: float32 [5120], P(('uly', 'blk'))
- grad_gate_scale: float32 [5120], P(('uly', 'blk'))
Inputs may be any that keep to these rules, and one draw needn't show every extreme that they name: In each sequence every position occurs once. With spans of 128 consecutive positions, the rows of one index b of blk (over all indices of uly, in order of uly) hold two whole spans, c and 15 - c, each in increasing order, the two spans in either order; every c occurs on one index of blk.
All inputs are finite; a program needn't handle non-finite values.
Results may differ from a plain program's by a relative error of at most 0.029.
Values may be sent and summed in bfloat16 or wider, within the bound.
A program may use at most 320 MiB of HBM per device.

v0:
```python
import math

import jax
import jax.numpy as jnp
from jax import lax
from jax.sharding import PartitionSpec as P

D = 1280
HEADS = 20
HEAD_DIM = 64


rotary_base = 10000.0
tiny_eps = 1e-06
masked_score = -1e30


def unit_rows(values):
    entries = values.shape[-1]
    return (
        values
        * lax.rsqrt(jnp.mean(values * values, axis=-1, keepdims=True) + tiny_eps)
        * entries ** (-0.5)
    )


def rotate_pairs(values, places):
    half_dim = values.shape[-1] // 2
    freqs = rotary_base ** (-(jnp.arange(half_dim, dtype=jnp.float32) * (2.0 / values.shape[-1])))
    angles = places.astype(jnp.float32)[..., None, None] * freqs
    cosine = jnp.cos(angles)
    sine = jnp.sin(angles)
    former = values[..., :half_dim]
    latter = values[..., half_dim:]
    return jnp.concatenate(
        [former * cosine - latter * sine, latter * cosine + former * sine], axis=-1
    )


def project(input_arrays, weight_matrix):
    return lax.dot_general(
        input_arrays, weight_matrix, (((1,), (1,)), ((), ())), preferred_element_type=jnp.float32
    )


def weight_grad(grads, input_arrays):
    return lax.dot_general(
        grads, input_arrays, (((0,), (0,)), ((), ())), preferred_element_type=jnp.float32
    )


def pull_input(grads, weight_matrix):
    return jnp.dot(grads, weight_matrix, preferred_element_type=jnp.float32)


def residual_step(base, branch_output, rate):
    return unit_rows(base + rate * (unit_rows(branch_output) - base))


def gated(up_rows, gate_rows, up_wide, gate_wide):
    return jax.nn.silu(gate_rows * gate_wide * D**0.5) * (up_rows * up_wide)


def post_heads(raw_rows, scale_row, places, factor):
    seq_count, rows_each = places.shape
    shaped = raw_rows.reshape(seq_count, rows_each, HEADS, HEAD_DIM)
    turned = unit_rows(rotate_pairs(shaped, places)) * scale_row.reshape(HEADS, HEAD_DIM) * factor
    return turned.reshape(raw_rows.shape)


def local(
    hidden,
    positions,
    w_query,
    w_key,
    w_value,
    w_out,
    w_up,
    w_gate,
    w_down,
    qk_scale,
    alpha_attn,
    alpha_mlp,
    up_scale,
    gate_scale,
    cotangent,
):
    seq_count, rows_each, model_width = hidden.shape
    uly_count = lax.axis_size("uly")
    local_width = model_width // uly_count
    local_heads = HEADS // uly_count
    group_rows = uly_count * rows_each
    token_count = seq_count * rows_each
    gathered = (
        lax.all_gather(w_query, ("uly", "blk"), axis=0, tiled=True),
        lax.all_gather(w_key, ("uly", "blk"), axis=0, tiled=True),
        lax.all_gather(w_value, ("uly", "blk"), axis=0, tiled=True),
        lax.all_gather(w_out, ("uly", "blk"), axis=0, tiled=True),
        lax.all_gather(w_up, ("uly", "blk"), axis=0, tiled=True),
        lax.all_gather(w_gate, ("uly", "blk"), axis=0, tiled=True),
        lax.all_gather(w_down, ("uly", "blk"), axis=0, tiled=True),
        lax.all_gather(qk_scale, ("uly", "blk"), axis=0, tiled=True),
        lax.all_gather(alpha_attn, ("uly", "blk"), axis=0, tiled=True),
        lax.all_gather(alpha_mlp, ("uly", "blk"), axis=0, tiled=True),
        lax.all_gather(up_scale, ("uly", "blk"), axis=0, tiled=True),
        lax.all_gather(gate_scale, ("uly", "blk"), axis=0, tiled=True),
    )
    query_full, key_full, value_full, out_full, up_full, gate_full, down_full = (
        gathered[0],
        gathered[1],
        gathered[2],
        gathered[3],
        gathered[4],
        gathered[5],
        gathered[6],
    )
    scale_wide = gathered[7].astype(jnp.float32)
    attn_rate = gathered[8].astype(jnp.float32)
    mlp_rate = gathered[9].astype(jnp.float32)
    up_wide = gathered[10].astype(jnp.float32)
    gate_wide = gathered[11].astype(jnp.float32)
    all_places = lax.all_gather(positions, ("uly", "blk"), axis=1, tiled=True)
    blk_count = all_places.shape[1] // group_rows
    key_places = jnp.transpose(
        all_places.reshape(seq_count, uly_count, blk_count, rows_each), (0, 2, 1, 3)
    ).reshape(seq_count, blk_count * group_rows)
    query_places = lax.dynamic_slice_in_dim(
        key_places, lax.axis_index("blk") * group_rows, group_rows, 1
    )
    flat_rows = hidden.reshape(token_count, model_width)
    hidden_wide = flat_rows.astype(jnp.float32)
    q_raw = project(flat_rows, query_full)
    k_raw = project(flat_rows, key_full)
    query_rows, pull_query = jax.vjp(
        lambda raw_rows, scale_row: post_heads(raw_rows, scale_row, positions, HEAD_DIM**0.5),
        q_raw,
        scale_wide,
    )
    key_rows, pull_key = jax.vjp(
        lambda raw_rows, scale_row: post_heads(raw_rows, scale_row, positions, 1.0),
        k_raw,
        scale_wide,
    )
    query_send = query_rows.reshape(seq_count, rows_each, model_width).astype(jnp.bfloat16)
    key_send = key_rows.reshape(seq_count, rows_each, model_width).astype(jnp.bfloat16)
    value_send = (
        project(flat_rows, value_full)
        .astype(jnp.bfloat16)
        .reshape(seq_count, rows_each, model_width)
    )
    query_heads, key_heads, value_heads = (
        lax.all_to_all(query_send, "uly", split_axis=2, concat_axis=1, tiled=True),
        lax.all_to_all(key_send, "uly", split_axis=2, concat_axis=1, tiled=True),
        lax.all_to_all(value_send, "uly", split_axis=2, concat_axis=1, tiled=True),
    )
    query_four = query_heads.reshape(seq_count, group_rows, local_heads, HEAD_DIM)

    def block_parts(pieces, offset, block_rows):
        key_piece, value_piece = pieces
        key_part = lax.dynamic_slice_in_dim(key_piece, offset, block_rows, 1).reshape(
            seq_count, block_rows, local_heads, HEAD_DIM
        )
        value_part = lax.dynamic_slice_in_dim(value_piece, offset, block_rows, 1).reshape(
            seq_count, block_rows, local_heads, HEAD_DIM
        )
        place_part = lax.dynamic_slice_in_dim(key_places, offset, block_rows, 1)
        scores = jnp.einsum(
            "sqhd,skhd->shqk", query_four, key_part, preferred_element_type=jnp.float32
        )
        allowed = place_part[:, None, None, :] <= query_places[:, None, :, None]
        return (key_part, value_part, jnp.where(allowed, scores, masked_score), allowed)

    start_state = (
        jnp.full((seq_count, local_heads, group_rows), masked_score, jnp.float32),
        jnp.zeros((seq_count, local_heads, group_rows), jnp.float32),
        jnp.zeros((seq_count, group_rows, local_heads, HEAD_DIM), jnp.float32),
    )
    pieces = (
        lax.all_gather(key_heads, "blk", axis=1, tiled=True),
        lax.all_gather(value_heads, "blk", axis=1, tiled=True),
    )
    piece_rows = pieces[0].shape[1]
    block_rows = math.gcd(piece_rows, 512)

    def forward_step_forward(block_index, running):
        running_max, running_sum, running_acc = running
        offset = block_index * block_rows
        key_part, value_part, scores, allowed = block_parts(pieces, offset, block_rows)
        new_max = jnp.maximum(running_max, jnp.max(scores, axis=-1))
        weights = jnp.where(allowed, jnp.exp(scores - new_max[..., None]), 0.0)
        shrink = jnp.exp(running_max - new_max)
        running_sum = running_sum * shrink + jnp.sum(weights, axis=-1)
        update = jnp.einsum(
            "shqk,skhd->sqhd",
            weights.astype(jnp.bfloat16),
            value_part,
            preferred_element_type=jnp.float32,
        )
        running_acc = running_acc * jnp.transpose(shrink, (0, 2, 1))[..., None] + update
        return (new_max, running_sum, running_acc)

    running_max, running_sum, running_acc = lax.fori_loop(
        0, piece_rows // block_rows, forward_step_forward, start_state
    )
    log_total = running_max + jnp.log(running_sum)
    attended = running_acc / jnp.transpose(running_sum, (0, 2, 1))[..., None]
    attended_send = attended.reshape(seq_count, group_rows, local_width).astype(jnp.bfloat16)
    mixed_rows = lax.all_to_all(attended_send, "uly", split_axis=1, concat_axis=2, tiled=True)
    mixed_flat = mixed_rows.reshape(token_count, model_width)
    att_proj = project(mixed_flat, out_full)
    first_out, pull_attn = jax.vjp(residual_step, hidden_wide, att_proj, attn_rate)
    mlp_input = first_out.astype(jnp.bfloat16)
    up_rows = project(mlp_input, up_full)
    gate_rows = project(mlp_input, gate_full)
    inner_rows, pull_inner = jax.vjp(gated, up_rows, gate_rows, up_wide, gate_wide)
    inner_send = inner_rows.astype(jnp.bfloat16)
    branch_output = project(inner_send, down_full)
    final_rows, pull_mlp = jax.vjp(residual_step, first_out, branch_output, mlp_rate)
    layer_out = final_rows.astype(jnp.bfloat16).reshape(seq_count, rows_each, model_width)
    upstream = cotangent.reshape(token_count, model_width).astype(jnp.float32)
    grad_first, grad_branch, grad_alpha_mlp = pull_mlp(upstream)
    again = (
        lax.all_gather(w_query, ("uly", "blk"), axis=0, tiled=True),
        lax.all_gather(w_key, ("uly", "blk"), axis=0, tiled=True),
        lax.all_gather(w_value, ("uly", "blk"), axis=0, tiled=True),
        lax.all_gather(w_out, ("uly", "blk"), axis=0, tiled=True),
        lax.all_gather(w_up, ("uly", "blk"), axis=0, tiled=True),
        lax.all_gather(w_gate, ("uly", "blk"), axis=0, tiled=True),
        lax.all_gather(w_down, ("uly", "blk"), axis=0, tiled=True),
        lax.all_gather(qk_scale, ("uly", "blk"), axis=0, tiled=True),
        lax.all_gather(alpha_attn, ("uly", "blk"), axis=0, tiled=True),
        lax.all_gather(alpha_mlp, ("uly", "blk"), axis=0, tiled=True),
        lax.all_gather(up_scale, ("uly", "blk"), axis=0, tiled=True),
        lax.all_gather(gate_scale, ("uly", "blk"), axis=0, tiled=True),
    )
    back_query, back_key, back_value, back_out, back_up, back_gate, back_down = (
        again[0],
        again[1],
        again[2],
        again[3],
        again[4],
        again[5],
        again[6],
    )
    branch_low = grad_branch.astype(jnp.bfloat16)
    down_weight_gradient = weight_grad(branch_low, inner_send)
    grad_inner = pull_input(branch_low, back_down)
    grad_up_rows, grad_gate_rows, grad_up_scale, grad_gate_scale = pull_inner(grad_inner)
    up_low = grad_up_rows.astype(jnp.bfloat16)
    gate_low = grad_gate_rows.astype(jnp.bfloat16)
    grad_up = weight_grad(up_low, mlp_input)
    grad_gate = weight_grad(gate_low, mlp_input)
    grad_first = grad_first + pull_input(up_low, back_up) + pull_input(gate_low, back_gate)
    mlp_parts = (
        lax.psum_scatter(grad_up, ("uly", "blk"), scatter_dimension=0, tiled=True),
        lax.psum_scatter(grad_gate, ("uly", "blk"), scatter_dimension=0, tiled=True),
        lax.psum_scatter(down_weight_gradient, ("uly", "blk"), scatter_dimension=0, tiled=True),
        lax.psum_scatter(grad_up_scale, ("uly", "blk"), scatter_dimension=0, tiled=True),
        lax.psum_scatter(grad_gate_scale, ("uly", "blk"), scatter_dimension=0, tiled=True),
        lax.psum_scatter(grad_alpha_mlp, ("uly", "blk"), scatter_dimension=0, tiled=True),
    )
    grad_residual, grad_att, grad_alpha_attn = pull_attn(grad_first)
    att_low = grad_att.astype(jnp.bfloat16)
    grad_out = weight_grad(att_low, mixed_flat)
    grad_mixed = (
        pull_input(att_low, back_out)
        .astype(jnp.bfloat16)
        .reshape(seq_count, rows_each, model_width)
    )
    grad_heads = lax.all_to_all(grad_mixed, "uly", split_axis=2, concat_axis=1, tiled=True)
    grad_four = grad_heads.reshape(seq_count, group_rows, local_heads, HEAD_DIM)
    row_delta = jnp.transpose(jnp.sum(grad_four.astype(jnp.float32) * attended, axis=-1), (0, 2, 1))
    back_state = (
        jnp.zeros((seq_count, group_rows, local_heads, HEAD_DIM), jnp.float32),
        jnp.zeros((2, seq_count, blk_count * group_rows, local_width), jnp.float32),
    )
    backward_pieces = (
        lax.all_gather(key_heads, "blk", axis=1, tiled=True),
        lax.all_gather(value_heads, "blk", axis=1, tiled=True),
    )
    piece_rows = backward_pieces[0].shape[1]
    backward_block_rows = math.gcd(piece_rows, 512)

    def backward_step_forward(block_index, running):
        grad_query_acc, grad_pairs = running
        offset = block_index * backward_block_rows
        key_part, value_part, scores, allowed = block_parts(
            backward_pieces, offset, backward_block_rows
        )
        probs = jnp.exp(scores - log_total[..., None])
        grad_values = jnp.einsum(
            "shqk,sqhd->skhd",
            probs.astype(jnp.bfloat16),
            grad_four,
            preferred_element_type=jnp.float32,
        )
        grad_probs = jnp.einsum(
            "sqhd,skhd->shqk", grad_four, value_part, preferred_element_type=jnp.float32
        )
        grad_scores = (probs * (grad_probs - row_delta[..., None])).astype(jnp.bfloat16)
        grad_query_acc = grad_query_acc + jnp.einsum(
            "shqk,skhd->sqhd", grad_scores, key_part, preferred_element_type=jnp.float32
        )
        grad_keys = jnp.einsum(
            "shqk,sqhd->skhd", grad_scores, query_four, preferred_element_type=jnp.float32
        )
        stacked = jnp.stack([grad_keys, grad_values]).reshape(
            2, seq_count, backward_block_rows, local_width
        )
        current = lax.dynamic_slice_in_dim(grad_pairs, offset, backward_block_rows, 2)
        grad_pairs = lax.dynamic_update_slice_in_dim(grad_pairs, current + stacked, offset, 2)
        return (grad_query_acc, grad_pairs)

    grad_query_acc, grad_pairs = lax.fori_loop(
        0, piece_rows // backward_block_rows, backward_step_forward, back_state
    )
    own_pairs = lax.psum_scatter(
        grad_pairs.astype(jnp.bfloat16), "blk", scatter_dimension=2, tiled=True
    ).astype(jnp.float32)
    query_low = grad_query_acc.reshape(seq_count, group_rows, local_width).astype(jnp.bfloat16)
    key_low = own_pairs[0].astype(jnp.bfloat16)
    value_low = own_pairs[1].astype(jnp.bfloat16)
    query_back, key_back, value_back = (
        lax.all_to_all(query_low, "uly", split_axis=1, concat_axis=2, tiled=True),
        lax.all_to_all(key_low, "uly", split_axis=1, concat_axis=2, tiled=True),
        lax.all_to_all(value_low, "uly", split_axis=1, concat_axis=2, tiled=True),
    )
    grad_q_raw, grad_scale_query = pull_query(
        query_back.reshape(token_count, model_width).astype(jnp.float32)
    )
    grad_k_raw, grad_scale_key = pull_key(
        key_back.reshape(token_count, model_width).astype(jnp.float32)
    )
    raw_query_low = grad_q_raw.astype(jnp.bfloat16)
    raw_key_low = grad_k_raw.astype(jnp.bfloat16)
    value_rows_low = value_back.reshape(token_count, model_width)
    grad_query = weight_grad(raw_query_low, flat_rows)
    grad_key = weight_grad(raw_key_low, flat_rows)
    grad_value = weight_grad(value_rows_low, flat_rows)
    grad_hidden = (
        grad_residual
        + pull_input(raw_query_low, back_query)
        + pull_input(raw_key_low, back_key)
        + pull_input(value_rows_low, back_value)
    )
    attn_parts = (
        lax.psum_scatter(grad_query, ("uly", "blk"), scatter_dimension=0, tiled=True),
        lax.psum_scatter(grad_key, ("uly", "blk"), scatter_dimension=0, tiled=True),
        lax.psum_scatter(grad_value, ("uly", "blk"), scatter_dimension=0, tiled=True),
        lax.psum_scatter(grad_out, ("uly", "blk"), scatter_dimension=0, tiled=True),
        lax.psum_scatter(
            grad_scale_query + grad_scale_key, ("uly", "blk"), scatter_dimension=0, tiled=True
        ),
        lax.psum_scatter(grad_alpha_attn, ("uly", "blk"), scatter_dimension=0, tiled=True),
    )
    return (
        layer_out,
        grad_hidden.reshape(seq_count, rows_each, model_width),
        attn_parts[0],
        attn_parts[1],
        attn_parts[2],
        attn_parts[3],
        mlp_parts[0],
        mlp_parts[1],
        mlp_parts[2],
        attn_parts[4],
        attn_parts[5],
        mlp_parts[5],
        mlp_parts[3],
        mlp_parts[4],
    )


def solution(mesh):
    return jax.shard_map(
        local,
        mesh=mesh,
        in_specs=(
            P(None, ("uly", "blk"), None),
            P(None, ("uly", "blk")),
            P(("uly", "blk"), None),
            P(("uly", "blk"), None),
            P(("uly", "blk"), None),
            P(("uly", "blk"), None),
            P(("uly", "blk"), None),
            P(("uly", "blk"), None),
            P(("uly", "blk"), None),
            P(("uly", "blk")),
            P(("uly", "blk")),
            P(("uly", "blk")),
            P(("uly", "blk")),
            P(("uly", "blk")),
            P(None, ("uly", "blk"), None),
        ),
        out_specs=(
            P(None, ("uly", "blk"), None),
            P(None, ("uly", "blk"), None),
            P(("uly", "blk"), None),
            P(("uly", "blk"), None),
            P(("uly", "blk"), None),
            P(("uly", "blk"), None),
            P(("uly", "blk"), None),
            P(("uly", "blk"), None),
            P(("uly", "blk"), None),
            P(("uly", "blk")),
            P(("uly", "blk")),
            P(("uly", "blk")),
            P(("uly", "blk")),
            P(("uly", "blk")),
        ),
        check_vma=False,
    )
```

profile of v0, /device:TPU:0, one launch (start us, length us, event | category | flops | bytes accessed | tf_op | source)
XLA Modules:
  0.0 3212.1 jit_solution(4870155590316130350)
XLA Ops:
  9.4 63.5 %all-gather.17.cloned.1.call-done = bf16[1280,1280]{1,0:T(8,128)(2,1)} async-done(((bf16[40,1280]{1,0:T(8,128)(2,1)}), bf16[1280,1280]{1,0:T(8,128)(2,1)}) %all-gather.17.cloned.1.call-update) | async-done | bytes 3276816 | tf_op jit(solution)/shard_map/all_gather | solution.py:97
  77.3 10.0 all_to_all.114
  90.7 38.6 %all-reduce.15 = (bf16[1280]{0:T(1024)(128)(2,1)S(1)}, bf16[1280]{0:T(1024)(128)(2,1)S(1)}, bf16[5120]{0:T(1024)(128)(2,1)S(1)}, bf16[5120]{0:T(1024)(128)(2,1)S(1)}, bf16[1280]{0:T(1024)(128)(2,1)S(1)}) all-reduce(bf16[1280]{0:T(1024)(128)(2,1)S(1)} %dynamic-update-slice.1, ...), channel_id=1, replica_groups=mesh['uly'=4,'blk'=8] {'uly','blk'}, use_global_device_ids=true, to_apply=%add.5 | all-reduce | flops 14080 | bytes 56320
  129.5 4.9 all-gather.11.cloned.1.call-done
  137.4 58.1 %all-gather.15.cloned.1.call-done = bf16[1280,1280]{1,0:T(8,128)(2,1)} async-done(((bf16[40,1280]{1,0:T(8,128)(2,1)}), bf16[1280,1280]{1,0:T(8,128)(2,1)}) %all-gather.15.cloned.1.call-update) | async-done | bytes 3276816 | tf_op jit(solution)/shard_map/all_gather | solution.py:95
  207.4 9.2 all_to_all.115
  226.7 68.3 %all-gather = s32[32,64,2]{1,2,0:T(2,128)S(1)} all-gather(s32[1,64,2]{1,2,0:T(2,128)S(1)} %bitcast.317), channel_id=1, replica_groups=mesh['uly'=4,'blk'=8] {'uly','blk'}, dimensions={0}, use_global_device_ids=true | all-gather | bytes 16896 | tf_op jit(solution)/shard_map/all_gather | solution.py:122
  299.9 19.7 all-gather.13.cloned.1.call-done
  319.5 4.6 copy.216
  324.2 20.4 while.34
  348.3 4.1 all-to-all-start.3
  352.5 7.4 all-to-all-done.3
  364.2 16.1 all-gather.21.cloned.1.call-done
  386.4 94.1 %all-gather.23.cloned.1.call-done = bf16[5120,1280]{1,0:T(8,128)(2,1)} async-done(((bf16[160,1280]{1,0:T(8,128)(2,1)}), bf16[5120,1280]{1,0:T(8,128)(2,1)}) %all-gather.23.cloned.1.call-update) | async-done | bytes 13107216 | tf_op jit(solution)/shard_map/all_gather | solution.py:100
  480.5 10.6 fusion.52
  491.2 89.0 %all-gather.25.cloned.1.call-done = bf16[5120,1280]{1,0:T(8,128)(2,1)} async-done(((bf16[160,1280]{1,0:T(8,128)(2,1)}), bf16[5120,1280]{1,0:T(8,128)(2,1)}) %all-gather.25.cloned.1.call-update) | async-done | bytes 13107216 | tf_op jit(solution)/shard_map/all_gather | solution.py:99
  580.1 12.0 multiply_convert_fusion.2
  592.1 87.7 %all-gather.27.cloned.1.call-done = bf16[1280,5120]{1,0:T(8,128)(2,1)} async-done(((bf16[40,5120]{1,0:T(8,128)(2,1)}), bf16[1280,5120]{1,0:T(8,128)(2,1)}) %all-gather.27.cloned.1.call-update) | async-done | bytes 13107216 | tf_op jit(solution)/shard_map/all_gather | solution.py:101
  679.7 9.7 multiply_reduce_fusion.15
  692.0 12.9 multiply_reduce_fusion
  705.0 5.2 convolution_add_fusion.4
  723.3 6.6 all-to-all-done.4
  736.4 5.3 broadcast_in_dim.129
  741.7 43.5 %while.35 = (s32[]{:T(128)}, f32[2,256,5,64]{1,3,2,0:T(8,128)}, f32[2,2,2048,320]{2,3,1,0:T(8,128)}, bf16[2,2048,320]{1,2,0:T(8,128)(2,1)}, s32[2,2048]{1,0:T(2,...) while((s32[]{:T(128)}, f32[2,256,5,64]{1,3,2,0:T(8,128)}, ...), condition=%wide.region_16.17_spmd.clone, body=%wide.region_15.16_spmd.clone.sunk | while | flops 851247104 | bytes 47362320 | solution.py:314
  748.9 3.9 fusion.158
  759.7 3.9 fusion.158
  770.5 3.9 fusion.158
  781.3 3.9 fusion.158
  785.2 7.1 convert_element_type.190
  792.3 16.1 copy.251
  808.4 13.7 reshape.372
  827.1 95.9 %reduce-scatter.25.cloned.1.call-done = bf16[256,1280]{1,0:T(8,128)(2,1)} async-done(((bf16[2048,1280]{1,0:T(8,128)(2,1)}), bf16[256,1280]{1,0:T(8,128)(2,1)}) %reduce-scatter.25.cloned.1.call-update) | async-done | bytes 655376
  926.8 10.4 all_to_all.116
  937.8 3.8 fusion.55
  947.6 8.6 all-to-all-done.5
  957.7 4.1 all-to-all-start.6
  963.8 6.6 all-to-all-done.6
  986.7 3.8 fusion.53
  991.9 10.8 fusion.58
  1004.4 10.9 fusion.36
  1016.6 10.6 fusion.57
  1034.1 43.7 %all-reduce.14 = (f32[1280]{0:T(1024)S(1)}, f32[1280]{0:T(1024)S(1)}, f32[1280]{0:T(1024)S(1)}, f32[5120]{0:T(1024)S(1)}, f32[5120]{0:T(1024)S(1)}) all-reduce(f32[1280]{0:T(1024)S(1)} %add.236, f32[1280]{0:T(1024)S(1)} %copy-done.56, f32[1280]{0:T(1024)S(1)} %copy-done.55, ...), channel_id=10, replica_groups=mesh['uly'=4,'blk'=8] {'uly','blk'}, use_global_device_ids=true, to_apply=%region_29.30.clone | all-reduce | flops 14080 | bytes 112640
  1086.8 143.4 %reduce-scatter.15.cloned.1.call-done = f32[40,1280]{1,0:T(8,128)} async-done(((f32[1280,1280]{1,0:T(8,128)}), f32[40,1280]{1,0:T(8,128)}) %reduce-scatter.15.cloned.1.call-update) | async-done | bytes 204816 | tf_op jit(solution)/shard_map/reduce_scatter | solution.py:349
  1230.1 154.6 %reduce-scatter.13.cloned.1.call-done = f32[40,1280]{1,0:T(8,128)} async-done(((f32[1280,1280]{1,0:T(8,128)}), f32[40,1280]{1,0:T(8,128)}) %reduce-scatter.13.cloned.1.call-update) | async-done | bytes 204816 | tf_op jit(solution)/shard_map/reduce_scatter | solution.py:348
  1384.7 153.4 %reduce-scatter.11.cloned.1.call-done = f32[40,1280]{1,0:T(8,128)} async-done(((f32[1280,1280]{1,0:T(8,128)}), f32[40,1280]{1,0:T(8,128)}) %reduce-scatter.11.cloned.1.call-update) | async-done | bytes 204816 | tf_op jit(solution)/shard_map/reduce_scatter | solution.py:347
  1538.1 554.9 %reduce-scatter.23.cloned.1.call-done = f32[40,5120]{1,0:T(8,128)} async-done(((f32[1280,5120]{1,0:T(8,128)}), f32[40,5120]{1,0:T(8,128)}) %reduce-scatter.23.cloned.1.call-update) | async-done | bytes 819216 | tf_op jit(solution)/shard_map/reduce_scatter | solution.py:257
  2093.0 556.2 %reduce-scatter.21.cloned.1.call-done = f32[160,1280]{1,0:T(8,128)} async-done(((f32[5120,1280]{1,0:T(8,128)}), f32[160,1280]{1,0:T(8,128)}) %reduce-scatter.21.cloned.1.call-update) | async-done | bytes 819216 | tf_op jit(solution)/shard_map/reduce_scatter | solution.py:256
  2649.2 556.2 %reduce-scatter.19.cloned.1.call-done = f32[160,1280]{1,0:T(8,128)} async-done(((f32[5120,1280]{1,0:T(8,128)}), f32[160,1280]{1,0:T(8,128)}) %reduce-scatter.19.cloned.1.call-update) | async-done | bytes 819216 | tf_op jit(solution)/shard_map/reduce_scatter | solution.py:255
  (412 shorter events, 178.1 us)
Async XLA Ops:
  7.2 65.8 %all-gather.17.cloned.1.call-start = ((), (), s32[]{:S(2)}) async-start(), calls=%async_computation.19 | async-start | bytes 3379200 | tf_op jit(solution)/shard_map/all_gather | solution.py:97
  7.9 126.5 %all-gather.11.cloned.1.call-start = ((), (), s32[]{:S(2)}) async-start(), calls=%async_computation.16 | async-start | bytes 3379200 | tf_op jit(solution)/shard_map/all_gather | solution.py:96
  8.7 186.8 %all-gather.15.cloned.1.call-start = ((), (), s32[]{:S(2)}) async-start(), calls=%async_computation.18 | async-start | bytes 3379200 | tf_op jit(solution)/shard_map/all_gather | solution.py:95
  9.4 287.3 %all-gather.19.cloned.1.call-start = ((), (), s32[]{:S(2)}) async-start(), calls=%async_computation.20 | async-start | bytes 3538944 | tf_op jit(solution)/shard_map/all_gather | solution.py:180
  76.7 12.7 copy-start.61
  76.7 12.7 copy-start.62
  76.7 12.9 copy-start.63
  76.7 13.2 copy-start.64
  76.8 13.4 copy-start.65
  76.8 13.7 copy-start.66
  76.8 57.6 %copy-start.17 = (bf16[2,64,1280]{2,1,0:T(8,128)(2,1)S(1)}, bf16[2,64,1280]{2,1,0:T(8,128)(2,1)}, u32[]{:S(2)}) copy-start(bf16[2,64,1280]{2,1,0:T(8,128)(2,1)} %param.19) | copy-start | bytes 983044
  89.3 230.2 %all-gather.13.cloned.1.call-start = ((), (), s32[]{:S(2)}) async-start(), calls=%async_computation.17 | async-start | bytes 3538944 | tf_op jit(solution)/shard_map/all_gather | solution.py:179
  129.5 68.9 %copy-start.45 = (f32[2,64,32]{1,2,0:T(8,128)}, f32[2,64,32]{1,2,0:T(8,128)S(1)}, u32[]{:S(2)}) copy-start(f32[2,64,32]{1,2,0:T(8,128)S(1)} %get-tuple-element.646) | copy-start | bytes 49156
  129.5 68.9 %copy-start.47 = (f32[2,64,32]{1,2,0:T(8,128)}, f32[2,64,32]{1,2,0:T(8,128)S(1)}, u32[]{:S(2)}) copy-start(f32[2,64,32]{1,2,0:T(8,128)S(1)} %get-tuple-element.647) | copy-start | bytes 49156
  218.7 161.5 %all-gather.21.cloned.1.call-start = ((), (), s32[]{:S(2)}) async-start(), calls=%async_computation.21 | async-start | bytes 3379200 | tf_op jit(solution)/shard_map/all_gather | solution.py:98
  219.3 261.2 %all-gather.23.cloned.1.call-start = ((), (), s32[]{:S(2)}) async-start(), calls=%async_computation.22 | async-start | bytes 13516800 | tf_op jit(solution)/shard_map/all_gather | solution.py:100
  220.0 360.1 %all-gather.25.cloned.1.call-start = ((), (), s32[]{:S(2)}) async-start(), calls=%async_computation.23 | async-start | bytes 13516800 | tf_op jit(solution)/shard_map/all_gather | solution.py:99
  220.8 459.0 %all-gather.27.cloned.1.call-start = ((), (), s32[]{:S(2)}) async-start(), calls=%async_computation.24 | async-start | bytes 13516800 | tf_op jit(solution)/shard_map/all_gather | solution.py:101
  223.2 72.1 %all-to-all-start.1 = ((bf16[4,2,20480]{2,1,0:T(2,128)(2,1)}), bf16[4,2,20480]{2,1,0:T(2,128)(2,1)S(1)}, u32[]{:S(2)}, u32[]{:S(2)}) async-start(bf16[4,2,20480]{2,1,0:T(2,128)(2,1)} %reshape.376), calls=%async_computation.1 | async-start | bytes 655360 | tf_op jit(solution)/shard_map/all_to_all | solution.py:152
  348.3 11.6 all-to-all-start.3
  352.5 362.2 %copy-start.53 = (f32[1280]{0:T(1024)}, f32[1280]{0:T(1024)S(1)}, u32[]{:S(2)}) copy-start(f32[1280]{0:T(1024)S(1)} %convert_element_type.160) | copy-start | bytes 15364
  691.7 13.2 slice-start.4
  691.9 13.0 copy-start.42
  691.9 13.0 slice-start.5
  691.9 13.0 slice-start.6
  692.0 13.0 slice-start.7
  692.0 18.2 slice-start
  692.0 18.2 slice-start.1
  692.0 18.2 slice-start.2
  719.7 10.2 all-to-all-start.4
  723.2 199.8 %reduce-scatter.25.cloned.1.call-start = ((), (), s32[]{:S(2)}) async-start(), calls=%async_computation.32 | async-start | bytes 5898240
  822.2 264.6 %reduce-scatter.17.cloned.1.call-start = ((), (), s32[]{:S(2)}) async-start(), calls=%async_computation.28 | async-start | bytes 6758400 | tf_op jit(solution)/shard_map/reduce_scatter | solution.py:350
  827.0 403.1 %reduce-scatter.15.cloned.1.call-start = ((), (), s32[]{:S(2)}) async-start(), calls=%async_computation.27 | async-start | bytes 6758400 | tf_op jit(solution)/shard_map/reduce_scatter | solution.py:349
  943.9 18.0 copy-start.8
  943.9 18.0 copy-start.10
  943.9 12.3 all-to-all-start.5
  957.7 12.7 all-to-all-start.6
  961.8 422.9 %reduce-scatter.13.cloned.1.call-start = ((), (), s32[]{:S(2)}) async-start(), calls=%async_computation.26 | async-start | bytes 6758400 | tf_op jit(solution)/shard_map/reduce_scatter | solution.py:348
  961.9 13.3 copy-start.12
  961.9 13.3 copy-start.14
  984.5 553.7 %reduce-scatter.11.cloned.1.call-start = ((), (), s32[]{:S(2)}) async-start(), calls=%async_computation.25 | async-start | bytes 6758400 | tf_op jit(solution)/shard_map/reduce_scatter | solution.py:347
  990.5 1102.5 %reduce-scatter.23.cloned.1.call-start = ((), (), s32[]{:S(2)}) async-start(), calls=%async_computation.31 | async-start | bytes 27033600 | tf_op jit(solution)/shard_map/reduce_scatter | solution.py:257
  1002.6 1646.5 %reduce-scatter.21.cloned.1.call-start = ((), (), s32[]{:S(2)}) async-start(), calls=%async_computation.30 | async-start | bytes 27033600 | tf_op jit(solution)/shard_map/reduce_scatter | solution.py:256
  1015.3 2190.1 %reduce-scatter.19.cloned.1.call-start = ((), (), s32[]{:S(2)}) async-start(), calls=%async_computation.29 | async-start | bytes 27033600 | tf_op jit(solution)/shard_map/reduce_scatter | solution.py:255
  1029.9 50.9 %copy-start.25 = (f32[128,1280]{1,0:T(8,128)S(1)}, f32[128,1280]{1,0:T(8,128)}, u32[]{:S(2)}) copy-start(f32[128,1280]{1,0:T(8,128)} %copy-done.24) | copy-start | bytes 1966084
  1029.9 50.9 %copy-start.33 = (bf16[128,1280]{0,1:T(8,128)(2,1)S(1)}, bf16[128,1280]{0,1:T(8,128)(2,1)}, u32[]{:S(2)}) copy-start(bf16[128,1280]{0,1:T(8,128)(2,1)} %copy-done.32) | copy-start | bytes 983044
  1029.9 50.9 %copy-start.54 = (f32[1280]{0:T(1024)S(1)}, f32[1280]{0:T(1024)}, u32[]{:S(2)}) copy-start(f32[1280]{0:T(1024)} %copy-done.53) | copy-start | bytes 15364
  1034.0 49.4 %copy-start.31 = (bf16[128,1280]{0,1:T(8,128)(2,1)S(1)}, bf16[128,1280]{0,1:T(8,128)(2,1)}, u32[]{:S(2)}) copy-start(bf16[128,1280]{0,1:T(8,128)(2,1)} %copy-done.30) | copy-start | bytes 983044
  (61 other events, 187.6 us)
Sparse Core Ops, SparseCore 0:
  10.8 62.0 all-gather.16
  75.8 58.5 all-gather.10
  137.2 58.1 all-gather.14
  198.1 59.6 all-gather.18
  260.3 59.1 all-gather.12
  322.2 57.9 all-gather.20
  383.1 97.3 all-gather.22
  483.4 96.7 all-gather.24
  583.0 96.7 all-gather.26
  822.3 100.6 reduce-scatter.24
  925.9 150.9 reduce-scatter.16
  1079.6 150.4 reduce-scatter.14
  1233.0 151.6 reduce-scatter.12
  1387.4 150.6 reduce-scatter.10
  1540.9 552.0 reduce-scatter.22
  2095.7 553.3 reduce-scatter.20
  2651.9 553.3 reduce-scatter.18
where the time goes:
time: 3220 us; the launch traced here: 3210 us
  waiting for transfers between devices  2680 us (83%)
  blocking collectives  180 us (6%)
  matrix products  150 us (5%)
  local copies, waits for them, and re-layouts  112 us (3%)
  other arithmetic  53.2 us (2%)
    reduce_scatter x1, waiting for transfers between devices, local(): lax.psum_scatter(grad_gate, ('uly', 'blk'), scatter_dimension=0, tiled=True)  556 us
    reduce_scatter x1, waiting for transfers between devices, local(): lax.psum_scatter(grad_up, ('uly', 'blk'), scatter_dimension=0, tiled=True)  556 us
    reduce_scatter x1, waiting for transfers between devices, local(): lax.psum_scatter(down_weight_gradient, ('uly', 'blk'), scatter_dimension=...  555 us
    reduce_scatter x1, waiting for transfers between devices, local(): lax.psum_scatter(grad_key, ('uly', 'blk'), scatter_dimension=0, tiled=True)  155 us
    reduce_scatter x1, waiting for transfers between devices, local(): lax.psum_scatter(grad_query, ('uly', 'blk'), scatter_dimension=0, tiled=T...  153 us
    reduce_scatter x1, waiting for transfers between devices, local(): lax.psum_scatter(grad_value, ('uly', 'blk'), scatter_dimension=0, tiled=T...  143 us
    unnamed x18, waiting for transfers between devices  101 us
    all_gather x1, waiting for transfers between devices, local(): lax.all_gather(w_gate, ('uly', 'blk'), axis=0, tiled=True)  94.1 us
  transfers between devices with their start and end apart: 22, of which 19 were waited for; matrix products, arithmetic and copies ran while one was open for 5% of the time, Pallas kernels for 0%

commit v1 on v0

v1 whole, which is shorter than its diff:
```python
import math

import jax
import jax.numpy as jnp
from jax import lax
from jax.sharding import PartitionSpec as P

D = 1280
HEADS = 20
HEAD_DIM = 64

rotary_base = 10000.0
tiny_eps = 1e-06
masked_score = -1e30
BF = jnp.bfloat16
F32 = jnp.float32


def unit_rows(values):
    entries = values.shape[-1]
    return (
        values
        * lax.rsqrt(jnp.mean(values * values, axis=-1, keepdims=True) + tiny_eps)
        * entries ** (-0.5)
    )


def rotate_pairs(values, places):
    half_dim = values.shape[-1] // 2
    freqs = rotary_base ** (-(jnp.arange(half_dim, dtype=F32) * (2.0 / values.shape[-1])))
    angles = places.astype(F32)[..., None, None] * freqs
    cosine = jnp.cos(angles)
    sine = jnp.sin(angles)
    former = values[..., :half_dim]
    latter = values[..., half_dim:]
    return jnp.concatenate(
        [former * cosine - latter * sine, latter * cosine + former * sine], axis=-1
    )


def project(rows, weight):
    return lax.dot_general(rows, weight, (((1,), (1,)), ((), ())), preferred_element_type=F32)


def weight_grad(grads, rows):
    return lax.dot_general(grads, rows, (((0,), (0,)), ((), ())), preferred_element_type=F32)


def pull_input(grads, weight):
    return jnp.dot(grads, weight, preferred_element_type=F32)


def residual_step(base, branch_output, rate):
    return unit_rows(base + rate * (unit_rows(branch_output) - base))


def gated(up_rows, gate_rows, up_wide, gate_wide):
    return jax.nn.silu(gate_rows * gate_wide * D**0.5) * (up_rows * up_wide)


def post_heads(raw_rows, scale_row, places, factor):
    seq_count, rows_each = places.shape
    heads = raw_rows.shape[-1] // HEAD_DIM
    shaped = raw_rows.reshape(seq_count, rows_each, heads, HEAD_DIM)
    turned = unit_rows(rotate_pairs(shaped, places)) * scale_row.reshape(heads, HEAD_DIM) * factor
    return turned.reshape(raw_rows.shape)


def local(
    hidden,
    positions,
    w_query,
    w_key,
    w_value,
    w_out,
    w_up,
    w_gate,
    w_down,
    qk_scale,
    alpha_attn,
    alpha_mlp,
    up_scale,
    gate_scale,
    cotangent,
):
    seq_count, rows_each, model_width = hidden.shape
    uly_count = lax.axis_size("uly")
    blk_count = lax.axis_size("blk")
    local_width = model_width // uly_count
    local_heads = HEADS // uly_count
    group_rows = uly_count * rows_each
    token_count = seq_count * rows_each
    group_tokens = seq_count * group_rows
    attn_each = w_query.shape[0]
    ff_each = w_up.shape[0]
    ff_local = ff_each * blk_count

    def uly_gather(rows):
        return lax.all_gather(
            rows.reshape(seq_count, rows_each, model_width), "uly", axis=1, tiled=True
        ).reshape(group_tokens, model_width)

    def uly_reduce(partial):
        return (
            lax.psum_scatter(
                partial.astype(BF).reshape(seq_count, group_rows, model_width),
                "uly",
                scatter_dimension=1,
                tiled=True,
            )
            .reshape(token_count, model_width)
            .astype(F32)
        )

    def by_owner(grad):
        shaped = grad.reshape(uly_count, blk_count, attn_each, grad.shape[1])
        return jnp.transpose(shaped, (1, 0, 2, 3)).reshape(blk_count, -1, grad.shape[1])

    packed = jnp.concatenate([qk_scale, alpha_attn, alpha_mlp, up_scale, gate_scale])[None]
    scales = lax.all_gather(packed, ("uly", "blk"), axis=0, tiled=True)
    cuts = [0, attn_each, 2 * attn_each, 3 * attn_each, 3 * attn_each + ff_each]
    uly_index = lax.axis_index("uly")
    own = lax.dynamic_slice_in_dim(scales, uly_index * blk_count, blk_count, 0)
    scale_wide = own[:, : cuts[1]].reshape(-1).astype(F32)
    attn_rate = scales[:, cuts[1] : cuts[2]].reshape(-1).astype(F32)
    mlp_rate = scales[:, cuts[2] : cuts[3]].reshape(-1).astype(F32)
    up_wide = own[:, cuts[3] : cuts[4]].reshape(-1).astype(F32)
    gate_wide = own[:, cuts[4] :].reshape(-1).astype(F32)

    query_places = lax.all_gather(positions, "uly", axis=1, tiled=True)
    key_places = lax.all_gather(query_places, "blk", axis=1, tiled=True)

    flat_rows = hidden.reshape(token_count, model_width)
    hidden_wide = flat_rows.astype(F32)
    group_hidden = uly_gather(flat_rows)

    qkv_full = lax.all_gather(jnp.stack([w_query, w_key, w_value]), "blk", axis=1, tiled=True)
    query_full, key_full, value_full = qkv_full[0], qkv_full[1], qkv_full[2]

    out_cols = lax.all_to_all(
        jnp.transpose(w_out.reshape(attn_each, uly_count, local_width), (1, 0, 2)),
        "uly", split_axis=0, concat_axis=0, tiled=True,
    )
    down_cols = lax.all_to_all(
        jnp.transpose(w_down.reshape(attn_each, uly_count, ff_local), (1, 0, 2)),
        "uly", split_axis=0, concat_axis=0, tiled=True,
    )
    out_full = lax.all_gather(out_cols, "blk", axis=1, tiled=True).reshape(model_width, local_width)
    down_full = lax.all_gather(down_cols, "blk", axis=1, tiled=True).reshape(model_width, ff_local)
    up_full = lax.all_gather(w_up, "blk", axis=0, tiled=True)
    gate_full = lax.all_gather(w_gate, "blk", axis=0, tiled=True)

    q_raw = project(group_hidden, query_full)
    k_raw = project(group_hidden, key_full)
    query_rows, pull_query = jax.vjp(
        lambda raw, row: post_heads(raw, row, query_places, HEAD_DIM**0.5), q_raw, scale_wide
    )
    key_rows, pull_key = jax.vjp(
        lambda raw, row: post_heads(raw, row, query_places, 1.0), k_raw, scale_wide
    )
    query_heads = query_rows.astype(BF).reshape(seq_count, group_rows, local_width)
    key_heads = key_rows.astype(BF).reshape(seq_count, group_rows, local_width)
    value_heads = (
        project(group_hidden, value_full).astype(BF).reshape(seq_count, group_rows, local_width)
    )
    query_four = query_heads.reshape(seq_count, group_rows, local_heads, HEAD_DIM)
    pieces = lax.all_gather(
        jnp.stack([key_heads, value_heads]), "blk", axis=2, tiled=True
    )

    def block_parts(offset, block_rows):
        both = lax.dynamic_slice_in_dim(pieces, offset, block_rows, 2).reshape(
            2, seq_count, block_rows, local_heads, HEAD_DIM
        )
        key_part, value_part = both[0], both[1]
        place_part = lax.dynamic_slice_in_dim(key_places, offset, block_rows, 1)
        scores = jnp.einsum("sqhd,skhd->shqk", query_four, key_part, preferred_element_type=F32)
        allowed = place_part[:, None, None, :] <= query_places[:, None, :, None]
        return (key_part, value_part, jnp.where(allowed, scores, masked_score), allowed)

    start_state = (
        jnp.full((seq_count, local_heads, group_rows), masked_score, F32),
        jnp.zeros((seq_count, local_heads, group_rows), F32),
        jnp.zeros((seq_count, group_rows, local_heads, HEAD_DIM), F32),
    )
    piece_rows = pieces.shape[2]
    block_rows = math.gcd(piece_rows, 512)

    def forward_step(block_index, running):
        running_max, running_sum, running_acc = running
        key_part, value_part, scores, allowed = block_parts(block_index * block_rows, block_rows)
        new_max = jnp.maximum(running_max, jnp.max(scores, axis=-1))
        weights = jnp.where(allowed, jnp.exp(scores - new_max[..., None]), 0.0)
        shrink = jnp.exp(running_max - new_max)
        running_sum = running_sum * shrink + jnp.sum(weights, axis=-1)
        update = jnp.einsum(
            "shqk,skhd->sqhd", weights.astype(BF), value_part, preferred_element_type=F32
        )
        running_acc = running_acc * jnp.transpose(shrink, (0, 2, 1))[..., None] + update
        return (new_max, running_sum, running_acc)

    running_max, running_sum, running_acc = lax.fori_loop(
        0, piece_rows // block_rows, forward_step, start_state
    )
    log_total = running_max + jnp.log(running_sum)
    attended = running_acc / jnp.transpose(running_sum, (0, 2, 1))[..., None]
    mixed_group = attended.reshape(group_tokens, local_width).astype(BF)
    att_proj = uly_reduce(project(mixed_group, out_full))
    first_out, pull_attn = jax.vjp(residual_step, hidden_wide, att_proj, attn_rate)
    mlp_group = uly_gather(first_out.astype(BF))
    up_rows = project(mlp_group, up_full)
    gate_rows = project(mlp_group, gate_full)
    inner_rows, pull_inner = jax.vjp(gated, up_rows, gate_rows, up_wide, gate_wide)
    inner_send = inner_rows.astype(BF)
    branch_output = uly_reduce(project(inner_send, down_full))
    final_rows, pull_mlp = jax.vjp(residual_step, first_out, branch_output, mlp_rate)
    layer_out = final_rows.astype(BF).reshape(seq_count, rows_each, model_width)
    upstream = cotangent.reshape(token_count, model_width).astype(F32)
    grad_first, grad_branch, grad_alpha_mlp = pull_mlp(upstream)

    branch_low = uly_gather(grad_branch.astype(BF))
    grad_down = weight_grad(branch_low, inner_send)
    grad_inner = pull_input(branch_low, down_full)
    grad_up_rows, grad_gate_rows, grad_up_scale, grad_gate_scale = pull_inner(grad_inner)
    up_low = grad_up_rows.astype(BF)
    gate_low = grad_gate_rows.astype(BF)
    grad_up = weight_grad(up_low, mlp_group)
    grad_gate = weight_grad(gate_low, mlp_group)
    mlp_own = lax.psum_scatter(
        jnp.concatenate(
            [
                grad_up.astype(BF).reshape(blk_count, ff_each, model_width),
                grad_gate.astype(BF).reshape(blk_count, ff_each, model_width),
                by_owner(grad_down.astype(BF)),
            ],
            axis=1,
        ),
        "blk", scatter_dimension=0, tiled=True,
    )[0]
    down_own = lax.all_to_all(
        mlp_own[2 * ff_each :].reshape(uly_count, attn_each, ff_local),
        "uly", split_axis=0, concat_axis=0, tiled=True,
    )
    down_weight_gradient = jnp.transpose(down_own, (1, 0, 2)).reshape(attn_each, -1).astype(F32)

    grad_first = grad_first + uly_reduce(pull_input(up_low, up_full) + pull_input(gate_low, gate_full))
    grad_residual, grad_att, grad_alpha_attn = pull_attn(grad_first)
    att_low = uly_gather(grad_att.astype(BF))
    grad_out = weight_grad(att_low, mixed_group)
    grad_four = (
        pull_input(att_low, out_full).astype(BF).reshape(seq_count, group_rows, local_heads, HEAD_DIM)
    )
    row_delta = jnp.transpose(jnp.sum(grad_four.astype(F32) * attended, axis=-1), (0, 2, 1))
    back_state = (
        jnp.zeros((seq_count, group_rows, local_heads, HEAD_DIM), F32),
        jnp.zeros((2, seq_count, piece_rows, local_width), BF),
    )

    def backward_step(block_index, running):
        grad_query_acc, grad_pairs = running
        offset = block_index * block_rows
        key_part, value_part, scores, allowed = block_parts(offset, block_rows)
        probs = jnp.exp(scores - log_total[..., None])
        grad_values = jnp.einsum(
            "shqk,sqhd->skhd", probs.astype(BF), grad_four, preferred_element_type=F32
        )
        grad_probs = jnp.einsum("sqhd,skhd->shqk", grad_four, value_part, preferred_element_type=F32)
        grad_scores = (probs * (grad_probs - row_delta[..., None])).astype(BF)
        grad_query_acc = grad_query_acc + jnp.einsum(
            "shqk,skhd->sqhd", grad_scores, key_part, preferred_element_type=F32
        )
        grad_keys = jnp.einsum("shqk,sqhd->skhd", grad_scores, query_four, preferred_element_type=F32)
        stacked = (
            jnp.stack([grad_keys, grad_values])
            .reshape(2, seq_count, block_rows, local_width)
            .astype(BF)
        )
        grad_pairs = lax.dynamic_update_slice_in_dim(grad_pairs, stacked, offset, 2)
        return (grad_query_acc, grad_pairs)

    grad_query_acc, grad_pairs = lax.fori_loop(
        0, piece_rows // block_rows, backward_step, back_state
    )
    own_pairs = lax.psum_scatter(grad_pairs, "blk", scatter_dimension=2, tiled=True)
    query_low = grad_query_acc.reshape(group_tokens, local_width).astype(BF)
    key_low = own_pairs[0].reshape(group_tokens, local_width)
    value_low = own_pairs[1].reshape(group_tokens, local_width)
    grad_q_raw, grad_scale_query = pull_query(query_low.astype(F32))
    grad_k_raw, grad_scale_key = pull_key(key_low.astype(F32))
    raw_query_low = grad_q_raw.astype(BF)
    raw_key_low = grad_k_raw.astype(BF)
    grad_query = weight_grad(raw_query_low, group_hidden)
    grad_key = weight_grad(raw_key_low, group_hidden)
    grad_value = weight_grad(value_low, group_hidden)
    grad_hidden = grad_residual + uly_reduce(
        pull_input(raw_query_low, query_full)
        + pull_input(raw_key_low, key_full)
        + pull_input(value_low, value_full)
    )
    attn_own = lax.psum_scatter(
        jnp.concatenate(
            [
                grad.astype(BF).reshape(blk_count, attn_each, model_width)
                for grad in (grad_query, grad_key, grad_value)
            ],
            axis=1,
        ),
        "blk", scatter_dimension=0, tiled=True,
    )[0].reshape(3, attn_each, model_width).astype(F32)
    out_own = lax.psum_scatter(
        by_owner(grad_out.astype(BF)), "blk", scatter_dimension=0, tiled=True
    ).reshape(uly_count, attn_each, local_width)
    out_own = lax.all_to_all(out_own, "uly", split_axis=0, concat_axis=0, tiled=True)
    out_gradient = jnp.transpose(out_own, (1, 0, 2)).reshape(attn_each, -1).astype(F32)

    own_sums = jnp.concatenate(
        [
            (grad_scale_query + grad_scale_key).reshape(blk_count, attn_each),
            grad_up_scale.reshape(blk_count, ff_each),
            grad_gate_scale.reshape(blk_count, ff_each),
        ],
        axis=1,
    )
    alpha_sums = jnp.concatenate(
        [
            grad_alpha_attn.reshape(uly_count, blk_count, attn_each),
            grad_alpha_mlp.reshape(uly_count, blk_count, attn_each),
        ],
        axis=2,
    )
    alpha_sums = lax.all_to_all(alpha_sums, "uly", split_axis=0, concat_axis=0, tiled=True).sum(axis=0)
    sums = jnp.concatenate([own_sums, alpha_sums], axis=1)
    sums = lax.all_to_all(sums, "blk", split_axis=0, concat_axis=0, tiled=True).sum(axis=0)
    c0, c1 = attn_each, attn_each + ff_each
    c2 = c1 + ff_each
    c3 = c2 + attn_each
    return (
        layer_out,
        grad_hidden.reshape(seq_count, rows_each, model_width),
        attn_own[0],
        attn_own[1],
        attn_own[2],
        out_gradient,
        mlp_own[:ff_each].astype(F32),
        mlp_own[ff_each : 2 * ff_each].astype(F32),
        down_weight_gradient,
        sums[:c0],
        sums[c2:c3],
        sums[c3:],
        sums[c0:c1],
        sums[c1:c2],
    )


def solution(mesh):
    both = ("uly", "blk")
    rows, tokens, flat = P(both, None), P(None, both, None), P(both)
    return jax.shard_map(
        local,
        mesh=mesh,
        in_specs=(tokens, P(None, both)) + (rows,) * 7 + (flat,) * 5 + (tokens,),
        out_specs=(tokens, tokens) + (rows,) * 7 + (flat,) * 5,
        check_vma=False,
    )
```

time: 3220 us -> 1080 us (0.34)
  waiting for transfers between devices: 2680 us -> 736 us
  local copies, waits for them, and re-layouts: 112 us -> 43.8 us
  matrix products: 150 us -> 87.4 us
  blocking collectives: 180 us -> 121 us
    reduce_scatter x7 -> x8, waiting for transfers between devices: 2120 us -> 436 us  [the longest x1 152 us: local(): lax.psum_scatter(jnp.concatenate([grad_up.astype(BF).reshape(blk_count, f...]
    all_gather x9, waiting for transfers between devices: 433 us -> 285 us  [the longest x1 59.1 us: local(): lax.all_gather(down_cols, 'blk', axis=1, tiled=True)]
    unnamed x18 -> x17, waiting for transfers between devices: 101 us -> 2.13 us
    dot_general x41, matrix products: 142 us -> 79.9 us  [the longest x7 22.9 us: project(): lax.dot_general(rows, weight, (((1,), (1,)), ((), ())), preferred_element...]
    unnamed x171 -> x106, local copies, waits for them, and re-layouts: 65.6 us -> 6.59 us
    unnamed x2 -> x1, blocking collectives: 82.2 us -> 41.8 us
    all_gather x1 -> x3, blocking collectives: 68.3 us -> 68.8 us  [the longest x1 36.4 us: local(): lax.all_gather(out_cols, 'blk', axis=1, tiled=True)]
  transfers between devices with their start and end apart: 22 -> 22, of which waited for: 19 -> 19; matrix products, arithmetic and copies ran while one was open for 5% -> 6% of each run, Pallas kernels for 0% -> 0%
where the time goes in v1:
time: 1080 us; the launch traced here: 1070 us
  waiting for transfers between devices  736 us (68%)
  blocking collectives  121 us (11%)
  matrix products  87.4 us (8%)
  other arithmetic  46.8 us (4%)
  local copies, waits for them, and re-layouts  43.8 us (4%)
  starting transfers between devices  18.3 us (2%)
  between operations  15.5 us (1%)
    reduce_scatter x1, waiting for transfers between devices, local(): lax.psum_scatter(jnp.concatenate([grad_up.astype(BF).reshape(blk_count, f...  152 us
    reduce_scatter x4, waiting for transfers between devices, uly_reduce(): lax.psum_scatter(partial.astype(BF).reshape(seq_count, group_rows, model_...  87.6 us
    reduce_scatter x1, waiting for transfers between devices, local(): lax.psum_scatter(grad_pairs, 'blk', scatter_dimension=2, tiled=True)  78.5 us
    reduce_scatter x1, waiting for transfers between devices, local(): lax.psum_scatter(jnp.concatenate([grad.astype(BF).reshape(blk_count, attn...  70.7 us
    all_gather x1, waiting for transfers between devices, local(): lax.all_gather(down_cols, 'blk', axis=1, tiled=True)  59.1 us
    all_gather x1, waiting for transfers between devices, local(): gate_full = lax.all_gather(w_gate, 'blk', axis=0, tiled=True)  58.8 us
    all_gather x1, waiting for transfers between devices, local(): up_full = lax.all_gather(w_up, 'blk', axis=0, tiled=True)  58.6 us
    all_gather x4, waiting for transfers between devices, uly_gather(): lax.all_gather(rows.reshape(seq_count, rows_each, model_width), 'uly', ax...  55.6 us
  transfers between devices with their start and end apart: 22, of which 19 were waited for; matrix products, arithmetic and copies ran while one was open for 6% of the time, Pallas kernels for 0%

profile of v1, /device:TPU:0, one launch (start us, length us, event | category | flops | bytes accessed | tf_op | source)
XLA Modules:
  0.0 1069.5 jit_solution(6416626109853387073)
XLA Ops:
  9.8 6.3 all-gather.1
  16.2 3.4 concatenate.25
  19.8 41.8 %all-reduce.4 = bf16[14080]{0:T(1024)(128)(2,1)S(1)} all-reduce(bf16[14080]{0:T(1024)(128)(2,1)S(1)} %dynamic-update-slice), channel_id=2, replica_groups=mesh['uly'=4,'blk'=8] {'uly','blk'}, use_global_device_ids=true, to_apply=%add.4 | all-reduce | flops 14080 | bytes 56320
  62.2 24.9 %all-gather.12.cloned.1.call-done = bf16[3,320,1280]{2,1,0:T(8,128)(2,1)} async-done(((bf16[3,40,1280]{2,1,0:T(8,128)(2,1)}), bf16[3,320,1280]{2,1,0:T(8,128)(2,1)}) %all-gather.12.cloned.1.call-update) | async-done | bytes 2457616 | tf_op jit(solution)/shard_map/all_gather | solution.py:137
  87.1 2.2 fusion.35
  98.2 3.3 all-to-all-start
  102.2 26.2 %all_gather.41 = s32[2,2048]{1,0:T(2,128)S(1)} all-gather(s32[2,256]{1,0:T(2,128)S(1)} %bitcast.315), channel_id=1, replica_groups=mesh['uly'=4,'blk'=8] {'blk'}, dimensions={1}, use_global_device_ids=true | all-gather | bytes 18432 | tf_op jit(solution)/shard_map/all_gather | solution.py:131
  128.5 36.4 %all_gather.45 = bf16[4,320,320]{2,0,1:T(4,128)(2,1)S(1)} all-gather(bf16[4,40,320]{2,0,1:T(4,128)(2,1)S(1)} %copy.150), channel_id=1, replica_groups=mesh['uly'=4,'blk'=8] {'blk'}, dimensions={1}, use_global_device_ids=true | all-gather | bytes 921600 | tf_op jit(solution)/shard_map/all_gather | solution.py:148
  168.1 27.8 %all-gather.16.cloned.1.call-done = bf16[2,2,2048,320]{2,3,1,0:T(8,128)(2,1)} async-done(((bf16[2,2,256,320]{2,3,1,0:T(8,128)(2,1)}), bf16[2,2,2048,320]{2,3,1,0:T(8,128)(2,1)}) %all-gather.16.cloned.1.call-update) | async-done | bytes 5242896 | tf_op jit(solution)/shard_map/all_gather | solution.py:167
  195.9 20.8 %while.34 = (s32[]{:T(128)}, f32[2,5,256]{2,1,0:T(8,128)S(1)}, f32[2,5,256]{2,1,0:T(8,128)S(1)}, f32[2,256,5,64]{1,3,2,0:T(8,128)S(1)}, s32[2,2048]{1,0:T(2,128)...) while((s32[]{:T(128)}, f32[2,5,256]{2,1,0:T(8,128)S(1)}, ...), condition=%wide.region_5.6_spmd.clone, body=%wide.region_2.5_spmd.clone.sunk | while | flops 349420544 | bytes 22526168 | solution.py:202
  219.6 10.2 all_to_all.34
  231.5 14.0 %reduce-scatter.9.cloned.1.call-done = bf16[2,64,1280]{2,1,0:T(8,128)(2,1)} async-done(((bf16[2,256,1280]{2,1,0:T(8,128)(2,1)}), bf16[2,64,1280]{2,1,0:T(8,128)(2,1)}) %reduce-scatter.9.cloned.1.call-update) | async-done | bytes 327696 | tf_op jit(solution)/shard_map/reduce_scatter | solution.py:105
  248.0 2.1 fusion.55
  251.4 59.1 %all-gather.24.cloned.1.call-done = bf16[4,320,1280]{2,0,1:T(4,128)(2,1)} async-done(((bf16[4,40,1280]{2,0,1:T(4,128)(2,1)}), bf16[4,320,1280]{2,0,1:T(4,128)(2,1)}) %all-gather.24.cloned.1.call-update) | async-done | bytes 3276816 | tf_op jit(solution)/shard_map/all_gather | solution.py:149
  310.4 4.0 copy.154
  314.5 58.8 %all-gather.20.cloned.1.call-done = bf16[1280,1280]{1,0:T(8,128)(2,1)} async-done(((bf16[160,1280]{1,0:T(8,128)(2,1)}), bf16[1280,1280]{1,0:T(8,128)(2,1)}) %all-gather.20.cloned.1.call-update) | async-done | bytes 3276816 | tf_op jit(solution)/shard_map/all_gather | solution.py:151
  373.3 19.0 %all-gather.18.cloned.1.call-done = bf16[2,256,1280]{2,1,0:T(8,128)(2,1)} async-done(((bf16[2,64,1280]{2,1,0:T(8,128)(2,1)}), bf16[2,256,1280]{2,1,0:T(8,128)(2,1)}) %all-gather.18.cloned.1.call-update) | async-done | bytes 1310736 | tf_op jit(solution)/shard_map/all_gather | solution.py:99
  392.3 5.8 fusion.73
  398.1 58.6 %all-gather.22.cloned.1.call-done = bf16[1280,1280]{1,0:T(8,128)(2,1)} async-done(((bf16[160,1280]{1,0:T(8,128)(2,1)}), bf16[1280,1280]{1,0:T(8,128)(2,1)}) %all-gather.22.cloned.1.call-update) | async-done | bytes 3276816 | tf_op jit(solution)/shard_map/all_gather | solution.py:150
  456.7 6.5 multiply_convert_fusion.2
  463.2 3.0 convolution_convert_fusion.4
  466.3 25.1 %reduce-scatter.11.cloned.1.call-done = bf16[2,64,1280]{2,1,0:T(8,128)(2,1)} async-done(((bf16[2,256,1280]{2,1,0:T(8,128)(2,1)}), bf16[2,64,1280]{2,1,0:T(8,128)(2,1)}) %reduce-scatter.11.cloned.1.call-update) | async-done | bytes 327696 | tf_op jit(solution)/shard_map/reduce_scatter | solution.py:105
  494.3 2.1 fusion.53
  497.4 18.3 %all-gather.26.cloned.1.call-done = bf16[2,256,1280]{2,1,0:T(8,128)(2,1)} async-done(((bf16[2,64,1280]{2,1,0:T(8,128)(2,1)}), bf16[2,256,1280]{2,1,0:T(8,128)(2,1)}) %all-gather.26.cloned.1.call-update) | async-done | bytes 1310736 | tf_op jit(solution)/shard_map/all_gather | solution.py:99
  515.7 7.4 multiply_reduce_fusion.1
  526.5 3.0 fusion.31
  529.7 26.4 %reduce-scatter.13.cloned.1.call-done = bf16[2,64,1280]{2,1,0:T(8,128)(2,1)} async-done(((bf16[2,256,1280]{2,1,0:T(8,128)(2,1)}), bf16[2,64,1280]{2,1,0:T(8,128)(2,1)}) %reduce-scatter.13.cloned.1.call-update) | async-done | bytes 327696 | tf_op jit(solution)/shard_map/reduce_scatter | solution.py:105
  560.3 18.3 %all-gather.28.cloned.1.call-done = bf16[2,256,1280]{2,1,0:T(8,128)(2,1)} async-done(((bf16[2,64,1280]{2,1,0:T(8,128)(2,1)}), bf16[2,256,1280]{2,1,0:T(8,128)(2,1)}) %all-gather.28.cloned.1.call-update) | async-done | bytes 1310736 | tf_op jit(solution)/shard_map/all_gather | solution.py:99
  578.6 2.2 convolution_convert_fusion.10
  581.0 3.0 broadcast_in_dim.133
  584.0 33.2 %while.35 = (s32[]{:T(128)}, f32[2,256,5,64]{1,3,2,0:T(8,128)S(1)}, bf16[2,2,2048,320]{2,3,1,0:T(8,128)(2,1)}, bf16[2,2,2048,320]{2,3,1,0:T(8,128)(2,1)}, s32[2,...) while((s32[]{:T(128)}, f32[2,256,5,64]{1,3,2,0:T(8,128)S(1)}, ...), condition=%wide.region_19.20_spmd.clone, body=%wide.region_18.19_spmd.clone.sunk | while | flops 853213184 | bytes 35565800 | solution.py:281
  617.3 5.4 convolution_convert_fusion.1
  622.7 3.6 convolution_convert_fusion.2
  629.0 3.8 convolution_convert_fusion.3
  634.7 4.7 pad_maximum_fusion
  641.9 78.5 %reduce-scatter.15.cloned.1.call-done = bf16[2,2,256,320]{2,3,1,0:T(8,128)(2,1)} async-done(((bf16[2,2,2048,320]{2,3,1,0:T(8,128)(2,1)}), bf16[2,2,256,320]{2,3,1,0:T(8,128)(2,1)}) %reduce-scatter.15.cloned.1.call-update) | async-done | bytes 655376 | tf_op jit(solution)/shard_map/reduce_scatter | solution.py:284
  732.7 3.3 all-to-all-start.4
  736.1 3.7 all-to-all-done.4
  739.8 47.2 %reduce-scatter.21.cloned.1.call-done = bf16[1,160,320]{2,1,0:T(8,128)(2,1)} async-done(((bf16[8,160,320]{2,1,0:T(8,128)(2,1)}), bf16[1,160,320]{2,1,0:T(8,128)(2,1)}) %reduce-scatter.21.cloned.1.call-update) | async-done | bytes 102416 | tf_op jit(solution)/shard_map/reduce_scatter | solution.py:310
  787.0 3.3 all-to-all-start.2
  791.3 3.5 all-to-all-done.2
  794.9 3.6 all-to-all-start.5
  799.5 5.8 all-to-all-done.5
  806.5 152.4 %reduce-scatter.23.cloned.1.call-done = bf16[1,480,1280]{2,1,0:T(8,128)(2,1)} async-done(((bf16[8,480,1280]{2,1,0:T(8,128)(2,1)}), bf16[1,480,1280]{2,1,0:T(8,128)(2,1)}) %reduce-scatter.23.cloned.1.call-update) | async-done | bytes 1228816 | tf_op jit(solution)/shard_map/reduce_scatter | solution.py:229
  959.0 2.6 fusion.66
  961.6 3.5 all-to-all-start.3
  965.0 22.0 %reduce-scatter.17.cloned.1.call-done = bf16[2,64,1280]{2,1,0:T(8,128)(2,1)} async-done(((bf16[2,256,1280]{2,1,0:T(8,128)(2,1)}), bf16[2,64,1280]{2,1,0:T(8,128)(2,1)}) %reduce-scatter.17.cloned.1.call-update) | async-done | bytes 327696 | tf_op jit(solution)/shard_map/reduce_scatter | solution.py:105
  990.0 70.7 %reduce-scatter.19.cloned.1.call-done = bf16[1,120,1280]{2,1,0:T(8,128)(2,1)} async-done(((bf16[8,120,1280]{2,1,0:T(8,128)(2,1)}), bf16[1,120,1280]{2,1,0:T(8,128)(2,1)}) %reduce-scatter.19.cloned.1.call-update) | async-done | bytes 307216 | tf_op jit(solution)/shard_map/reduce_scatter | solution.py:300
  (330 shorter events, 116.7 us)
Async XLA Ops:
  7.2 55.0 %all-gather.14.cloned.1.call-start = ((), (), s32[]{:S(2)}) async-start(), calls=%async_computation.15 | async-start | bytes 1638400 | tf_op jit(solution)/shard_map/all_gather | solution.py:99
  7.9 79.2 %all-gather.12.cloned.1.call-start = ((), (), s32[]{:S(2)}) async-start(), calls=%async_computation.14 | async-start | bytes 2764800 | tf_op jit(solution)/shard_map/all_gather | solution.py:137
  9.7 186.2 %all-gather.16.cloned.1.call-start = ((), (), s32[]{:S(2)}) async-start(), calls=%async_computation.16 | async-start | bytes 5898240 | tf_op jit(solution)/shard_map/all_gather | solution.py:167
  62.2 32.1 %copy-start.26 = (f32[2,256,32]{1,2,0:T(8,128)}, f32[2,256,32]{1,2,0:T(8,128)S(1)}, u32[]{:S(2)}) copy-start(f32[2,256,32]{1,2,0:T(8,128)S(1)} %get-tuple-element.547) | copy-start | bytes 196612
  62.2 32.1 %copy-start.28 = (f32[2,256,32]{1,2,0:T(8,128)}, f32[2,256,32]{1,2,0:T(8,128)S(1)}, u32[]{:S(2)}) copy-start(f32[2,256,32]{1,2,0:T(8,128)S(1)} %get-tuple-element.548) | copy-start | bytes 196612
  62.2 27.2 %copy-start.2 = (bf16[2,256,1280]{2,1,0:T(8,128)(2,1)S(1)}, bf16[2,256,1280]{2,1,0:T(8,128)(2,1)}, u32[]{:S(2)}) copy-start(bf16[2,256,1280]{2,1,0:T(8,128)(2,1)} %all-gather.14.cloned.1.call-done) | copy-start | bytes 3932164
  94.5 73.4 %copy-start.5 = (f32[2,256,5,32]{1,3,2,0:T(8,128)}, f32[2,256,5,32]{1,3,2,0:T(8,128)S(1)}, u32[]{:S(2)}) copy-start(f32[2,256,5,32]{1,3,2,0:T(8,128)S(1)} %get-tuple-element.517) | copy-start | bytes 983044
  94.6 73.4 %copy-start.7 = (f32[2,256,5,32]{1,3,2,0:T(8,128)}, f32[2,256,5,32]{1,3,2,0:T(8,128)S(1)}, u32[]{:S(2)}) copy-start(f32[2,256,5,32]{1,3,2,0:T(8,128)S(1)} %get-tuple-element.518) | copy-start | bytes 983044
  98.2 30.3 %all-to-all-start = ((bf16[4,40,320]{2,1,0:T(8,128)(2,1)}), bf16[4,40,320]{2,1,0:T(8,128)(2,1)S(1)}, u32[]{:S(2)}, u32[]{:S(2)}) async-start(bf16[4,40,320]{2,1,0:T(8,128)(2,1)} %copy.149), calls=%async_computation | async-start | bytes 245760 | tf_op jit(solution)/shard_map/all_to_all | solution.py:140
  101.5 144.1 %reduce-scatter.9.cloned.1.call-start = ((), (), s32[]{:S(2)}) async-start(), calls=%async_computation.17 | async-start | bytes 1638400 | tf_op jit(solution)/shard_map/reduce_scatter | solution.py:105
  101.6 66.2 %copy-start.38 = (f32[5,64]{1,0:T(8,128)}, f32[5,64]{1,0:T(8,128)S(1)}, u32[]{:S(2)}) copy-start(f32[5,64]{1,0:T(8,128)S(1)} %reshape.992) | copy-start | bytes 3844
  166.1 29.8 %copy-start.18 = (f32[2,256,5,64]{1,3,2,0:T(8,128)S(1)}, f32[2,256,5,64]{1,3,2,0:T(8,128)}, u32[]{:S(2)}) copy-start(f32[2,256,5,64]{1,3,2,0:T(8,128)} %custom-call.2) | copy-start | bytes 1966084
  167.9 28.0 %copy-start.35 = (f32[2,256,5]{1,2,0:T(8,128)}, f32[2,256,5]{1,2,0:T(8,128)S(1)}, u32[]{:S(2)}) copy-start(f32[2,256,5]{1,2,0:T(8,128)S(1)} %multiply_reduce_fusion.10) | copy-start | bytes 30724
  167.9 28.0 %copy-start.31 = (f32[2,256,5]{1,2,0:T(8,128)}, f32[2,256,5]{1,2,0:T(8,128)S(1)}, u32[]{:S(2)}) copy-start(f32[2,256,5]{1,2,0:T(8,128)S(1)} %fusion.60) | copy-start | bytes 30724
  195.9 21.3 %copy-start.25 = (bf16[1280,320]{0,1:T(8,128)(2,1)S(1)}, bf16[1280,320]{0,1:T(8,128)(2,1)}, u32[]{:S(2)}) copy-start(bf16[1280,320]{0,1:T(8,128)(2,1)} %reshape.963) | copy-start | bytes 2457604
  219.1 27.6 %copy-start.1 = (bf16[2,64,1280]{2,1,0:T(8,128)(2,1)S(1)}, bf16[2,64,1280]{2,1,0:T(8,128)(2,1)}, u32[]{:S(2)}) copy-start(bf16[2,64,1280]{2,1,0:T(8,128)(2,1)} %param.19) | copy-start | bytes 983044
  219.2 91.3 %all-gather.24.cloned.1.call-start = ((), (), s32[]{:S(2)}) async-start(), calls=%async_computation.21 | async-start | bytes 3686400 | tf_op jit(solution)/shard_map/all_gather | solution.py:149
  230.7 142.5 %all-gather.20.cloned.1.call-start = ((), (), s32[]{:S(2)}) async-start(), calls=%async_computation.19 | async-start | bytes 3686400 | tf_op jit(solution)/shard_map/all_gather | solution.py:151
  231.3 161.0 %all-gather.18.cloned.1.call-start = ((), (), s32[]{:S(2)}) async-start(), calls=%async_computation.18 | async-start | bytes 1638400 | tf_op jit(solution)/shard_map/all_gather | solution.py:99
  250.1 206.6 %all-gather.22.cloned.1.call-start = ((), (), s32[]{:S(2)}) async-start(), calls=%async_computation.20 | async-start | bytes 3686400 | tf_op jit(solution)/shard_map/all_gather | solution.py:150
  250.9 240.6 %reduce-scatter.11.cloned.1.call-start = ((), (), s32[]{:S(2)}) async-start(), calls=%async_computation.22 | async-start | bytes 1638400 | tf_op jit(solution)/shard_map/reduce_scatter | solution.py:105
  392.3 64.4 %copy-start.43 = (bf16[2,256,1280]{2,1,0:T(8,128)(2,1)S(1)}, bf16[2,256,1280]{2,1,0:T(8,128)(2,1)}, u32[]{:S(2)}) copy-start(bf16[2,256,1280]{2,1,0:T(8,128)(2,1)} %all-gather.18.cloned.1.call-done) | copy-start | bytes 3932164
  456.7 6.5 copy-start.14
  463.2 29.5 %copy-start = (bf16[2,64,1280]{2,1,0:T(8,128)(2,1)S(1)}, bf16[2,64,1280]{2,1,0:T(8,128)(2,1)}, u32[]{:S(2)}) copy-start(bf16[2,64,1280]{2,1,0:T(8,128)(2,1)} %reduce-scatter.9.cloned.1.call-done) | copy-start | bytes 983044
  463.2 29.5 %copy-start.21 = (bf16[2,64,1280]{2,1,0:T(8,128)(2,1)S(1)}, bf16[2,64,1280]{2,1,0:T(8,128)(2,1)}, u32[]{:S(2)}) copy-start(bf16[2,64,1280]{2,1,0:T(8,128)(2,1)} %param.33) | copy-start | bytes 983044
  466.2 49.5 %all-gather.26.cloned.1.call-start = ((), (), s32[]{:S(2)}) async-start(), calls=%async_computation.23 | async-start | bytes 1638400 | tf_op jit(solution)/shard_map/all_gather | solution.py:99
  491.5 4.9 copy-start.4
  497.3 58.8 %reduce-scatter.13.cloned.1.call-start = ((), (), s32[]{:S(2)}) async-start(), calls=%async_computation.24 | async-start | bytes 1638400 | tf_op jit(solution)/shard_map/reduce_scatter | solution.py:105
  515.7 7.4 copy-start.42
  529.4 49.2 %all-gather.28.cloned.1.call-start = ((), (), s32[]{:S(2)}) async-start(), calls=%async_computation.25 | async-start | bytes 1638400 | tf_op jit(solution)/shard_map/all_gather | solution.py:99
  560.2 160.1 %reduce-scatter.15.cloned.1.call-start = ((), (), s32[]{:S(2)}) async-start(), calls=%async_computation.26 | async-start | bytes 5898240 | tf_op jit(solution)/shard_map/reduce_scatter | solution.py:284
  617.2 169.8 %reduce-scatter.21.cloned.1.call-start = ((), (), s32[]{:S(2)}) async-start(), calls=%async_computation.29 | async-start | bytes 1105920 | tf_op jit(solution)/shard_map/reduce_scatter | solution.py:310
  617.3 5.5 copy-start.44
  617.3 5.5 copy-start.46
  628.7 330.3 %reduce-scatter.23.cloned.1.call-start = ((), (), s32[]{:S(2)}) async-start(), calls=%async_computation.30 | async-start | bytes 11059200 | tf_op jit(solution)/shard_map/reduce_scatter | solution.py:229
  629.0 3.8 copy-start.15
  639.5 347.6 %reduce-scatter.17.cloned.1.call-start = ((), (), s32[]{:S(2)}) async-start(), calls=%async_computation.27 | async-start | bytes 1638400 | tf_op jit(solution)/shard_map/reduce_scatter | solution.py:105
  640.8 81.2 %copy-start.10 = (f32[2,256,5,32]{1,3,2,0:T(8,128)S(1)}, f32[2,256,5,32]{1,3,2,0:T(8,128)}, u32[]{:S(2)}) copy-start(f32[2,256,5,32]{1,3,2,0:T(8,128)} %copy-done.9) | copy-start | bytes 983044
  640.8 81.2 %copy-start.12 = (f32[2,256,5,32]{1,3,2,0:T(8,128)S(1)}, f32[2,256,5,32]{1,3,2,0:T(8,128)}, u32[]{:S(2)}) copy-start(f32[2,256,5,32]{1,3,2,0:T(8,128)} %copy-done.11) | copy-start | bytes 983044
  640.8 81.2 %copy-start.39 = (f32[5,64]{1,0:T(8,128)S(1)}, f32[5,64]{1,0:T(8,128)}, u32[]{:S(2)}) copy-start(f32[5,64]{1,0:T(8,128)} %copy-done.38) | copy-start | bytes 3844
  641.8 80.3 %copy-start.34 = (f32[2,256,5]{1,2,0:T(8,128)S(1)}, f32[2,256,5]{1,2,0:T(8,128)}, u32[]{:S(2)}) copy-start(f32[2,256,5]{1,2,0:T(8,128)} %copy-done.33) | copy-start | bytes 30724
  728.3 332.4 %reduce-scatter.19.cloned.1.call-start = ((), (), s32[]{:S(2)}) async-start(), calls=%async_computation.28 | async-start | bytes 2764800 | tf_op jit(solution)/shard_map/reduce_scatter | solution.py:300
  731.8 58.6 %copy-start.16 = (f32[1,2,256,320]{2,3,1,0:T(8,128)S(1)}, f32[1,2,256,320]{2,3,1,0:T(8,128)}, u32[]{:S(2)}) copy-start(f32[1,2,256,320]{2,3,1,0:T(8,128)} %get-tuple-element.521) | copy-start | bytes 1966084
  731.8 58.6 %copy-start.20 = (bf16[2,2,256,320]{2,3,1,0:T(8,128)(2,1)S(1)}, bf16[2,2,256,320]{2,3,1,0:T(8,128)(2,1)}, u32[]{:S(2)}) copy-start(bf16[2,2,256,320]{2,3,1,0:T(8,128)(2,1)} %reduce-scatter.15.cloned.1.call-done) | copy-start | bytes 1966084
  732.7 7.1 all-to-all-start.4
  787.0 7.8 all-to-all-start.2
  794.9 10.4 all-to-all-start.5
  961.6 27.4 %all-to-all-start.3 = ((bf16[4,40,1280]{2,1,0:T(8,128)(2,1)}), bf16[4,40,1280]{2,1,0:T(8,128)(2,1)S(1)}, u32[]{:S(2)}, u32[]{:S(2)}) async-start(bf16[4,40,1280]{2,1,0:T(8,128)(2,1)} %bitcast.45), calls=%async_computation.11 | async-start | bytes 819200 | tf_op jit(solution)/shard_map/all_to_all | solution.py:240
  (23 other events, 41.5 us)
Sparse Core Ops, SparseCore 0:
  9.6 21.2 all-gather.13
  33.7 53.3 all-gather.11
  97.4 98.4 all-gather.15
  219.3 26.2 reduce-scatter.8
  248.4 61.9 all-gather.23
  312.7 60.5 all-gather.19
  375.5 16.7 all-gather.17
  394.7 61.9 all-gather.21
  466.3 25.1 reduce-scatter.10
  497.4 18.1 all-gather.25
  529.5 26.5 reduce-scatter.12
  560.4 18.1 all-gather.27
  617.3 102.9 reduce-scatter.14
  723.9 63.0 reduce-scatter.20
  790.5 168.3 reduce-scatter.22
  961.3 25.6 reduce-scatter.16
  991.0 69.6 reduce-scatter.18

commit v2 on v1

v2 whole, which is shorter than its diff:
```python
import functools

import jax
import jax.numpy as jnp
from jax import lax
from jax.experimental import pallas as pl
from jax.experimental.pallas import tpu as pltpu
from jax.sharding import Mesh
from jax.sharding import PartitionSpec as P

D = 1280
HEADS = 20
HEAD_DIM = 64
AXES = ("far", "core", "line", "side")
PLANE = ("far", "core", "side")
VMEM_BYTES = 60 * 1024 * 1024

rotary_base = 10000.0
tiny_eps = 1e-06
BF = jnp.bfloat16
F32 = jnp.float32


def place():
    return tuple(lax.axis_index(name) for name in AXES)


def remote(src, dst, send, recv, device):
    return pltpu.make_async_remote_copy(
        src_ref=src,
        dst_ref=dst,
        send_sem=send,
        recv_sem=recv,
        device_id=device,
        device_id_type=pl.DeviceIdType.MESH,
    )


def signal_to(device):
    pl.semaphore_signal(
        pltpu.get_barrier_semaphore(), inc=1, device_id=device, device_id_type=pl.DeviceIdType.MESH
    )


def greet(devices, maybe=()):
    count = len(devices)
    for device in devices:
        signal_to(device)
    for there, device in maybe:
        pl.when(there)(functools.partial(signal_to, device))
        count = count + jnp.where(there, 1, 0)
    pl.semaphore_wait(pltpu.get_barrier_semaphore(), count)


def params(collective_id):
    return pltpu.CompilerParams(
        collective_id=collective_id, has_side_effects=True, vmem_limit_bytes=VMEM_BYTES
    )


class UlyGather:
    sems = staticmethod(lambda parts: [pltpu.SemaphoreType.DMA((3, parts))] * 2 + [pltpu.SemaphoreType.DMA((parts,))])

    def __init__(self, x, o, send, recv, local):
        y, c, z, s = place()
        u, v = y * 2 + c, (1 - y) * 2 + c
        mate, across = (y, 1 - c, z, s), (1 - y, c, z, s)
        self.parts = x.shape[0]
        parts = range(self.parts)
        self.far = [remote(x.at[i], o.at[i, u], send.at[0, i], recv.at[0, i], across) for i in parts]
        self.near = [remote(x.at[i], o.at[i, u], send.at[1, i], recv.at[1, i], mate) for i in parts]
        self.on = [remote(o.at[i, v], o.at[i, v], send.at[2, i], recv.at[2, i], mate) for i in parts]
        self.own = [pltpu.make_async_copy(x.at[i], o.at[i, u], local.at[i]) for i in parts]

    def start_part(self, i):
        self.far[i].start()
        self.near[i].start()
        self.own[i].start()

    def start(self):
        for i in range(self.parts):
            self.start_part(i)

    def forward(self):
        for i in range(self.parts):
            self.far[i].wait_recv()
            self.on[i].start()

    def finish(self):
        for i in range(self.parts):
            self.near[i].wait_recv()
            self.on[i].wait_recv()
            self.own[i].wait()
            self.far[i].wait_send()
            self.near[i].wait_send()
            self.on[i].wait_send()


def uly_peers():
    y, c, z, s = place()
    return [(y, 1 - c, z, s), (1 - y, c, z, s)]


def add_low(*terms):
    total = terms[0].astype(F32)
    for term in terms[1:]:
        total = total + term.astype(F32)
    return total


class UlyReduce:
    @staticmethod
    def scratch(x):
        parts, _, rows, width = x.shape
        return [
            pltpu.VMEM((parts, 2, rows, width), x.dtype),
            pltpu.VMEM((parts, rows, width), x.dtype),
            pltpu.VMEM((parts, rows, width), x.dtype),
            pltpu.SemaphoreType.DMA((3, parts)),
            pltpu.SemaphoreType.DMA((3, parts)),
        ]

    def __init__(self, x, near, mid, far_in, send, recv):
        y, c, z, s = place()
        mate, across = uly_peers()
        self.x, self.near_ref, self.mid, self.far_in = x, near, mid, far_in
        self.y, self.c, self.parts = y, c, x.shape[0]
        parts = range(self.parts)
        self.near = [
            [
                remote(x.at[i, f * 2 + 1 - c], near.at[i, k], send.at[k, i], recv.at[k, i], mate)
                for k, f in enumerate((1 - y, y))
            ]
            for i in parts
        ]
        self.far = [remote(mid.at[i], far_in.at[i], send.at[2, i], recv.at[2, i], across) for i in parts]

    def start(self):
        for i in range(self.parts):
            for copy in self.near[i]:
                copy.start()

    def middle(self):
        for i in range(self.parts):
            self.near[i][0].wait_recv()
            self.mid[i] = add_low(self.x[i, (1 - self.y) * 2 + self.c], self.near_ref[i, 0]).astype(BF)
            self.far[i].start()

    def result(self, i):
        self.near[i][1].wait_recv()
        self.far[i].wait_recv()
        return add_low(self.x[i, self.y * 2 + self.c], self.near_ref[i, 1], self.far_in[i])

    def finish(self):
        for i in range(self.parts):
            for copy in self.near[i] + [self.far[i]]:
                copy.wait_send()


def plane_peers():
    y, c, z, s = place()
    return [(y, 1 - c, z, s), (1 - y, c, z, s), (y, c, z, 1 - s)]


def plane_index(y, c, s):
    return (y * 2 + c) * 2 + s


class PlaneGather:
    sems = [pltpu.SemaphoreType.DMA((14,))] * 2 + [pltpu.SemaphoreType.DMA((2,))]

    def __init__(self, x, o, send, recv, local):
        y, c, z, s = place()
        mate, across, cross = plane_peers()
        me, py, px, pd = (
            plane_index(y, c, s),
            plane_index(1 - y, c, s),
            plane_index(y, c, 1 - s),
            plane_index(1 - y, c, 1 - s),
        )

        def copy(source, target, slot, device):
            return remote(source, target, send.at[slot], recv.at[slot], device)

        def on(p, i, slot, device):
            return copy(o.at[p, i], o.at[p, i], slot, device)

        self.by_y = [copy(x.at[i], o.at[me, i], i, across) for i in (0, 1)]
        self.by_x = [copy(x.at[i], o.at[me, i], 2 + i, cross) for i in (0, 1)]
        self.near = [copy(x.at[i], o.at[me, i], 4 + i, mate) for i in (0, 1)]
        self.corner = [on(py, 0, 6, cross), on(px, 1, 7, across)]
        self.pass_y = [on(py, 0, 8, mate), on(py, 1, 10, mate)]
        self.pass_x = [on(px, 0, 11, mate), on(px, 1, 9, mate)]
        self.pass_d = [on(pd, 0, 12, mate), on(pd, 1, 13, mate)]
        self.own = [pltpu.make_async_copy(x.at[i], o.at[me, i], local.at[i]) for i in (0, 1)]

    def start_part(self, i):
        for copy in (self.by_y[i], self.by_x[i], self.near[i], self.own[i]):
            copy.start()

    def forward_part(self, i):
        first, then = ((self.by_y, self.pass_y), (self.by_x, self.pass_x))[:: 1 - 2 * i]
        first[0][i].wait_recv()
        self.corner[i].start()
        first[1][i].start()
        then[0][i].wait_recv()
        then[1][i].start()

    def finish(self):
        for i in (0, 1):
            self.corner[i].wait_recv()
            self.pass_d[i].start()
        for i in (0, 1):
            for copy in (self.near[i], self.pass_y[i], self.pass_x[i], self.pass_d[i]):
                copy.wait()
            for copy in (self.by_y[i], self.by_x[i], self.corner[i]):
                copy.wait_send()
            self.own[i].wait()


class PlaneReduce:
    @staticmethod
    def scratch(x):
        one = pltpu.VMEM(x.shape[1:], x.dtype)
        return [pltpu.VMEM((4,) + x.shape[1:], x.dtype)] + [one] * 6 + [pltpu.SemaphoreType.DMA((14,))] * 2

    def __init__(self, x, near, out_x, out_y, out_d, in_x, in_y, in_d, send, recv):
        y, c, z, s = place()
        mate, across, cross = plane_peers()
        self.c = c
        self.spots = ((1 - y, 1 - s), (y, 1 - s), (1 - y, s), (y, s))
        self.x, self.near_ref = x, near
        self.out_x, self.out_y, self.out_d = out_x, out_y, out_d
        self.in_x, self.in_y, self.in_d = in_x, in_y, in_d

        def copy(source, target, slot, device):
            return remote(source, target, send.at[slot], recv.at[slot], device)

        self.near = [
            [copy(x.at[plane_index(sy, 1 - c, ss), i], near.at[k, i], 2 * k + i, mate) for i in (0, 1)]
            for k, (sy, ss) in enumerate(self.spots)
        ]
        self.corner = [
            copy(out_d.at[0], in_d.at[0], 8, cross),
            copy(out_d.at[1], in_d.at[1], 9, across),
        ]
        self.by_x = [copy(out_x.at[i], in_x.at[i], 10 + i, cross) for i in (0, 1)]
        self.by_y = [copy(out_y.at[i], in_y.at[i], 12 + i, across) for i in (0, 1)]

    def pair(self, k, i):
        sy, ss = self.spots[k]
        self.near[k][i].wait_recv()
        return add_low(self.x[plane_index(sy, self.c, ss), i], self.near_ref[k, i])

    def start(self):
        for spot in self.near:
            for copy in spot:
                copy.start()

    def middle(self):
        for i in (0, 1):
            self.out_d[i] = self.pair(0, i).astype(BF)
            self.corner[i].start()
        self.out_x[0] = self.pair(1, 0).astype(BF)
        self.by_x[0].start()
        self.out_y[1] = self.pair(2, 1).astype(BF)
        self.by_y[1].start()

    def last(self):
        part = self.pair(2, 0)
        self.corner[0].wait_recv()
        self.out_y[0] = (part + self.in_d[0].astype(F32)).astype(BF)
        self.by_y[0].start()
        part = self.pair(1, 1)
        self.corner[1].wait_recv()
        self.out_x[1] = (part + self.in_d[1].astype(F32)).astype(BF)
        self.by_x[1].start()

    def result(self, i):
        own = self.pair(3, i)
        self.by_x[i].wait_recv()
        self.by_y[i].wait_recv()
        return own + add_low(self.in_x[i], self.in_y[i])

    def finish(self):
        for copy in [c for spot in self.near for c in spot] + self.corner + self.by_x + self.by_y:
            copy.wait_send()


def plane_corners():
    y, c, z, s = place()
    return [
        (y, 1 - c, s), (1 - y, c, s), (1 - y, 1 - c, s),
        (y, c, 1 - s), (y, 1 - c, 1 - s), (1 - y, c, 1 - s), (1 - y, 1 - c, 1 - s),
    ]


def line_ends(n_line):
    y, c, z, s = place()
    return (z > 0, (y, c, z - 1, s)), (z < n_line - 1, (y, c, z + 1, s)), (y, c, z, 1 - s)


class BlkGather:
    @staticmethod
    def sems(n_line):
        return [
            pltpu.SemaphoreType.DMA((3,)),
            pltpu.SemaphoreType.DMA((1,)),
            pltpu.SemaphoreType.DMA((4, n_line)),
            pltpu.SemaphoreType.DMA((4, n_line)),
            pltpu.SemaphoreType.DMA((1,)),
        ]

    def __init__(self, n_line, pick_x, pick_o, own_send, own_recv, send, recv, local):
        y, c, z, s = place()
        self.z, self.s, self.n = z, s, n_line
        (self.has_low, self.low), (self.has_high, self.high), self.cross = line_ends(n_line)
        self.pick_x, self.pick_o = pick_x, pick_o
        self.sem = (own_send, own_recv, send, recv, local)

    def block(self, way, k):
        z = self.z - k if way == 0 else self.z + k
        return self.pick_o(z * 2 + self.s)

    def own(self, way):
        own_send, own_recv, send, recv, local = self.sem
        arrival = own_recv.at[0] if way == 2 else recv.at[way, 0]
        target = (self.high, self.low, self.cross)[way]
        return remote(self.pick_x(), self.pick_o(self.z * 2 + self.s), own_send.at[way], arrival, target)

    def keep(self):
        return pltpu.make_async_copy(self.pick_x(), self.pick_o(self.z * 2 + self.s), self.sem[4].at[0])

    def onward(self, way, k):
        send, recv = self.sem[2:4]
        target = self.high if way == 0 else self.low
        return remote(self.block(way, k), self.block(way, k), send.at[way, k], recv.at[way, k], target)

    def over(self, way, k):
        send, recv = self.sem[2:4]
        return remote(self.block(way, k), self.block(way, k), send.at[2 + way, k], recv.at[2 + way, k], self.cross)

    def arrive(self, way, k):
        send, recv = self.sem[2:4]
        return remote(self.block(way, k), self.block(way, k), send.at[way, k], recv.at[way, k - 1], self.cross)

    def there(self, way, k):
        return self.z >= k if way == 0 else self.z + k < self.n

    def start(self):
        pl.when(self.has_high)(lambda: self.own(0).start())
        pl.when(self.has_low)(lambda: self.own(1).start())
        self.own(2).start()
        self.keep().start()

    def step(self, k):
        for way in (0, 1):
            @pl.when(self.there(way, k))
            def _():
                self.arrive(way, k).wait_recv()

                @pl.when((self.has_high, self.has_low)[way])
                def _():
                    self.onward(way, k).start()

                self.over(way, k).start()

    def finish_arrivals(self):
        self.own(2).wait_recv()
        for k in range(1, self.n):
            for way in (0, 1):
                pl.when(self.there(way, k))(lambda: self.over(way, k).wait_recv())
        self.keep().wait()

    def finish_sends(self):
        pl.when(self.has_high)(lambda: self.own(0).wait_send())
        pl.when(self.has_low)(lambda: self.own(1).wait_send())
        self.own(2).wait_send()
        for k in range(1, self.n):
            for way in (0, 1):
                @pl.when(self.there(way, k))
                def _():
                    self.over(way, k).wait_send()

                    @pl.when((self.has_high, self.has_low)[way])
                    def _():
                        self.onward(way, k).wait_send()


def blk_greet(n_line):
    low, high, cross = line_ends(n_line)
    greet([cross], [low, high])


def blk_gather_kernel(n_line, count, *refs):
    ins, outs, sems = refs[:count], refs[count : 2 * count], refs[2 * count :]
    blk_greet(n_line)
    jobs, at = [], 0
    for x, o in zip(ins, outs):
        for i in range(x.shape[0]):
            jobs.append(
                BlkGather(
                    n_line,
                    lambda x=x, i=i: x.at[i],
                    lambda block, o=o, i=i: o.at[block, i],
                    *sems[5 * at : 5 * at + 5],
                )
            )
            at += 1
    for job in jobs:
        job.start()
    for k in range(1, n_line):
        for job in jobs:
            job.step(k)
    for job in jobs:
        job.finish_arrivals()
    for job in jobs:
        job.finish_sends()


def blk_gather(n_line, *arrays):
    count = len(arrays)
    chunks = sum(a.shape[0] for a in arrays)
    return pl.pallas_call(
        functools.partial(blk_gather_kernel, n_line, count),
        out_shape=[jax.ShapeDtypeStruct((2 * n_line,) + a.shape, a.dtype) for a in arrays],
        in_specs=[pl.BlockSpec(memory_space=pltpu.VMEM)] * count,
        out_specs=[pl.BlockSpec(memory_space=pl.ANY)] * count,
        scratch_shapes=BlkGather.sems(n_line) * chunks,
        compiler_params=params(5),
        cost_estimate=pl.CostEstimate(flops=0, bytes_accessed=70 * 3_000_000, transcendentals=0),
        name="blk_gather",
    )(*arrays)


class BlkReduce:
    @staticmethod
    def scratch(n_line, a):
        return [
            pltpu.VMEM((n_line,) + a.shape[1:], a.dtype),
            pltpu.VMEM((n_line + 1,) + a.shape[1:], a.dtype),
            pltpu.SemaphoreType.DMA((n_line,)),
            pltpu.SemaphoreType.DMA((n_line,)),
            pltpu.SemaphoreType.DMA((2, n_line)),
            pltpu.SemaphoreType.DMA((2, n_line)),
        ]

    def __init__(self, n_line, x, side_in, line_in, side_send, side_recv, send, recv):
        y, c, self.z, self.s = place()
        self.n = n_line
        (self.has_low, self.low), (self.has_high, self.high), self.cross = line_ends(n_line)
        self.x, self.side_in, self.line_in = x, side_in, line_in
        self.sem = (side_send, side_recv, send, recv)

    def spot(self, way, k):
        return self.z + k if way == 0 else self.z - k

    def exists(self, way, k):
        return self.z + k < self.n if way == 0 else self.z >= k

    def side(self, zz):
        side_send, side_recv = self.sem[:2]
        return remote(
            self.x.at[zz * 2 + 1 - self.s], self.side_in.at[zz], side_send.at[zz], side_recv.at[zz], self.cross
        )

    def slot(self, way, k):
        return self.n if way == 1 and k == 0 else self.spot(way, k)

    def move(self, way, k):
        send, recv = self.sem[2:]
        target = self.high if way == 0 else self.low
        zz = self.spot(way, k)
        there = self.n if way == 1 and k == 1 else zz
        return remote(
            self.side_in.at[zz], self.line_in.at[there], send.at[way, k], recv.at[way, k - 1], target
        )

    def arrive(self, way, k):
        send, recv = self.sem[2:]
        there = self.line_in.at[self.slot(way, k)]
        return remote(there, there, send.at[way, k], recv.at[way, k], self.cross)

    def start(self, k):
        for way in (0, 1) if k > 0 else (0,):
            pl.when(self.exists(way, k))(lambda: self.side(self.spot(way, k)).start())

    def step(self, k):
        for way in (0, 1):
            @pl.when(self.exists(way, k))
            def _():
                zz = self.spot(way, k)
                self.side(zz).wait_recv()
                passed = self.has_low if way == 0 else self.has_high

                @pl.when(passed)
                def _():
                    self.arrive(way, k).wait_recv()
                    self.side_in[zz] = add_low(
                        self.x[zz * 2 + self.s], self.side_in[zz], self.line_in[zz]
                    ).astype(self.side_in.dtype)

                @pl.when(jnp.logical_not(passed))
                def _():
                    self.side_in[zz] = add_low(self.x[zz * 2 + self.s], self.side_in[zz]).astype(
                        self.side_in.dtype
                    )

                self.move(way, k).start()

    def result(self, o):
        z = self.z
        self.side(z).wait_recv()
        pl.when(self.has_low)(lambda: self.arrive(0, 0).wait_recv())
        pl.when(self.has_high)(lambda: self.arrive(1, 0).wait_recv())
        own = add_low(self.x[z * 2 + self.s], self.side_in[z])

        @pl.when(jnp.logical_and(self.has_low, self.has_high))
        def _():
            o[...] = (own + add_low(self.line_in[z], self.line_in[self.n])).astype(o.dtype)

        @pl.when(jnp.logical_not(self.has_low))
        def _():
            o[...] = (own + self.line_in[self.n].astype(F32)).astype(o.dtype)

        @pl.when(jnp.logical_not(self.has_high))
        def _():
            o[...] = (own + self.line_in[z].astype(F32)).astype(o.dtype)

    def finish(self):
        for k in range(self.n - 1, -1, -1):
            for way in (0, 1) if k > 0 else (0,):
                @pl.when(self.exists(way, k))
                def _():
                    self.side(self.spot(way, k)).wait_send()
                    if k > 0:
                        self.move(way, k).wait_send()


def blk_reduce_kernel(n_line, count, *refs):
    ins, outs, scratch = refs[:count], refs[count : 2 * count], refs[2 * count :]
    blk_greet(n_line)
    jobs, places = [], []
    for x, o in zip(ins, outs):
        for i in range(x.shape[1]):
            at = 6 * len(jobs)
            jobs.append(BlkReduce(n_line, x.at[:, i], *scratch[at : at + 6]))
            places.append(o.at[i])
    for k in range(n_line - 1, -1, -1):
        for job in jobs:
            job.start(k)
    for k in range(n_line - 1, 0, -1):
        for job in jobs:
            job.step(k)
    for job, o in zip(jobs, places):
        job.result(o)
    for job in jobs:
        job.finish()


def blk_reduce(n_line, *arrays):
    count, scratch = len(arrays), []
    for x in arrays:
        one = jax.ShapeDtypeStruct(x.shape[:1] + x.shape[2:], x.dtype)
        scratch += BlkReduce.scratch(n_line, one) * x.shape[1]
    return pl.pallas_call(
        functools.partial(blk_reduce_kernel, n_line, count),
        out_shape=[jax.ShapeDtypeStruct(x.shape[1:], x.dtype) for x in arrays],
        in_specs=[pl.BlockSpec(memory_space=pltpu.VMEM)] * count,
        out_specs=[pl.BlockSpec(memory_space=pltpu.VMEM)] * count,
        scratch_shapes=scratch,
        compiler_params=params(7),
        cost_estimate=pl.CostEstimate(flops=0, bytes_accessed=70 * 3_000_000, transcendentals=0),
        name="blk_reduce",
    )(*arrays)


def exit_kernel(
    n_line, gq, gk, gv, gh, res, oc, dc, alpha, rest,
    gq_o, gk_o, gv_o, gh_o, oc_o, dc_o, sum_o,
    alpha_in, line_out, line_all, oc_s, oc_r, dc_s, dc_r, al_s, al_r, su_s, su_r, keep, *scratch,
):
    y, c, z, s = place()
    u, p, b, n_blk = y * 2 + c, plane_index(y, c, s), z * 2 + s, 2 * n_line
    low, high, cross = line_ends(n_line)
    corners = plane_corners()
    others = []
    for i in range(1, n_blk):
        to = lax.rem(b + i, n_blk)
        others.append((y, c, to // 2, lax.rem(to, 2)))
    once = [(to[3] != 1 - s) | (to[2] != z) for to in others]
    greet([(yy, cc, z, ss) for yy, cc, ss in corners], list(zip(once, others)))
    heads = 6
    jobs = [BlkReduce(n_line, x, *scratch[heads * i : heads * (i + 1)]) for i, x in enumerate((gq, gk, gv))]
    hid = UlyReduce(gh, *scratch[heads * 3 :])
    small, cols = [], []
    for k, (yy, cc, ss) in enumerate(corners):
        target = (yy, cc, z, ss)
        cols.append(remote(dc.at[plane_index(yy, cc, ss)], dc_o.at[p], dc_s.at[k], dc_r.at[k], target))
        if k < 3:
            cols.append(remote(oc.at[yy * 2 + cc], oc_o.at[u], oc_s.at[k], oc_r.at[k], target))
            small.append(remote(alpha.at[yy * 2 + cc], alpha_in.at[k], al_s.at[k], al_r.at[k], target))
    for job in small:
        job.start()
    hid.start()
    for k in range(n_line - 1, -1, -1):
        for job in jobs:
            job.start(k)
    mine = [
        pltpu.make_async_copy(dc.at[p], dc_o.at[p], keep.at[0]),
        pltpu.make_async_copy(oc.at[u], oc_o.at[u], keep.at[1]),
    ]
    for job in mine:
        job.start()
    hid.middle()
    for job in cols:
        job.start()
    for job in small:
        job.wait_recv()
    line_out[...] = rest[...]
    line_out[:, :, :128] = rest[:, :, :128] + alpha[u] + alpha_in[0] + alpha_in[1] + alpha_in[2]
    line_jobs = []
    for i in range(1, n_blk):
        to = lax.rem(b + i, n_blk)
        line_jobs.append(
            remote(line_out.at[to], line_all.at[i - 1], su_s.at[i - 1], su_r.at[i - 1], others[i - 1])
        )
    for job in line_jobs:
        job.start()
    for k in range(n_line - 1, 0, -1):
        for job in jobs:
            job.step(k)
    for i in range(gh.shape[0]):
        gh_o[i] = res[i] + hid.result(i)
    total = line_out[b]
    for i, job in enumerate(line_jobs):
        job.wait_recv()
        total = total + line_all[i]
    sum_o[...] = total
    for job, o in zip(jobs, (gq_o, gk_o, gv_o)):
        job.result(o)
    hid.finish()
    for job in jobs:
        job.finish()
    for job in line_jobs + small:
        job.wait_send()
    for job in cols + mine:
        job.wait()


def leave(n_line, gq, gk, gv, gh, res, oc, dc, alpha, rest):
    n_blk = 2 * n_line
    vmem = pl.BlockSpec(memory_space=pltpu.VMEM)
    dma = pltpu.SemaphoreType.DMA
    scratch = [
        pltpu.VMEM((3,) + alpha.shape[1:], F32),
        pltpu.VMEM(rest.shape, F32),
        pltpu.VMEM((n_blk - 1,) + rest.shape[1:], F32),
        dma((3,)), dma((3,)), dma((7,)), dma((7,)), dma((3,)), dma((3,)),
        dma((n_blk - 1,)), dma((n_blk - 1,)), dma((2,)),
    ]
    for g in (gq, gk, gv):
        scratch += BlkReduce.scratch(n_line, g)
    scratch += UlyReduce.scratch(gh)
    grad = jax.ShapeDtypeStruct(gq.shape[1:], F32)
    return pl.pallas_call(
        functools.partial(exit_kernel, n_line),
        out_shape=[
            grad, grad, grad,
            jax.ShapeDtypeStruct(res.shape, F32),
            jax.ShapeDtypeStruct(oc.shape, oc.dtype),
            jax.ShapeDtypeStruct(dc.shape, dc.dtype),
            jax.ShapeDtypeStruct(rest.shape[1:], F32),
        ],
        in_specs=[vmem] * 9,
        out_specs=[vmem] * 7,
        scratch_shapes=scratch,
        compiler_params=params(8),
        cost_estimate=pl.CostEstimate(flops=0, bytes_accessed=40 * 3_000_000, transcendentals=0),
        name="leave",
    )(gq, gk, gv, gh, res, oc, dc, alpha, rest)


def entry_kernel(
    n_line, hid, small, wq, wk, wv, oc, dc, hid_o, small_o, wq_o, wk_o, wv_o, oc_o, dc_o, *sems
):
    y, c, z, s = place()
    u, p = y * 2 + c, plane_index(y, c, s)
    low, high, cross = line_ends(n_line)
    corners = plane_corners()
    greet([(yy, cc, z, ss) for yy, cc, ss in corners], [low, high])
    hid_job = UlyGather(hid, hid_o, *sems[:3])
    at, jobs = 3, []
    for x, pick in (
        (small, lambda block: small_o.at[u, block]),
        (wq, lambda block: wq_o.at[block]),
        (wk, lambda block: wk_o.at[block]),
        (wv, lambda block: wv_o.at[block]),
    ):
        jobs.append(BlkGather(n_line, lambda x=x: x, pick, *sems[at : at + 5]))
        at += 5
    oc_s, oc_r, dc_s, dc_r, sm_s, sm_r, keep = sems[at:]
    jobs[0].start()
    for job in jobs[1:]:
        job.start()
    hid_job.start()
    col_jobs = []
    for k, (yy, cc, ss) in enumerate(corners):
        target = (yy, cc, z, ss)
        col_jobs.append(
            remote(dc.at[plane_index(yy, cc, ss)], dc_o.at[p], dc_s.at[k], dc_r.at[k], target)
        )
        if k < 3:
            col_jobs.append(remote(oc.at[yy * 2 + cc], oc_o.at[u], oc_s.at[k], oc_r.at[k], target))
    for job in col_jobs:
        job.start()
    mine = [
        pltpu.make_async_copy(dc.at[p], dc_o.at[p], keep.at[0]),
        pltpu.make_async_copy(oc.at[u], oc_o.at[u], keep.at[1]),
    ]
    for job in mine:
        job.start()
    for k in range(1, n_line):
        for job in jobs:
            job.step(k)
        if k == 1:
            hid_job.forward()
    jobs[0].finish_arrivals()
    small_jobs = [
        remote(small_o.at[u], small_o.at[u], sm_s.at[k], sm_r.at[k], (yy, cc, z, ss))
        for k, (yy, cc, ss) in enumerate(corners[:3])
    ]
    for job in small_jobs:
        job.start()
    for job in jobs[1:]:
        job.finish_arrivals()
    hid_job.finish()
    for job in small_jobs + col_jobs:
        job.wait()
    for job in mine:
        job.wait()
    for job in jobs:
        job.finish_sends()


def entry(n_line, hid, small, wq, wk, wv, oc, dc):
    n_blk = 2 * n_line
    parts = hid.shape[0]
    vmem, anyway = pl.BlockSpec(memory_space=pltpu.VMEM), pl.BlockSpec(memory_space=pl.ANY)

    def out(shape, like):
        return jax.ShapeDtypeStruct(shape, like.dtype)

    return pl.pallas_call(
        functools.partial(entry_kernel, n_line),
        out_shape=[
            out((parts, 4) + hid.shape[1:], hid),
            out((4, n_blk) + small.shape, small),
            out((n_blk,) + wq.shape, wq),
            out((n_blk,) + wk.shape, wk),
            out((n_blk,) + wv.shape, wv),
            out(oc.shape, oc),
            out(dc.shape, dc),
        ],
        in_specs=[vmem] * 7,
        out_specs=[vmem, vmem, anyway, anyway, anyway, vmem, vmem],
        scratch_shapes=UlyGather.sems(parts)
        + BlkGather.sems(n_line) * 4
        + [pltpu.SemaphoreType.DMA((3,))] * 2
        + [pltpu.SemaphoreType.DMA((7,))] * 2
        + [pltpu.SemaphoreType.DMA((3,))] * 2
        + [pltpu.SemaphoreType.DMA((2,))],
        compiler_params=params(6),
        cost_estimate=pl.CostEstimate(flops=0, bytes_accessed=40 * 3_000_000, transcendentals=0),
        name="entry",
    )(hid, small, wq, wk, wv, oc, dc)
def dot_nt(a, b):
    return lax.dot_general(a, b, (((1,), (1,)), ((), ())), preferred_element_type=F32)


def dot_nn(a, b):
    return lax.dot_general(a, b, (((1,), (0,)), ((), ())), preferred_element_type=F32)


def dot_tn(a, b):
    return lax.dot_general(a, b, (((0,), (0,)), ((), ())), preferred_element_type=F32)


def lanes_of(shape):
    return lax.broadcasted_iota(jnp.int32, shape, len(shape) - 1)


def halves(x):
    row = lax.broadcasted_iota(jnp.int32, (128, 128), 0) // HEAD_DIM
    same = jnp.where(row == lanes_of((128, 128)) // HEAD_DIM, 1.0, 0.0).astype(BF)
    high = x.astype(BF)
    rest = (x - high.astype(F32)).astype(BF)
    return dot_nn(high, same) + dot_nn(rest, same)


def turn(x):
    first = lanes_of(x.shape) % HEAD_DIM < HEAD_DIM // 2
    return jnp.where(first, pltpu.roll(x, 128 - 32, 1), pltpu.roll(x, 32, 1))


def heads_kernel(x_ref, wq_ref, wk_ref, wv_ref, cos_ref, sin_ref, scale_ref, qz_ref, kv_ref, y_ref, c_ref):
    x = x_ref[...]
    wqk = jnp.concatenate([wq_ref[0], wk_ref[0]], axis=0)
    wv = wv_ref[0]
    raw = dot_nt(x, wqk)
    value = dot_nt(x, jnp.concatenate([jnp.zeros_like(wv), wv], axis=0))
    low = lanes_of(raw.shape) < HEAD_DIM
    turned = raw * cos_ref[...] + turn(raw) * sin_ref[...]
    c = lax.rsqrt(halves(turned * turned) + HEAD_DIM * tiny_eps)
    y = turned * c
    both = y * scale_ref[0]
    qz_ref[...] = jnp.where(low, both, 0.0).astype(BF)
    kv_ref[...] = jnp.where(low, pltpu.roll(both, HEAD_DIM, 1), value).astype(BF)
    y_ref[...] = y
    c_ref[...] = c


def heads_forward(x, wq, wk, wv, cos, sin, scale):
    rows, width = x.shape
    heads = wq.shape[0]
    whole = lambda shape: pl.BlockSpec(shape, lambda h: (0,) * len(shape))
    weight = pl.BlockSpec((1, HEAD_DIM, width), lambda h: (h, 0, 0))
    head = pl.BlockSpec((rows, 128), lambda h: (0, h))
    wide = lambda dtype: jax.ShapeDtypeStruct((rows, heads * 128), dtype)
    return pl.pallas_call(
        heads_kernel,
        grid=(heads,),
        out_shape=[wide(BF), wide(BF), wide(F32), wide(F32)],
        in_specs=[whole((rows, width)), weight, weight, weight, whole((rows, 128)), whole((rows, 128)),
                  pl.BlockSpec((1, 1, 128), lambda h: (h, 0, 0))],
        out_specs=[head] * 4,
        compiler_params=pltpu.CompilerParams(vmem_limit_bytes=VMEM_BYTES),
        cost_estimate=pl.CostEstimate(flops=rows * width * heads * 384, bytes_accessed=rows * width * 8, transcendentals=0),
        name="heads_forward",
    )(x, wq, wk, wv, cos, sin, scale)


def attend_kernel(blocks, q_ref, kv_ref, qp_ref, kp_ref, o_ref, low_ref, inv_ref):
    q = q_ref[0]
    rows = q.shape[0]
    acc = jnp.zeros((rows, 128), F32)
    total = jnp.zeros((rows, 128), F32)
    q_place = qp_ref[0]

    def step(b, state):
        acc, total = state
        kv = kv_ref[b, 0]
        allowed = kp_ref[0, b] <= q_place
        p = jnp.where(allowed, jnp.exp(dot_nt(q, kv)), 0.0)
        for i in range(p.shape[1] // 128):
            total = total + p[:, i * 128 : (i + 1) * 128]
        return acc + dot_nn(p.astype(BF), kv), total

    if blocks <= 8:
        for b in range(blocks):
            acc, total = step(b, (acc, total))
    else:
        acc, total = lax.fori_loop(0, blocks, step, (acc, total))
    inverse = 1.0 / jnp.broadcast_to(jnp.sum(total, axis=-1, keepdims=True), (rows, 128))
    out = acc * inverse
    o_ref[0] = out
    low_ref[0] = out.astype(BF)
    inv_ref[0, 0] = jnp.transpose(inverse)[:8]


def attend(q, kv, q_places, k_places):
    seqs, rows, wide = q.shape
    blocks, heads = kv.shape[0], wide // 128
    mine = pl.BlockSpec((1, rows, 128), lambda s, h: (s, 0, h))
    return pl.pallas_call(
        functools.partial(attend_kernel, blocks),
        grid=(seqs, heads),
        out_shape=[
            jax.ShapeDtypeStruct(q.shape, F32),
            jax.ShapeDtypeStruct(q.shape, BF),
            jax.ShapeDtypeStruct((seqs, heads, 8, rows), F32),
        ],
        in_specs=[
            mine,
            pl.BlockSpec((blocks, 1, rows, 128), lambda s, h: (0, s, 0, h)),
            pl.BlockSpec((1, rows, 1), lambda s, h: (s, 0, 0)),
            pl.BlockSpec((1, blocks, 1, rows), lambda s, h: (s, 0, 0, 0)),
        ],
        out_specs=[mine, mine, pl.BlockSpec((1, 1, 8, rows), lambda s, h: (s, h, 0, 0))],
        compiler_params=pltpu.CompilerParams(vmem_limit_bytes=VMEM_BYTES),
        cost_estimate=pl.CostEstimate(
            flops=4 * blocks * seqs * rows * rows * wide, bytes_accessed=2 * blocks * seqs * rows * wide,
            transcendentals=blocks * seqs * rows * rows * heads,
        ),
        name="attend",
    )(q, kv, q_places, k_places)


def attend_back_kernel(blocks, q_ref, d_ref, o_ref, inv_ref, kv_ref, qp_ref, kp_ref, dq_ref, dkv_ref):
    q, d = q_ref[0], d_ref[0]
    rows = q.shape[0]
    delta = jnp.sum(d.astype(F32) * o_ref[0], axis=-1, keepdims=True)
    delta = jnp.transpose(jnp.broadcast_to(delta, (rows, 128)))[:1]
    inverse = inv_ref[0, 0][:1]
    pair = jnp.concatenate([q, d], axis=0)
    q_place = qp_ref[0]

    def step(b, dq):
        kv = kv_ref[b, 0]
        scores = dot_nt(kv, pair)
        allowed = kp_ref[0, b] <= q_place
        p = jnp.where(allowed, jnp.exp(scores[:, :rows]) * inverse, 0.0)
        ds = (p * (scores[:, rows:] - delta)).astype(BF)
        dkv_ref[b, 0] = dot_nn(jnp.concatenate([ds, p.astype(BF)], axis=1), pair).astype(BF)
        return dq + dot_tn(ds, kv)

    dq = jnp.zeros((rows, 128), F32)
    if blocks <= 8:
        for b in range(blocks):
            dq = step(b, dq)
    else:
        dq = lax.fori_loop(0, blocks, step, dq)
    dq_ref[0] = dq.astype(BF)


def attend_back(q, d, o, inv, kv, q_places, k_places):
    seqs, rows, wide = q.shape
    blocks, heads = kv.shape[0], wide // 128
    mine = pl.BlockSpec((1, rows, 128), lambda s, h: (s, 0, h))
    keys = pl.BlockSpec((blocks, 1, rows, 128), lambda s, h: (0, s, 0, h))
    return pl.pallas_call(
        functools.partial(attend_back_kernel, blocks),
        grid=(seqs, heads),
        out_shape=[jax.ShapeDtypeStruct(q.shape, BF), jax.ShapeDtypeStruct(kv.shape, BF)],
        in_specs=[
            mine, mine, mine,
            pl.BlockSpec((1, 1, 8, rows), lambda s, h: (s, h, 0, 0)),
            keys,
            pl.BlockSpec((1, 1, rows), lambda s, h: (s, 0, 0)),
            pl.BlockSpec((1, blocks, rows, 1), lambda s, h: (s, 0, 0, 0)),
        ],
        out_specs=[mine, keys],
        compiler_params=pltpu.CompilerParams(vmem_limit_bytes=VMEM_BYTES),
        cost_estimate=pl.CostEstimate(
            flops=10 * blocks * seqs * rows * rows * wide, bytes_accessed=4 * blocks * seqs * rows * wide,
            transcendentals=blocks * seqs * rows * rows * heads,
        ),
        name="attend_back",
    )(q, d, o, inv, kv, q_places, k_places)


def heads_back_kernel(
    x_ref, dq_ref, dkv_ref, y_ref, c_ref, cos_ref, sin_ref, scale_ref, wq_ref, wk_ref, wv_ref,
    gq_ref, gk_ref, gv_ref, gs_ref, gh_ref, acc_ref,
):
    h = pl.program_id(0)
    dq, dkv = dq_ref[...], dkv_ref[...]
    low = lanes_of(dq.shape) < HEAD_DIM
    dy = jnp.where(low, dq.astype(F32), pltpu.roll(dkv.astype(F32), HEAD_DIM, 1))
    y = y_ref[...]
    factor = jnp.where(lanes_of((1, 128)) < HEAD_DIM, HEAD_DIM**0.5, 1.0)
    gs_ref[0] = jnp.sum(dy * y, axis=0, keepdims=True) * factor
    dy = dy * scale_ref[0]
    dr = c_ref[...] * (dy - y * halves(y * dy))
    raw = (dr * cos_ref[...] - turn(dr) * sin_ref[...]).astype(BF)
    x = x_ref[...]
    grad = dot_tn(raw, x)
    gq_ref[0] = grad[:HEAD_DIM].astype(BF)
    gk_ref[0] = grad[HEAD_DIM:].astype(BF)
    value = jnp.where(low, jnp.zeros_like(dkv), dkv)
    gv_ref[0] = dot_tn(value, x)[HEAD_DIM:].astype(BF)
    wqk = jnp.concatenate([wq_ref[0], wk_ref[0]], axis=0)
    wv = wv_ref[0]
    more = dot_nn(raw, wqk) + dot_nn(value, jnp.concatenate([jnp.zeros_like(wv), wv], axis=0))

    @pl.when(h == 0)
    def _():
        acc_ref[...] = more

    @pl.when(h > 0)
    def _():
        acc_ref[...] = acc_ref[...] + more

    @pl.when(h == pl.num_programs(0) - 1)
    def _():
        gh_ref[...] = acc_ref[...].astype(BF)


def heads_back(x, dq, dkv, y, c, cos, sin, scale, wq, wk, wv):
    rows, width = x.shape
    heads = wq.shape[0]
    whole = lambda shape: pl.BlockSpec(shape, lambda h: (0,) * len(shape))
    weight = pl.BlockSpec((1, HEAD_DIM, width), lambda h: (h, 0, 0))
    head = pl.BlockSpec((rows, 128), lambda h: (0, h))
    row = pl.BlockSpec((1, 1, 128), lambda h: (h, 0, 0))
    return pl.pallas_call(
        heads_back_kernel,
        grid=(heads,),
        out_shape=[jax.ShapeDtypeStruct(wq.shape, BF)] * 3
        + [jax.ShapeDtypeStruct((heads, 1, 128), F32), jax.ShapeDtypeStruct((rows, width), BF)],
        in_specs=[whole((rows, width))] + [head] * 4 + [whole((rows, 128))] * 2 + [row] + [weight] * 3,
        out_specs=[weight] * 3 + [row, whole((rows, width))],
        scratch_shapes=[pltpu.VMEM((rows, width), F32)],
        compiler_params=pltpu.CompilerParams(vmem_limit_bytes=VMEM_BYTES),
        cost_estimate=pl.CostEstimate(flops=rows * width * heads * 1024, bytes_accessed=rows * width * 12, transcendentals=0),
        name="heads_back",
    )(x, dq, dkv, y, c, cos, sin, scale, wq, wk, wv)


def ff_kernel(x_ref, wu_ref, wg_ref, us_ref, gs_ref, inner_ref, up_ref, gate_ref):
    x = x_ref[...]
    up = dot_nt(x, wu_ref[...])
    gate = dot_nt(x, wg_ref[...])
    z = gate * gs_ref[...] * D**0.5
    inner_ref[...] = (z / (1.0 + jnp.exp(-z)) * (up * us_ref[...])).astype(BF)
    up_ref[...] = up
    gate_ref[...] = gate


def ff_forward(x, wu, wg, us, gs):
    rows, width = x.shape
    columns = wu.shape[0]
    block = rows // 4
    whole = lambda a: pl.BlockSpec(a.shape, lambda i: (0, 0))
    part = lambda n: pl.BlockSpec((block, n), lambda i: (i, 0))
    out = lambda dtype: jax.ShapeDtypeStruct((rows, columns), dtype)
    return pl.pallas_call(
        ff_kernel,
        grid=(4,),
        out_shape=[out(BF), out(F32), out(F32)],
        in_specs=[part(width)] + [whole(a) for a in (wu, wg, us, gs)],
        out_specs=[part(columns)] * 3,
        compiler_params=pltpu.CompilerParams(vmem_limit_bytes=VMEM_BYTES),
        cost_estimate=pl.CostEstimate(
            flops=4 * rows * width * columns, bytes_accessed=2 * rows * width + 10 * rows * columns,
            transcendentals=rows * columns,
        ),
        name="ff_forward",
    )(x, wu, wg, us, gs)


def ff_back_kernel(d_ref, wd_ref, up_ref, gate_ref, us_ref, gs_ref, du_ref, dg_ref, sum_ref):
    d = dot_nn(d_ref[...], wd_ref[...])
    up, gate = up_ref[...], gate_ref[...]
    us, gs = us_ref[...], gs_ref[...] * D**0.5
    z = gate * gs
    sig = 1.0 / (1.0 + jnp.exp(-z))
    du = d * (z * sig)
    dz = d * (up * us) * sig * (1.0 + z * (1.0 - sig))
    du_ref[...] = (du * us).astype(BF)
    dg_ref[...] = (dz * gs).astype(BF)
    sums = jnp.concatenate(
        [
            jnp.sum(du * up, axis=0, keepdims=True),
            jnp.sum(dz * gate, axis=0, keepdims=True) * D**0.5,
        ],
        axis=0,
    )
    i = pl.program_id(0)

    @pl.when(i == 0)
    def _():
        sum_ref[...] = sums

    @pl.when(i > 0)
    def _():
        sum_ref[...] = sum_ref[...] + sums


def ff_back(d, wd, up, gate, us, gs):
    rows, width = d.shape
    columns = wd.shape[1]
    block = rows // 4
    whole = lambda a: pl.BlockSpec(a.shape, lambda i: (0, 0))
    part = lambda n: pl.BlockSpec((block, n), lambda i: (i, 0))
    out = jax.ShapeDtypeStruct((rows, columns), BF)
    return pl.pallas_call(
        ff_back_kernel,
        grid=(4,),
        out_shape=[out, out, jax.ShapeDtypeStruct((2, columns), F32)],
        in_specs=[part(width), whole(wd), part(columns), part(columns), whole(us), whole(gs)],
        out_specs=[part(columns), part(columns), pl.BlockSpec((2, columns), lambda i: (0, 0))],
        compiler_params=pltpu.CompilerParams(vmem_limit_bytes=VMEM_BYTES),
        cost_estimate=pl.CostEstimate(
            flops=2 * rows * width * columns, bytes_accessed=2 * rows * width + 14 * rows * columns,
            transcendentals=rows * columns,
        ),
        name="ff_back",
    )(d, wd, up, gate, us, gs)


def unit_of(x):
    c = lax.rsqrt(jnp.sum(x * x, axis=-1, keepdims=True) + x.shape[-1] * tiny_eps)
    return x * c, c


def unit_back(y, c, dy):
    return c * (dy - y * jnp.sum(y * dy, axis=-1, keepdims=True))


def comm_call(kernel, name, collective_id, args, outs, scratch, micros):
    vmem = pl.BlockSpec(memory_space=pltpu.VMEM)
    return pl.pallas_call(
        kernel,
        out_shape=[jax.ShapeDtypeStruct(shape, dtype) for shape, dtype in outs],
        in_specs=[vmem] * len(args),
        out_specs=[vmem] * len(outs),
        scratch_shapes=scratch,
        compiler_params=params(collective_id),
        cost_estimate=pl.CostEstimate(flops=0, bytes_accessed=micros * 3_000_000, transcendentals=0),
        name=name,
    )(*args)


def attn_joint_kernel(mixed, w, hid, rate, first_o, ua_o, ca_o, cv_o, all_o, part, low, *scratch):
    mate, across, cross = plane_peers()
    greet([mate, across, cross])
    split = len(UlyReduce.scratch(part))
    job = UlyReduce(part, *scratch[:split])
    out = PlaneGather(low, all_o, *scratch[split:])
    seqs, _, rows, width = part.shape
    for i in range(seqs):
        part[i] = dot_nt(mixed[i], w[...]).astype(BF).reshape(4, rows, width)
        for copy in job.near[i]:
            copy.start()
    job.middle()
    for i in range(seqs):
        ua, ca = unit_of(job.result(i))
        h = hid[i].astype(F32)
        first, cv = unit_of(h + rate[...] * (ua - h))
        low[i] = first.astype(BF)
        out.start_part(i)
        first_o[i], ua_o[i] = first, ua
        ca_o[i] = jnp.broadcast_to(ca, (rows, 128))
        cv_o[i] = jnp.broadcast_to(cv, (rows, 128))
        if i > 0:
            out.forward_part(i - 1)
    out.forward_part(seqs - 1)
    out.finish()
    job.finish()


def attn_joint(mixed, w, hid, rate):
    seqs, rows, width = hid.shape
    part = jax.ShapeDtypeStruct((seqs, 4, rows, width), BF)
    thin = ((seqs, rows, 128), F32)
    return comm_call(
        attn_joint_kernel, "attn_joint", 1, (mixed, w, hid, rate),
        [(hid.shape, F32), (hid.shape, F32), thin, thin, ((8, seqs, rows, width), BF)],
        [pltpu.VMEM(part.shape, BF), pltpu.VMEM(hid.shape, BF)] + UlyReduce.scratch(part) + PlaneGather.sems,
        25,
    )


def plane_products(job, part, c, product):
    _, seqs, rows, width = part.shape
    for cc, first in ((1 - c, True), (c, False)):
        got = product(cc).astype(BF).reshape(2, 2, seqs, rows, width)
        for yy in (0, 1):
            for ss in (0, 1):
                part[plane_index(yy, cc, ss)] = got[yy, ss]
        if first:
            job.start()


def ff_joint_kernel(inner, w, first, rate, cot, out_o, d1_o, sum_o, all_o, part, low, *scratch):
    y, c, z, s = place()
    greet(plane_peers())
    split = len(PlaneReduce.scratch(part))
    job = PlaneReduce(part, *scratch[:split])
    out = PlaneGather(low, all_o, *scratch[split:])
    _, seqs, rows, width = part.shape
    columns = inner.shape[-1]
    plane_products(
        job, part, c, lambda cc: dot_nt(inner[:, cc].reshape(4 * seqs * rows, columns), w[...])
    )
    job.middle()
    job.last()
    for i in range(seqs):
        ub, cb = unit_of(job.result(i))
        f, b = first[i], rate[...]
        o, cw = unit_of(f + b * (ub - f))
        dw = unit_back(o, cw, cot[i].astype(F32))
        step = b * dw
        low[i] = unit_back(ub, cb, step).astype(BF)
        out.start_part(i)
        out_o[i] = o.astype(BF)
        d1_o[i] = dw - step
        total = jnp.sum(dw * (ub - f), axis=0, keepdims=True)
        sum_o[...] = total if i == 0 else sum_o[...] + total
        if i > 0:
            out.forward_part(i - 1)
    out.forward_part(seqs - 1)
    out.finish()
    job.finish()


def ff_joint(inner, w, first, rate, cot):
    seqs, rows, width = first.shape
    part = jax.ShapeDtypeStruct((8, seqs, rows, width), BF)
    return comm_call(
        ff_joint_kernel, "ff_joint", 2,
        (inner.reshape(2, 2, 2, seqs * rows, inner.shape[-1]), w, first, rate, cot),
        [(first.shape, BF), (first.shape, F32), ((1, width), F32), (part.shape, BF)],
        [pltpu.VMEM(part.shape, BF), pltpu.VMEM(first.shape, BF)] + PlaneReduce.scratch(part) + PlaneGather.sems,
        30,
    )


def back_joint_kernel(
    du, dg, wu, wg, d1, first, ua, ca, cv, hid, rate, res_o, sum_o, all_o, part, low, *scratch
):
    y, c, z, s = place()
    greet(plane_peers())
    split = len(PlaneReduce.scratch(part))
    job = PlaneReduce(part, *scratch[:split])
    out = UlyGather(low, all_o, *scratch[split:])
    _, seqs, rows, width = part.shape
    columns = du.shape[-1]
    tokens = 8 * seqs * rows
    half = lambda ref, cc: ref[:, cc].reshape(tokens // 2, columns)
    plane_products(
        job, part, c, lambda cc: dot_nn(half(du, cc), wu[...]) + dot_nn(half(dg, cc), wg[...])
    )
    job.middle()
    job.last()
    for i in range(seqs):
        f, h, u, a = first[i], hid[i].astype(F32), ua[i], rate[...]
        dv = unit_back(f, cv[i][:, :1], d1[i] + job.result(i))
        step = a * dv
        low[i] = unit_back(u, ca[i][:, :1], step).astype(BF)
        out.start_part(i)
        res_o[i] = dv - step
        total = jnp.sum(dv * (u - h), axis=0, keepdims=True)
        sum_o[...] = total if i == 0 else sum_o[...] + total
    out.forward()
    out.finish()
    job.finish()


def back_joint(du, dg, wu, wg, d1, first, ua, ca, cv, hid, rate):
    seqs, rows, width = first.shape
    part = jax.ShapeDtypeStruct((8, seqs, rows, width), BF)
    wide = lambda a: a.reshape(2, 2, 2, seqs * rows, a.shape[-1])
    return comm_call(
        back_joint_kernel, "back_joint", 3,
        (wide(du), wide(dg), wu, wg, d1, first, ua, ca, cv, hid, rate),
        [(first.shape, F32), ((1, width), F32), ((seqs, 4, rows, width), BF)],
        [pltpu.VMEM(part.shape, BF), pltpu.VMEM(first.shape, BF)]
        + PlaneReduce.scratch(part) + UlyGather.sems(seqs),
        30,
    )


def down_grad_kernel(d_ref, inner_ref, o_ref):
    grad = dot_tn(d_ref[...], inner_ref[...]).astype(BF)
    n_line, groups, each, _ = o_ref.shape
    for v in range(groups):
        for k in range(n_line):
            at = (v * n_line + k) * each
            o_ref[k, v] = grad[at : at + each]


def down_grad(n_line, d, inner):
    rows, width = d.shape
    columns = inner.shape[1]
    each = width // (4 * n_line)
    return pl.pallas_call(
        down_grad_kernel,
        grid=(2,),
        out_shape=jax.ShapeDtypeStruct((n_line, 4, each, columns), BF),
        in_specs=[
            pl.BlockSpec((rows, width // 2), lambda i: (0, i)),
            pl.BlockSpec((rows, columns), lambda i: (0, 0)),
        ],
        out_specs=pl.BlockSpec((n_line, 2, each, columns), lambda i: (0, i, 0, 0)),
        compiler_params=pltpu.CompilerParams(vmem_limit_bytes=VMEM_BYTES),
        cost_estimate=pl.CostEstimate(flops=2 * rows * width * columns, bytes_accessed=8_000_000, transcendentals=0),
        name="down_grad",
    )(d, inner)


def ff_grad_kernel(du_ref, dg_ref, x_ref, o_ref):
    n_line, both, _ = o_ref.shape
    each = both // 2
    for j, ref in enumerate((du_ref, dg_ref)):
        grad = dot_tn(ref[...], x_ref[...]).astype(BF)
        for k in range(n_line):
            o_ref[k, j * each : (j + 1) * each] = grad[k * each : (k + 1) * each]


def ff_grad(n_line, du, dg, x):
    rows, width = x.shape
    columns = du.shape[1]
    whole = pl.BlockSpec((rows, columns), lambda i: (0, 0))
    shape = (n_line, 2 * columns // n_line, width)
    return pl.pallas_call(
        ff_grad_kernel,
        grid=(2,),
        out_shape=jax.ShapeDtypeStruct(shape, BF),
        in_specs=[whole, whole, pl.BlockSpec((rows, width // 2), lambda i: (0, i))],
        out_specs=pl.BlockSpec(shape[:2] + (width // 2,), lambda i: (0, 0, i)),
        compiler_params=pltpu.CompilerParams(vmem_limit_bytes=VMEM_BYTES),
        cost_estimate=pl.CostEstimate(flops=4 * rows * width * columns, bytes_accessed=10_000_000, transcendentals=0),
        name="ff_grad",
    )(du, dg, x)
def local(
    hidden, positions, w_query, w_key, w_value, w_out, w_up, w_gate, w_down,
    qk_scale, alpha_attn, alpha_mlp, up_scale, gate_scale, cotangent,
):
    seqs, rows_each, width = hidden.shape
    n_line = lax.axis_size("line")
    n_blk = 2 * n_line
    heads = HEADS // 4
    local_width = heads * HEAD_DIM
    group_rows = 4 * rows_each
    tokens = seqs * rows_each
    group_tokens = 4 * tokens
    plane_tokens = 8 * tokens
    attn_each, ff_each = w_query.shape[0], w_up.shape[0]
    ff_local = ff_each * n_line
    far, core, line, side = place()
    uly = far * 2 + core

    pieces = [v.astype(F32) for v in (qk_scale, alpha_attn, alpha_mlp, up_scale, gate_scale)]
    pieces.append(positions.reshape(-1).astype(F32))
    used = sum(v.shape[0] for v in pieces)
    room, at, small = used + -used % 1024, 0, 0.0
    for v in pieces:
        small = small + jnp.pad(v, (at, room - at - v.shape[0]))
        at += v.shape[0]
    small = small.reshape(-1, 128)

    out_send = jnp.transpose(w_out.reshape(attn_each, 4, local_width), (1, 0, 2))
    down_send = jnp.transpose(
        w_down.reshape(attn_each, 4, n_line, 2, ff_each), (1, 3, 0, 2, 4)
    ).reshape(8, attn_each, ff_local)

    up_full = lax.all_gather(w_up, "line", axis=0, tiled=True)

    hid_all, small_all, wq_all, wk_all, wv_all, out_cols, down_cols = entry(
        n_line, hidden, small, w_query, w_key, w_value, out_send, down_send
    )
    w_gate, up_full, hid_all = lax.optimization_barrier((w_gate, up_full, hid_all))
    gate_full = lax.all_gather(w_gate, "line", axis=0, tiled=True)

    flat = small_all.reshape(4, n_blk, -1)
    cut = [0, attn_each, 2 * attn_each, 3 * attn_each, 3 * attn_each + ff_each, 3 * attn_each + 2 * ff_each, used]
    own = lax.dynamic_slice_in_dim(flat, uly, 1, 0)[0]
    scale_wide = own[:, : cut[1]].reshape(heads, HEAD_DIM)
    attn_rate = flat[:, :, cut[1] : cut[2]].reshape(-1)
    mlp_rate = flat[:, :, cut[2] : cut[3]].reshape(-1)
    mine = lax.dynamic_slice_in_dim(own.reshape(n_line, 2, -1), side, 1, 1)[:, 0]
    up_wide = mine[:, cut[3] : cut[4]].reshape(-1)
    gate_wide = mine[:, cut[4] : cut[5]].reshape(-1)
    places = jnp.transpose(
        flat[:, :, cut[5] : cut[6]].astype(jnp.int32).reshape(4, n_blk, seqs, rows_each), (2, 1, 0, 3)
    ).reshape(seqs, n_blk, group_rows)
    q_places = lax.dynamic_slice_in_dim(places, line * 2 + side, 1, 1)[:, 0]

    lane = jnp.arange(128) % HEAD_DIM
    freqs = rotary_base ** (-((lane % 32).astype(F32) * (2.0 / HEAD_DIM)))
    angles = q_places.reshape(group_tokens, 1).astype(F32) * freqs
    cos = jnp.cos(angles)
    sin = jnp.where(lane < 32, -1.0, 1.0) * jnp.sin(angles)
    scale_both = jnp.concatenate([scale_wide * HEAD_DIM**0.5, scale_wide], axis=1)[:, None]

    group_hidden = hid_all.reshape(group_tokens, width)
    wq = wq_all.reshape(heads, HEAD_DIM, width)
    wk = wk_all.reshape(heads, HEAD_DIM, width)
    wv = wv_all.reshape(heads, HEAD_DIM, width)
    qz, kv, y_both, c_both = heads_forward(group_hidden, wq, wk, wv, cos, sin, scale_both)
    qz = qz.reshape(seqs, group_rows, heads * 128)

    kv_all, out_all = blk_gather(
        n_line, kv.reshape(seqs, group_rows, heads * 128), out_cols.reshape(1, 4 * attn_each, local_width)
    )
    kv_all, out_all, gate_full, down_cols = lax.optimization_barrier(
        (kv_all, out_all, gate_full, down_cols)
    )
    down_all = lax.all_gather(down_cols.reshape(8 * attn_each, ff_local), "line", axis=0, tiled=False)
    down_full = jnp.transpose(
        down_all.reshape(n_line, 4, 2, attn_each, ff_local), (1, 0, 2, 3, 4)
    ).reshape(width, ff_local)

    out_full = jnp.transpose(
        out_all.reshape(n_blk, 4, attn_each, local_width), (1, 0, 2, 3)
    ).reshape(width, local_width)

    attended, mixed, inverse = attend(qz, kv_all, q_places[:, :, None], places[:, :, None, :])
    mixed = mixed.reshape(group_tokens, heads, 128)[:, :, HEAD_DIM:].reshape(
        seqs, group_rows, local_width
    )

    first, unit_att, att_c, first_c, mlp_in = attn_joint(mixed, out_full, hidden, attn_rate[None])
    mlp_in = mlp_in.reshape(plane_tokens, width)
    inner, up_rows, gate_rows = ff_forward(mlp_in, up_full, gate_full, up_wide[None], gate_wide[None])
    layer_out, grad_first, grad_alpha_mlp, branch_low = ff_joint(
        inner, down_full, first, mlp_rate[None], cotangent
    )
    branch_low = branch_low.reshape(plane_tokens, width)
    grad_down = down_grad(n_line, branch_low, inner)
    down_own = lax.psum_scatter(
        grad_down.reshape(n_line, 8 * attn_each, ff_local), "line", scatter_dimension=0, tiled=True
    ).reshape(8, attn_each, ff_local)
    up_low, gate_low, ff_scales = ff_back(
        branch_low, down_full, up_rows, gate_rows, up_wide[None], gate_wide[None]
    )
    grad_up_scale, grad_gate_scale = ff_scales[0], ff_scales[1]
    grad_ug = ff_grad(n_line, up_low, gate_low, mlp_in)
    mlp_own = lax.psum_scatter(grad_ug, "line", scatter_dimension=0, tiled=True)[0]
    up_low, grad_ug = lax.optimization_barrier((up_low, grad_ug))
    grad_residual, grad_alpha_attn, att_low = back_joint(
        up_low, gate_low, up_full, gate_full, grad_first, first, unit_att, att_c, first_c,
        hidden, attn_rate[None],
    )

    att_low = att_low.reshape(group_tokens, width)
    grad_mixed = jnp.pad(
        dot_nn(att_low, out_full).astype(BF).reshape(seqs, group_rows, heads, HEAD_DIM),
        ((0, 0), (0, 0), (0, 0), (HEAD_DIM, 0)),
    ).reshape(seqs, group_rows, heads * 128)
    grad_out = (
        dot_tn(att_low, mixed.reshape(group_tokens, local_width))
        .astype(BF)
        .reshape(4, n_blk, attn_each, local_width)
    )
    grad_out = jnp.transpose(grad_out, (1, 0, 2, 3)).reshape(n_blk, 1, 4 * attn_each, local_width)
    dq, dkv_all = attend_back(
        qz, grad_mixed, attended, inverse, kv_all, q_places[:, None, :], places[..., None]
    )
    dkv, out_own = blk_reduce(n_line, dkv_all, grad_out)
    out_own = out_own.reshape(4, attn_each, local_width)
    gq, gk, gv, gs, gh = heads_back(
        group_hidden, dq.reshape(group_tokens, -1), dkv.reshape(group_tokens, -1), y_both, c_both,
        cos, sin, scale_both, wq, wk, wv,
    )
    def row(x, wide):
        return jnp.pad(x, ((0, 0),) * (x.ndim - 1) + ((0, wide - x.shape[-1]),))

    alpha = jnp.concatenate(
        [grad_alpha_attn.reshape(4, n_blk, attn_each), grad_alpha_mlp.reshape(4, n_blk, attn_each)], axis=2
    )
    grad_scale = gs[:, 0, :HEAD_DIM] + gs[:, 0, HEAD_DIM:]
    ff_sums = jnp.concatenate(
        [grad_up_scale.reshape(n_line, ff_each), grad_gate_scale.reshape(n_line, ff_each)], axis=1
    )
    sides = (jnp.arange(2) == side)[None, :, None]
    ff_sums = jnp.where(sides, ff_sums[:, None], 0.0).reshape(n_blk, 2 * ff_each)
    rest = jnp.concatenate(
        [jnp.zeros((n_blk, 128), F32), row(grad_scale.reshape(n_blk, attn_each), 128), row(ff_sums, 384)], axis=1
    )
    mlp_own = mlp_own.astype(F32)
    gq, gk, gv, grad_hidden, out_own, down_own, sums = leave(
        n_line,
        *(g.reshape(n_blk, attn_each, width) for g in (gq, gk, gv)),
        gh.reshape(seqs, 4, rows_each, width),
        grad_residual,
        out_own, down_own, row(alpha, 128)[:, :, None], rest[:, None],
    )
    out_gradient = jnp.transpose(out_own, (1, 0, 2)).reshape(attn_each, width).astype(F32)
    down_gradient = jnp.transpose(
        down_own.reshape(4, 2, attn_each, n_line, ff_each), (2, 0, 3, 1, 4)
    ).reshape(attn_each, -1).astype(F32)
    sums = sums[0]
    return (
        layer_out,
        grad_hidden,
        gq,
        gk,
        gv,
        out_gradient,
        mlp_own[:ff_each],
        mlp_own[ff_each:],
        down_gradient,
        sums[128 : 128 + attn_each],
        sums[:attn_each],
        sums[attn_each : 2 * attn_each],
        sums[256 : 256 + ff_each],
        sums[256 + ff_each : 256 + 2 * ff_each],
    )


def solution(mesh):
    far = mesh.shape["uly"] // 2
    line = mesh.shape["blk"] // 2
    finer = Mesh(mesh.devices.reshape(far, 2, line, 2), AXES)
    rows, tokens, flat = P(AXES, None), P(None, AXES, None), P(AXES)
    return jax.shard_map(
        local,
        mesh=finer,
        in_specs=(tokens, P(None, AXES)) + (rows,) * 7 + (flat,) * 5 + (tokens,),
        out_specs=(tokens, tokens) + (rows,) * 7 + (flat,) * 5,
        check_vma=False,
    )
```

time: 1080 us -> 520 us (0.48)
  waiting for transfers between devices: 736 us -> 0.79 us
  Pallas kernels: 0 us -> 451 us
  blocking collectives: 121 us -> 0 us
  matrix products: 87.4 us -> 2.56 us
  other arithmetic: 46.8 us -> 5.68 us
  starting transfers between devices: 18.3 us -> 0.58 us
    pallas_call x0 -> x15, Pallas kernels: none -> 451 us  [the longest x3 98.3 us: comm_call(): pl.pallas_call(kernel, out_shape=[jax.ShapeDtypeStruct(shape, dtype) for...]
    reduce_scatter x8 -> x2, waiting for transfers between devices: 436 us -> 0.01 us  [the longest x1 0.01 us: local(): lax.psum_scatter(grad_down.reshape(n_line, 8 * attn_each, ff_local), 'lin...]
    all_gather x9 -> x3, waiting for transfers between devices: 285 us -> 0.04 us  [the longest x1 0.02 us: local(): up_full = lax.all_gather(w_up, 'line', axis=0, tiled=True)]
    dot_general x49 -> x2, matrix products: 87.4 us -> 2.56 us  [the longest x1 1.92 us: dot_tn(): lax.dot_general(a, b, (((0,), (0,)), ((), ())), preferred_element_type=F32)]
    all_gather x3 -> x0, blocking collectives: 68.8 us -> none  [the longest x1 36.4 us: local(): lax.all_gather(out_cols, 'blk', axis=1, tiled=True)]
    unnamed x1 -> x0, blocking collectives: 41.8 us -> none
    all_to_all x5 -> x0, starting transfers between devices: 17 us -> none  [the longest x1 3.61 us: local(): lax.all_to_all(sums, 'blk', split_axis=0, concat_axis=0, tiled=True)]
    reduce_sum x19 -> x0, other arithmetic: 15.8 us -> none  [the longest x4 4.41 us: forward_step(): running_sum = running_sum * shrink + jnp.sum(weights, axis=-1)]
  transfers between devices with their start and end apart: 22 -> 5, of which waited for: 19 -> 0; matrix products, arithmetic and copies ran while one was open for 6% -> 7% of each run, Pallas kernels for 0% -> 80%
where the time goes in v2:
time: 520 us; the launch traced here: 515 us
  Pallas kernels  451 us (87%)
  local copies, waits for them, and re-layouts  39.2 us (8%)
  between operations  14.5 us (3%)
  other arithmetic  5.68 us (1%)
    pallas_call x3, Pallas kernels, comm_call(): pl.pallas_call(kernel, out_shape=[jax.ShapeDtypeStruct(shape, dtype) for...  98.3 us
    pallas_call x1, Pallas kernels, blk_gather(): pl.pallas_call(functools.partial(blk_gather_kernel, n_line, count), out_s...  84.1 us
    pallas_call x1, Pallas kernels, blk_reduce(): pl.pallas_call(functools.partial(blk_reduce_kernel, n_line, count), out_s...  74 us
    pallas_call x1, Pallas kernels, entry(): pl.pallas_call(functools.partial(entry_kernel, n_line), out_shape=[out((p...  61.4 us
    pallas_call x1, Pallas kernels, leave(): pl.pallas_call(functools.partial(exit_kernel, n_line), out_shape=[grad, g...  39.9 us
    pallas_call x1, Pallas kernels, attend_back(): pl.pallas_call(functools.partial(attend_back_kernel, blocks), grid=(seqs,...  29.6 us
    pallas_call x1, Pallas kernels, heads_back(): pl.pallas_call(heads_back_kernel, grid=(heads,), out_shape=[jax.ShapeDtyp...  13.7 us
    pallas_call x1, Pallas kernels, attend(): pl.pallas_call(functools.partial(attend_kernel, blocks), grid=(seqs, head...  12.4 us
  transfers between devices with their start and end apart: 5, of which 0 were waited for; matrix products, arithmetic and copies ran while one was open for 7% of the time, Pallas kernels for 80%

profile of v2, /device:TPU:0, one launch (start us, length us, event | category | flops | bytes accessed | tf_op | source)
XLA Modules:
  0.0 514.7 jit_solution(963140149508129173)
XLA Ops:
  7.2 0.7 all-gather.4.cloned.1.call-update
  8.0 1.7 reshape.223
  10.0 1.2 reshape.224.dc
  11.3 0.7 copy.73
  12.1 0.7 add_bitcast_fusion.small
  12.8 61.4 %entry.1 = (bf16[2,4,64,1280]{3,2,1,0:T(8,128)(2,1)}, f32[4,8,8,128]{3,2,1,0:T(8,128)}, bf16[8,40,1280]{2,1,0:T(8,128)(2,1)}, bf16[8,40,1280]{2,1,0:T(8,128)(2,1...) custom-call(bf16[2,64,1280]{2,1,0:T(8,128)(2,1)} %hid.5, ...), custom_call_target="tpu_custom_call" | custom-call | bytes 120000000 | tf_op jit(solution)/shard_map/entry/pallas_call | solution.py:754
  74.3 0.9 reshape.229
  76.4 1.8 fusion
  78.2 8.6 %heads_forward.1 = (bf16[512,640]{1,0:T(8,128)(2,1)}, bf16[512,640]{1,0:T(8,128)(2,1)}, f32[512,640]{1,0:T(8,128)}, f32[512,640]{1,0:T(8,128)}) custom-call(bf16[512,1280]{1,0:T(8,128)(2,1)} %bitcast.118, bf16[5,64,1280]{2,1,0:T(8,128)(2,1)} %bitcast.120, bf16[5,64,1280]{2,1,0:T(8,128)(2,1)} %bitcast.122, bf16[5,64,1280]{2,1,0:T(8,128)(2,1)} %bitcast.124, ...), custom_call_target="tpu_custom_call" | custom-call | flops 1258291200 | bytes 5242880 | tf_op jit(solution)/shard_map/heads_forward/pallas_call | solution.py:830
  86.8 84.1 %blk_gather.1 = (bf16[8,2,256,640]{3,2,1,0:T(8,128)(2,1)}, bf16[8,1,160,320]{3,2,1,0:T(8,128)(2,1)}) custom-call(bf16[2,256,640]{2,1,0:T(8,128)(2,1)} %bitcast.104, bf16[1,160,320]{2,1,0:T(8,128)(2,1)} %bitcast.109), custom_call_target="tpu_custom_call" | custom-call | bytes 210000000 | tf_op jit(solution)/shard_map/blk_gather/pallas_call | solution.py:424
  171.1 0.7 broadcast_in_dim_reshape.21.kp_ref
  171.8 0.8 broadcast_in_dim_squeeze.4.qp_ref
  172.7 0.7 broadcast_in_dim_reshape.22.rate
  173.6 0.7 broadcast_in_dim_reshape.23.us_ref
  174.9 0.7 broadcast_in_dim_reshape.25.rate
  175.6 12.4 %attend.1 = (f32[2,256,640]{2,1,0:T(8,128)}, bf16[2,256,640]{2,1,0:T(8,128)(2,1)}, f32[2,5,8,256]{3,2,1,0:T(8,128)}) custom-call(bf16[2,256,640]{2,1,0:T(8,128)(2,1)} %bitcast.127, bf16[8,2,256,640]{3,2,1,0:T(8,128)(2,1)} %get-tuple-element.85.kv_ref, s32[2,256,1]{2,1,0:T(8,128)} %broadcast_in_dim_squeeze.4.qp_ref, ...), custom_call_target="tpu_custom_call" | custom-call | flops 2684354560 | bytes 5242880 | tf_op jit(solution)/shard_map/attend/pallas_call | solution.py:875
  188.0 2.4 copy.56
  190.9 1.2 copy.58.mixed
  192.2 1.1 copy.57
  193.2 27.8 %attn_joint.1 = (f32[2,64,1280]{2,1,0:T(8,128)}, f32[2,64,1280]{2,1,0:T(8,128)}, f32[2,64,128]{2,1,0:T(8,128)}, f32[2,64,128]{2,1,0:T(8,128)}, bf16[8,2,64,1280]{3,2,1,0:T(8,128)(2,1)}) custom-call(bf16[2,256,320]{2,1,0:T(8,128)(2,1)} %copy.58.mixed, bf16[1280,320]{1,0:T(8,128)(2,1)} %bitcast.84, bf16[2,64,1280]{2,1,0:T(8,128)(2,1)} %hid.5, ...), custom_call_target="tpu_custom_call" | custom-call | bytes 75000000 | tf_op jit(solution)/shard_map/attn_joint/pallas_call | solution.py:1103
  221.1 8.5 %ff_forward.1 = (bf16[1024,640]{1,0:T(8,128)(2,1)}, f32[1024,640]{1,0:T(8,128)}, f32[1024,640]{1,0:T(8,128)}) custom-call(bf16[1024,1280]{1,0:T(8,128)(2,1)} %bitcast.116, bf16[640,1280]{1,0:T(8,128)(2,1)} %all-gather.4.cloned.1.call-done.wu_ref.wu, bf16[640,1280]{1,0:T(8,128)(2,1)} %all-gather.6.cloned.1.call-done.wg_ref.wg, ...), custom_call_target="tpu_custom_call" | custom-call | flops 3355443200 | bytes 9175040 | tf_op jit(solution)/shard_map/ff_forward/pallas_call | solution.py:1027
  229.6 2.8 copy.59
  232.4 36.3 %ff_joint.1 = (bf16[2,64,1280]{2,1,0:T(8,128)(2,1)}, f32[2,64,1280]{2,1,0:T(8,128)}, f32[1,1280]{1,0:T(1,128)}, bf16[8,2,64,1280]{3,2,1,0:T(8,128)(2,1)}) custom-call(bf16[2,2,2,128,640]{4,3,2,1,0:T(8,128)(2,1)} %bitcast.96, bf16[1280,640]{1,0:T(8,128)(2,1)} %bitcast.80, f32[2,64,1280]{2,1,0:T(8,128)} %get-tuple-element.93.first, ...), custom_call_target="tpu_custom_call" | custom-call | bytes 90000000 | tf_op jit(solution)/shard_map/ff_joint/pallas_call | solution.py:1103
  268.6 5.1 down_grad.1
  274.0 8.1 %ff_back.1 = (bf16[1024,640]{1,0:T(8,128)(2,1)}, bf16[1024,640]{1,0:T(8,128)(2,1)}, f32[2,640]{1,0:T(2,128)}) custom-call(bf16[1024,1280]{1,0:T(8,128)(2,1)} %bitcast.91, bf16[1280,640]{1,0:T(8,128)(2,1)} %bitcast.81, f32[1024,640]{1,0:T(8,128)} %get-tuple-element.96.up_ref, f32[1024,640]{1,0:T(8,128)} %get-tuple-element.97.gate_ref, ...), custom_call_target="tpu_custom_call" | custom-call | flops 1677721600 | bytes 11796480 | tf_op jit(solution)/shard_map/ff_back/pallas_call | solution.py:1077
  282.1 7.8 %ff_grad.1 = bf16[4,320,1280]{2,1,0:T(8,128)(2,1)} custom-call(bf16[1024,640]{1,0:T(8,128)(2,1)} %get-tuple-element.100.du_ref, bf16[1024,640]{1,0:T(8,128)(2,1)} %get-tuple-element.99.dg_ref, bf16[1024,1280]{1,0:T(8,128)(2,1)} %bitcast.117), custom_call_target="tpu_custom_call" | custom-call | flops 3355443200 | bytes 10000000 | tf_op jit(solution)/shard_map/ff_grad/pallas_call | solution.py:1297
  289.9 3.4 broadcast_in_dim_reshape.27.kp_ref
  293.7 34.2 %back_joint.1 = (f32[2,64,1280]{2,1,0:T(8,128)}, f32[1,1280]{1,0:T(1,128)}, bf16[2,4,64,1280]{3,2,1,0:T(8,128)(2,1)}) custom-call(bf16[2,2,2,128,640]{4,3,2,1,0:T(8,128)(2,1)} %bitcast.94, bf16[2,2,2,128,640]{4,3,2,1,0:T(8,128)(2,1)} %bitcast.95, bf16[640,1280]{1,0:T(8,128)(2,1)} %all-gather.4.cloned.1.call-done.wu_ref.wu, ...), custom_call_target="tpu_custom_call" | custom-call | bytes 90000000 | tf_op jit(solution)/shard_map/back_joint/pallas_call | solution.py:1103
  327.9 1.9 convolution_convert_fusion
  330.5 1.1 copy.65
  333.0 1.1 copy.62.d_ref
  334.1 29.6 %attend_back.1 = (bf16[2,256,640]{2,1,0:T(8,128)(2,1)}, bf16[8,2,256,640]{3,2,1,0:T(8,128)(2,1)}) custom-call(bf16[2,256,640]{2,1,0:T(8,128)(2,1)} %bitcast.128, bf16[2,256,640]{2,1,0:T(8,128)(2,1)} %copy.62.d_ref, f32[2,256,640]{2,1,0:T(8,128)} %get-tuple-element.106.o_ref, f32[2,5,8,256]{3,2,1,0:T(8,128)} %get-tuple-element.107.inv_ref, ...), custom_call_target="tpu_custom_call" | custom-call | flops 6710886400 | bytes 10485760 | tf_op jit(solution)/shard_map/attend_back/pallas_call | solution.py:931
  363.6 74.0 %blk_reduce.1 = (bf16[2,256,640]{2,1,0:T(8,128)(2,1)}, bf16[1,160,320]{2,1,0:T(8,128)(2,1)}) custom-call(bf16[8,2,256,640]{3,2,1,0:T(8,128)(2,1)} %get-tuple-element.109.refs_0_, bf16[8,1,160,320]{3,2,1,0:T(8,128)(2,1)} %bitcast.86), custom_call_target="tpu_custom_call" | custom-call | bytes 210000000 | tf_op jit(solution)/shard_map/blk_reduce/pallas_call | solution.py:566
  437.7 13.7 %heads_back.1 = (bf16[5,64,1280]{2,1,0:T(8,128)(2,1)}, bf16[5,64,1280]{2,1,0:T(8,128)(2,1)}, bf16[5,64,1280]{2,1,0:T(8,128)(2,1)}, f32[5,1,128]{2,1,0:T(1,128)}, bf16[512,1280]{1,0:T(8,128)(2,1)}) custom-call(bf16[512,1280]{1,0:T(8,128)(2,1)} %bitcast.119, bf16[512,640]{1,0:T(8,128)(2,1)} %bitcast.129, bf16[512,640]{1,0:T(8,128)(2,1)} %bitcast.126, ...), custom_call_target="tpu_custom_call" | custom-call | flops 3355443200 | bytes 7864320 | tf_op jit(solution)/shard_map/heads_back/pallas_call | solution.py:996
  451.4 0.8 add_reduce_fusion
  453.3 0.7 select_maximum_fusion.2
  454.0 39.9 %leave.1 = (f32[40,1280]{1,0:T(8,128)}, f32[40,1280]{1,0:T(8,128)}, f32[40,1280]{1,0:T(8,128)}, f32[2,64,1280]{2,1,0:T(8,128)}, bf16[4,40,320]{2,1,0:T(8,128)(2,...) custom-call(bf16[8,40,1280]{2,1,0:T(8,128)(2,1)} %bitcast.101, bf16[8,40,1280]{2,1,0:T(8,128)(2,1)} %bitcast.102, ...), custom_call_target="tpu_custom_call" | custom-call | bytes 120000000 | tf_op jit(solution)/shard_map/leave/pallas_call | solution.py:666
  493.9 1.9 reshape.265
  495.8 1.0 copy.67
  496.9 2.7 reshape.264
  499.7 0.9 reshape.263
  501.8 1.3 convert_element_type.94
  503.0 1.3 slice_bitcast_fusion
  504.3 0.7 copy.80
  505.1 0.8 copy.81
  505.9 0.7 copy.82
  506.6 0.7 copy.83
  507.3 0.7 copy.84
  (111 shorter events, 8.5 us)
Async XLA Ops:
  7.2 67.0 %all-gather.4.cloned.1.call-start = ((), (), s32[]{:S(2)}) async-start(), calls=%async_computation.2 | async-start | bytes 2048000 | tf_op jit(solution)/shard_map/all_gather | solution.py:1339
  7.9 163.0 %all-gather.6.cloned.1.call-start = ((), (), s32[]{:S(2)}) async-start(), calls=%async_computation.3 | async-start | bytes 2048000 | tf_op jit(solution)/shard_map/all_gather | solution.py:1345
  9.7 1.5 copy-start.9
  9.7 2.3 copy-start.15
  9.7 2.4 copy-start.16
  9.7 2.4 copy-start.17
  9.7 2.4 copy-start.18
  9.7 2.4 copy-start.19
  9.7 2.4 copy-start.20
  74.2 155.3 %all-gather.8.cloned.1.call-start = ((), (), s32[]{:S(2)}) async-start(), calls=%async_computation.4 | async-start | bytes 2048000 | tf_op jit(solution)/shard_map/all_gather | solution.py:1381
  76.3 10.5 %copy-start.10 = (s32[2,1,256]{2,1,0:T(1,128)}, s32[2,1,256]{2,1,0:T(1,128)S(1)}, u32[]{:S(2)}) copy-start(s32[2,1,256]{2,1,0:T(1,128)S(1)} %get-tuple-element.133.qp_ref) | copy-start | bytes 6148
  170.9 283.1 %reduce-scatter.3.cloned.1.call-start = ((), (), s32[]{:S(2)}) async-start(), calls=%async_computation.5 | async-start | bytes 2048000 | tf_op jit(solution)/shard_map/reduce_scatter | solution.py:1403
  190.8 1.4 copy-start.2
  273.7 228.0 %reduce-scatter.5.cloned.1.call-start = ((), (), s32[]{:S(2)}) async-start(), calls=%async_computation.6 | async-start | bytes 4096000 | tf_op jit(solution)/shard_map/reduce_scatter | solution.py:1411
  289.9 3.5 copy-start.13
  329.8 1.7 copy-start.1
  330.5 1.7 copy-start
  437.7 15.4 %copy-start.12 = (f32[1,1280]{1,0:T(1,128)S(1)}, f32[1,1280]{1,0:T(1,128)}, u32[]{:S(2)}) copy-start(f32[1,1280]{1,0:T(1,128)} %get-tuple-element.119) | copy-start | bytes 15364
  437.7 15.5 %copy-start.11 = (f32[1,1280]{1,0:T(1,128)S(1)}, f32[1,1280]{1,0:T(1,128)}, u32[]{:S(2)}) copy-start(f32[1,1280]{1,0:T(1,128)} %get-tuple-element.120) | copy-start | bytes 15364
  496.9 2.7 copy-start.8
  496.9 3.7 copy-start.14
  503.0 1.3 copy-start.4
  503.0 2.0 copy-start.3
  504.3 1.6 copy-start.7
  504.3 2.3 copy-start.6
  504.3 2.9 copy-start.5
Sparse Core Ops, SparseCore 0:
  9.6 53.0 all-gather.3
  74.4 50.4 all-gather.5
  171.0 37.3 all-gather.7
  273.9 35.4 reduce-scatter.2
  311.6 61.2 reduce-scatter.4

commit v3 on v2

--- a/solution.py
+++ b/solution.py
@@ -52,9 +52,9 @@
     pl.semaphore_wait(pltpu.get_barrier_semaphore(), count)
 
 
-def params(collective_id):
+def params(collective_id, room=VMEM_BYTES):
     return pltpu.CompilerParams(
-        collective_id=collective_id, has_side_effects=True, vmem_limit_bytes=VMEM_BYTES
+        collective_id=collective_id, has_side_effects=True, vmem_limit_bytes=room
     )
 
 
@@ -353,17 +353,14 @@
         self.own(2).start()
         self.keep().start()
 
+    def take(self, way, k):
+        self.arrive(way, k).wait_recv()
+        pl.when((self.has_high, self.has_low)[way])(lambda: self.onward(way, k).start())
+        self.over(way, k).start()
+
     def step(self, k):
         for way in (0, 1):
-            @pl.when(self.there(way, k))
-            def _():
-                self.arrive(way, k).wait_recv()
-
-                @pl.when((self.has_high, self.has_low)[way])
-                def _():
-                    self.onward(way, k).start()
-
-                self.over(way, k).start()
+            pl.when(self.there(way, k))(lambda: self.take(way, k))
 
     def finish_arrivals(self):
         self.own(2).wait_recv()
@@ -390,47 +387,6 @@
 def blk_greet(n_line):
     low, high, cross = line_ends(n_line)
     greet([cross], [low, high])
-
-
-def blk_gather_kernel(n_line, count, *refs):
-    ins, outs, sems = refs[:count], refs[count : 2 * count], refs[2 * count :]
-    blk_greet(n_line)
-    jobs, at = [], 0
-    for x, o in zip(ins, outs):
-        for i in range(x.shape[0]):
-            jobs.append(
-                BlkGather(
-                    n_line,
-                    lambda x=x, i=i: x.at[i],
-                    lambda block, o=o, i=i: o.at[block, i],
-                    *sems[5 * at : 5 * at + 5],
-                )
-            )
-            at += 1
-    for job in jobs:
-        job.start()
-    for k in range(1, n_line):
-        for job in jobs:
-            job.step(k)
-    for job in jobs:
-        job.finish_arrivals()
-    for job in jobs:
-        job.finish_sends()
-
-
-def blk_gather(n_line, *arrays):
-    count = len(arrays)
-    chunks = sum(a.shape[0] for a in arrays)
-    return pl.pallas_call(
-        functools.partial(blk_gather_kernel, n_line, count),
-        out_shape=[jax.ShapeDtypeStruct((2 * n_line,) + a.shape, a.dtype) for a in arrays],
-        in_specs=[pl.BlockSpec(memory_space=pltpu.VMEM)] * count,
-        out_specs=[pl.BlockSpec(memory_space=pl.ANY)] * count,
-        scratch_shapes=BlkGather.sems(n_line) * chunks,
-        compiler_params=params(5),
-        cost_estimate=pl.CostEstimate(flops=0, bytes_accessed=70 * 3_000_000, transcendentals=0),
-        name="blk_gather",
-    )(*arrays)
 
 
 class BlkReduce:
@@ -449,7 +405,12 @@
         y, c, self.z, self.s = place()
         self.n = n_line
         (self.has_low, self.low), (self.has_high, self.high), self.cross = line_ends(n_line)
-        self.x, self.side_in, self.line_in = x, side_in, line_in
+        s = self.s
+        if isinstance(x, tuple):
+            self.leaves, self.stays = (lambda zz: x[0].at[zz]), (lambda zz: x[1][...])
+        else:
+            self.leaves, self.stays = (lambda zz: x.at[zz * 2 + 1 - s]), (lambda zz: x[zz * 2 + s])
+        self.side_in, self.line_in = side_in, line_in
         self.sem = (side_send, side_recv, send, recv)
 
     def spot(self, way, k):
@@ -461,17 +422,17 @@
     def side(self, zz):
         side_send, side_recv = self.sem[:2]
         return remote(
-            self.x.at[zz * 2 + 1 - self.s], self.side_in.at[zz], side_send.at[zz], side_recv.at[zz], self.cross
+            self.leaves(zz), self.side_in.at[zz], side_send.at[zz], side_recv.at[zz], self.cross
         )
 
     def slot(self, way, k):
-        return self.n if way == 1 and k == 0 else self.spot(way, k)
+        return jnp.where(k == 0, self.n, self.spot(way, k)) if way == 1 else self.spot(way, k)
 
     def move(self, way, k):
         send, recv = self.sem[2:]
         target = self.high if way == 0 else self.low
         zz = self.spot(way, k)
-        there = self.n if way == 1 and k == 1 else zz
+        there = jnp.where(k == 1, self.n, zz) if way == 1 else zz
         return remote(
             self.side_in.at[zz], self.line_in.at[there], send.at[way, k], recv.at[way, k - 1], target
         )
@@ -485,35 +446,36 @@
         for way in (0, 1) if k > 0 else (0,):
             pl.when(self.exists(way, k))(lambda: self.side(self.spot(way, k)).start())
 
+    def move_on(self, way, k):
+        zz = self.spot(way, k)
+        self.side(zz).wait_recv()
+        passed = self.has_low if way == 0 else self.has_high
+
+        @pl.when(passed)
+        def _():
+            self.arrive(way, k).wait_recv()
+            self.side_in[zz] = add_low(
+                self.stays(zz), self.side_in[zz], self.line_in[zz]
+            ).astype(self.side_in.dtype)
+
+        @pl.when(jnp.logical_not(passed))
+        def _():
+            self.side_in[zz] = add_low(self.stays(zz), self.side_in[zz]).astype(
+                self.side_in.dtype
+            )
+
+        self.move(way, k).start()
+
     def step(self, k):
         for way in (0, 1):
-            @pl.when(self.exists(way, k))
-            def _():
-                zz = self.spot(way, k)
-                self.side(zz).wait_recv()
-                passed = self.has_low if way == 0 else self.has_high
-
-                @pl.when(passed)
-                def _():
-                    self.arrive(way, k).wait_recv()
-                    self.side_in[zz] = add_low(
-                        self.x[zz * 2 + self.s], self.side_in[zz], self.line_in[zz]
-                    ).astype(self.side_in.dtype)
-
-                @pl.when(jnp.logical_not(passed))
-                def _():
-                    self.side_in[zz] = add_low(self.x[zz * 2 + self.s], self.side_in[zz]).astype(
-                        self.side_in.dtype
-                    )
-
-                self.move(way, k).start()
+            pl.when(self.exists(way, k))(lambda: self.move_on(way, k))
 
     def result(self, o):
         z = self.z
         self.side(z).wait_recv()
         pl.when(self.has_low)(lambda: self.arrive(0, 0).wait_recv())
         pl.when(self.has_high)(lambda: self.arrive(1, 0).wait_recv())
-        own = add_low(self.x[z * 2 + self.s], self.side_in[z])
+        own = add_low(self.stays(z), self.side_in[z])
 
         @pl.when(jnp.logical_and(self.has_low, self.has_high))
         def _():
@@ -537,47 +499,9 @@
                         self.move(way, k).wait_send()
 
 
-def blk_reduce_kernel(n_line, count, *refs):
-    ins, outs, scratch = refs[:count], refs[count : 2 * count], refs[2 * count :]
-    blk_greet(n_line)
-    jobs, places = [], []
-    for x, o in zip(ins, outs):
-        for i in range(x.shape[1]):
-            at = 6 * len(jobs)
-            jobs.append(BlkReduce(n_line, x.at[:, i], *scratch[at : at + 6]))
-            places.append(o.at[i])
-    for k in range(n_line - 1, -1, -1):
-        for job in jobs:
-            job.start(k)
-    for k in range(n_line - 1, 0, -1):
-        for job in jobs:
-            job.step(k)
-    for job, o in zip(jobs, places):
-        job.result(o)
-    for job in jobs:
-        job.finish()
-
-
-def blk_reduce(n_line, *arrays):
-    count, scratch = len(arrays), []
-    for x in arrays:
-        one = jax.ShapeDtypeStruct(x.shape[:1] + x.shape[2:], x.dtype)
-        scratch += BlkReduce.scratch(n_line, one) * x.shape[1]
-    return pl.pallas_call(
-        functools.partial(blk_reduce_kernel, n_line, count),
-        out_shape=[jax.ShapeDtypeStruct(x.shape[1:], x.dtype) for x in arrays],
-        in_specs=[pl.BlockSpec(memory_space=pltpu.VMEM)] * count,
-        out_specs=[pl.BlockSpec(memory_space=pltpu.VMEM)] * count,
-        scratch_shapes=scratch,
-        compiler_params=params(7),
-        cost_estimate=pl.CostEstimate(flops=0, bytes_accessed=70 * 3_000_000, transcendentals=0),
-        name="blk_reduce",
-    )(*arrays)
-
-
 def exit_kernel(
     n_line, gq, gk, gv, gh, res, oc, dc, alpha, rest,
-    gq_o, gk_o, gv_o, gh_o, oc_o, dc_o, sum_o,
+    gq_o, gk_o, gv_o, gh_o, go_o, gd_o, sum_o, oc_o, dc_o,
     alpha_in, line_out, line_all, oc_s, oc_r, dc_s, dc_r, al_s, al_r, su_s, su_r, keep, *scratch,
 ):
     y, c, z, s = place()
@@ -632,6 +556,17 @@
             job.step(k)
     for i in range(gh.shape[0]):
         gh_o[i] = res[i] + hid.result(i)
+    for job in cols:
+        job.wait_recv()
+    for job in mine:
+        job.wait()
+    wide, ff_each = oc.shape[-1], dc.shape[-1] // n_line
+    for v in range(4):
+        go_o[:, v * wide : (v + 1) * wide] = oc_o[v].astype(F32)
+        for t in (0, 1):
+            for k in range(n_line):
+                at = ((v * n_line + k) * 2 + t) * ff_each
+                gd_o[:, at : at + ff_each] = dc_o[v * 2 + t, :, k * ff_each : (k + 1) * ff_each].astype(F32)
     total = line_out[b]
     for i, job in enumerate(line_jobs):
         job.wait_recv()
@@ -644,8 +579,8 @@
         job.finish()
     for job in line_jobs + small:
         job.wait_send()
-    for job in cols + mine:
-        job.wait()
+    for job in cols:
+        job.wait_send()
 
 
 def leave(n_line, gq, gk, gv, gh, res, oc, dc, alpha, rest):
@@ -653,6 +588,8 @@
     vmem = pl.BlockSpec(memory_space=pltpu.VMEM)
     dma = pltpu.SemaphoreType.DMA
     scratch = [
+        pltpu.VMEM(oc.shape, oc.dtype),
+        pltpu.VMEM(dc.shape, dc.dtype),
         pltpu.VMEM((3,) + alpha.shape[1:], F32),
         pltpu.VMEM(rest.shape, F32),
         pltpu.VMEM((n_blk - 1,) + rest.shape[1:], F32),
@@ -668,8 +605,8 @@
         out_shape=[
             grad, grad, grad,
             jax.ShapeDtypeStruct(res.shape, F32),
-            jax.ShapeDtypeStruct(oc.shape, oc.dtype),
-            jax.ShapeDtypeStruct(dc.shape, dc.dtype),
+            jax.ShapeDtypeStruct((oc.shape[1], 4 * oc.shape[2]), F32),
+            jax.ShapeDtypeStruct((dc.shape[1], 8 * dc.shape[2]), F32),
             jax.ShapeDtypeStruct(rest.shape[1:], F32),
         ],
         in_specs=[vmem] * 9,
@@ -682,7 +619,7 @@
 
 
 def entry_kernel(
-    n_line, hid, small, wq, wk, wv, oc, dc, hid_o, small_o, wq_o, wk_o, wv_o, oc_o, dc_o, *sems
+    n_line, hid, small, wq, wk, wv, wo, wd, hid_o, small_o, wq_o, wk_o, wv_o, oc_o, dc_o, oc, dc, *sems
 ):
     y, c, z, s = place()
     u, p = y * 2 + c, plane_index(y, c, s)
@@ -704,6 +641,14 @@
     for job in jobs[1:]:
         job.start()
     hid_job.start()
+    for v in range(4):
+        wide = oc.shape[-1]
+        oc[v] = wo[:, v * wide : (v + 1) * wide]
+        ff_each = dc.shape[-1] // n_line
+        for t in (0, 1):
+            for k in range(n_line):
+                at = ((v * n_line + k) * 2 + t) * ff_each
+                dc[v * 2 + t, :, k * ff_each : (k + 1) * ff_each] = wd[:, at : at + ff_each]
     col_jobs = []
     for k, (yy, cc, ss) in enumerate(corners):
         target = (yy, cc, z, ss)
@@ -743,8 +688,10 @@
         job.finish_sends()
 
 
-def entry(n_line, hid, small, wq, wk, wv, oc, dc):
+def entry(n_line, hid, small, wq, wk, wv, wo, wd):
     n_blk = 2 * n_line
+    oc = jax.ShapeDtypeStruct((4, wo.shape[0], wo.shape[1] // 4), wo.dtype)
+    dc = jax.ShapeDtypeStruct((8, wd.shape[0], wd.shape[1] // 8), wd.dtype)
     parts = hid.shape[0]
     vmem, anyway = pl.BlockSpec(memory_space=pltpu.VMEM), pl.BlockSpec(memory_space=pl.ANY)
 
@@ -764,7 +711,8 @@
         ],
         in_specs=[vmem] * 7,
         out_specs=[vmem, vmem, anyway, anyway, anyway, vmem, vmem],
-        scratch_shapes=UlyGather.sems(parts)
+        scratch_shapes=[pltpu.VMEM(oc.shape, oc.dtype), pltpu.VMEM(dc.shape, dc.dtype)]
+        + UlyGather.sems(parts)
         + BlkGather.sems(n_line) * 4
         + [pltpu.SemaphoreType.DMA((3,))] * 2
         + [pltpu.SemaphoreType.DMA((7,))] * 2
@@ -773,7 +721,7 @@
         compiler_params=params(6),
         cost_estimate=pl.CostEstimate(flops=0, bytes_accessed=40 * 3_000_000, transcendentals=0),
         name="entry",
-    )(hid, small, wq, wk, wv, oc, dc)
+    )(hid, small, wq, wk, wv, wo, wd)
 def dot_nt(a, b):
     return lax.dot_general(a, b, (((1,), (1,)), ((), ())), preferred_element_type=F32)
 
@@ -805,10 +753,9 @@
 
 def heads_kernel(x_ref, wq_ref, wk_ref, wv_ref, cos_ref, sin_ref, scale_ref, qz_ref, kv_ref, y_ref, c_ref):
     x = x_ref[...]
-    wqk = jnp.concatenate([wq_ref[0], wk_ref[0]], axis=0)
     wv = wv_ref[0]
-    raw = dot_nt(x, wqk)
-    value = dot_nt(x, jnp.concatenate([jnp.zeros_like(wv), wv], axis=0))
+    got = dot_nt(x, jnp.concatenate([wq_ref[0], wk_ref[0], jnp.zeros_like(wv), wv], axis=0))
+    raw, value = got[:, :128], got[:, 128:]
     low = lanes_of(raw.shape) < HEAD_DIM
     turned = raw * cos_ref[...] + turn(raw) * sin_ref[...]
     c = lax.rsqrt(halves(turned * turned) + HEAD_DIM * tiny_eps)
@@ -840,113 +787,217 @@
     )(x, wq, wk, wv, cos, sin, scale)
 
 
-def attend_kernel(blocks, q_ref, kv_ref, qp_ref, kp_ref, o_ref, low_ref, inv_ref):
-    q = q_ref[0]
-    rows = q.shape[0]
-    acc = jnp.zeros((rows, 128), F32)
-    total = jnp.zeros((rows, 128), F32)
-    q_place = qp_ref[0]
-
-    def step(b, state):
-        acc, total = state
-        kv = kv_ref[b, 0]
-        allowed = kp_ref[0, b] <= q_place
-        p = jnp.where(allowed, jnp.exp(dot_nt(q, kv)), 0.0)
-        for i in range(p.shape[1] // 128):
-            total = total + p[:, i * 128 : (i + 1) * 128]
-        return acc + dot_nn(p.astype(BF), kv), total
-
-    if blocks <= 8:
-        for b in range(blocks):
-            acc, total = step(b, (acc, total))
-    else:
-        acc, total = lax.fori_loop(0, blocks, step, (acc, total))
-    inverse = 1.0 / jnp.broadcast_to(jnp.sum(total, axis=-1, keepdims=True), (rows, 128))
-    out = acc * inverse
-    o_ref[0] = out
-    low_ref[0] = out.astype(BF)
-    inv_ref[0, 0] = jnp.transpose(inverse)[:8]
-
-
-def attend(q, kv, q_places, k_places):
+def down_columns(row):
+    n = row.shape[1]
+    one = jnp.transpose(jnp.broadcast_to(row, (128, n)))
+    return jnp.concatenate([one] * (n // 128), axis=1)
+
+
+def arrivals(n_line, body):
+    each = 2 * n_line - 1
+
+    def step(t, carry):
+        stage, r = t // each, lax.rem(t, each)
+        body(stage, (r + 1) // 2, lax.rem(r + 1, 2))
+        return carry
+
+    lax.fori_loop(0, 2 * each, step, 0)
+
+
+def attend_kernel(
+    n_line, q_ref, kv_ref, oc_ref, qp_ref, kp_ref,
+    kv_o, oc_o, o_ref, mixed_ref, inv_ref, acc, total, place_q, *sems,
+):
+    y, c, z, s = place()
+    blk_greet(n_line)
+    seqs, rows, wide = q_ref.shape
+    heads = wide // 128
+    each = len(BlkGather.sems(n_line))
+    picks = [
+        (lambda i=i: kv_ref.at[i], lambda block, i=i: kv_o.at[block, i]) for i in range(seqs)
+    ] + [(lambda: oc_ref.at[0], lambda block: oc_o.at[block, 0])]
+    jobs = [
+        BlkGather(n_line, *pick, *sems[each * i : each * (i + 1)]) for i, pick in enumerate(picks)
+    ]
+    for job in jobs:
+        job.start()
+    acc[...] = jnp.zeros_like(acc)
+    total[...] = jnp.zeros_like(total)
+    for i in range(seqs):
+        place_q[i] = down_columns(qp_ref[i])
+
+    def attend_to(i, block, keys):
+        allowed = kp_ref[i, block] <= place_q[i]
+        for h in range(heads):
+            kv = keys(h)
+            p = jnp.where(allowed, jnp.exp(dot_nt(q_ref[i, :, h * 128 : (h + 1) * 128], kv)), 0.0)
+            part = p[:, :128]
+            for j in range(1, rows // 128):
+                part = part + p[:, j * 128 : (j + 1) * 128]
+            total[i, h] = total[i, h] + part
+            acc[i, h] = acc[i, h] + dot_nn(p.astype(BF), kv)
+
+    def body(stage, k, way):
+        there = (k == 0) | jnp.where(way == 0, z >= k, z + k < n_line)
+
+        @pl.when(there)
+        def _():
+            for job in jobs:
+                for w in (0, 1):
+                    pl.when((stage == 0) & (k > 0) & (way == w))(lambda: job.take(w, k))
+                    pl.when((stage == 1) & (k > 0) & (way == w))(lambda: job.over(w, k).wait_recv())
+                pl.when((stage == 1) & (k == 0))(lambda: job.own(2).wait_recv())
+                pl.when((stage == 0) & (k == 0))(lambda: job.keep().wait())
+            zz = jnp.where(way == 0, z - k, z + k)
+            block = zz * 2 + jnp.where(stage == 0, s, 1 - s)
+            for i in range(seqs):
+                attend_to(i, block, lambda h: kv_o[block, i, :, h * 128 : (h + 1) * 128])
+
+    arrivals(n_line, body)
+    low = lanes_of((rows, 128)) < HEAD_DIM
+    for i in range(seqs):
+        outs = []
+        for h in range(heads):
+            inverse = 1.0 / jnp.broadcast_to(jnp.sum(total[i, h], axis=-1, keepdims=True), (rows, 128))
+            out = acc[i, h] * inverse
+            o_ref[i, h] = out
+            inv_ref[i, h] = jnp.transpose(inverse)[:8]
+            outs.append(out)
+        for h in range(0, heads - 1, 2):
+            mixed_ref[i, :, h * HEAD_DIM : (h + 2) * HEAD_DIM] = jnp.where(
+                low, pltpu.roll(outs[h], HEAD_DIM, 1), outs[h + 1]
+            ).astype(BF)
+        if heads % 2 == 1:
+            mixed_ref[i, :, (heads - 1) * HEAD_DIM :] = pltpu.roll(outs[-1], HEAD_DIM, 1)[:, :HEAD_DIM].astype(BF)
+    for job in jobs:
+        job.finish_sends()
+
+
+def attend(n_line, q, kv, oc, q_places, k_places):
     seqs, rows, wide = q.shape
-    blocks, heads = kv.shape[0], wide // 128
-    mine = pl.BlockSpec((1, rows, 128), lambda s, h: (s, 0, h))
-    return pl.pallas_call(
-        functools.partial(attend_kernel, blocks),
-        grid=(seqs, heads),
-        out_shape=[
-            jax.ShapeDtypeStruct(q.shape, F32),
-            jax.ShapeDtypeStruct(q.shape, BF),
-            jax.ShapeDtypeStruct((seqs, heads, 8, rows), F32),
+    n_blk, heads = 2 * n_line, wide // 128
+    head = (seqs, heads, rows, 128)
+    return comm_call(
+        functools.partial(attend_kernel, n_line), "attend", 5, (q, kv, oc, q_places, k_places),
+        [
+            ((n_blk,) + kv.shape, BF), ((n_blk,) + oc.shape, BF), (head, F32),
+            ((seqs, rows, heads * HEAD_DIM), BF), ((seqs, heads, 8, rows), F32),
         ],
-        in_specs=[
-            mine,
-            pl.BlockSpec((blocks, 1, rows, 128), lambda s, h: (0, s, 0, h)),
-            pl.BlockSpec((1, rows, 1), lambda s, h: (s, 0, 0)),
-            pl.BlockSpec((1, blocks, 1, rows), lambda s, h: (s, 0, 0, 0)),
-        ],
-        out_specs=[mine, mine, pl.BlockSpec((1, 1, 8, rows), lambda s, h: (s, h, 0, 0))],
-        compiler_params=pltpu.CompilerParams(vmem_limit_bytes=VMEM_BYTES),
-        cost_estimate=pl.CostEstimate(
-            flops=4 * blocks * seqs * rows * rows * wide, bytes_accessed=2 * blocks * seqs * rows * wide,
-            transcendentals=blocks * seqs * rows * rows * heads,
-        ),
-        name="attend",
-    )(q, kv, q_places, k_places)
-
-
-def attend_back_kernel(blocks, q_ref, d_ref, o_ref, inv_ref, kv_ref, qp_ref, kp_ref, dq_ref, dkv_ref):
-    q, d = q_ref[0], d_ref[0]
-    rows = q.shape[0]
-    delta = jnp.sum(d.astype(F32) * o_ref[0], axis=-1, keepdims=True)
-    delta = jnp.transpose(jnp.broadcast_to(delta, (rows, 128)))[:1]
-    inverse = inv_ref[0, 0][:1]
-    pair = jnp.concatenate([q, d], axis=0)
-    q_place = qp_ref[0]
-
-    def step(b, dq):
-        kv = kv_ref[b, 0]
-        scores = dot_nt(kv, pair)
-        allowed = kp_ref[0, b] <= q_place
-        p = jnp.where(allowed, jnp.exp(scores[:, :rows]) * inverse, 0.0)
-        ds = (p * (scores[:, rows:] - delta)).astype(BF)
-        dkv_ref[b, 0] = dot_nn(jnp.concatenate([ds, p.astype(BF)], axis=1), pair).astype(BF)
-        return dq + dot_tn(ds, kv)
-
-    dq = jnp.zeros((rows, 128), F32)
-    if blocks <= 8:
-        for b in range(blocks):
-            dq = step(b, dq)
-    else:
-        dq = lax.fori_loop(0, blocks, step, dq)
-    dq_ref[0] = dq.astype(BF)
-
-
-def attend_back(q, d, o, inv, kv, q_places, k_places):
+        [pltpu.VMEM(head, F32), pltpu.VMEM(head, F32), pltpu.VMEM((seqs, rows, rows), F32)]
+        + BlkGather.sems(n_line) * (seqs + 1),
+        75,
+    )
+
+
+def attend_back_kernel(
+    n_line, q_ref, low_ref, w_ref, mixed_ref, o_ref, inv_ref, kv_ref, qp_ref, kp_ref,
+    dq_ref, dkv_ref, oc_ref, dz, delta, dq, parts, oparts, *scratch,
+):
+    y, c, z, s = place()
+    blk_greet(n_line)
+    seqs, rows, wide = q_ref.shape
+    heads, width = wide // 128, low_ref.shape[-1]
+    low_rows = low_ref[...].reshape(seqs * rows, width)
+    grad = dot_tn(low_rows, mixed_ref[...].reshape(seqs * rows, mixed_ref.shape[-1])).astype(BF)
+    n_blk, each_out = 2 * n_line, width // (8 * n_line)
+    for b in range(n_blk):
+        for v in range(4):
+            at = (v * n_blk + b) * each_out
+            oparts[b, v * each_out : (v + 1) * each_out] = grad[at : at + each_out]
+    each = 6
+    jobs = [
+        BlkReduce(n_line, (parts.at[:, i], parts.at[n_line, i]), *scratch[each * i : each * (i + 1)])
+        for i in range(seqs)
+    ]
+    out_job = BlkReduce(n_line, oparts, *scratch[each * seqs :])
+    for k in range(n_line - 1, -1, -1):
+        out_job.start(k)
+    low = lanes_of((rows, 128)) < HEAD_DIM
+    for i in range(seqs):
+        d = dot_nn(low_rows[i * rows : (i + 1) * rows], w_ref[...]).astype(BF).astype(F32)
+        for h in range(heads):
+            at = h // 2 * 128
+            if h == heads - 1 and heads % 2 == 1:
+                tile = jnp.concatenate([jnp.zeros((rows, HEAD_DIM), F32), d[:, at:]], axis=1)
+            else:
+                tile = d[:, at : at + 128]
+                if h % 2 == 0:
+                    tile = pltpu.roll(tile, HEAD_DIM, 1)
+                tile = jnp.where(low, 0.0, tile)
+            dz[i, h] = tile.astype(BF)
+            row = jnp.sum(tile * o_ref[i, h], axis=-1, keepdims=True)
+            delta[i, h] = jnp.transpose(jnp.broadcast_to(row, (rows, 128)))[:8]
+    dq[...] = jnp.zeros_like(dq)
+
+    def block_of(block, spot):
+        for i in range(seqs):
+            allowed = down_columns(kp_ref[i, block]) <= qp_ref[i]
+            for h in range(heads):
+                lanes = slice(h * 128, (h + 1) * 128)
+                kv = kv_ref[block, i, :, lanes]
+                pair = jnp.concatenate([q_ref[i, :, lanes], dz[i, h]], axis=0)
+                scores = dot_nt(kv, pair)
+                p = jnp.where(allowed, jnp.exp(scores[:, :rows]) * inv_ref[i, h][:1], 0.0)
+                ds = (p * (scores[:, rows:] - delta[i, h][:1])).astype(BF)
+                parts[spot, i, :, lanes] = dot_nn(
+                    jnp.concatenate([ds, p.astype(BF)], axis=1), pair
+                ).astype(BF)
+                dq[i, h] = dq[i, h] + dot_tn(ds, kv)
+
+    def body(stage, k, way):
+        there = jnp.where(k == 0, way == 0, jnp.where(way == 0, z + k < n_line, z >= k))
+
+        @pl.when(there)
+        def _():
+            zz = jnp.where(way == 0, z + k, z - k)
+            block_of(zz * 2 + jnp.where(stage == 0, 1 - s, s), jnp.where(stage == 0, zz, n_line))
+
+            @pl.when(stage == 0)
+            def _():
+                for job in jobs:
+                    job.side(zz).start()
+
+            for w in (0, 1):
+                @pl.when((stage == 1) & (k > 0) & (way == w))
+                def _():
+                    for job in jobs + [out_job]:
+                        job.move_on(w, k)
+
+    def step(t, carry):
+        r = lax.rem(t, 2 * n_line)
+        body(t // (2 * n_line), n_line - 1 - r // 2, lax.rem(r, 2))
+        return carry
+
+    lax.fori_loop(0, 4 * n_line, step, 0)
+    for i in range(seqs):
+        for h in range(heads):
+            dq_ref[i, :, h * 128 : (h + 1) * 128] = dq[i, h].astype(BF)
+    out_job.result(oc_ref)
+    for i, job in enumerate(jobs):
+        job.result(dkv_ref.at[i])
+    for job in jobs + [out_job]:
+        job.finish()
+
+
+def attend_back(n_line, q, low, w, mixed, o, inv, kv, q_places, k_places):
     seqs, rows, wide = q.shape
-    blocks, heads = kv.shape[0], wide // 128
-    mine = pl.BlockSpec((1, rows, 128), lambda s, h: (s, 0, h))
-    keys = pl.BlockSpec((blocks, 1, rows, 128), lambda s, h: (0, s, 0, h))
-    return pl.pallas_call(
-        functools.partial(attend_back_kernel, blocks),
-        grid=(seqs, heads),
-        out_shape=[jax.ShapeDtypeStruct(q.shape, BF), jax.ShapeDtypeStruct(kv.shape, BF)],
-        in_specs=[
-            mine, mine, mine,
-            pl.BlockSpec((1, 1, 8, rows), lambda s, h: (s, h, 0, 0)),
-            keys,
-            pl.BlockSpec((1, 1, rows), lambda s, h: (s, 0, 0)),
-            pl.BlockSpec((1, blocks, rows, 1), lambda s, h: (s, 0, 0, 0)),
-        ],
-        out_specs=[mine, keys],
-        compiler_params=pltpu.CompilerParams(vmem_limit_bytes=VMEM_BYTES),
-        cost_estimate=pl.CostEstimate(
-            flops=10 * blocks * seqs * rows * rows * wide, bytes_accessed=4 * blocks * seqs * rows * wide,
-            transcendentals=blocks * seqs * rows * rows * heads,
-        ),
-        name="attend_back",
-    )(q, d, o, inv, kv, q_places, k_places)
+    n_blk, heads = 2 * n_line, wide // 128
+    head = (seqs, heads, rows, 128)
+    width, columns = w.shape
+    out_shape = (width // n_blk, columns)
+    one = jax.ShapeDtypeStruct((n_blk,) + kv.shape[2:], BF)
+    out_one = jax.ShapeDtypeStruct((n_blk,) + out_shape, BF)
+    return comm_call(
+        functools.partial(attend_back_kernel, n_line), "attend_back", 7,
+        (q, low, w, mixed, o, inv, kv, q_places, k_places),
+        [(q.shape, BF), (kv.shape[1:], BF), (out_shape, BF)],
+        [
+            pltpu.VMEM(head, BF), pltpu.VMEM((seqs, heads, 8, rows), F32), pltpu.VMEM(head, F32),
+            pltpu.VMEM((n_line + 1,) + kv.shape[1:], BF), pltpu.VMEM(out_one.shape, BF),
+        ]
+        + BlkReduce.scratch(n_line, one) * seqs + BlkReduce.scratch(n_line, out_one),
+        75, 67_000_000,
+    )
 
 
 def heads_back_kernel(
@@ -964,14 +1015,14 @@
     dr = c_ref[...] * (dy - y * halves(y * dy))
     raw = (dr * cos_ref[...] - turn(dr) * sin_ref[...]).astype(BF)
     x = x_ref[...]
-    grad = dot_tn(raw, x)
+    value = jnp.where(low, jnp.zeros_like(dkv), dkv)
+    both = jnp.concatenate([raw, value], axis=1)
+    grad = dot_tn(both, x)
     gq_ref[0] = grad[:HEAD_DIM].astype(BF)
-    gk_ref[0] = grad[HEAD_DIM:].astype(BF)
-    value = jnp.where(low, jnp.zeros_like(dkv), dkv)
-    gv_ref[0] = dot_tn(value, x)[HEAD_DIM:].astype(BF)
-    wqk = jnp.concatenate([wq_ref[0], wk_ref[0]], axis=0)
+    gk_ref[0] = grad[HEAD_DIM : 2 * HEAD_DIM].astype(BF)
+    gv_ref[0] = grad[3 * HEAD_DIM :].astype(BF)
     wv = wv_ref[0]
-    more = dot_nn(raw, wqk) + dot_nn(value, jnp.concatenate([jnp.zeros_like(wv), wv], axis=0))
+    more = dot_nn(both, jnp.concatenate([wq_ref[0], wk_ref[0], jnp.zeros_like(wv), wv], axis=0))
 
     @pl.when(h == 0)
     def _():
@@ -1098,7 +1149,7 @@
     return c * (dy - y * jnp.sum(y * dy, axis=-1, keepdims=True))
 
 
-def comm_call(kernel, name, collective_id, args, outs, scratch, micros):
+def comm_call(kernel, name, collective_id, args, outs, scratch, micros, room=VMEM_BYTES):
     vmem = pl.BlockSpec(memory_space=pltpu.VMEM)
     return pl.pallas_call(
         kernel,
@@ -1106,7 +1157,7 @@
         in_specs=[vmem] * len(args),
         out_specs=[vmem] * len(outs),
         scratch_shapes=scratch,
-        compiler_params=params(collective_id),
+        compiler_params=params(collective_id, room),
         cost_estimate=pl.CostEstimate(flops=0, bytes_accessed=micros * 3_000_000, transcendentals=0),
         name=name,
     )(*args)
@@ -1280,26 +1331,25 @@
     )(d, inner)
 
 
-def ff_grad_kernel(du_ref, dg_ref, x_ref, o_ref):
-    n_line, both, _ = o_ref.shape
-    each = both // 2
-    for j, ref in enumerate((du_ref, dg_ref)):
+def ff_grad_kernel(du_ref, dg_ref, x_ref, u_ref, g_ref):
+    n_line, each, _ = u_ref.shape
+    for ref, o_ref in ((du_ref, u_ref), (dg_ref, g_ref)):
         grad = dot_tn(ref[...], x_ref[...]).astype(BF)
         for k in range(n_line):
-            o_ref[k, j * each : (j + 1) * each] = grad[k * each : (k + 1) * each]
+            o_ref[k] = grad[k * each : (k + 1) * each]
 
 
 def ff_grad(n_line, du, dg, x):
     rows, width = x.shape
     columns = du.shape[1]
     whole = pl.BlockSpec((rows, columns), lambda i: (0, 0))
-    shape = (n_line, 2 * columns // n_line, width)
+    shape = (n_line, columns // n_line, width)
     return pl.pallas_call(
         ff_grad_kernel,
         grid=(2,),
-        out_shape=jax.ShapeDtypeStruct(shape, BF),
+        out_shape=[jax.ShapeDtypeStruct(shape, BF)] * 2,
         in_specs=[whole, whole, pl.BlockSpec((rows, width // 2), lambda i: (0, i))],
-        out_specs=pl.BlockSpec(shape[:2] + (width // 2,), lambda i: (0, 0, i)),
+        out_specs=[pl.BlockSpec(shape[:2] + (width // 2,), lambda i: (0, 0, i))] * 2,
         compiler_params=pltpu.CompilerParams(vmem_limit_bytes=VMEM_BYTES),
         cost_estimate=pl.CostEstimate(flops=4 * rows * width * columns, bytes_accessed=10_000_000, transcendentals=0),
         name="ff_grad",
@@ -1331,15 +1381,10 @@
         at += v.shape[0]
     small = small.reshape(-1, 128)
 
-    out_send = jnp.transpose(w_out.reshape(attn_each, 4, local_width), (1, 0, 2))
-    down_send = jnp.transpose(
-        w_down.reshape(attn_each, 4, n_line, 2, ff_each), (1, 3, 0, 2, 4)
-    ).reshape(8, attn_each, ff_local)
-
     up_full = lax.all_gather(w_up, "line", axis=0, tiled=True)
 
     hid_all, small_all, wq_all, wk_all, wv_all, out_cols, down_cols = entry(
-        n_line, hidden, small, w_query, w_key, w_value, out_send, down_send
+        n_line, hidden, small, w_query, w_key, w_value, w_out, w_down
     )
     w_gate, up_full, hid_all = lax.optimization_barrier((w_gate, up_full, hid_all))
     gate_full = lax.all_gather(w_gate, "line", axis=0, tiled=True)
@@ -1354,13 +1399,13 @@
     up_wide = mine[:, cut[3] : cut[4]].reshape(-1)
     gate_wide = mine[:, cut[4] : cut[5]].reshape(-1)
     places = jnp.transpose(
-        flat[:, :, cut[5] : cut[6]].astype(jnp.int32).reshape(4, n_blk, seqs, rows_each), (2, 1, 0, 3)
-    ).reshape(seqs, n_blk, group_rows)
+        flat[:, :, cut[5] : cut[6]].reshape(4, n_blk, seqs, rows_each), (2, 1, 0, 3)
+    ).reshape(seqs, n_blk, 1, group_rows)
     q_places = lax.dynamic_slice_in_dim(places, line * 2 + side, 1, 1)[:, 0]
 
     lane = jnp.arange(128) % HEAD_DIM
     freqs = rotary_base ** (-((lane % 32).astype(F32) * (2.0 / HEAD_DIM)))
-    angles = q_places.reshape(group_tokens, 1).astype(F32) * freqs
+    angles = q_places.reshape(group_tokens, 1) * freqs
     cos = jnp.cos(angles)
     sin = jnp.where(lane < 32, -1.0, 1.0) * jnp.sin(angles)
     scale_both = jnp.concatenate([scale_wide * HEAD_DIM**0.5, scale_wide], axis=1)[:, None]
@@ -1372,25 +1417,18 @@
     qz, kv, y_both, c_both = heads_forward(group_hidden, wq, wk, wv, cos, sin, scale_both)
     qz = qz.reshape(seqs, group_rows, heads * 128)
 
-    kv_all, out_all = blk_gather(
-        n_line, kv.reshape(seqs, group_rows, heads * 128), out_cols.reshape(1, 4 * attn_each, local_width)
-    )
-    kv_all, out_all, gate_full, down_cols = lax.optimization_barrier(
-        (kv_all, out_all, gate_full, down_cols)
-    )
+    kv_all, out_all, attended, mixed, inverse = attend(
+        n_line, qz, kv.reshape(seqs, group_rows, heads * 128),
+        out_cols.reshape(1, 4 * attn_each, local_width), q_places, places,
+    )
+    out_all, gate_full, down_cols = lax.optimization_barrier((out_all, gate_full, down_cols))
     down_all = lax.all_gather(down_cols.reshape(8 * attn_each, ff_local), "line", axis=0, tiled=False)
     down_full = jnp.transpose(
         down_all.reshape(n_line, 4, 2, attn_each, ff_local), (1, 0, 2, 3, 4)
     ).reshape(width, ff_local)
-
     out_full = jnp.transpose(
         out_all.reshape(n_blk, 4, attn_each, local_width), (1, 0, 2, 3)
     ).reshape(width, local_width)
-
-    attended, mixed, inverse = attend(qz, kv_all, q_places[:, :, None], places[:, :, None, :])
-    mixed = mixed.reshape(group_tokens, heads, 128)[:, :, HEAD_DIM:].reshape(
-        seqs, group_rows, local_width
-    )
 
     first, unit_att, att_c, first_c, mlp_in = attn_joint(mixed, out_full, hidden, attn_rate[None])
     mlp_in = mlp_in.reshape(plane_tokens, width)
@@ -1400,6 +1438,7 @@
     )
     branch_low = branch_low.reshape(plane_tokens, width)
     grad_down = down_grad(n_line, branch_low, inner)
+    branch_low, grad_down = lax.optimization_barrier((branch_low, grad_down))
     down_own = lax.psum_scatter(
         grad_down.reshape(n_line, 8 * attn_each, ff_local), "line", scatter_dimension=0, tiled=True
     ).reshape(8, attn_each, ff_local)
@@ -1407,29 +1446,21 @@
         branch_low, down_full, up_rows, gate_rows, up_wide[None], gate_wide[None]
     )
     grad_up_scale, grad_gate_scale = ff_scales[0], ff_scales[1]
-    grad_ug = ff_grad(n_line, up_low, gate_low, mlp_in)
-    mlp_own = lax.psum_scatter(grad_ug, "line", scatter_dimension=0, tiled=True)[0]
-    up_low, grad_ug = lax.optimization_barrier((up_low, grad_ug))
+    grad_up, grad_gate = ff_grad(n_line, up_low, gate_low, mlp_in)
+    up_own = lax.psum_scatter(grad_up, "line", scatter_dimension=0, tiled=True)[0]
+    up_low, grad_up, grad_gate = lax.optimization_barrier((up_low, grad_up, grad_gate))
     grad_residual, grad_alpha_attn, att_low = back_joint(
         up_low, gate_low, up_full, gate_full, grad_first, first, unit_att, att_c, first_c,
         hidden, attn_rate[None],
     )
 
-    att_low = att_low.reshape(group_tokens, width)
-    grad_mixed = jnp.pad(
-        dot_nn(att_low, out_full).astype(BF).reshape(seqs, group_rows, heads, HEAD_DIM),
-        ((0, 0), (0, 0), (0, 0), (HEAD_DIM, 0)),
-    ).reshape(seqs, group_rows, heads * 128)
-    grad_out = (
-        dot_tn(att_low, mixed.reshape(group_tokens, local_width))
-        .astype(BF)
-        .reshape(4, n_blk, attn_each, local_width)
-    )
-    grad_out = jnp.transpose(grad_out, (1, 0, 2, 3)).reshape(n_blk, 1, 4 * attn_each, local_width)
-    dq, dkv_all = attend_back(
-        qz, grad_mixed, attended, inverse, kv_all, q_places[:, None, :], places[..., None]
-    )
-    dkv, out_own = blk_reduce(n_line, dkv_all, grad_out)
+    att_low, down_own = lax.optimization_barrier((att_low, down_own))
+    dq, dkv, out_own = attend_back(
+        n_line, qz, att_low.reshape(seqs, group_rows, width), out_full, mixed, attended, inverse,
+        kv_all, q_places, places,
+    )
+    dkv, grad_gate, up_own = lax.optimization_barrier((dkv, grad_gate, up_own))
+    gate_own = lax.psum_scatter(grad_gate, "line", scatter_dimension=0, tiled=True)[0].astype(F32)
     out_own = out_own.reshape(4, attn_each, local_width)
     gq, gk, gv, gs, gh = heads_back(
         group_hidden, dq.reshape(group_tokens, -1), dkv.reshape(group_tokens, -1), y_both, c_both,
@@ -1450,18 +1481,13 @@
     rest = jnp.concatenate(
         [jnp.zeros((n_blk, 128), F32), row(grad_scale.reshape(n_blk, attn_each), 128), row(ff_sums, 384)], axis=1
     )
-    mlp_own = mlp_own.astype(F32)
-    gq, gk, gv, grad_hidden, out_own, down_own, sums = leave(
+    gq, gk, gv, grad_hidden, out_gradient, down_gradient, sums = leave(
         n_line,
         *(g.reshape(n_blk, attn_each, width) for g in (gq, gk, gv)),
         gh.reshape(seqs, 4, rows_each, width),
         grad_residual,
         out_own, down_own, row(alpha, 128)[:, :, None], rest[:, None],
     )
-    out_gradient = jnp.transpose(out_own, (1, 0, 2)).reshape(attn_each, width).astype(F32)
-    down_gradient = jnp.transpose(
-        down_own.reshape(4, 2, attn_each, n_line, ff_each), (2, 0, 3, 1, 4)
-    ).reshape(attn_each, -1).astype(F32)
     sums = sums[0]
     return (
         layer_out,
@@ -1470,8 +1496,8 @@
         gk,
         gv,
         out_gradient,
-        mlp_own[:ff_each],
-        mlp_own[ff_each:],
+        up_own.astype(F32),
+        gate_own,
         down_gradient,
         sums[128 : 128 + attn_each],
         sums[:attn_each],

time: 520 us -> 466 us (0.90)
  Pallas kernels: 451 us -> 421 us
  local copies, waits for them, and re-layouts: 39.2 us -> 20.1 us
    pallas_call x5 -> x1, Pallas kernels: 208 us -> 7.57 us  [ff_grad(): pl.pallas_call(ff_grad_kernel, grid=(2,), out_shape=[jax.ShapeDtypeStruct...]
    pallas_call x3 -> x5, Pallas kernels: 98.3 us -> 271 us  [comm_call(): pl.pallas_call(kernel, out_shape=[jax.ShapeDtypeStruct(shape, dtype) for...]
    convert_element_type x6 -> x0, local copies, waits for them, and re-layouts: 7.19 us -> none  [the longest x3 5.6 us: local(): down_gradient = jnp.transpose(down_own.reshape(4, 2, attn_each, n_line, f...]
    reshape x13 -> x2, local copies, waits for them, and re-layouts: 7.06 us -> 0.18 us  [the longest x1 0.09 us: local(): places = jnp.transpose(flat[:, :, cut[5]:cut[6]].reshape(4, n_blk, seqs,...]
  transfers between devices with their start and end apart: 5 -> 6, of which waited for: 0 -> 0; matrix products, arithmetic and copies ran while one was open for 7% -> 4% of each run, Pallas kernels for 80% -> 82%
where the time goes in v3:
time: 466 us; the launch traced here: 465 us
  Pallas kernels  421 us (90%)
  local copies, waits for them, and re-layouts  20.1 us (4%)
  between operations  14.4 us (3%)
  other arithmetic  8.63 us (2%)
    pallas_call x5, Pallas kernels, comm_call(): pl.pallas_call(kernel, out_shape=[jax.ShapeDtypeStruct(shape, dtype) for...  271 us
    pallas_call x1, Pallas kernels, entry(): pl.pallas_call(functools.partial(entry_kernel, n_line), out_shape=[out((p...  60.9 us
    pallas_call x1, Pallas kernels, leave(): pl.pallas_call(functools.partial(exit_kernel, n_line), out_shape=[grad, g...  39.8 us
    pallas_call x1, Pallas kernels, heads_back(): pl.pallas_call(heads_back_kernel, grid=(heads,), out_shape=[jax.ShapeDtyp...  11.6 us
  transfers between devices with their start and end apart: 6, of which 0 were waited for; matrix products, arithmetic and copies ran while one was open for 4% of the time, Pallas kernels for 82%

profile of v3, /device:TPU:0, one launch (start us, length us, event | category | flops | bytes accessed | tf_op | source)
XLA Modules:
  0.0 465.1 jit_solution(2545629754918106257)
XLA Ops:
  7.2 0.7 all-gather.4.cloned.1.call-update
  8.0 0.7 convert_element_type.45
  8.6 0.1 convert_element_type.46
  8.7 1.4 add_bitcast_fusion.small
  10.1 60.9 %entry.1 = (bf16[2,4,64,1280]{3,2,1,0:T(8,128)(2,1)}, f32[4,8,8,128]{3,2,1,0:T(8,128)}, bf16[8,40,1280]{2,1,0:T(8,128)(2,1)}, bf16[8,40,1280]{2,1,0:T(8,128)(2,1...) custom-call(bf16[2,64,1280]{2,1,0:T(8,128)(2,1)} %hid.5, ...), custom_call_target="tpu_custom_call" | custom-call | bytes 120000000 | tf_op jit(solution)/shard_map/entry/pallas_call | solution.py:701
  71.1 0.9 reshape.182
  72.3 0.6 broadcast_in_dim.52.scale_ref
  72.9 0.1 reshape.183
  73.0 0.1 reshape.184.kp_ref
  73.1 0.6 fusion.10.qp_ref
  73.7 1.8 fusion
  75.5 8.1 %heads_forward.1 = (bf16[512,640]{1,0:T(8,128)(2,1)}, bf16[512,640]{1,0:T(8,128)(2,1)}, f32[512,640]{1,0:T(8,128)}, f32[512,640]{1,0:T(8,128)}) custom-call(bf16[512,1280]{1,0:T(8,128)(2,1)} %bitcast.90, bf16[5,64,1280]{2,1,0:T(8,128)(2,1)} %bitcast.92, bf16[5,64,1280]{2,1,0:T(8,128)(2,1)} %bitcast.94, bf16[5,64,1280]{2,1,0:T(8,128)(2,1)} %bitcast.96, ...), custom_call_target="tpu_custom_call" | custom-call | flops 1258291200 | bytes 5242880 | tf_op jit(solution)/shard_map/heads_forward/pallas_call | solution.py:777
  83.7 89.3 %attend.1 = (bf16[8,2,256,640]{3,2,1,0:T(8,128)(2,1)}, bf16[8,1,160,320]{3,2,1,0:T(8,128)(2,1)}, f32[2,5,256,128]{3,2,1,0:T(8,128)}, bf16[2,256,320]{2,1,0:T(8,128)(2,1)}, f32[2,5,8,256]{3,2,1,0:T(8,128)}) custom-call(bf16[2,256,640]{2,1,0:T(8,128)(2,1)} %bitcast.63, bf16[2,256,640]{2,1,0:T(8,128)(2,1)} %bitcast.76, bf16[1,160,320]{2,1,0:T(8,128)(2,1)} %bitcast.81, ...), custom_call_target="tpu_custom_call" | custom-call | bytes 225000000 | tf_op jit(solution)/shard_map/attend/pallas_call | solution.py:1154
  173.1 0.2 reduce-scatter.4.cloned.1.call-start
  173.4 0.7 broadcast_in_dim_reshape.15.rate
  174.2 0.7 broadcast_in_dim_reshape.16.us_ref
  174.9 0.7 broadcast_in_dim_reshape.17.gs_ref
  175.5 0.7 broadcast_in_dim_reshape.18.rate
  176.2 2.3 copy.34
  178.5 28.0 %attn_joint.1 = (f32[2,64,1280]{2,1,0:T(8,128)}, f32[2,64,1280]{2,1,0:T(8,128)}, f32[2,64,128]{2,1,0:T(8,128)}, f32[2,64,128]{2,1,0:T(8,128)}, bf16[8,2,64,1280]{3,2,1,0:T(8,128)(2,1)}) custom-call(bf16[2,256,320]{2,1,0:T(8,128)(2,1)} %get-tuple-element.89.mixed.mixed_ref, bf16[1280,320]{1,0:T(8,128)(2,1)} %bitcast.59, bf16[2,64,1280]{2,1,0:T(8,128)(2,1)} %hid.5, ...), custom_call_target="tpu_custom_call" | custom-call | bytes 75000000 | tf_op jit(solution)/shard_map/attn_joint/pallas_call | solution.py:1154
  206.5 8.5 %ff_forward.1 = (bf16[1024,640]{1,0:T(8,128)(2,1)}, f32[1024,640]{1,0:T(8,128)}, f32[1024,640]{1,0:T(8,128)}) custom-call(bf16[1024,1280]{1,0:T(8,128)(2,1)} %bitcast.88, bf16[640,1280]{1,0:T(8,128)(2,1)} %all-gather.4.cloned.1.call-done.wu_ref.wu, bf16[640,1280]{1,0:T(8,128)(2,1)} %all-gather.6.cloned.1.call-done.wg_ref.wg, ...), custom_call_target="tpu_custom_call" | custom-call | flops 3355443200 | bytes 9175040 | tf_op jit(solution)/shard_map/ff_forward/pallas_call | solution.py:1078
  215.0 2.8 copy.35
  217.8 36.3 %ff_joint.1 = (bf16[2,64,1280]{2,1,0:T(8,128)(2,1)}, f32[2,64,1280]{2,1,0:T(8,128)}, f32[1,1280]{1,0:T(1,128)}, bf16[8,2,64,1280]{3,2,1,0:T(8,128)(2,1)}) custom-call(bf16[2,2,2,128,640]{4,3,2,1,0:T(8,128)(2,1)} %bitcast.69, bf16[1280,640]{1,0:T(8,128)(2,1)} %bitcast.57, f32[2,64,1280]{2,1,0:T(8,128)} %get-tuple-element.99.first, ...), custom_call_target="tpu_custom_call" | custom-call | bytes 90000000 | tf_op jit(solution)/shard_map/ff_joint/pallas_call | solution.py:1154
  254.0 5.1 %down_grad.1 = bf16[4,4,80,640]{3,2,1,0:T(8,128)(2,1)} custom-call(bf16[1024,1280]{1,0:T(8,128)(2,1)} %bitcast.61, bf16[1024,640]{1,0:T(8,128)(2,1)} %get-tuple-element.97.inner_ref), custom_call_target="tpu_custom_call" | custom-call | flops 1677721600 | bytes 8000000 | tf_op jit(solution)/shard_map/down_grad/pallas_call | solution.py:1319
  259.2 8.1 %ff_back.1 = (bf16[1024,640]{1,0:T(8,128)(2,1)}, bf16[1024,640]{1,0:T(8,128)(2,1)}, f32[2,640]{1,0:T(2,128)}) custom-call(bf16[1024,1280]{1,0:T(8,128)(2,1)} %bitcast.62, bf16[1280,640]{1,0:T(8,128)(2,1)} %bitcast.58, f32[1024,640]{1,0:T(8,128)} %get-tuple-element.103.up_ref, f32[1024,640]{1,0:T(8,128)} %get-tuple-element.104.gate_ref, ...), custom_call_target="tpu_custom_call" | custom-call | flops 1677721600 | bytes 11796480 | tf_op jit(solution)/shard_map/ff_back/pallas_call | solution.py:1128
  267.3 7.6 %ff_grad.1 = (bf16[4,160,1280]{2,1,0:T(8,128)(2,1)}, bf16[4,160,1280]{2,1,0:T(8,128)(2,1)}) custom-call(bf16[1024,640]{1,0:T(8,128)(2,1)} %get-tuple-element.109.du_ref, bf16[1024,640]{1,0:T(8,128)(2,1)} %get-tuple-element.106.dg_ref, bf16[1024,1280]{1,0:T(8,128)(2,1)} %bitcast.89), custom_call_target="tpu_custom_call" | custom-call | flops 3355443200 | bytes 10000000 | tf_op jit(solution)/shard_map/ff_grad/pallas_call | solution.py:1347
  274.9 0.3 reduce-scatter.8.cloned.1.call-start
  275.2 34.2 %back_joint.1 = (f32[2,64,1280]{2,1,0:T(8,128)}, f32[1,1280]{1,0:T(1,128)}, bf16[2,4,64,1280]{3,2,1,0:T(8,128)(2,1)}) custom-call(bf16[2,2,2,128,640]{4,3,2,1,0:T(8,128)(2,1)} %bitcast.67, bf16[2,2,2,128,640]{4,3,2,1,0:T(8,128)(2,1)} %bitcast.68, bf16[640,1280]{1,0:T(8,128)(2,1)} %all-gather.4.cloned.1.call-done.wu_ref.wu, ...), custom_call_target="tpu_custom_call" | custom-call | bytes 90000000 | tf_op jit(solution)/shard_map/back_joint/pallas_call | solution.py:1154
  309.4 83.0 %attend_back.1 = (bf16[2,256,640]{2,1,0:T(8,128)(2,1)}, bf16[2,256,640]{2,1,0:T(8,128)(2,1)}, bf16[160,320]{1,0:T(8,128)(2,1)}) custom-call(bf16[2,256,640]{2,1,0:T(8,128)(2,1)} %bitcast.64, bf16[2,256,1280]{2,1,0:T(8,128)(2,1)} %bitcast.71, bf16[1280,320]{1,0:T(8,128)(2,1)} %bitcast.60, bf16[2,256,320]{2,1,0:T(8,128)(2,1)} %get-tuple-element.89.mixed.mixed_ref, ...), custom_call_target="tpu_custom_call" | custom-call | bytes 225000000 | tf_op jit(solution)/shard_map/attend_back/pallas_call | solution.py:1154
  392.6 0.1 broadcast_in_dim.56
  392.7 0.5 copy-done.11
  393.6 0.1 reshape.209
  393.7 0.7 select_maximum_fusion.2
  394.5 11.6 %heads_back.1 = (bf16[5,64,1280]{2,1,0:T(8,128)(2,1)}, bf16[5,64,1280]{2,1,0:T(8,128)(2,1)}, bf16[5,64,1280]{2,1,0:T(8,128)(2,1)}, f32[5,1,128]{2,1,0:T(1,128)}, bf16[512,1280]{1,0:T(8,128)(2,1)}) custom-call(bf16[512,1280]{1,0:T(8,128)(2,1)} %bitcast.91, bf16[512,640]{1,0:T(8,128)(2,1)} %bitcast.98, bf16[512,640]{1,0:T(8,128)(2,1)} %bitcast.99, ...), custom_call_target="tpu_custom_call" | custom-call | flops 3355443200 | bytes 7864320 | tf_op jit(solution)/shard_map/heads_back/pallas_call | solution.py:1047
  406.1 0.8 add_reduce_fusion
  407.0 0.6 broadcast_in_dim.61.rest
  407.6 39.8 %leave.1 = (f32[40,1280]{1,0:T(8,128)}, f32[40,1280]{1,0:T(8,128)}, f32[40,1280]{1,0:T(8,128)}, f32[2,64,1280]{2,1,0:T(8,128)}, f32[40,1280]{1,0:T(8,128)}, /*index=5*/f32[40,5120]{1,0:T(8,128)}, f32[1,640]{1,0:T(1,128)}) custom-call(bf16[8,40,1280]{2,1,0:T(8,128)(2,1)} %bitcast.73, bf16[8,40,1280]{2,1,0:T(8,128)(2,1)} %bitcast.74, ...), custom_call_target="tpu_custom_call" | custom-call | bytes 120000000 | tf_op jit(solution)/shard_map/leave/pallas_call | solution.py:603
  447.5 0.9 convert_element_type.48
  448.4 1.3 slice_bitcast_fusion
  449.7 1.4 fusion.9
  451.1 2.0 bitcast_convert_fusion
  453.1 0.7 copy.46
  453.8 0.8 copy.47
  454.7 0.7 copy.48
  455.3 0.7 copy.49
  456.0 0.7 copy.50
  456.7 0.7 copy.51
  457.4 0.9 copy.52
  (69 shorter events, 1.4 us)
Async XLA Ops:
  7.2 63.8 %all-gather.4.cloned.1.call-start = ((), (), s32[]{:S(2)}) async-start(), calls=%async_computation.3 | async-start | bytes 2048000 | tf_op jit(solution)/shard_map/all_gather | solution.py:1384
  7.9 165.1 %all-gather.6.cloned.1.call-start = ((), (), s32[]{:S(2)}) async-start(), calls=%async_computation.4 | async-start | bytes 2048000 | tf_op jit(solution)/shard_map/all_gather | solution.py:1390
  71.0 143.9 %all-gather.8.cloned.1.call-start = ((), (), s32[]{:S(2)}) async-start(), calls=%async_computation.5 | async-start | bytes 2048000 | tf_op jit(solution)/shard_map/all_gather | solution.py:1425
  73.1 10.6 %copy-start.8 = (f32[2,8,1,256]{3,2,1,0:T(1,128)}, f32[2,8,1,256]{3,2,1,0:T(1,128)S(1)}, u32[]{:S(2)}) copy-start(f32[2,8,1,256]{3,2,1,0:T(1,128)S(1)} %reshape.184.kp_ref) | copy-start | bytes 49156
  173.1 136.4 %reduce-scatter.4.cloned.1.call-start = ((), (), s32[]{:S(2)}) async-start(), calls=%async_computation.6 | async-start | bytes 2048000 | tf_op jit(solution)/shard_map/reduce_scatter | solution.py:1442
  259.1 133.4 %reduce-scatter.6.cloned.1.call-start = ((), (), s32[]{:S(2)}) async-start(), calls=%async_computation.7 | async-start | bytes 2048000 | tf_op jit(solution)/shard_map/reduce_scatter | solution.py:1450
  274.9 176.2 %reduce-scatter.8.cloned.1.call-start = ((), (), s32[]{:S(2)}) async-start(), calls=%async_computation.8 | async-start | bytes 2048000 | tf_op jit(solution)/shard_map/reduce_scatter | solution.py:1463
  392.5 0.7 copy-start.11
  392.5 1.0 copy-start.10
  392.5 1.1 copy-start.9
  407.6 39.8 %copy-start.2 = (bf16[1,160,1280]{2,1,0:T(8,128)(2,1)S(1)}, bf16[1,160,1280]{2,1,0:T(8,128)(2,1)}, u32[]{:S(2)}) copy-start(bf16[1,160,1280]{2,1,0:T(8,128)(2,1)} %reduce-scatter.6.cloned.1.call-done) | copy-start | bytes 1228804
  447.4 5.7 %copy-start.3 = (bf16[2,64,1280]{2,1,0:T(8,128)(2,1)S(1)}, bf16[2,64,1280]{2,1,0:T(8,128)(2,1)}, u32[]{:S(2)}) copy-start(bf16[2,64,1280]{2,1,0:T(8,128)(2,1)} %get-tuple-element.175) | copy-start | bytes 983044
  447.4 6.4 %copy-start.1 = (f32[2,64,1280]{2,1,0:T(8,128)S(1)}, f32[2,64,1280]{2,1,0:T(8,128)}, u32[]{:S(2)}) copy-start(f32[2,64,1280]{2,1,0:T(8,128)} %get-tuple-element.176) | copy-start | bytes 1966084
  448.4 6.2 %copy-start.7 = (f32[40,1280]{1,0:T(8,128)S(1)}, f32[40,1280]{1,0:T(8,128)}, u32[]{:S(2)}) copy-start(f32[40,1280]{1,0:T(8,128)} %get-tuple-element.177) | copy-start | bytes 614404
  451.1 4.2 copy-start.6
  453.1 2.9 copy-start.5
  453.1 3.6 copy-start.4
  453.8 3.6 copy-start
Sparse Core Ops, SparseCore 0:
  9.6 53.0 all-gather.3
  71.2 50.9 all-gather.5
  173.2 37.4 all-gather.7
  259.3 35.4 reduce-scatter.3
  297.0 35.3 reduce-scatter.5
  392.7 40.0 reduce-scatter.7

commit v4 on v3

--- a/solution.py
+++ b/solution.py
@@ -61,16 +61,17 @@
 class UlyGather:
     sems = staticmethod(lambda parts: [pltpu.SemaphoreType.DMA((3, parts))] * 2 + [pltpu.SemaphoreType.DMA((parts,))])
 
-    def __init__(self, x, o, send, recv, local):
+    def __init__(self, x, o, send, recv, local, pick=None):
+        pick = pick or (lambda i, u: o.at[i, u])
         y, c, z, s = place()
         u, v = y * 2 + c, (1 - y) * 2 + c
         mate, across = (y, 1 - c, z, s), (1 - y, c, z, s)
         self.parts = x.shape[0]
         parts = range(self.parts)
-        self.far = [remote(x.at[i], o.at[i, u], send.at[0, i], recv.at[0, i], across) for i in parts]
-        self.near = [remote(x.at[i], o.at[i, u], send.at[1, i], recv.at[1, i], mate) for i in parts]
-        self.on = [remote(o.at[i, v], o.at[i, v], send.at[2, i], recv.at[2, i], mate) for i in parts]
-        self.own = [pltpu.make_async_copy(x.at[i], o.at[i, u], local.at[i]) for i in parts]
+        self.far = [remote(x.at[i], pick(i, u), send.at[0, i], recv.at[0, i], across) for i in parts]
+        self.near = [remote(x.at[i], pick(i, u), send.at[1, i], recv.at[1, i], mate) for i in parts]
+        self.on = [remote(pick(i, v), pick(i, v), send.at[2, i], recv.at[2, i], mate) for i in parts]
+        self.own = [pltpu.make_async_copy(x.at[i], pick(i, u), local.at[i]) for i in parts]
 
     def start_part(self, i):
         self.far[i].start()
@@ -167,11 +168,14 @@
 
 
 class PlaneGather:
-    sems = [pltpu.SemaphoreType.DMA((14,))] * 2 + [pltpu.SemaphoreType.DMA((2,))]
+    @staticmethod
+    def sems(parts):
+        return [pltpu.SemaphoreType.DMA((7, parts))] * 2 + [pltpu.SemaphoreType.DMA((parts,))]
 
     def __init__(self, x, o, send, recv, local):
         y, c, z, s = place()
         mate, across, cross = plane_peers()
+        self.parts = parts = range(x.shape[0])
         me, py, px, pd = (
             plane_index(y, c, s),
             plane_index(1 - y, c, s),
@@ -179,38 +183,39 @@
             plane_index(1 - y, c, 1 - s),
         )
 
-        def copy(source, target, slot, device):
-            return remote(source, target, send.at[slot], recv.at[slot], device)
+        def copy(source, p, i, slot, device):
+            return remote(source, o.at[p, i], send.at[slot, i], recv.at[slot, i], device)
 
         def on(p, i, slot, device):
-            return copy(o.at[p, i], o.at[p, i], slot, device)
-
-        self.by_y = [copy(x.at[i], o.at[me, i], i, across) for i in (0, 1)]
-        self.by_x = [copy(x.at[i], o.at[me, i], 2 + i, cross) for i in (0, 1)]
-        self.near = [copy(x.at[i], o.at[me, i], 4 + i, mate) for i in (0, 1)]
-        self.corner = [on(py, 0, 6, cross), on(px, 1, 7, across)]
-        self.pass_y = [on(py, 0, 8, mate), on(py, 1, 10, mate)]
-        self.pass_x = [on(px, 0, 11, mate), on(px, 1, 9, mate)]
-        self.pass_d = [on(pd, 0, 12, mate), on(pd, 1, 13, mate)]
-        self.own = [pltpu.make_async_copy(x.at[i], o.at[me, i], local.at[i]) for i in (0, 1)]
+            return copy(o.at[p, i], p, i, slot, device)
+
+        self.by_y = [copy(x.at[i], me, i, 0, across) for i in parts]
+        self.by_x = [copy(x.at[i], me, i, 1, cross) for i in parts]
+        self.near = [copy(x.at[i], me, i, 2, mate) for i in parts]
+        self.corner = [on(px, i, 3, across) if i % 2 else on(py, i, 3, cross) for i in parts]
+        self.pass_y = [on(py, i, 4, mate) for i in parts]
+        self.pass_x = [on(px, i, 5, mate) for i in parts]
+        self.pass_d = [on(pd, i, 6, mate) for i in parts]
+        self.own = [pltpu.make_async_copy(x.at[i], o.at[me, i], local.at[i]) for i in parts]
 
     def start_part(self, i):
         for copy in (self.by_y[i], self.by_x[i], self.near[i], self.own[i]):
             copy.start()
 
     def forward_part(self, i):
-        first, then = ((self.by_y, self.pass_y), (self.by_x, self.pass_x))[:: 1 - 2 * i]
-        first[0][i].wait_recv()
+        ways = [(self.by_y[i], self.pass_y[i]), (self.by_x[i], self.pass_x[i])]
+        first, then = ways[:: 1 - 2 * (i % 2)]
+        first[0].wait_recv()
         self.corner[i].start()
-        first[1][i].start()
-        then[0][i].wait_recv()
-        then[1][i].start()
+        first[1].start()
+        then[0].wait_recv()
+        then[1].start()
 
     def finish(self):
-        for i in (0, 1):
+        for i in self.parts:
             self.corner[i].wait_recv()
             self.pass_d[i].start()
-        for i in (0, 1):
+        for i in self.parts:
             for copy in (self.near[i], self.pass_y[i], self.pass_x[i], self.pass_d[i]):
                 copy.wait()
             for copy in (self.by_y[i], self.by_x[i], self.corner[i]):
@@ -222,30 +227,29 @@
     @staticmethod
     def scratch(x):
         one = pltpu.VMEM(x.shape[1:], x.dtype)
-        return [pltpu.VMEM((4,) + x.shape[1:], x.dtype)] + [one] * 6 + [pltpu.SemaphoreType.DMA((14,))] * 2
+        sems = pltpu.SemaphoreType.DMA((7, x.shape[1]))
+        return [pltpu.VMEM((4,) + x.shape[1:], x.dtype)] + [one] * 6 + [sems] * 2
 
     def __init__(self, x, near, out_x, out_y, out_d, in_x, in_y, in_d, send, recv):
         y, c, z, s = place()
         mate, across, cross = plane_peers()
         self.c = c
+        self.parts = parts = range(x.shape[1])
         self.spots = ((1 - y, 1 - s), (y, 1 - s), (1 - y, s), (y, s))
         self.x, self.near_ref = x, near
         self.out_x, self.out_y, self.out_d = out_x, out_y, out_d
         self.in_x, self.in_y, self.in_d = in_x, in_y, in_d
 
-        def copy(source, target, slot, device):
-            return remote(source, target, send.at[slot], recv.at[slot], device)
+        def copy(source, target, i, slot, device):
+            return remote(source, target, send.at[slot, i], recv.at[slot, i], device)
 
         self.near = [
-            [copy(x.at[plane_index(sy, 1 - c, ss), i], near.at[k, i], 2 * k + i, mate) for i in (0, 1)]
+            [copy(x.at[plane_index(sy, 1 - c, ss), i], near.at[k, i], i, k, mate) for i in parts]
             for k, (sy, ss) in enumerate(self.spots)
         ]
-        self.corner = [
-            copy(out_d.at[0], in_d.at[0], 8, cross),
-            copy(out_d.at[1], in_d.at[1], 9, across),
-        ]
-        self.by_x = [copy(out_x.at[i], in_x.at[i], 10 + i, cross) for i in (0, 1)]
-        self.by_y = [copy(out_y.at[i], in_y.at[i], 12 + i, across) for i in (0, 1)]
+        self.corner = [copy(out_d.at[i], in_d.at[i], i, 4, across if i % 2 else cross) for i in parts]
+        self.by_x = [copy(out_x.at[i], in_x.at[i], i, 5, cross) for i in parts]
+        self.by_y = [copy(out_y.at[i], in_y.at[i], i, 6, across) for i in parts]
 
     def pair(self, k, i):
         sy, ss = self.spots[k]
@@ -258,23 +262,23 @@
                 copy.start()
 
     def middle(self):
-        for i in (0, 1):
+        for i in self.parts:
             self.out_d[i] = self.pair(0, i).astype(BF)
             self.corner[i].start()
-        self.out_x[0] = self.pair(1, 0).astype(BF)
-        self.by_x[0].start()
-        self.out_y[1] = self.pair(2, 1).astype(BF)
-        self.by_y[1].start()
+            if i % 2 == 0:
+                self.out_x[i] = self.pair(1, i).astype(BF)
+                self.by_x[i].start()
+            else:
+                self.out_y[i] = self.pair(2, i).astype(BF)
+                self.by_y[i].start()
 
     def last(self):
-        part = self.pair(2, 0)
-        self.corner[0].wait_recv()
-        self.out_y[0] = (part + self.in_d[0].astype(F32)).astype(BF)
-        self.by_y[0].start()
-        part = self.pair(1, 1)
-        self.corner[1].wait_recv()
-        self.out_x[1] = (part + self.in_d[1].astype(F32)).astype(BF)
-        self.by_x[1].start()
+        for i in self.parts:
+            k, out, by = (1, self.out_x, self.by_x) if i % 2 else (2, self.out_y, self.by_y)
+            part = self.pair(k, i)
+            self.corner[i].wait_recv()
+            out[i] = (part + self.in_d[i].astype(F32)).astype(BF)
+            by[i].start()
 
     def result(self, i):
         own = self.pair(3, i)
@@ -405,11 +409,7 @@
         y, c, self.z, self.s = place()
         self.n = n_line
         (self.has_low, self.low), (self.has_high, self.high), self.cross = line_ends(n_line)
-        s = self.s
-        if isinstance(x, tuple):
-            self.leaves, self.stays = (lambda zz: x[0].at[zz]), (lambda zz: x[1][...])
-        else:
-            self.leaves, self.stays = (lambda zz: x.at[zz * 2 + 1 - s]), (lambda zz: x[zz * 2 + s])
+        self.x = x
         self.side_in, self.line_in = side_in, line_in
         self.sem = (side_send, side_recv, send, recv)
 
@@ -422,7 +422,7 @@
     def side(self, zz):
         side_send, side_recv = self.sem[:2]
         return remote(
-            self.leaves(zz), self.side_in.at[zz], side_send.at[zz], side_recv.at[zz], self.cross
+            self.x.at[zz * 2 + 1 - self.s], self.side_in.at[zz], side_send.at[zz], side_recv.at[zz], self.cross
         )
 
     def slot(self, way, k):
@@ -455,12 +455,12 @@
         def _():
             self.arrive(way, k).wait_recv()
             self.side_in[zz] = add_low(
-                self.stays(zz), self.side_in[zz], self.line_in[zz]
+                self.x[zz * 2 + self.s], self.side_in[zz], self.line_in[zz]
             ).astype(self.side_in.dtype)
 
         @pl.when(jnp.logical_not(passed))
         def _():
-            self.side_in[zz] = add_low(self.stays(zz), self.side_in[zz]).astype(
+            self.side_in[zz] = add_low(self.x[zz * 2 + self.s], self.side_in[zz]).astype(
                 self.side_in.dtype
             )
 
@@ -475,7 +475,7 @@
         self.side(z).wait_recv()
         pl.when(self.has_low)(lambda: self.arrive(0, 0).wait_recv())
         pl.when(self.has_high)(lambda: self.arrive(1, 0).wait_recv())
-        own = add_low(self.stays(z), self.side_in[z])
+        own = add_low(self.x[z * 2 + self.s], self.side_in[z])
 
         @pl.when(jnp.logical_and(self.has_low, self.has_high))
         def _():
@@ -499,9 +499,182 @@
                         self.move(way, k).wait_send()
 
 
+class LineGather:
+    @staticmethod
+    def sems(n_line):
+        dma = pltpu.SemaphoreType.DMA
+        return [dma((2,)), dma((2, n_line)), dma((2, n_line)), dma((1,))]
+
+    def __init__(self, n_line, pick_x, pick_o, own_send, send, recv, local):
+        y, c, self.z, s = place()
+        self.n = n_line
+        (self.has_low, self.low), (self.has_high, self.high), _ = line_ends(n_line)
+        self.pick_x, self.pick_o = pick_x, pick_o
+        self.own_send, self.send, self.recv, self.local = own_send, send, recv, local
+
+    def goes(self, way):
+        return (self.has_high, self.has_low)[way]
+
+    def own(self, way):
+        target = (self.high, self.low)[way]
+        return remote(self.pick_x(), self.pick_o(self.z), self.own_send.at[way], self.recv.at[way, 0], target)
+
+    def keep(self):
+        return pltpu.make_async_copy(self.pick_x(), self.pick_o(self.z), self.local.at[0])
+
+    def onward(self, way, k):
+        block = self.pick_o(self.z - k if way == 0 else self.z + k)
+        target = (self.high, self.low)[way]
+        return remote(block, block, self.send.at[way, k], self.recv.at[way, k], target)
+
+    def arrive(self, way, k):
+        block = self.pick_o(self.z - k if way == 0 else self.z + k)
+        return remote(block, block, self.send.at[way, k], self.recv.at[way, k - 1], (self.low, self.high)[way])
+
+    def there(self, way, k):
+        return self.z >= k if way == 0 else self.z + k < self.n
+
+    def start(self):
+        for way in (0, 1):
+            pl.when(self.goes(way))(lambda: self.own(way).start())
+        self.keep().start()
+
+    def step(self, k):
+        for way in (0, 1):
+            @pl.when(self.there(way, k))
+            def _():
+                self.arrive(way, k).wait_recv()
+                pl.when(self.goes(way))(lambda: self.onward(way, k).start())
+
+    def finish(self):
+        self.keep().wait()
+        for way in (0, 1):
+            pl.when(self.goes(way))(lambda: self.own(way).wait_send())
+            for k in range(1, self.n):
+                pl.when(self.there(way, k) & self.goes(way))(lambda: self.onward(way, k).wait_send())
+
+
+class LineReduce:
+    @staticmethod
+    def scratch(n_line, a):
+        dma = pltpu.SemaphoreType.DMA
+        return [
+            pltpu.VMEM((n_line,) + a.shape[1:], a.dtype),
+            pltpu.VMEM((n_line + 1,) + a.shape[1:], a.dtype),
+            dma((2, n_line)), dma((2, n_line)),
+        ]
+
+    def __init__(self, n_line, x, sums, line_in, send, recv):
+        y, c, self.z, s = place()
+        self.n, self.x, self.sums, self.line_in, self.send, self.recv = n_line, x, sums, line_in, send, recv
+        (self.has_low, self.low), (self.has_high, self.high), _ = line_ends(n_line)
+
+    def spot(self, way, k):
+        return self.z + k if way == 0 else self.z - k
+
+    def exists(self, way, k):
+        return self.z + k < self.n if way == 0 else self.z >= k
+
+    def slot(self, way, k):
+        return jnp.where(k == 0, self.n, self.spot(way, k)) if way == 1 else self.spot(way, k)
+
+    def move(self, way, k):
+        zz = self.spot(way, k)
+        there = jnp.where(k == 1, self.n, zz) if way == 1 else zz
+        return remote(
+            self.sums.at[zz], self.line_in.at[there], self.send.at[way, k], self.recv.at[way, k - 1],
+            (self.high, self.low)[way],
+        )
+
+    def arrive(self, way, k):
+        there = self.line_in.at[self.slot(way, k)]
+        return remote(there, there, self.send.at[way, k], self.recv.at[way, k], (self.low, self.high)[way])
+
+    def step(self, k):
+        for way in (0, 1):
+            @pl.when(self.exists(way, k))
+            def _():
+                zz = self.spot(way, k)
+                passed = (self.has_low, self.has_high)[way]
+
+                @pl.when(passed)
+                def _():
+                    self.arrive(way, k).wait_recv()
+                    self.sums[zz] = add_low(self.x[zz], self.line_in[zz]).astype(self.sums.dtype)
+
+                @pl.when(jnp.logical_not(passed))
+                def _():
+                    self.sums[zz] = self.x[zz]
+
+                self.move(way, k).start()
+
+    def result(self, o):
+        z = self.z
+        pl.when(self.has_low)(lambda: self.arrive(0, 0).wait_recv())
+        pl.when(self.has_high)(lambda: self.arrive(1, 0).wait_recv())
+
+        @pl.when(self.has_low & self.has_high)
+        def _():
+            o[...] = add_low(self.x[z], self.line_in[z], self.line_in[self.n]).astype(o.dtype)
+
+        @pl.when(jnp.logical_not(self.has_low))
+        def _():
+            o[...] = add_low(self.x[z], self.line_in[self.n]).astype(o.dtype)
+
+        @pl.when(jnp.logical_not(self.has_high))
+        def _():
+            o[...] = add_low(self.x[z], self.line_in[z]).astype(o.dtype)
+
+    def finish(self):
+        for k in range(self.n - 1, 0, -1):
+            for way in (0, 1):
+                pl.when(self.exists(way, k))(lambda: self.move(way, k).wait_send())
+
+
+def lane_chunks(width):
+    cut = width // 256 * 128
+    return [slice(0, cut), slice(cut, width)]
+
+
+LINE_CHUNKS = 2
+
+
+def line_gathers(n_line, x, pick_o, sems):
+    jobs = []
+    for i, lanes in enumerate(lane_chunks(x.shape[-1])):
+        cut = (slice(None),) * (len(x.shape) - 1) + (lanes,)
+        jobs.append(
+            LineGather(
+                n_line, lambda cut=cut: x.at[cut], lambda z, cut=cut: pick_o(z).at[cut],
+                *sems[4 * i : 4 * i + 4],
+            )
+        )
+    return jobs
+
+
+def line_gather_sems(n_line):
+    return LineGather.sems(n_line) * LINE_CHUNKS
+
+
+def line_reduces(n_line, x, scratch):
+    jobs = []
+    for i, lanes in enumerate(lane_chunks(x.shape[-1])):
+        cut = (slice(None),) * (len(x.shape) - 1) + (lanes,)
+        jobs.append((LineReduce(n_line, x.at[cut], *scratch[4 * i : 4 * i + 4]), cut[1:]))
+    return jobs
+
+
+def line_reduce_scratch(n_line, a):
+    scratch = []
+    for lanes in lane_chunks(a.shape[-1]):
+        one = jax.ShapeDtypeStruct(a.shape[:-1] + (lanes.stop - lanes.start,), a.dtype)
+        scratch += LineReduce.scratch(n_line, one)
+    return scratch
+
+
 def exit_kernel(
-    n_line, gq, gk, gv, gh, res, oc, dc, alpha, rest,
-    gq_o, gk_o, gv_o, gh_o, go_o, gd_o, sum_o, oc_o, dc_o,
+    n_line, gq, gk, gv, gh, res, oc, dc, alpha, rest, gg,
+    gq_o, gk_o, gv_o, gh_o, go_o, gd_o, sum_o, gg_o, oc_o, dc_o,
     alpha_in, line_out, line_all, oc_s, oc_r, dc_s, dc_r, al_s, al_r, su_s, su_r, keep, *scratch,
 ):
     y, c, z, s = place()
@@ -516,7 +689,9 @@
     greet([(yy, cc, z, ss) for yy, cc, ss in corners], list(zip(once, others)))
     heads = 6
     jobs = [BlkReduce(n_line, x, *scratch[heads * i : heads * (i + 1)]) for i, x in enumerate((gq, gk, gv))]
-    hid = UlyReduce(gh, *scratch[heads * 3 :])
+    split = heads * 3 + len(UlyReduce.scratch(gh))
+    hid = UlyReduce(gh, *scratch[heads * 3 : split])
+    gates = line_reduces(n_line, gg, scratch[split:])
     small, cols = [], []
     for k, (yy, cc, ss) in enumerate(corners):
         target = (yy, cc, z, ss)
@@ -551,9 +726,14 @@
         )
     for job in line_jobs:
         job.start()
+    for job, _ in gates:
+        job.step(n_line - 1)
     for k in range(n_line - 1, 0, -1):
         for job in jobs:
             job.step(k)
+        if k > 1:
+            for job, _ in gates:
+                job.step(k - 1)
     for i in range(gh.shape[0]):
         gh_o[i] = res[i] + hid.result(i)
     for job in cols:
@@ -574,6 +754,9 @@
     sum_o[...] = total
     for job, o in zip(jobs, (gq_o, gk_o, gv_o)):
         job.result(o)
+    for job, cut in gates:
+        job.result(gg_o.at[cut])
+        job.finish()
     hid.finish()
     for job in jobs:
         job.finish()
@@ -583,7 +766,7 @@
         job.wait_send()
 
 
-def leave(n_line, gq, gk, gv, gh, res, oc, dc, alpha, rest):
+def leave(n_line, gq, gk, gv, gh, res, oc, dc, alpha, rest, gg):
     n_blk = 2 * n_line
     vmem = pl.BlockSpec(memory_space=pltpu.VMEM)
     dma = pltpu.SemaphoreType.DMA
@@ -598,7 +781,7 @@
     ]
     for g in (gq, gk, gv):
         scratch += BlkReduce.scratch(n_line, g)
-    scratch += UlyReduce.scratch(gh)
+    scratch += UlyReduce.scratch(gh) + line_reduce_scratch(n_line, gg)
     grad = jax.ShapeDtypeStruct(gq.shape[1:], F32)
     return pl.pallas_call(
         functools.partial(exit_kernel, n_line),
@@ -608,18 +791,20 @@
             jax.ShapeDtypeStruct((oc.shape[1], 4 * oc.shape[2]), F32),
             jax.ShapeDtypeStruct((dc.shape[1], 8 * dc.shape[2]), F32),
             jax.ShapeDtypeStruct(rest.shape[1:], F32),
+            jax.ShapeDtypeStruct(gg.shape[1:], F32),
         ],
-        in_specs=[vmem] * 9,
-        out_specs=[vmem] * 7,
+        in_specs=[vmem] * 10,
+        out_specs=[vmem] * 8,
         scratch_shapes=scratch,
         compiler_params=params(8),
         cost_estimate=pl.CostEstimate(flops=0, bytes_accessed=40 * 3_000_000, transcendentals=0),
         name="leave",
-    )(gq, gk, gv, gh, res, oc, dc, alpha, rest)
+    )(gq, gk, gv, gh, res, oc, dc, alpha, rest, gg)
 
 
 def entry_kernel(
-    n_line, hid, small, wq, wk, wv, wo, wd, hid_o, small_o, wq_o, wk_o, wv_o, oc_o, dc_o, oc, dc, *sems
+    n_line, hid, small, wq, wk, wv, wo, wd, wu,
+    hid_o, small_o, wq_o, wk_o, wv_o, oc_o, dc_o, wu_o, oc, dc, *sems
 ):
     y, c, z, s = place()
     u, p = y * 2 + c, plane_index(y, c, s)
@@ -636,7 +821,9 @@
     ):
         jobs.append(BlkGather(n_line, lambda x=x: x, pick, *sems[at : at + 5]))
         at += 5
-    oc_s, oc_r, dc_s, dc_r, sm_s, sm_r, keep = sems[at:]
+    line_count = 4 * LINE_CHUNKS
+    up_jobs = line_gathers(n_line, wu, lambda z: wu_o.at[z], sems[at : at + line_count])
+    oc_s, oc_r, dc_s, dc_r, sm_s, sm_r, keep = sems[at + line_count :]
     jobs[0].start()
     for job in jobs[1:]:
         job.start()
@@ -659,6 +846,8 @@
             col_jobs.append(remote(oc.at[yy * 2 + cc], oc_o.at[u], oc_s.at[k], oc_r.at[k], target))
     for job in col_jobs:
         job.start()
+    for job in up_jobs:
+        job.start()
     mine = [
         pltpu.make_async_copy(dc.at[p], dc_o.at[p], keep.at[0]),
         pltpu.make_async_copy(oc.at[u], oc_o.at[u], keep.at[1]),
@@ -677,9 +866,14 @@
     ]
     for job in small_jobs:
         job.start()
+    for k in range(1, n_line):
+        for job in up_jobs:
+            job.step(k)
     for job in jobs[1:]:
         job.finish_arrivals()
     hid_job.finish()
+    for job in up_jobs:
+        job.finish()
     for job in small_jobs + col_jobs:
         job.wait()
     for job in mine:
@@ -688,7 +882,7 @@
         job.finish_sends()
 
 
-def entry(n_line, hid, small, wq, wk, wv, wo, wd):
+def entry(n_line, hid, small, wq, wk, wv, wo, wd, wu):
     n_blk = 2 * n_line
     oc = jax.ShapeDtypeStruct((4, wo.shape[0], wo.shape[1] // 4), wo.dtype)
     dc = jax.ShapeDtypeStruct((8, wd.shape[0], wd.shape[1] // 8), wd.dtype)
@@ -708,12 +902,14 @@
             out((n_blk,) + wv.shape, wv),
             out(oc.shape, oc),
             out(dc.shape, dc),
+            out((n_line,) + wu.shape, wu),
         ],
-        in_specs=[vmem] * 7,
-        out_specs=[vmem, vmem, anyway, anyway, anyway, vmem, vmem],
+        in_specs=[vmem] * 8,
+        out_specs=[vmem, vmem, anyway, anyway, anyway, vmem, vmem, anyway],
         scratch_shapes=[pltpu.VMEM(oc.shape, oc.dtype), pltpu.VMEM(dc.shape, dc.dtype)]
         + UlyGather.sems(parts)
         + BlkGather.sems(n_line) * 4
+        + line_gather_sems(n_line)
         + [pltpu.SemaphoreType.DMA((3,))] * 2
         + [pltpu.SemaphoreType.DMA((7,))] * 2
         + [pltpu.SemaphoreType.DMA((3,))] * 2
@@ -721,7 +917,7 @@
         compiler_params=params(6),
         cost_estimate=pl.CostEstimate(flops=0, bytes_accessed=40 * 3_000_000, transcendentals=0),
         name="entry",
-    )(hid, small, wq, wk, wv, wo, wd)
+    )(hid, small, wq, wk, wv, wo, wd, wu)
 def dot_nt(a, b):
     return lax.dot_general(a, b, (((1,), (1,)), ((), ())), preferred_element_type=F32)
 
@@ -805,8 +1001,8 @@
 
 
 def attend_kernel(
-    n_line, q_ref, kv_ref, oc_ref, qp_ref, kp_ref,
-    kv_o, oc_o, o_ref, mixed_ref, inv_ref, acc, total, place_q, *sems,
+    n_line, q_ref, kv_ref, oc_ref, wg_ref, qp_ref, kp_ref,
+    kv_o, oc_o, wg_o, o_ref, mixed_ref, inv_ref, acc, total, place_q, *sems,
 ):
     y, c, z, s = place()
     blk_greet(n_line)
@@ -815,12 +1011,15 @@
     each = len(BlkGather.sems(n_line))
     picks = [
         (lambda i=i: kv_ref.at[i], lambda block, i=i: kv_o.at[block, i]) for i in range(seqs)
-    ] + [(lambda: oc_ref.at[0], lambda block: oc_o.at[block, 0])]
+    ] + [(lambda: oc_ref, lambda block: oc_o.at[:, block])]
     jobs = [
         BlkGather(n_line, *pick, *sems[each * i : each * (i + 1)]) for i, pick in enumerate(picks)
     ]
+    gates = line_gathers(n_line, wg_ref, lambda z: wg_o.at[z], sems[each * (seqs + 1) :])
     for job in jobs:
         job.start()
+    for job in gates:
+        job.keep().start()
     acc[...] = jnp.zeros_like(acc)
     total[...] = jnp.zeros_like(total)
     for i in range(seqs):
@@ -829,8 +1028,9 @@
     def attend_to(i, block, keys):
         allowed = kp_ref[i, block] <= place_q[i]
         for h in range(heads):
-            kv = keys(h)
-            p = jnp.where(allowed, jnp.exp(dot_nt(q_ref[i, :, h * 128 : (h + 1) * 128], kv)), 0.0)
+            lanes = slice(h * 128, (h + 1) * 128)
+            kv = keys(lanes)
+            p = jnp.where(allowed, jnp.exp(dot_nt(q_ref[i, :, lanes], kv)), 0.0)
             part = p[:, :128]
             for j in range(1, rows // 128):
                 part = part + p[:, j * 128 : (j + 1) * 128]
@@ -838,6 +1038,13 @@
             acc[i, h] = acc[i, h] + dot_nn(p.astype(BF), kv)
 
     def body(stage, k, way):
+        ahead = jnp.where(k == 0, 1, k + 1)
+
+        @pl.when((stage == 1) & ((k == 0) | (way == 1)) & (ahead < n_line))
+        def _():
+            for job in gates:
+                job.step(ahead)
+
         there = (k == 0) | jnp.where(way == 0, z >= k, z + k < n_line)
 
         @pl.when(there)
@@ -848,10 +1055,15 @@
                     pl.when((stage == 1) & (k > 0) & (way == w))(lambda: job.over(w, k).wait_recv())
                 pl.when((stage == 1) & (k == 0))(lambda: job.own(2).wait_recv())
                 pl.when((stage == 0) & (k == 0))(lambda: job.keep().wait())
+            for w, last in ((0, z), (1, n_line - 1 - z)):
+                @pl.when((stage == 0) & (k == last) & ((k == 0) | (way == w)))
+                def _():
+                    for job in gates:
+                        pl.when(job.goes(w))(lambda: job.own(w).start())
             zz = jnp.where(way == 0, z - k, z + k)
             block = zz * 2 + jnp.where(stage == 0, s, 1 - s)
             for i in range(seqs):
-                attend_to(i, block, lambda h: kv_o[block, i, :, h * 128 : (h + 1) * 128])
+                attend_to(i, block, lambda lanes: kv_o[block, i, :, lanes])
 
     arrivals(n_line, body)
     low = lanes_of((rows, 128)) < HEAD_DIM
@@ -871,27 +1083,30 @@
             mixed_ref[i, :, (heads - 1) * HEAD_DIM :] = pltpu.roll(outs[-1], HEAD_DIM, 1)[:, :HEAD_DIM].astype(BF)
     for job in jobs:
         job.finish_sends()
-
-
-def attend(n_line, q, kv, oc, q_places, k_places):
+    for job in gates:
+        job.finish()
+
+
+def attend(n_line, q, kv, oc, wg, q_places, k_places):
     seqs, rows, wide = q.shape
     n_blk, heads = 2 * n_line, wide // 128
     head = (seqs, heads, rows, 128)
     return comm_call(
-        functools.partial(attend_kernel, n_line), "attend", 5, (q, kv, oc, q_places, k_places),
+        functools.partial(attend_kernel, n_line), "attend", 5, (q, kv, oc, wg, q_places, k_places),
         [
-            ((n_blk,) + kv.shape, BF), ((n_blk,) + oc.shape, BF), (head, F32),
+            ((n_blk,) + kv.shape, BF), (oc.shape[:1] + (n_blk,) + oc.shape[1:], BF),
+            ((n_line,) + wg.shape, BF), (head, F32),
             ((seqs, rows, heads * HEAD_DIM), BF), ((seqs, heads, 8, rows), F32),
         ],
         [pltpu.VMEM(head, F32), pltpu.VMEM(head, F32), pltpu.VMEM((seqs, rows, rows), F32)]
-        + BlkGather.sems(n_line) * (seqs + 1),
-        75,
+        + BlkGather.sems(n_line) * (seqs + 1) + line_gather_sems(n_line),
+        75, far_outs=(1, 2),
     )
 
 
 def attend_back_kernel(
-    n_line, q_ref, low_ref, w_ref, mixed_ref, o_ref, inv_ref, kv_ref, qp_ref, kp_ref,
-    dq_ref, dkv_ref, oc_ref, dz, delta, dq, parts, oparts, *scratch,
+    n_line, fits, q_ref, low_ref, w_ref, mixed_ref, o_ref, inv_ref, kv_ref, qp_ref, kp_ref, gu_ref,
+    dq_ref, dkv_ref, oc_ref, gu_o, dz, delta, dq, parts, oparts, key_s, key_sem, *scratch,
 ):
     y, c, z, s = place()
     blk_greet(n_line)
@@ -905,11 +1120,9 @@
             at = (v * n_blk + b) * each_out
             oparts[b, v * each_out : (v + 1) * each_out] = grad[at : at + each_out]
     each = 6
-    jobs = [
-        BlkReduce(n_line, (parts.at[:, i], parts.at[n_line, i]), *scratch[each * i : each * (i + 1)])
-        for i in range(seqs)
-    ]
-    out_job = BlkReduce(n_line, oparts, *scratch[each * seqs :])
+    jobs = [BlkReduce(n_line, parts.at[:, i], *scratch[each * i : each * (i + 1)]) for i in range(seqs)]
+    out_job = BlkReduce(n_line, oparts, *scratch[each * seqs : each * (seqs + 1)])
+    ups = line_reduces(n_line, gu_ref, scratch[each * (seqs + 1) :])
     for k in range(n_line - 1, -1, -1):
         out_job.start(k)
     low = lanes_of((rows, 128)) < HEAD_DIM
@@ -929,43 +1142,57 @@
             delta[i, h] = jnp.transpose(jnp.broadcast_to(row, (rows, 128)))[:8]
     dq[...] = jnp.zeros_like(dq)
 
-    def block_of(block, spot):
+    def block_of(block):
+        if fits:
+            keys = kv_ref.at[block]
+        else:
+            keys = key_s
+            copy = pltpu.make_async_copy(kv_ref.at[block], key_s, key_sem.at[0])
+            copy.start()
+            copy.wait()
         for i in range(seqs):
             allowed = down_columns(kp_ref[i, block]) <= qp_ref[i]
             for h in range(heads):
                 lanes = slice(h * 128, (h + 1) * 128)
-                kv = kv_ref[block, i, :, lanes]
+                kv = keys[i, :, lanes]
                 pair = jnp.concatenate([q_ref[i, :, lanes], dz[i, h]], axis=0)
                 scores = dot_nt(kv, pair)
                 p = jnp.where(allowed, jnp.exp(scores[:, :rows]) * inv_ref[i, h][:1], 0.0)
                 ds = (p * (scores[:, rows:] - delta[i, h][:1])).astype(BF)
-                parts[spot, i, :, lanes] = dot_nn(
+                parts[block, i, :, lanes] = dot_nn(
                     jnp.concatenate([ds, p.astype(BF)], axis=1), pair
                 ).astype(BF)
                 dq[i, h] = dq[i, h] + dot_tn(ds, kv)
 
-    def body(stage, k, way):
+    def step(t, carry):
+        k, r = n_line - 1 - t // 4, lax.rem(t, 4)
+        way, stays = r // 2, lax.rem(r, 2)
+
+        @pl.when((r == 0) & (k > 0))
+        def _():
+            for line_job, _ in ups:
+                line_job.step(k)
+
         there = jnp.where(k == 0, way == 0, jnp.where(way == 0, z + k < n_line, z >= k))
 
         @pl.when(there)
         def _():
             zz = jnp.where(way == 0, z + k, z - k)
-            block_of(zz * 2 + jnp.where(stage == 0, 1 - s, s), jnp.where(stage == 0, zz, n_line))
-
-            @pl.when(stage == 0)
+            block_of(zz * 2 + jnp.where(stays == 0, 1 - s, s))
+
+            @pl.when(stays == 0)
             def _():
                 for job in jobs:
                     job.side(zz).start()
 
+        @pl.when((r == 3) & (k + 1 < n_line))
+        def _():
             for w in (0, 1):
-                @pl.when((stage == 1) & (k > 0) & (way == w))
+                @pl.when(jobs[0].exists(w, k + 1))
                 def _():
                     for job in jobs + [out_job]:
-                        job.move_on(w, k)
-
-    def step(t, carry):
-        r = lax.rem(t, 2 * n_line)
-        body(t // (2 * n_line), n_line - 1 - r // 2, lax.rem(r, 2))
+                        job.move_on(w, k + 1)
+
         return carry
 
     lax.fori_loop(0, 4 * n_line, step, 0)
@@ -975,11 +1202,13 @@
     out_job.result(oc_ref)
     for i, job in enumerate(jobs):
         job.result(dkv_ref.at[i])
-    for job in jobs + [out_job]:
+    for job, cut in ups:
+        job.result(gu_o.at[cut])
+    for job in jobs + [out_job] + [job for job, _ in ups]:
         job.finish()
 
 
-def attend_back(n_line, q, low, w, mixed, o, inv, kv, q_places, k_places):
+def attend_back(n_line, q, low, w, mixed, o, inv, kv, q_places, k_places, gu):
     seqs, rows, wide = q.shape
     n_blk, heads = 2 * n_line, wide // 128
     head = (seqs, heads, rows, 128)
@@ -987,16 +1216,19 @@
     out_shape = (width // n_blk, columns)
     one = jax.ShapeDtypeStruct((n_blk,) + kv.shape[2:], BF)
     out_one = jax.ShapeDtypeStruct((n_blk,) + out_shape, BF)
+    fits = kv.size * 2 <= 8_000_000
     return comm_call(
-        functools.partial(attend_back_kernel, n_line), "attend_back", 7,
-        (q, low, w, mixed, o, inv, kv, q_places, k_places),
-        [(q.shape, BF), (kv.shape[1:], BF), (out_shape, BF)],
+        functools.partial(attend_back_kernel, n_line, fits), "attend_back", 7,
+        (q, low, w, mixed, o, inv, kv, q_places, k_places, gu),
+        [(q.shape, BF), (kv.shape[1:], BF), (out_shape, BF), (gu.shape[1:], F32)],
         [
             pltpu.VMEM(head, BF), pltpu.VMEM((seqs, heads, 8, rows), F32), pltpu.VMEM(head, F32),
-            pltpu.VMEM((n_line + 1,) + kv.shape[1:], BF), pltpu.VMEM(out_one.shape, BF),
+            pltpu.VMEM(kv.shape, BF), pltpu.VMEM(out_one.shape, BF),
+            pltpu.VMEM((16, 128) if fits else kv.shape[1:], BF), pltpu.SemaphoreType.DMA((1,)),
         ]
-        + BlkReduce.scratch(n_line, one) * seqs + BlkReduce.scratch(n_line, out_one),
-        75, 67_000_000,
+        + BlkReduce.scratch(n_line, one) * seqs + BlkReduce.scratch(n_line, out_one)
+        + line_reduce_scratch(n_line, gu),
+        75, 67_000_000, () if fits else (6,),
     )
 
 
@@ -1090,56 +1322,6 @@
     )(x, wu, wg, us, gs)
 
 
-def ff_back_kernel(d_ref, wd_ref, up_ref, gate_ref, us_ref, gs_ref, du_ref, dg_ref, sum_ref):
-    d = dot_nn(d_ref[...], wd_ref[...])
-    up, gate = up_ref[...], gate_ref[...]
-    us, gs = us_ref[...], gs_ref[...] * D**0.5
-    z = gate * gs
-    sig = 1.0 / (1.0 + jnp.exp(-z))
-    du = d * (z * sig)
-    dz = d * (up * us) * sig * (1.0 + z * (1.0 - sig))
-    du_ref[...] = (du * us).astype(BF)
-    dg_ref[...] = (dz * gs).astype(BF)
-    sums = jnp.concatenate(
-        [
-            jnp.sum(du * up, axis=0, keepdims=True),
-            jnp.sum(dz * gate, axis=0, keepdims=True) * D**0.5,
-        ],
-        axis=0,
-    )
-    i = pl.program_id(0)
-
-    @pl.when(i == 0)
-    def _():
-        sum_ref[...] = sums
-
-    @pl.when(i > 0)
-    def _():
-        sum_ref[...] = sum_ref[...] + sums
-
-
-def ff_back(d, wd, up, gate, us, gs):
-    rows, width = d.shape
-    columns = wd.shape[1]
-    block = rows // 4
-    whole = lambda a: pl.BlockSpec(a.shape, lambda i: (0, 0))
-    part = lambda n: pl.BlockSpec((block, n), lambda i: (i, 0))
-    out = jax.ShapeDtypeStruct((rows, columns), BF)
-    return pl.pallas_call(
-        ff_back_kernel,
-        grid=(4,),
-        out_shape=[out, out, jax.ShapeDtypeStruct((2, columns), F32)],
-        in_specs=[part(width), whole(wd), part(columns), part(columns), whole(us), whole(gs)],
-        out_specs=[part(columns), part(columns), pl.BlockSpec((2, columns), lambda i: (0, 0))],
-        compiler_params=pltpu.CompilerParams(vmem_limit_bytes=VMEM_BYTES),
-        cost_estimate=pl.CostEstimate(
-            flops=2 * rows * width * columns, bytes_accessed=2 * rows * width + 14 * rows * columns,
-            transcendentals=rows * columns,
-        ),
-        name="ff_back",
-    )(d, wd, up, gate, us, gs)
-
-
 def unit_of(x):
     c = lax.rsqrt(jnp.sum(x * x, axis=-1, keepdims=True) + x.shape[-1] * tiny_eps)
     return x * c, c
@@ -1149,13 +1331,31 @@
     return c * (dy - y * jnp.sum(y * dy, axis=-1, keepdims=True))
 
 
-def comm_call(kernel, name, collective_id, args, outs, scratch, micros, room=VMEM_BYTES):
-    vmem = pl.BlockSpec(memory_space=pltpu.VMEM)
+class Late:
+    @staticmethod
+    def scratch(arrays):
+        return [pltpu.VMEM(a.shape, a.dtype) for a in arrays] + [pltpu.SemaphoreType.DMA((len(arrays),))]
+
+    def __init__(self, refs, scratch):
+        *self.bufs, sem = scratch
+        self.copies = [
+            pltpu.make_async_copy(ref, buf, sem.at[i]) for i, (ref, buf) in enumerate(zip(refs, self.bufs))
+        ]
+        for copy in self.copies:
+            copy.start()
+
+    def __call__(self, i):
+        self.copies[i].wait()
+        return self.bufs[i]
+
+
+def comm_call(kernel, name, collective_id, args, outs, scratch, micros, room=VMEM_BYTES, far_args=(), far_outs=()):
+    vmem, anyway = pl.BlockSpec(memory_space=pltpu.VMEM), pl.BlockSpec(memory_space=pl.ANY)
     return pl.pallas_call(
         kernel,
         out_shape=[jax.ShapeDtypeStruct(shape, dtype) for shape, dtype in outs],
-        in_specs=[vmem] * len(args),
-        out_specs=[vmem] * len(outs),
+        in_specs=[anyway if i in far_args else vmem for i in range(len(args))],
+        out_specs=[anyway if i in far_outs else vmem for i in range(len(outs))],
         scratch_shapes=scratch,
         compiler_params=params(collective_id, room),
         cost_estimate=pl.CostEstimate(flops=0, bytes_accessed=micros * 3_000_000, transcendentals=0),
@@ -1163,19 +1363,33 @@
     )(*args)
 
 
-def attn_joint_kernel(mixed, w, hid, rate, first_o, ua_o, ca_o, cv_o, all_o, part, low, *scratch):
-    mate, across, cross = plane_peers()
-    greet([mate, across, cross])
+def attn_joint_kernel(
+    n_line, mixed, w, hid, rate, dc, first_o, ua_o, ca_o, cv_o, all_o, down_o, part, low, *scratch
+):
+    ends = line_ends(n_line)
+    greet(plane_peers(), ends[:2])
     split = len(UlyReduce.scratch(part))
     job = UlyReduce(part, *scratch[:split])
-    out = PlaneGather(low, all_o, *scratch[split:])
-    seqs, _, rows, width = part.shape
+    out = PlaneGather(low, all_o, *scratch[split : split + 3])
+    downs = line_gathers(n_line, dc, lambda z: down_o.at[:, z], scratch[split + 3 :])
+    for line_job in downs:
+        line_job.start()
+    steps = [(k, line_job) for k in range(1, n_line) for line_job in downs]
+    parts, _, rows, width = part.shape
+    seqs = mixed.shape[0]
+    each = parts // seqs
     for i in range(seqs):
-        part[i] = dot_nt(mixed[i], w[...]).astype(BF).reshape(4, rows, width)
-        for copy in job.near[i]:
-            copy.start()
+        got = dot_nt(mixed[i], w[...]).astype(BF)
+        for k in range(each):
+            for u in range(4):
+                at = (u * each + k) * rows
+                part[i * each + k, u] = got[at : at + rows]
+            for copy in job.near[i * each + k]:
+                copy.start()
     job.middle()
-    for i in range(seqs):
+    k, line_job = steps.pop(0)
+    line_job.step(k)
+    for i in range(parts):
         ua, ca = unit_of(job.result(i))
         h = hid[i].astype(F32)
         first, cv = unit_of(h + rate[...] * (ua - h))
@@ -1186,24 +1400,35 @@
         cv_o[i] = jnp.broadcast_to(cv, (rows, 128))
         if i > 0:
             out.forward_part(i - 1)
-    out.forward_part(seqs - 1)
+        if len(steps) > 0:
+            k, line_job = steps.pop(0)
+            line_job.step(k)
+    out.forward_part(parts - 1)
+    for k, line_job in steps:
+        line_job.step(k)
     out.finish()
     job.finish()
-
-
-def attn_joint(mixed, w, hid, rate):
-    seqs, rows, width = hid.shape
-    part = jax.ShapeDtypeStruct((seqs, 4, rows, width), BF)
-    thin = ((seqs, rows, 128), F32)
+    for line_job in downs:
+        line_job.finish()
+
+
+def attn_joint(n_line, mixed, w, hid, rate, dc):
+    parts, rows, width = hid.shape
+    part = jax.ShapeDtypeStruct((parts, 4, rows, width), BF)
+    thin = ((parts, rows, 128), F32)
     return comm_call(
-        attn_joint_kernel, "attn_joint", 1, (mixed, w, hid, rate),
-        [(hid.shape, F32), (hid.shape, F32), thin, thin, ((8, seqs, rows, width), BF)],
-        [pltpu.VMEM(part.shape, BF), pltpu.VMEM(hid.shape, BF)] + UlyReduce.scratch(part) + PlaneGather.sems,
-        25,
-    )
-
-
-def plane_products(job, part, c, product):
+        functools.partial(attn_joint_kernel, n_line), "attn_joint", 1, (mixed, w, hid, rate, dc),
+        [
+            (hid.shape, F32), (hid.shape, F32), thin, thin, ((8, parts, rows, width), BF),
+            (dc.shape[:1] + (n_line,) + dc.shape[1:], BF),
+        ],
+        [pltpu.VMEM(part.shape, BF), pltpu.VMEM(hid.shape, BF)]
+        + UlyReduce.scratch(part) + PlaneGather.sems(parts) + line_gather_sems(n_line),
+        25, far_outs=(5,),
+    )
+
+
+def plane_products(job, part, c, product, between=lambda: None):
     _, seqs, rows, width = part.shape
     for cc, first in ((1 - c, True), (c, False)):
         got = product(cc).astype(BF).reshape(2, 2, seqs, rows, width)
@@ -1212,6 +1437,7 @@
                 part[plane_index(yy, cc, ss)] = got[yy, ss]
         if first:
             job.start()
+            between()
 
 
 def ff_joint_kernel(inner, w, first, rate, cot, out_o, d1_o, sum_o, all_o, part, low, *scratch):
@@ -1253,29 +1479,80 @@
         ff_joint_kernel, "ff_joint", 2,
         (inner.reshape(2, 2, 2, seqs * rows, inner.shape[-1]), w, first, rate, cot),
         [(first.shape, BF), (first.shape, F32), ((1, width), F32), (part.shape, BF)],
-        [pltpu.VMEM(part.shape, BF), pltpu.VMEM(first.shape, BF)] + PlaneReduce.scratch(part) + PlaneGather.sems,
+        [pltpu.VMEM(part.shape, BF), pltpu.VMEM(first.shape, BF)] + PlaneReduce.scratch(part) + PlaneGather.sems(seqs),
         30,
     )
 
 
 def back_joint_kernel(
-    du, dg, wu, wg, d1, first, ua, ca, cv, hid, rate, res_o, sum_o, all_o, part, low, *scratch
+    n_line, d, inner, us, gs, d1, first, ua, ca, cv, hid, rate, wd_h, up_h, gate_h, wu_h, wg_h, x_h,
+    res_o, sum_o, ff_sum_o, all_o, up_o, gate_o, down_o, part, low, down_s, du, dg, *scratch,
 ):
     y, c, z, s = place()
-    greet(plane_peers())
+    late = Late((wd_h, up_h, gate_h, wu_h, wg_h, x_h), scratch[:7])
+    scratch = scratch[7:]
+    greet(plane_peers(), line_ends(n_line)[:2])
     split = len(PlaneReduce.scratch(part))
     job = PlaneReduce(part, *scratch[:split])
-    out = UlyGather(low, all_o, *scratch[split:])
-    _, seqs, rows, width = part.shape
+    _, parts, rows, width = part.shape
     columns = du.shape[-1]
-    tokens = 8 * seqs * rows
-    half = lambda ref, cc: ref[:, cc].reshape(tokens // 2, columns)
-    plane_products(
-        job, part, c, lambda cc: dot_nn(half(du, cc), wu[...]) + dot_nn(half(dg, cc), wg[...])
-    )
+    tokens = 8 * parts * rows
+    each = parts // all_o.shape[0]
+    out = UlyGather(
+        low, all_o, *scratch[split : split + 3],
+        pick=lambda i, u: all_o.at[i // each, u, pl.ds(i % each * rows, rows)],
+    )
+    downs = line_reduces(n_line, down_s, scratch[split + 3 :])
+    flat = lambda ref: ref[...].reshape(tokens, ref.shape[-1])
+
+    grad = dot_tn(flat(d), flat(inner)).astype(BF)
+    deep = width // (4 * n_line)
+    for v in range(4):
+        for k in range(n_line):
+            at = (v * n_line + k) * deep
+            down_s[k, v] = grad[at : at + deep]
+    for line_job, _ in downs:
+        line_job.step(n_line - 1)
+
+    wd, up_ref, gate_ref = late(0), late(1), late(2)
+    u_scale, g_scale = us[...], gs[...] * D**0.5
+
+    def gated_back(yy, cc):
+        got = dot_nn(d[yy, cc].reshape(tokens // 4, width), wd[...])
+        up, gate = up_ref[yy, cc].reshape(got.shape), gate_ref[yy, cc].reshape(got.shape)
+        gz = gate * g_scale
+        sig = 1.0 / (1.0 + jnp.exp(-gz))
+        d_up = got * (gz * sig)
+        d_gate = got * (up * u_scale) * sig * (1.0 + gz * (1.0 - sig))
+        du[yy, cc] = (d_up * u_scale).astype(BF).reshape(du.shape[2:])
+        dg[yy, cc] = (d_gate * g_scale).astype(BF).reshape(dg.shape[2:])
+        return jnp.sum(d_up * up, axis=0, keepdims=True), jnp.sum(d_gate * gate, axis=0, keepdims=True)
+
+    sums = [gated_back(0, 1 - c), gated_back(1, 1 - c)]
+    wu, wg = late(3), late(4)
+
+    def product(cc):
+        half = lambda ref: ref[:, cc].reshape(tokens // 2, columns)
+        return dot_nn(half(du), wu[...]) + dot_nn(half(dg), wg[...])
+
+    def rest():
+        sums.extend([gated_back(0, c), gated_back(1, c)])
+        ff_sum_o[0:1] = sum(a for a, _ in sums)
+        ff_sum_o[1:2] = sum(b for _, b in sums) * D**0.5
+
+    plane_products(job, part, c, product, rest)
     job.middle()
+    steps = [(k, line_job) for k in range(n_line - 2, 0, -1) for line_job, _ in downs]
     job.last()
-    for i in range(seqs):
+    x = late(5)
+
+    def by_line(o, grad):
+        n = columns // n_line
+        for k in range(n_line):
+            o[k] = grad[k * n : (k + 1) * n].astype(BF)
+
+    by_line(up_o, dot_tn(flat(du), x[...]))
+    for i in range(parts):
         f, h, u, a = first[i], hid[i].astype(F32), ua[i], rate[...]
         dv = unit_back(f, cv[i][:, :1], d1[i] + job.result(i))
         step = a * dv
@@ -1284,76 +1561,59 @@
         res_o[i] = dv - step
         total = jnp.sum(dv * (u - h), axis=0, keepdims=True)
         sum_o[...] = total if i == 0 else sum_o[...] + total
+        if len(steps) > 0:
+            k, line_job = steps.pop(0)
+            line_job.step(k)
+    for k, line_job in steps:
+        line_job.step(k)
+    by_line(gate_o, dot_tn(flat(dg), x[...]))
     out.forward()
     out.finish()
     job.finish()
-
-
-def back_joint(du, dg, wu, wg, d1, first, ua, ca, cv, hid, rate):
-    seqs, rows, width = first.shape
-    part = jax.ShapeDtypeStruct((8, seqs, rows, width), BF)
-    wide = lambda a: a.reshape(2, 2, 2, seqs * rows, a.shape[-1])
+    for line_job, cut in downs:
+        line_job.result(down_o.at[cut])
+        line_job.finish()
+
+
+def back_joint(n_line, seqs, d, wd, up, gate, us, gs, wu, wg, x, inner, d1, first, ua, ca, cv, hid, rate):
+    parts, rows, width = first.shape
+    columns = wd.shape[1]
+    part = jax.ShapeDtypeStruct((8, parts, rows, width), BF)
+    down = jax.ShapeDtypeStruct((n_line, 4, width // (4 * n_line), columns), BF)
+    by_line = ((n_line, columns // n_line, width), BF)
+    wide = lambda a: a.reshape(2, 2, 2, parts * rows, a.shape[-1])
+    thin = pltpu.VMEM((2, 2, 2, parts * rows, columns), BF)
+    late = (wd, wide(up), wide(gate), wu, wg, x)
     return comm_call(
-        back_joint_kernel, "back_joint", 3,
-        (wide(du), wide(dg), wu, wg, d1, first, ua, ca, cv, hid, rate),
-        [(first.shape, F32), ((1, width), F32), ((seqs, 4, rows, width), BF)],
-        [pltpu.VMEM(part.shape, BF), pltpu.VMEM(first.shape, BF)]
-        + PlaneReduce.scratch(part) + UlyGather.sems(seqs),
-        30,
-    )
-
-
-def down_grad_kernel(d_ref, inner_ref, o_ref):
-    grad = dot_tn(d_ref[...], inner_ref[...]).astype(BF)
-    n_line, groups, each, _ = o_ref.shape
-    for v in range(groups):
-        for k in range(n_line):
-            at = (v * n_line + k) * each
-            o_ref[k, v] = grad[at : at + each]
-
-
-def down_grad(n_line, d, inner):
-    rows, width = d.shape
-    columns = inner.shape[1]
-    each = width // (4 * n_line)
+        functools.partial(back_joint_kernel, n_line), "back_joint", 3,
+        (wide(d), wide(inner), us, gs, d1, first, ua, ca, cv, hid, rate) + late,
+        [
+            (first.shape, F32), ((1, width), F32), ((2, columns), F32),
+            ((seqs, 4, parts * rows // seqs, width), BF), by_line, by_line, (down.shape[1:], BF),
+        ],
+        [pltpu.VMEM(part.shape, BF), pltpu.VMEM(first.shape, BF), pltpu.VMEM(down.shape, BF), thin, thin]
+        + Late.scratch(late) + PlaneReduce.scratch(part) + UlyGather.sems(parts)
+        + line_reduce_scratch(n_line, down),
+        40, VMEM_BYTES, tuple(range(11, 17)),
+    )
+
+
+def settle_kernel(*refs):
+    count = len(refs) // 2
+    for x, o in zip(refs[:count], refs[count:]):
+        o[...] = x[...]
+
+
+def settle(*arrays):
+    vmem = pl.BlockSpec(memory_space=pltpu.VMEM)
     return pl.pallas_call(
-        down_grad_kernel,
-        grid=(2,),
-        out_shape=jax.ShapeDtypeStruct((n_line, 4, each, columns), BF),
-        in_specs=[
-            pl.BlockSpec((rows, width // 2), lambda i: (0, i)),
-            pl.BlockSpec((rows, columns), lambda i: (0, 0)),
-        ],
-        out_specs=pl.BlockSpec((n_line, 2, each, columns), lambda i: (0, i, 0, 0)),
+        settle_kernel,
+        out_shape=[jax.ShapeDtypeStruct(a.shape, a.dtype) for a in arrays],
+        in_specs=[vmem] * len(arrays),
+        out_specs=[vmem] * len(arrays),
         compiler_params=pltpu.CompilerParams(vmem_limit_bytes=VMEM_BYTES),
-        cost_estimate=pl.CostEstimate(flops=2 * rows * width * columns, bytes_accessed=8_000_000, transcendentals=0),
-        name="down_grad",
-    )(d, inner)
-
-
-def ff_grad_kernel(du_ref, dg_ref, x_ref, u_ref, g_ref):
-    n_line, each, _ = u_ref.shape
-    for ref, o_ref in ((du_ref, u_ref), (dg_ref, g_ref)):
-        grad = dot_tn(ref[...], x_ref[...]).astype(BF)
-        for k in range(n_line):
-            o_ref[k] = grad[k * each : (k + 1) * each]
-
-
-def ff_grad(n_line, du, dg, x):
-    rows, width = x.shape
-    columns = du.shape[1]
-    whole = pl.BlockSpec((rows, columns), lambda i: (0, 0))
-    shape = (n_line, columns // n_line, width)
-    return pl.pallas_call(
-        ff_grad_kernel,
-        grid=(2,),
-        out_shape=[jax.ShapeDtypeStruct(shape, BF)] * 2,
-        in_specs=[whole, whole, pl.BlockSpec((rows, width // 2), lambda i: (0, i))],
-        out_specs=[pl.BlockSpec(shape[:2] + (width // 2,), lambda i: (0, 0, i))] * 2,
-        compiler_params=pltpu.CompilerParams(vmem_limit_bytes=VMEM_BYTES),
-        cost_estimate=pl.CostEstimate(flops=4 * rows * width * columns, bytes_accessed=10_000_000, transcendentals=0),
-        name="ff_grad",
-    )(du, dg, x)
+        name="settle",
+    )(*arrays)
 def local(
     hidden, positions, w_query, w_key, w_value, w_out, w_up, w_gate, w_down,
     qk_scale, alpha_attn, alpha_mlp, up_scale, gate_scale, cotangent,
@@ -1381,13 +1641,10 @@
         at += v.shape[0]
     small = small.reshape(-1, 128)
 
-    up_full = lax.all_gather(w_up, "line", axis=0, tiled=True)
-
-    hid_all, small_all, wq_all, wk_all, wv_all, out_cols, down_cols = entry(
-        n_line, hidden, small, w_query, w_key, w_value, w_out, w_down
-    )
-    w_gate, up_full, hid_all = lax.optimization_barrier((w_gate, up_full, hid_all))
-    gate_full = lax.all_gather(w_gate, "line", axis=0, tiled=True)
+    hid_all, small_all, wq_all, wk_all, wv_all, out_cols, down_cols, up_full = entry(
+        n_line, hidden, small, w_query, w_key, w_value, w_out, w_down, w_up
+    )
+    up_full = up_full.reshape(ff_local, width)
 
     flat = small_all.reshape(4, n_blk, -1)
     cut = [0, attn_each, 2 * attn_each, 3 * attn_each, 3 * attn_each + ff_each, 3 * attn_each + 2 * ff_each, used]
@@ -1417,50 +1674,38 @@
     qz, kv, y_both, c_both = heads_forward(group_hidden, wq, wk, wv, cos, sin, scale_both)
     qz = qz.reshape(seqs, group_rows, heads * 128)
 
-    kv_all, out_all, attended, mixed, inverse = attend(
+    kv_all, out_all, gate_full, attended, mixed, inverse = attend(
         n_line, qz, kv.reshape(seqs, group_rows, heads * 128),
-        out_cols.reshape(1, 4 * attn_each, local_width), q_places, places,
-    )
-    out_all, gate_full, down_cols = lax.optimization_barrier((out_all, gate_full, down_cols))
-    down_all = lax.all_gather(down_cols.reshape(8 * attn_each, ff_local), "line", axis=0, tiled=False)
-    down_full = jnp.transpose(
-        down_all.reshape(n_line, 4, 2, attn_each, ff_local), (1, 0, 2, 3, 4)
-    ).reshape(width, ff_local)
-    out_full = jnp.transpose(
-        out_all.reshape(n_blk, 4, attn_each, local_width), (1, 0, 2, 3)
-    ).reshape(width, local_width)
-
-    first, unit_att, att_c, first_c, mlp_in = attn_joint(mixed, out_full, hidden, attn_rate[None])
+        out_cols, w_gate, q_places, places,
+    )
+    gate_full = gate_full.reshape(ff_local, width)
+    out_full = out_all.reshape(width, local_width)
+
+    fine = (2 * seqs, rows_each // 2, width)
+    hidden_fine = hidden.reshape(fine)
+    first, unit_att, att_c, first_c, mlp_in, down_full = attn_joint(
+        n_line, mixed, out_full, hidden_fine, attn_rate[None],
+        down_cols.reshape(4, 2 * attn_each, ff_local),
+    )
+    down_full = down_full.reshape(width, ff_local)
     mlp_in = mlp_in.reshape(plane_tokens, width)
     inner, up_rows, gate_rows = ff_forward(mlp_in, up_full, gate_full, up_wide[None], gate_wide[None])
     layer_out, grad_first, grad_alpha_mlp, branch_low = ff_joint(
-        inner, down_full, first, mlp_rate[None], cotangent
+        inner, down_full, first, mlp_rate[None], cotangent.reshape(fine)
     )
     branch_low = branch_low.reshape(plane_tokens, width)
-    grad_down = down_grad(n_line, branch_low, inner)
-    branch_low, grad_down = lax.optimization_barrier((branch_low, grad_down))
-    down_own = lax.psum_scatter(
-        grad_down.reshape(n_line, 8 * attn_each, ff_local), "line", scatter_dimension=0, tiled=True
-    ).reshape(8, attn_each, ff_local)
-    up_low, gate_low, ff_scales = ff_back(
-        branch_low, down_full, up_rows, gate_rows, up_wide[None], gate_wide[None]
+    grad_residual, grad_alpha_attn, ff_scales, att_low, grad_up, grad_gate, down_own = back_joint(
+        n_line, seqs, branch_low, down_full, up_rows, gate_rows, up_wide[None], gate_wide[None],
+        up_full, gate_full, mlp_in, inner, grad_first, first, unit_att, att_c, first_c, hidden_fine,
+        attn_rate[None],
     )
     grad_up_scale, grad_gate_scale = ff_scales[0], ff_scales[1]
-    grad_up, grad_gate = ff_grad(n_line, up_low, gate_low, mlp_in)
-    up_own = lax.psum_scatter(grad_up, "line", scatter_dimension=0, tiled=True)[0]
-    up_low, grad_up, grad_gate = lax.optimization_barrier((up_low, grad_up, grad_gate))
-    grad_residual, grad_alpha_attn, att_low = back_joint(
-        up_low, gate_low, up_full, gate_full, grad_first, first, unit_att, att_c, first_c,
-        hidden, attn_rate[None],
-    )
-
-    att_low, down_own = lax.optimization_barrier((att_low, down_own))
-    dq, dkv, out_own = attend_back(
+    down_own = down_own.reshape(8, attn_each, ff_local)
+
+    dq, dkv, out_own, up_own = attend_back(
         n_line, qz, att_low.reshape(seqs, group_rows, width), out_full, mixed, attended, inverse,
-        kv_all, q_places, places,
-    )
-    dkv, grad_gate, up_own = lax.optimization_barrier((dkv, grad_gate, up_own))
-    gate_own = lax.psum_scatter(grad_gate, "line", scatter_dimension=0, tiled=True)[0].astype(F32)
+        kv_all, q_places, places, grad_up,
+    )
     out_own = out_own.reshape(4, attn_each, local_width)
     gq, gk, gv, gs, gh = heads_back(
         group_hidden, dq.reshape(group_tokens, -1), dkv.reshape(group_tokens, -1), y_both, c_both,
@@ -1481,14 +1726,18 @@
     rest = jnp.concatenate(
         [jnp.zeros((n_blk, 128), F32), row(grad_scale.reshape(n_blk, attn_each), 128), row(ff_sums, 384)], axis=1
     )
-    gq, gk, gv, grad_hidden, out_gradient, down_gradient, sums = leave(
+    gq, gk, gv, grad_hidden, out_gradient, down_gradient, sums, gate_own = leave(
         n_line,
         *(g.reshape(n_blk, attn_each, width) for g in (gq, gk, gv)),
         gh.reshape(seqs, 4, rows_each, width),
-        grad_residual,
-        out_own, down_own, row(alpha, 128)[:, :, None], rest[:, None],
+        grad_residual.reshape(seqs, rows_each, width),
+        out_own, down_own, row(alpha, 128)[:, :, None], rest[:, None], grad_gate,
     )
     sums = sums[0]
+    layer_out, grad_hidden, gq, gk, gv, out_gradient, up_own, gate_own, down_gradient = settle(
+        layer_out.reshape(hidden.shape), grad_hidden, gq, gk, gv, out_gradient, up_own, gate_own,
+        down_gradient,
+    )
     return (
         layer_out,
         grad_hidden,
@@ -1496,7 +1745,7 @@
         gk,
         gv,
         out_gradient,
-        up_own.astype(F32),
+        up_own,
         gate_own,
         down_gradient,
         sums[128 : 128 + attn_each],

time: 466 us -> 467 us (level); the launches traced: 465 us -> 460 us
  Pallas kernels: 421 us -> 444 us
  between operations: 14.4 us -> 1.14 us
  local copies, waits for them, and re-layouts: 20.1 us -> 8.63 us
    pallas_call x5, Pallas kernels: 271 us -> 295 us  [comm_call(): pl.pallas_call(kernel, out_shape=[jax.ShapeDtypeStruct(shape, dtype) for...]
    pallas_call x1, Pallas kernels: 39.8 us -> 59.5 us  [leave(): pl.pallas_call(functools.partial(exit_kernel, n_line), out_shape=[grad, g...]
    pallas_call x3 -> x1, Pallas kernels: 20.8 us -> 4.35 us  [settle(): pl.pallas_call(settle_kernel, out_shape=[jax.ShapeDtypeStruct(a.shape, a....]
    unnamed x32 -> x9, local copies, waits for them, and re-layouts: 5.71 us -> 0.02 us
  transfers between devices with their start and end apart: 6 -> 0, of which waited for: 0 -> 0; matrix products, arithmetic and copies ran while one was open for 4% -> 0% of each run, Pallas kernels for 82% -> 0%
where the time goes in v4:
time: 467 us; the launch traced here: 460 us
  Pallas kernels  444 us (95%)
  local copies, waits for them, and re-layouts  8.63 us (2%)
  other arithmetic  5.73 us (1%)
    pallas_call x5, Pallas kernels, comm_call(): pl.pallas_call(kernel, out_shape=[jax.ShapeDtypeStruct(shape, dtype) for...  295 us
    pallas_call x1, Pallas kernels, leave(): pl.pallas_call(functools.partial(exit_kernel, n_line), out_shape=[grad, g...  59.5 us
    pallas_call x1, Pallas kernels, entry(): pl.pallas_call(functools.partial(entry_kernel, n_line), out_shape=[out((p...  57.8 us
    pallas_call x1, Pallas kernels, heads_back(): pl.pallas_call(heads_back_kernel, grid=(heads,), out_shape=[jax.ShapeDtyp...  11.3 us

profile of v4, /device:TPU:0, one launch (start us, length us, event | category | flops | bytes accessed | tf_op | source)
XLA Modules:
  0.0 459.9 jit_solution(3185334260595712595)
XLA Ops:
  0.7 0.7 convert_element_type.36
  1.3 0.1 convert_element_type.37
  1.4 1.4 add_bitcast_fusion.small
  2.8 57.8 %entry.1 = (bf16[2,4,64,1280]{3,2,1,0:T(8,128)(2,1)}, f32[4,8,8,128]{3,2,1,0:T(8,128)}, bf16[8,40,1280]{2,1,0:T(8,128)(2,1)}, bf16[8,40,1280]{2,1,0:T(8,128)(2,1...) custom-call(bf16[2,64,1280]{2,1,0:T(8,128)(2,1)} %hid.1, ...), custom_call_target="tpu_custom_call" | custom-call | bytes 120000000 | tf_op jit(solution)/shard_map/entry/pallas_call | solution.py:895
  60.6 0.9 reshape.187
  61.6 0.1 reshape.190
  61.7 0.1 pad_maximum_fusion.1
  61.8 0.6 broadcast_in_dim.52.scale_ref
  62.4 0.1 slice.80
  62.4 0.1 reshape.188
  62.5 0.1 reshape.189.kp_ref
  62.6 0.0 copy-start
  62.7 1.8 fusion
  64.5 8.0 %heads_forward.1 = (bf16[512,640]{1,0:T(8,128)(2,1)}, bf16[512,640]{1,0:T(8,128)(2,1)}, f32[512,640]{1,0:T(8,128)}, f32[512,640]{1,0:T(8,128)}) custom-call(bf16[512,1280]{1,0:T(8,128)(2,1)} %bitcast.88, bf16[5,64,1280]{2,1,0:T(8,128)(2,1)} %bitcast.90, bf16[5,64,1280]{2,1,0:T(8,128)(2,1)} %bitcast.92, bf16[5,64,1280]{2,1,0:T(8,128)(2,1)} %bitcast.94, ...), custom_call_target="tpu_custom_call" | custom-call | flops 1258291200 | bytes 5242880 | tf_op jit(solution)/shard_map/heads_forward/pallas_call | solution.py:973
  72.6 0.0 copy-done
  72.6 0.6 fusion.10.qp_ref
  73.1 89.1 %attend.1 = (bf16[8,2,256,640]{3,2,1,0:T(8,128)(2,1)}, bf16[4,8,40,320]{3,2,1,0:T(8,128)(2,1)}, bf16[4,160,1280]{2,1,0:T(8,128)(2,1)}, f32[2,5,256,128]{3,2,1,0:...) custom-call(bf16[2,256,640]{2,1,0:T(8,128)(2,1)} %bitcast.59, bf16[2,256,640]{2,1,0:T(8,128)(2,1)} %bitcast.75, ...), custom_call_target="tpu_custom_call" | custom-call | bytes 225000000 | tf_op jit(solution)/shard_map/attend/pallas_call | solution.py:1354
  162.2 0.1 fusion.7
  162.3 0.7 broadcast_in_dim_reshape.15.rate
  163.0 32.6 %attn_joint.1 = (f32[4,32,1280]{2,1,0:T(8,128)}, f32[4,32,1280]{2,1,0:T(8,128)}, f32[4,32,128]{2,1,0:T(8,128)}, f32[4,32,128]{2,1,0:T(8,128)}, bf16[8,4,32,1280]...) custom-call(bf16[2,256,320]{2,1,0:T(8,128)(2,1)} %get-tuple-element.86.mixed.mixed_ref, bf16[1280,320]{1,0:T(8,128)(2,1)} %bitcast.55, ...), custom_call_target="tpu_custom_call" | custom-call | bytes 75000000 | tf_op jit(solution)/shard_map/attn_joint/pallas_call | solution.py:1354
  195.7 0.1 fusion.8
  195.8 0.7 broadcast_in_dim_reshape.16.us_ref.us
  196.4 0.7 broadcast_in_dim_reshape.17.gs_ref.gs
  197.1 8.4 %ff_forward.1 = (bf16[1024,640]{1,0:T(8,128)(2,1)}, f32[1024,640]{1,0:T(8,128)}, f32[1024,640]{1,0:T(8,128)}) custom-call(bf16[1024,1280]{1,0:T(8,128)(2,1)} %bitcast.61, bf16[640,1280]{1,0:T(8,128)(2,1)} %bitcast.66, bf16[640,1280]{1,0:T(8,128)(2,1)} %bitcast.68, f32[1,640]{1,0:T(1,128)} %broadcast_in_dim_reshape.16.us_ref.us, ...), custom_call_target="tpu_custom_call" | custom-call | flops 3355443200 | bytes 9175040 | tf_op jit(solution)/shard_map/ff_forward/pallas_call | solution.py:1310
  205.5 0.7 broadcast_in_dim_reshape.18.rate
  206.2 36.5 %ff_joint.1 = (bf16[4,32,1280]{2,1,0:T(8,128)(2,1)}, f32[4,32,1280]{2,1,0:T(8,128)}, f32[1,1280]{1,0:T(1,128)}, bf16[8,4,32,1280]{3,2,1,0:T(8,128)(2,1)}) custom-call(bf16[2,2,2,128,640]{4,3,2,1,0:T(8,128)(2,1)} %bitcast.53, bf16[1280,640]{1,0:T(8,128)(2,1)} %bitcast.51, f32[4,32,1280]{2,1,0:T(8,128)} %get-tuple-element.94.first, ...), custom_call_target="tpu_custom_call" | custom-call | bytes 90000000 | tf_op jit(solution)/shard_map/ff_joint/pallas_call | solution.py:1354
  242.7 48.7 %back_joint.1 = (f32[4,32,1280]{2,1,0:T(8,128)}, f32[1,1280]{1,0:T(1,128)}, f32[2,640]{1,0:T(2,128)}, bf16[2,4,64,1280]{3,2,1,0:T(8,128)(2,1)}, bf16[4,160,1280]...) custom-call(bf16[2,2,2,128,1280]{4,3,2,1,0:T(8,128)(2,1)} %bitcast.65, ...), custom_call_target="tpu_custom_call" | custom-call | bytes 120000000 | tf_op jit(solution)/shard_map/back_joint/pallas_call | solution.py:1354
  291.4 0.8 slice_reduce_fusion.1
  292.2 0.1 reshape_squeeze.11
  292.3 0.1 reshape_squeeze.12
  292.4 0.1 pad_maximum_fusion
  292.5 0.1 broadcast_in_dim.56
  292.6 0.1 broadcast_select_fusion
  292.7 88.1 %attend_back.1 = (bf16[2,256,640]{2,1,0:T(8,128)(2,1)}, bf16[2,256,640]{2,1,0:T(8,128)(2,1)}, bf16[160,320]{1,0:T(8,128)(2,1)}, f32[160,1280]{1,0:T(8,128)}) custom-call(bf16[2,256,640]{2,1,0:T(8,128)(2,1)} %bitcast.60, bf16[2,256,1280]{2,1,0:T(8,128)(2,1)} %bitcast.70, bf16[1280,320]{1,0:T(8,128)(2,1)} %bitcast.56, ...), custom_call_target="tpu_custom_call" | custom-call | bytes 225000000 | tf_op jit(solution)/shard_map/attend_back/pallas_call | solution.py:1354
  380.8 0.0 copy-start.2
  380.8 11.3 %heads_back.1 = (bf16[5,64,1280]{2,1,0:T(8,128)(2,1)}, bf16[5,64,1280]{2,1,0:T(8,128)(2,1)}, bf16[5,64,1280]{2,1,0:T(8,128)(2,1)}, f32[5,1,128]{2,1,0:T(1,128)}, bf16[512,1280]{1,0:T(8,128)(2,1)}) custom-call(bf16[512,1280]{1,0:T(8,128)(2,1)} %bitcast.89, bf16[512,640]{1,0:T(8,128)(2,1)} %bitcast.96, bf16[512,640]{1,0:T(8,128)(2,1)} %bitcast.97, ...), custom_call_target="tpu_custom_call" | custom-call | flops 3355443200 | bytes 7864320 | tf_op jit(solution)/shard_map/heads_back/pallas_call | solution.py:1279
  392.1 0.8 add_reduce_fusion
  393.0 0.1 add.91
  393.1 0.6 broadcast_in_dim.61.rest
  393.7 0.0 copy-done.2
  393.7 0.1 reshape.215
  393.9 0.1 reshape.216
  393.9 0.7 select_maximum_fusion.2
  394.6 59.5 %leave.1 = (f32[40,1280]{1,0:T(8,128)}, f32[40,1280]{1,0:T(8,128)}, f32[40,1280]{1,0:T(8,128)}, f32[2,64,1280]{2,1,0:T(8,128)}, f32[40,1280]{1,0:T(8,128)}, /*in...) custom-call(bf16[8,40,1280]{2,1,0:T(8,128)(2,1)} %bitcast.72, bf16[8,40,1280]{2,1,0:T(8,128)(2,1)} %bitcast.73, ...), custom_call_target="tpu_custom_call" | custom-call | bytes 120000000 | tf_op jit(solution)/shard_map/leave/pallas_call | solution.py:786
  454.1 0.0 copy-start.3
  454.1 4.3 settle.1
  458.5 0.6 fusion.9
  459.1 0.6 slice_bitcast_fusion
  (22 shorter events, 0.2 us)
Async XLA Ops:
  62.6 9.9 %copy-start = (f32[2,8,1,256]{3,2,1,0:T(1,128)}, f32[2,8,1,256]{3,2,1,0:T(1,128)S(1)}, u32[]{:S(2)}) copy-start(f32[2,8,1,256]{3,2,1,0:T(1,128)S(1)} %reshape.189.kp_ref) | copy-start | bytes 49156
  380.8 13.0 %copy-start.2 = (f32[1,1280]{1,0:T(1,128)S(1)}, f32[1,1280]{1,0:T(1,128)}, u32[]{:S(2)}) copy-start(f32[1,1280]{1,0:T(1,128)} %get-tuple-element.119) | copy-start | bytes 15364
  380.8 13.1 %copy-start.1 = (f32[1,1280]{1,0:T(1,128)S(1)}, f32[1,1280]{1,0:T(1,128)}, u32[]{:S(2)}) copy-start(f32[1,1280]{1,0:T(1,128)} %get-tuple-element.120) | copy-start | bytes 15364
  454.1 4.4 copy-start.3

commit v5 on v4

--- a/solution.py
+++ b/solution.py
@@ -414,10 +414,14 @@
         self.sem = (side_send, side_recv, send, recv)
 
     def spot(self, way, k):
-        return self.z + k if way == 0 else self.z - k
+        return self.z + k * (1 - 2 * way)
 
     def exists(self, way, k):
-        return self.z + k < self.n if way == 0 else self.z >= k
+        return (self.spot(way, k) >= 0) & (self.spot(way, k) < self.n)
+
+    def toward(self, way):
+        y, c, z, s = place()
+        return (y, c, z + 1 - 2 * way, s)
 
     def side(self, zz):
         side_send, side_recv = self.sem[:2]
@@ -426,21 +430,20 @@
         )
 
     def slot(self, way, k):
-        return jnp.where(k == 0, self.n, self.spot(way, k)) if way == 1 else self.spot(way, k)
+        return jnp.where((way == 1) & (k == 0), self.n, self.spot(way, k))
 
     def move(self, way, k):
         send, recv = self.sem[2:]
-        target = self.high if way == 0 else self.low
         zz = self.spot(way, k)
-        there = jnp.where(k == 1, self.n, zz) if way == 1 else zz
+        there = jnp.where((way == 1) & (k == 1), self.n, zz)
         return remote(
-            self.side_in.at[zz], self.line_in.at[there], send.at[way, k], recv.at[way, k - 1], target
+            self.side_in.at[zz], self.line_in.at[there], send.at[way, k], recv.at[way, k - 1], self.toward(way)
         )
 
     def arrive(self, way, k):
         send, recv = self.sem[2:]
         there = self.line_in.at[self.slot(way, k)]
-        return remote(there, there, send.at[way, k], recv.at[way, k], self.cross)
+        return remote(there, there, send.at[way, k], recv.at[way, k], self.toward(1 - way))
 
     def start(self, k):
         for way in (0, 1) if k > 0 else (0,):
@@ -449,7 +452,7 @@
     def move_on(self, way, k):
         zz = self.spot(way, k)
         self.side(zz).wait_recv()
-        passed = self.has_low if way == 0 else self.has_high
+        passed = jnp.where(way == 0, self.has_low, self.has_high)
 
         @pl.when(passed)
         def _():
@@ -467,27 +470,28 @@
         self.move(way, k).start()
 
     def step(self, k):
-        for way in (0, 1):
+        def one(way, carry):
             pl.when(self.exists(way, k))(lambda: self.move_on(way, k))
+            return carry
+
+        lax.fori_loop(0, 2, one, 0)
 
     def result(self, o):
         z = self.z
         self.side(z).wait_recv()
         pl.when(self.has_low)(lambda: self.arrive(0, 0).wait_recv())
         pl.when(self.has_high)(lambda: self.arrive(1, 0).wait_recv())
-        own = add_low(self.x[z * 2 + self.s], self.side_in[z])
-
-        @pl.when(jnp.logical_and(self.has_low, self.has_high))
+        own = lambda: add_low(self.x[z * 2 + self.s], self.side_in[z])
+        both = self.has_low & self.has_high
+
+        @pl.when(both)
         def _():
-            o[...] = (own + add_low(self.line_in[z], self.line_in[self.n])).astype(o.dtype)
-
-        @pl.when(jnp.logical_not(self.has_low))
+            o[...] = (own() + add_low(self.line_in[z], self.line_in[self.n])).astype(o.dtype)
+
+        @pl.when(jnp.logical_not(both))
         def _():
-            o[...] = (own + self.line_in[self.n].astype(F32)).astype(o.dtype)
-
-        @pl.when(jnp.logical_not(self.has_high))
-        def _():
-            o[...] = (own + self.line_in[z].astype(F32)).astype(o.dtype)
+            other = self.line_in[jnp.where(self.has_low, z, self.n)].astype(F32)
+            o[...] = (own() + other).astype(o.dtype)
 
     def finish(self):
         for k in range(self.n - 1, -1, -1):
@@ -570,65 +574,66 @@
         (self.has_low, self.low), (self.has_high, self.high), _ = line_ends(n_line)
 
     def spot(self, way, k):
-        return self.z + k if way == 0 else self.z - k
+        return self.z + k * (1 - 2 * way)
 
     def exists(self, way, k):
-        return self.z + k < self.n if way == 0 else self.z >= k
+        return (self.spot(way, k) >= 0) & (self.spot(way, k) < self.n)
+
+    def passed(self, way):
+        return jnp.where(way == 0, self.has_low, self.has_high)
 
     def slot(self, way, k):
-        return jnp.where(k == 0, self.n, self.spot(way, k)) if way == 1 else self.spot(way, k)
-
-    def move(self, way, k):
+        return jnp.where((way == 1) & (k == 0), self.n, self.spot(way, k))
+
+    def toward(self, way):
+        y, c, z, s = place()
+        return (y, c, z + 1 - 2 * way, s)
+
+    def move(self, way, k, source):
         zz = self.spot(way, k)
-        there = jnp.where(k == 1, self.n, zz) if way == 1 else zz
+        there = jnp.where((way == 1) & (k == 1), self.n, zz)
         return remote(
-            self.sums.at[zz], self.line_in.at[there], self.send.at[way, k], self.recv.at[way, k - 1],
-            (self.high, self.low)[way],
+            source.at[zz], self.line_in.at[there], self.send.at[way, k], self.recv.at[way, k - 1], self.toward(way)
         )
 
     def arrive(self, way, k):
         there = self.line_in.at[self.slot(way, k)]
-        return remote(there, there, self.send.at[way, k], self.recv.at[way, k], (self.low, self.high)[way])
+        return remote(there, there, self.send.at[way, k], self.recv.at[way, k], self.toward(1 - way))
 
     def step(self, k):
-        for way in (0, 1):
-            @pl.when(self.exists(way, k))
+        def one(way, carry):
+            exists, passed = self.exists(way, k), self.passed(way)
+
+            @pl.when(exists & passed)
             def _():
                 zz = self.spot(way, k)
-                passed = (self.has_low, self.has_high)[way]
-
-                @pl.when(passed)
-                def _():
-                    self.arrive(way, k).wait_recv()
-                    self.sums[zz] = add_low(self.x[zz], self.line_in[zz]).astype(self.sums.dtype)
-
-                @pl.when(jnp.logical_not(passed))
-                def _():
-                    self.sums[zz] = self.x[zz]
-
-                self.move(way, k).start()
+                self.arrive(way, k).wait_recv()
+                self.sums[zz] = add_low(self.x[zz], self.line_in[zz]).astype(self.sums.dtype)
+                self.move(way, k, self.sums).start()
+
+            pl.when(exists & jnp.logical_not(passed))(lambda: self.move(way, k, self.x).start())
+            return carry
+
+        lax.fori_loop(0, 2, one, 0)
 
     def result(self, o):
         z = self.z
         pl.when(self.has_low)(lambda: self.arrive(0, 0).wait_recv())
         pl.when(self.has_high)(lambda: self.arrive(1, 0).wait_recv())
-
-        @pl.when(self.has_low & self.has_high)
+        both = self.has_low & self.has_high
+
+        @pl.when(both)
         def _():
             o[...] = add_low(self.x[z], self.line_in[z], self.line_in[self.n]).astype(o.dtype)
 
-        @pl.when(jnp.logical_not(self.has_low))
+        @pl.when(jnp.logical_not(both))
         def _():
-            o[...] = add_low(self.x[z], self.line_in[self.n]).astype(o.dtype)
-
-        @pl.when(jnp.logical_not(self.has_high))
-        def _():
-            o[...] = add_low(self.x[z], self.line_in[z]).astype(o.dtype)
+            o[...] = add_low(self.x[z], self.line_in[jnp.where(self.has_low, z, self.n)]).astype(o.dtype)
 
     def finish(self):
         for k in range(self.n - 1, 0, -1):
             for way in (0, 1):
-                pl.when(self.exists(way, k))(lambda: self.move(way, k).wait_send())
+                pl.when(self.exists(way, k))(lambda: self.move(way, k, self.sums).wait_send())
 
 
 def lane_chunks(width):
@@ -673,8 +678,9 @@
 
 
 def exit_kernel(
-    n_line, gq, gk, gv, gh, res, oc, dc, alpha, rest, gg,
+    n_line, x, dq, dkv, yy_ref, cc_ref, cos, sin, scale, wq, wk, wv, res, oc, dc, alpha, rest, gg,
     gq_o, gk_o, gv_o, gh_o, go_o, gd_o, sum_o, gg_o, oc_o, dc_o,
+    flat, acc, gq, gk, gv, gh, scale_s,
     alpha_in, line_out, line_all, oc_s, oc_r, dc_s, dc_r, al_s, al_r, su_s, su_r, keep, *scratch,
 ):
     y, c, z, s = place()
@@ -687,10 +693,10 @@
         others.append((y, c, to // 2, lax.rem(to, 2)))
     once = [(to[3] != 1 - s) | (to[2] != z) for to in others]
     greet([(yy, cc, z, ss) for yy, cc, ss in corners], list(zip(once, others)))
-    heads = 6
-    jobs = [BlkReduce(n_line, x, *scratch[heads * i : heads * (i + 1)]) for i, x in enumerate((gq, gk, gv))]
-    split = heads * 3 + len(UlyReduce.scratch(gh))
-    hid = UlyReduce(gh, *scratch[heads * 3 : split])
+    each = 6
+    jobs = [BlkReduce(n_line, g, *scratch[each * i : each * (i + 1)]) for i, g in enumerate((gq, gk, gv))]
+    split = each * 3 + len(UlyReduce.scratch(gh))
+    hid = UlyReduce(gh, *scratch[each * 3 : split])
     gates = line_reduces(n_line, gg, scratch[split:])
     small, cols = [], []
     for k, (yy, cc, ss) in enumerate(corners):
@@ -701,6 +707,56 @@
             small.append(remote(alpha.at[yy * 2 + cc], alpha_in.at[k], al_s.at[k], al_r.at[k], target))
     for job in small:
         job.start()
+    for job, _ in gates:
+        job.step(n_line - 1)
+    rows_all = x[...]
+    seqs, group_rows, wide = dq.shape
+    heads = wide // 128
+    factor = jnp.where(lanes_of((1, 128)) < HEAD_DIM, HEAD_DIM**0.5, 1.0)
+    late_steps = [(min(1 + 2 * i, heads - 1), k) for i, k in enumerate(range(n_line - 2, 0, -1))]
+
+    def head(h, carry):
+        lanes = pl.ds(pl.multiple_of(h * 128, 128), 128)
+        queries = jnp.concatenate([dq[i, :, lanes] for i in range(seqs)], axis=0)
+        pairs = jnp.concatenate([dkv[i, :, lanes] for i in range(seqs)], axis=0)
+        low_half = lanes_of(queries.shape) < HEAD_DIM
+        dy = jnp.where(low_half, queries.astype(F32), pltpu.roll(pairs.astype(F32), HEAD_DIM, 1))
+        unit = yy_ref[:, lanes]
+        scale_s[h] = jnp.sum(dy * unit, axis=0, keepdims=True) * factor
+        dy = dy * scale[pl.ds(h, 1)]
+        dr = cc_ref[:, lanes] * (dy - unit * halves(unit * dy))
+        raw = (dr * cos[...] - turn(dr) * sin[...]).astype(BF)
+        both = jnp.concatenate([raw, jnp.where(low_half, jnp.zeros_like(pairs), pairs)], axis=1)
+        grad = dot_tn(both, rows_all).astype(BF)
+        at = pl.ds(pl.multiple_of(h * HEAD_DIM, HEAD_DIM), HEAD_DIM)
+        for j, lo in enumerate((0, HEAD_DIM, 3 * HEAD_DIM)):
+            flat[j, at] = grad[lo : lo + HEAD_DIM]
+        w_value = wv[h]
+        more = dot_nn(both, jnp.concatenate([wq[h], wk[h], jnp.zeros_like(w_value), w_value], axis=0))
+
+        @pl.when(h == 0)
+        def _():
+            acc[...] = more
+
+        @pl.when(h > 0)
+        def _():
+            acc[...] = acc[...] + more
+
+        for when, k in late_steps:
+            @pl.when(h == when)
+            def _():
+                for job, _ in gates:
+                    job.step(k)
+
+        return carry
+
+    lax.fori_loop(0, heads, head, 0)
+    each_rows = gq.shape[1]
+    for i, g in enumerate((gq, gk, gv)):
+        for k in range(n_blk):
+            g[k] = flat[i, k * each_rows : (k + 1) * each_rows]
+    for i in range(seqs):
+        gh[i] = acc[i * group_rows : (i + 1) * group_rows].astype(BF).reshape(gh.shape[1:])
     hid.start()
     for k in range(n_line - 1, -1, -1):
         for job in jobs:
@@ -717,7 +773,12 @@
     for job in small:
         job.wait_recv()
     line_out[...] = rest[...]
-    line_out[:, :, :128] = rest[:, :, :128] + alpha[u] + alpha_in[0] + alpha_in[1] + alpha_in[2]
+    line_out[:, :, :128] = alpha[u] + alpha_in[0] + alpha_in[1] + alpha_in[2]
+    scales = jnp.concatenate(
+        [scale_s[h][:, :HEAD_DIM] + scale_s[h][:, HEAD_DIM:] for h in range(heads)], axis=1
+    )
+    for k in range(n_blk):
+        line_out[k, :, 128 : 128 + each_rows] = scales[:, k * each_rows : (k + 1) * each_rows]
     line_jobs = []
     for i in range(1, n_blk):
         to = lax.rem(b + i, n_blk)
@@ -726,14 +787,9 @@
         )
     for job in line_jobs:
         job.start()
-    for job, _ in gates:
-        job.step(n_line - 1)
     for k in range(n_line - 1, 0, -1):
         for job in jobs:
             job.step(k)
-        if k > 1:
-            for job, _ in gates:
-                job.step(k - 1)
     for i in range(gh.shape[0]):
         gh_o[i] = res[i] + hid.result(i)
     for job in cols:
@@ -766,40 +822,43 @@
         job.wait_send()
 
 
-def leave(n_line, gq, gk, gv, gh, res, oc, dc, alpha, rest, gg):
+def leave(n_line, x, dq, dkv, y, c, cos, sin, scale, wq, wk, wv, res, oc, dc, alpha, rest, gg):
     n_blk = 2 * n_line
+    heads, _, width = wq.shape
+    seqs, rows, _ = res.shape
     vmem = pl.BlockSpec(memory_space=pltpu.VMEM)
     dma = pltpu.SemaphoreType.DMA
+    grad = jax.ShapeDtypeStruct((n_blk, heads * HEAD_DIM // n_blk, width), BF)
+    gh = jax.ShapeDtypeStruct((seqs, 4, rows, width), BF)
     scratch = [
         pltpu.VMEM(oc.shape, oc.dtype),
         pltpu.VMEM(dc.shape, dc.dtype),
+        pltpu.VMEM((3, heads * HEAD_DIM, width), BF),
+        pltpu.VMEM(x.shape, F32),
+        pltpu.VMEM(grad.shape, BF), pltpu.VMEM(grad.shape, BF), pltpu.VMEM(grad.shape, BF),
+        pltpu.VMEM(gh.shape, BF),
+        pltpu.VMEM((heads, 1, 128), F32),
         pltpu.VMEM((3,) + alpha.shape[1:], F32),
         pltpu.VMEM(rest.shape, F32),
         pltpu.VMEM((n_blk - 1,) + rest.shape[1:], F32),
         dma((3,)), dma((3,)), dma((7,)), dma((7,)), dma((3,)), dma((3,)),
         dma((n_blk - 1,)), dma((n_blk - 1,)), dma((2,)),
     ]
-    for g in (gq, gk, gv):
-        scratch += BlkReduce.scratch(n_line, g)
+    scratch += BlkReduce.scratch(n_line, grad) * 3
     scratch += UlyReduce.scratch(gh) + line_reduce_scratch(n_line, gg)
-    grad = jax.ShapeDtypeStruct(gq.shape[1:], F32)
+    args = (x, dq, dkv, y, c, cos, sin, scale, wq, wk, wv, res, oc, dc, alpha, rest, gg)
+    outs = [grad.shape[1:]] * 3 + [
+        res.shape, (oc.shape[1], 4 * oc.shape[2]), (dc.shape[1], 8 * dc.shape[2]), rest.shape[1:], gg.shape[1:]
+    ]
     return pl.pallas_call(
         functools.partial(exit_kernel, n_line),
-        out_shape=[
-            grad, grad, grad,
-            jax.ShapeDtypeStruct(res.shape, F32),
-            jax.ShapeDtypeStruct((oc.shape[1], 4 * oc.shape[2]), F32),
-            jax.ShapeDtypeStruct((dc.shape[1], 8 * dc.shape[2]), F32),
-            jax.ShapeDtypeStruct(rest.shape[1:], F32),
-            jax.ShapeDtypeStruct(gg.shape[1:], F32),
-        ],
-        in_specs=[vmem] * 10,
-        out_specs=[vmem] * 8,
+        out_shape=[jax.ShapeDtypeStruct(shape, F32) for shape in outs],
+        in_specs=[vmem] * len(args),
+        out_specs=[vmem] * len(outs),
         scratch_shapes=scratch,
         compiler_params=params(8),
-        cost_estimate=pl.CostEstimate(flops=0, bytes_accessed=40 * 3_000_000, transcendentals=0),
         name="leave",
-    )(gq, gk, gv, gh, res, oc, dc, alpha, rest, gg)
+    )(*args)
 
 
 def entry_kernel(
@@ -821,9 +880,11 @@
     ):
         jobs.append(BlkGather(n_line, lambda x=x: x, pick, *sems[at : at + 5]))
         at += 5
-    line_count = 4 * LINE_CHUNKS
-    up_jobs = line_gathers(n_line, wu, lambda z: wu_o.at[z], sems[at : at + line_count])
-    oc_s, oc_r, dc_s, dc_r, sm_s, sm_r, keep = sems[at + line_count :]
+    first = wu_o.shape[-1]
+    up_jobs = [
+        LineGather(n_line, lambda: wu.at[:, slice(0, first)], lambda z: wu_o.at[z], *sems[at : at + 4])
+    ]
+    oc_s, oc_r, dc_s, dc_r, sm_s, sm_r, keep = sems[at + 4 :]
     jobs[0].start()
     for job in jobs[1:]:
         job.start()
@@ -902,14 +963,14 @@
             out((n_blk,) + wv.shape, wv),
             out(oc.shape, oc),
             out(dc.shape, dc),
-            out((n_line,) + wu.shape, wu),
+            out((n_line, wu.shape[0], lane_chunks(wu.shape[1])[0].stop), wu),
         ],
         in_specs=[vmem] * 8,
         out_specs=[vmem, vmem, anyway, anyway, anyway, vmem, vmem, anyway],
         scratch_shapes=[pltpu.VMEM(oc.shape, oc.dtype), pltpu.VMEM(dc.shape, dc.dtype)]
         + UlyGather.sems(parts)
         + BlkGather.sems(n_line) * 4
-        + line_gather_sems(n_line)
+        + LineGather.sems(n_line)
         + [pltpu.SemaphoreType.DMA((3,))] * 2
         + [pltpu.SemaphoreType.DMA((7,))] * 2
         + [pltpu.SemaphoreType.DMA((3,))] * 2
@@ -947,42 +1008,6 @@
     return jnp.where(first, pltpu.roll(x, 128 - 32, 1), pltpu.roll(x, 32, 1))
 
 
-def heads_kernel(x_ref, wq_ref, wk_ref, wv_ref, cos_ref, sin_ref, scale_ref, qz_ref, kv_ref, y_ref, c_ref):
-    x = x_ref[...]
-    wv = wv_ref[0]
-    got = dot_nt(x, jnp.concatenate([wq_ref[0], wk_ref[0], jnp.zeros_like(wv), wv], axis=0))
-    raw, value = got[:, :128], got[:, 128:]
-    low = lanes_of(raw.shape) < HEAD_DIM
-    turned = raw * cos_ref[...] + turn(raw) * sin_ref[...]
-    c = lax.rsqrt(halves(turned * turned) + HEAD_DIM * tiny_eps)
-    y = turned * c
-    both = y * scale_ref[0]
-    qz_ref[...] = jnp.where(low, both, 0.0).astype(BF)
-    kv_ref[...] = jnp.where(low, pltpu.roll(both, HEAD_DIM, 1), value).astype(BF)
-    y_ref[...] = y
-    c_ref[...] = c
-
-
-def heads_forward(x, wq, wk, wv, cos, sin, scale):
-    rows, width = x.shape
-    heads = wq.shape[0]
-    whole = lambda shape: pl.BlockSpec(shape, lambda h: (0,) * len(shape))
-    weight = pl.BlockSpec((1, HEAD_DIM, width), lambda h: (h, 0, 0))
-    head = pl.BlockSpec((rows, 128), lambda h: (0, h))
-    wide = lambda dtype: jax.ShapeDtypeStruct((rows, heads * 128), dtype)
-    return pl.pallas_call(
-        heads_kernel,
-        grid=(heads,),
-        out_shape=[wide(BF), wide(BF), wide(F32), wide(F32)],
-        in_specs=[whole((rows, width)), weight, weight, weight, whole((rows, 128)), whole((rows, 128)),
-                  pl.BlockSpec((1, 1, 128), lambda h: (h, 0, 0))],
-        out_specs=[head] * 4,
-        compiler_params=pltpu.CompilerParams(vmem_limit_bytes=VMEM_BYTES),
-        cost_estimate=pl.CostEstimate(flops=rows * width * heads * 384, bytes_accessed=rows * width * 8, transcendentals=0),
-        name="heads_forward",
-    )(x, wq, wk, wv, cos, sin, scale)
-
-
 def down_columns(row):
     n = row.shape[1]
     one = jnp.transpose(jnp.broadcast_to(row, (128, n)))
@@ -1001,13 +1026,41 @@
 
 
 def attend_kernel(
-    n_line, q_ref, kv_ref, oc_ref, wg_ref, qp_ref, kp_ref,
-    kv_o, oc_o, wg_o, o_ref, mixed_ref, inv_ref, acc, total, place_q, *sems,
+    n_line, x_ref, wq_ref, wk_ref, wv_ref, cos_ref, sin_ref, scale_ref, oc_ref, wg_ref, wu_ref, kp_ref,
+    q_ref, y_ref, c_ref, kv_o, oc_o, wg_o, wu_o, o_ref, mixed_ref, inv_ref, kv_ref, acc, total, place_q, *sems,
 ):
     y, c, z, s = place()
     blk_greet(n_line)
     seqs, rows, wide = q_ref.shape
     heads = wide // 128
+    chunk = 4 * LINE_CHUNKS
+    cut = wu_ref.shape[-1] - wu_o.shape[-1]
+    up = LineGather(
+        n_line, lambda: wu_ref.at[:, slice(cut, wu_ref.shape[-1])], lambda zz: wu_o.at[zz], *sems[-4:]
+    )
+    up.start()
+    x = x_ref[...]
+
+    def make(h, carry):
+        lanes = pl.ds(pl.multiple_of(h * 128, 128), 128)
+        wv = wv_ref[h]
+        got = dot_nt(x, jnp.concatenate([wq_ref[h], wk_ref[h], jnp.zeros_like(wv), wv], axis=0))
+        raw, value = got[:, :128], got[:, 128:]
+        low = lanes_of(raw.shape) < HEAD_DIM
+        turned = raw * cos_ref[...] + turn(raw) * sin_ref[...]
+        norm = lax.rsqrt(halves(turned * turned) + HEAD_DIM * tiny_eps)
+        unit = turned * norm
+        both = unit * scale_ref[pl.ds(h, 1)]
+        query = jnp.where(low, both, 0.0).astype(BF)
+        kv = jnp.where(low, pltpu.roll(both, HEAD_DIM, 1), value).astype(BF)
+        for i in range(seqs):
+            q_ref[i, :, lanes] = query[i * rows : (i + 1) * rows]
+            kv_ref[i, :, lanes] = kv[i * rows : (i + 1) * rows]
+        y_ref[:, lanes] = unit
+        c_ref[:, lanes] = norm
+        return carry
+
+    lax.fori_loop(0, heads, make, 0)
     each = len(BlkGather.sems(n_line))
     picks = [
         (lambda i=i: kv_ref.at[i], lambda block, i=i: kv_o.at[block, i]) for i in range(seqs)
@@ -1015,7 +1068,9 @@
     jobs = [
         BlkGather(n_line, *pick, *sems[each * i : each * (i + 1)]) for i, pick in enumerate(picks)
     ]
-    gates = line_gathers(n_line, wg_ref, lambda z: wg_o.at[z], sems[each * (seqs + 1) :])
+    gates = line_gathers(
+        n_line, wg_ref, lambda z: wg_o.at[z], sems[each * (seqs + 1) : each * (seqs + 1) + chunk]
+    )
     for job in jobs:
         job.start()
     for job in gates:
@@ -1023,7 +1078,7 @@
     acc[...] = jnp.zeros_like(acc)
     total[...] = jnp.zeros_like(total)
     for i in range(seqs):
-        place_q[i] = down_columns(qp_ref[i])
+        place_q[i] = down_columns(kp_ref[i, z * 2 + s])
 
     def attend_to(i, block, keys):
         allowed = kp_ref[i, block] <= place_q[i]
@@ -1042,7 +1097,7 @@
 
         @pl.when((stage == 1) & ((k == 0) | (way == 1)) & (ahead < n_line))
         def _():
-            for job in gates:
+            for job in gates + [up]:
                 job.step(ahead)
 
         there = (k == 0) | jnp.where(way == 0, z >= k, z + k < n_line)
@@ -1083,29 +1138,32 @@
             mixed_ref[i, :, (heads - 1) * HEAD_DIM :] = pltpu.roll(outs[-1], HEAD_DIM, 1)[:, :HEAD_DIM].astype(BF)
     for job in jobs:
         job.finish_sends()
-    for job in gates:
+    for job in gates + [up]:
         job.finish()
 
 
-def attend(n_line, q, kv, oc, wg, q_places, k_places):
-    seqs, rows, wide = q.shape
-    n_blk, heads = 2 * n_line, wide // 128
-    head = (seqs, heads, rows, 128)
+def attend(n_line, seqs, x, wq, wk, wv, cos, sin, scale, oc, wg, wu, k_places):
+    tokens, width = x.shape
+    n_blk, heads, rows = 2 * n_line, wq.shape[0], tokens // seqs
+    head, wide = (seqs, heads, rows, 128), (seqs, rows, heads * 128)
+    flat = ((tokens, heads * 128), F32)
+    first = lane_chunks(width)[0].stop
     return comm_call(
-        functools.partial(attend_kernel, n_line), "attend", 5, (q, kv, oc, wg, q_places, k_places),
+        functools.partial(attend_kernel, n_line), "attend", 5,
+        (x, wq, wk, wv, cos, sin, scale, oc, wg, wu, k_places),
         [
-            ((n_blk,) + kv.shape, BF), (oc.shape[:1] + (n_blk,) + oc.shape[1:], BF),
-            ((n_line,) + wg.shape, BF), (head, F32),
+            (wide, BF), flat, flat, ((n_blk,) + wide, BF), (oc.shape[:1] + (n_blk,) + oc.shape[1:], BF),
+            ((n_line,) + wg.shape, BF), ((n_line, wu.shape[0], width - first), BF), (head, F32),
             ((seqs, rows, heads * HEAD_DIM), BF), ((seqs, heads, 8, rows), F32),
         ],
-        [pltpu.VMEM(head, F32), pltpu.VMEM(head, F32), pltpu.VMEM((seqs, rows, rows), F32)]
-        + BlkGather.sems(n_line) * (seqs + 1) + line_gather_sems(n_line),
-        75, far_outs=(1, 2),
+        [pltpu.VMEM(wide, BF), pltpu.VMEM(head, F32), pltpu.VMEM(head, F32), pltpu.VMEM((seqs, rows, rows), F32)]
+        + BlkGather.sems(n_line) * (seqs + 1) + line_gather_sems(n_line) + LineGather.sems(n_line),
+        90, far_outs=(4, 5, 6),
     )
 
 
 def attend_back_kernel(
-    n_line, fits, q_ref, low_ref, w_ref, mixed_ref, o_ref, inv_ref, kv_ref, qp_ref, kp_ref, gu_ref,
+    n_line, fits, q_ref, low_ref, w_ref, mixed_ref, o_ref, inv_ref, kv_ref, kp_ref, gu_ref,
     dq_ref, dkv_ref, oc_ref, gu_o, dz, delta, dq, parts, oparts, key_s, key_sem, *scratch,
 ):
     y, c, z, s = place()
@@ -1151,7 +1209,7 @@
             copy.start()
             copy.wait()
         for i in range(seqs):
-            allowed = down_columns(kp_ref[i, block]) <= qp_ref[i]
+            allowed = down_columns(kp_ref[i, block]) <= kp_ref[i, z * 2 + s]
             for h in range(heads):
                 lanes = slice(h * 128, (h + 1) * 128)
                 kv = keys[i, :, lanes]
@@ -1208,7 +1266,7 @@
         job.finish()
 
 
-def attend_back(n_line, q, low, w, mixed, o, inv, kv, q_places, k_places, gu):
+def attend_back(n_line, q, low, w, mixed, o, inv, kv, k_places, gu):
     seqs, rows, wide = q.shape
     n_blk, heads = 2 * n_line, wide // 128
     head = (seqs, heads, rows, 128)
@@ -1219,7 +1277,7 @@
     fits = kv.size * 2 <= 8_000_000
     return comm_call(
         functools.partial(attend_back_kernel, n_line, fits), "attend_back", 7,
-        (q, low, w, mixed, o, inv, kv, q_places, k_places, gu),
+        (q, low, w, mixed, o, inv, kv, k_places, gu),
         [(q.shape, BF), (kv.shape[1:], BF), (out_shape, BF), (gu.shape[1:], F32)],
         [
             pltpu.VMEM(head, BF), pltpu.VMEM((seqs, heads, 8, rows), F32), pltpu.VMEM(head, F32),
@@ -1232,75 +1290,19 @@
     )
 
 
-def heads_back_kernel(
-    x_ref, dq_ref, dkv_ref, y_ref, c_ref, cos_ref, sin_ref, scale_ref, wq_ref, wk_ref, wv_ref,
-    gq_ref, gk_ref, gv_ref, gs_ref, gh_ref, acc_ref,
-):
-    h = pl.program_id(0)
-    dq, dkv = dq_ref[...], dkv_ref[...]
-    low = lanes_of(dq.shape) < HEAD_DIM
-    dy = jnp.where(low, dq.astype(F32), pltpu.roll(dkv.astype(F32), HEAD_DIM, 1))
-    y = y_ref[...]
-    factor = jnp.where(lanes_of((1, 128)) < HEAD_DIM, HEAD_DIM**0.5, 1.0)
-    gs_ref[0] = jnp.sum(dy * y, axis=0, keepdims=True) * factor
-    dy = dy * scale_ref[0]
-    dr = c_ref[...] * (dy - y * halves(y * dy))
-    raw = (dr * cos_ref[...] - turn(dr) * sin_ref[...]).astype(BF)
+def ff_kernel(x_ref, wu_ref, wu2_ref, wg_ref, vec_ref, inner_ref, up_ref, gate_ref):
     x = x_ref[...]
-    value = jnp.where(low, jnp.zeros_like(dkv), dkv)
-    both = jnp.concatenate([raw, value], axis=1)
-    grad = dot_tn(both, x)
-    gq_ref[0] = grad[:HEAD_DIM].astype(BF)
-    gk_ref[0] = grad[HEAD_DIM : 2 * HEAD_DIM].astype(BF)
-    gv_ref[0] = grad[3 * HEAD_DIM :].astype(BF)
-    wv = wv_ref[0]
-    more = dot_nn(both, jnp.concatenate([wq_ref[0], wk_ref[0], jnp.zeros_like(wv), wv], axis=0))
-
-    @pl.when(h == 0)
-    def _():
-        acc_ref[...] = more
-
-    @pl.when(h > 0)
-    def _():
-        acc_ref[...] = acc_ref[...] + more
-
-    @pl.when(h == pl.num_programs(0) - 1)
-    def _():
-        gh_ref[...] = acc_ref[...].astype(BF)
-
-
-def heads_back(x, dq, dkv, y, c, cos, sin, scale, wq, wk, wv):
-    rows, width = x.shape
-    heads = wq.shape[0]
-    whole = lambda shape: pl.BlockSpec(shape, lambda h: (0,) * len(shape))
-    weight = pl.BlockSpec((1, HEAD_DIM, width), lambda h: (h, 0, 0))
-    head = pl.BlockSpec((rows, 128), lambda h: (0, h))
-    row = pl.BlockSpec((1, 1, 128), lambda h: (h, 0, 0))
-    return pl.pallas_call(
-        heads_back_kernel,
-        grid=(heads,),
-        out_shape=[jax.ShapeDtypeStruct(wq.shape, BF)] * 3
-        + [jax.ShapeDtypeStruct((heads, 1, 128), F32), jax.ShapeDtypeStruct((rows, width), BF)],
-        in_specs=[whole((rows, width))] + [head] * 4 + [whole((rows, 128))] * 2 + [row] + [weight] * 3,
-        out_specs=[weight] * 3 + [row, whole((rows, width))],
-        scratch_shapes=[pltpu.VMEM((rows, width), F32)],
-        compiler_params=pltpu.CompilerParams(vmem_limit_bytes=VMEM_BYTES),
-        cost_estimate=pl.CostEstimate(flops=rows * width * heads * 1024, bytes_accessed=rows * width * 12, transcendentals=0),
-        name="heads_back",
-    )(x, dq, dkv, y, c, cos, sin, scale, wq, wk, wv)
-
-
-def ff_kernel(x_ref, wu_ref, wg_ref, us_ref, gs_ref, inner_ref, up_ref, gate_ref):
-    x = x_ref[...]
-    up = dot_nt(x, wu_ref[...])
+    cut = wu_ref.shape[1]
+    up = dot_nt(x[:, :cut], wu_ref[...]) + dot_nt(x[:, cut:], wu2_ref[...])
     gate = dot_nt(x, wg_ref[...])
-    z = gate * gs_ref[...] * D**0.5
-    inner_ref[...] = (z / (1.0 + jnp.exp(-z)) * (up * us_ref[...])).astype(BF)
+    columns = up.shape[1]
+    z = gate * vec_ref[3:4, :columns] * D**0.5
+    inner_ref[...] = (z / (1.0 + jnp.exp(-z)) * (up * vec_ref[2:3, :columns])).astype(BF)
     up_ref[...] = up
     gate_ref[...] = gate
 
 
-def ff_forward(x, wu, wg, us, gs):
+def ff_forward(x, wu, wu2, wg, vec):
     rows, width = x.shape
     columns = wu.shape[0]
     block = rows // 4
@@ -1311,7 +1313,7 @@
         ff_kernel,
         grid=(4,),
         out_shape=[out(BF), out(F32), out(F32)],
-        in_specs=[part(width)] + [whole(a) for a in (wu, wg, us, gs)],
+        in_specs=[part(width)] + [whole(a) for a in (wu, wu2, wg, vec)],
         out_specs=[part(columns)] * 3,
         compiler_params=pltpu.CompilerParams(vmem_limit_bytes=VMEM_BYTES),
         cost_estimate=pl.CostEstimate(
@@ -1319,7 +1321,7 @@
             transcendentals=rows * columns,
         ),
         name="ff_forward",
-    )(x, wu, wg, us, gs)
+    )(x, wu, wu2, wg, vec)
 
 
 def unit_of(x):
@@ -1392,7 +1394,7 @@
     for i in range(parts):
         ua, ca = unit_of(job.result(i))
         h = hid[i].astype(F32)
-        first, cv = unit_of(h + rate[...] * (ua - h))
+        first, cv = unit_of(h + rate[0:1] * (ua - h))
         low[i] = first.astype(BF)
         out.start_part(i)
         first_o[i], ua_o[i] = first, ua
@@ -1429,12 +1431,15 @@
 
 
 def plane_products(job, part, c, product, between=lambda: None):
-    _, seqs, rows, width = part.shape
+    _, parts, rows, width = part.shape
     for cc, first in ((1 - c, True), (c, False)):
-        got = product(cc).astype(BF).reshape(2, 2, seqs, rows, width)
-        for yy in (0, 1):
+        def one(yy, carry):
+            got = product(yy, cc).astype(BF).reshape(2, parts, rows, width)
             for ss in (0, 1):
-                part[plane_index(yy, cc, ss)] = got[yy, ss]
+                part[plane_index(yy, cc, ss)] = got[ss]
+            return carry
+
+        lax.fori_loop(0, 2, one, 0)
         if first:
             job.start()
             between()
@@ -1449,13 +1454,13 @@
     _, seqs, rows, width = part.shape
     columns = inner.shape[-1]
     plane_products(
-        job, part, c, lambda cc: dot_nt(inner[:, cc].reshape(4 * seqs * rows, columns), w[...])
+        job, part, c, lambda yy, cc: dot_nt(inner[yy, cc].reshape(2 * seqs * rows, columns), w[...])
     )
     job.middle()
     job.last()
     for i in range(seqs):
         ub, cb = unit_of(job.result(i))
-        f, b = first[i], rate[...]
+        f, b = first[i], rate[1:2]
         o, cw = unit_of(f + b * (ub - f))
         dw = unit_back(o, cw, cot[i].astype(F32))
         step = b * dw
@@ -1485,12 +1490,12 @@
 
 
 def back_joint_kernel(
-    n_line, d, inner, us, gs, d1, first, ua, ca, cv, hid, rate, wd_h, up_h, gate_h, wu_h, wg_h, x_h,
+    n_line, d, inner, rate, d1, first, ua, ca, cv, hid, wd_h, up_h, gate_h, wu_h, wu2_h, wg_h, x_h,
     res_o, sum_o, ff_sum_o, all_o, up_o, gate_o, down_o, part, low, down_s, du, dg, *scratch,
 ):
     y, c, z, s = place()
-    late = Late((wd_h, up_h, gate_h, wu_h, wg_h, x_h), scratch[:7])
-    scratch = scratch[7:]
+    late = Late((wd_h, up_h, gate_h, wu_h, wu2_h, wg_h, x_h), scratch[:8])
+    scratch = scratch[8:]
     greet(plane_peers(), line_ends(n_line)[:2])
     split = len(PlaneReduce.scratch(part))
     job = PlaneReduce(part, *scratch[:split])
@@ -1505,55 +1510,72 @@
     downs = line_reduces(n_line, down_s, scratch[split + 3 :])
     flat = lambda ref: ref[...].reshape(tokens, ref.shape[-1])
 
-    grad = dot_tn(flat(d), flat(inner)).astype(BF)
     deep = width // (4 * n_line)
-    for v in range(4):
-        for k in range(n_line):
-            at = (v * n_line + k) * deep
-            down_s[k, v] = grad[at : at + deep]
+    inner_all = flat(inner)
+
+    def down_half(i, carry):
+        lanes = pl.ds(pl.multiple_of(i * (width // 2), 128), width // 2)
+        grad = dot_tn(d[:, :, :, :, lanes].reshape(tokens, width // 2), inner_all).astype(BF)
+        for v in (0, 1):
+            for k in range(n_line):
+                at = (v * n_line + k) * deep
+                down_s[k, 2 * i + v] = grad[at : at + deep]
+        return carry
+
+    lax.fori_loop(0, 2, down_half, 0)
     for line_job, _ in downs:
         line_job.step(n_line - 1)
 
     wd, up_ref, gate_ref = late(0), late(1), late(2)
-    u_scale, g_scale = us[...], gs[...] * D**0.5
-
-    def gated_back(yy, cc):
-        got = dot_nn(d[yy, cc].reshape(tokens // 4, width), wd[...])
-        up, gate = up_ref[yy, cc].reshape(got.shape), gate_ref[yy, cc].reshape(got.shape)
-        gz = gate * g_scale
-        sig = 1.0 / (1.0 + jnp.exp(-gz))
-        d_up = got * (gz * sig)
-        d_gate = got * (up * u_scale) * sig * (1.0 + gz * (1.0 - sig))
-        du[yy, cc] = (d_up * u_scale).astype(BF).reshape(du.shape[2:])
-        dg[yy, cc] = (d_gate * g_scale).astype(BF).reshape(dg.shape[2:])
-        return jnp.sum(d_up * up, axis=0, keepdims=True), jnp.sum(d_gate * gate, axis=0, keepdims=True)
-
-    sums = [gated_back(0, 1 - c), gated_back(1, 1 - c)]
-    wu, wg = late(3), late(4)
-
-    def product(cc):
-        half = lambda ref: ref[:, cc].reshape(tokens // 2, columns)
-        return dot_nn(half(du), wu[...]) + dot_nn(half(dg), wg[...])
-
-    def rest():
-        sums.extend([gated_back(0, c), gated_back(1, c)])
-        ff_sum_o[0:1] = sum(a for a, _ in sums)
-        ff_sum_o[1:2] = sum(b for _, b in sums) * D**0.5
-
-    plane_products(job, part, c, product, rest)
+    u_scale, g_scale = rate[2:3, :columns], rate[3:4, :columns] * D**0.5
+
+    ff_sum_o[...] = jnp.zeros_like(ff_sum_o)
+
+    def gated_back(cc):
+        def one(yy, carry):
+            got = dot_nn(d[yy, cc].reshape(tokens // 4, width), wd[...])
+            up, gate = up_ref[yy, cc].reshape(got.shape), gate_ref[yy, cc].reshape(got.shape)
+            gz = gate * g_scale
+            sig = 1.0 / (1.0 + jnp.exp(-gz))
+            d_up = got * (gz * sig)
+            d_gate = got * (up * u_scale) * sig * (1.0 + gz * (1.0 - sig))
+            du[yy, cc] = (d_up * u_scale).astype(BF).reshape(du.shape[2:])
+            dg[yy, cc] = (d_gate * g_scale).astype(BF).reshape(dg.shape[2:])
+            ff_sum_o[0:1] = ff_sum_o[0:1] + jnp.sum(d_up * up, axis=0, keepdims=True)
+            ff_sum_o[1:2] = ff_sum_o[1:2] + jnp.sum(d_gate * gate, axis=0, keepdims=True) * D**0.5
+            return carry
+
+        lax.fori_loop(0, 2, one, 0)
+
+    gated_back(1 - c)
+    wu, wu2, wg = late(3), late(4), late(5)
+
+    def product(yy, cc):
+        u, g = du[yy, cc].reshape(tokens // 4, columns), dg[yy, cc].reshape(tokens // 4, columns)
+        got = jnp.concatenate([dot_nn(u, wu[...]), dot_nn(u, wu2[...])], axis=1)
+        return got + dot_nn(g, wg[...])
+
+    plane_products(job, part, c, product, lambda: gated_back(c))
     job.middle()
     steps = [(k, line_job) for k in range(n_line - 2, 0, -1) for line_job, _ in downs]
     job.last()
-    x = late(5)
-
-    def by_line(o, grad):
-        n = columns // n_line
-        for k in range(n_line):
-            o[k] = grad[k * n : (k + 1) * n].astype(BF)
-
-    by_line(up_o, dot_tn(flat(du), x[...]))
+    x = late(6)
+
+    def by_line(o, ref):
+        n, rows_all = columns // n_line, flat(ref)
+
+        def half(i, carry):
+            lanes = pl.ds(pl.multiple_of(i * (width // 2), 128), width // 2)
+            grad = dot_tn(rows_all, x[:, lanes]).astype(BF)
+            for k in range(n_line):
+                o[k, :, lanes] = grad[k * n : (k + 1) * n]
+            return carry
+
+        lax.fori_loop(0, 2, half, 0)
+
+    by_line(up_o, du)
     for i in range(parts):
-        f, h, u, a = first[i], hid[i].astype(F32), ua[i], rate[...]
+        f, h, u, a = first[i], hid[i].astype(F32), ua[i], rate[0:1]
         dv = unit_back(f, cv[i][:, :1], d1[i] + job.result(i))
         step = a * dv
         low[i] = unit_back(u, ca[i][:, :1], step).astype(BF)
@@ -1566,7 +1588,7 @@
             line_job.step(k)
     for k, line_job in steps:
         line_job.step(k)
-    by_line(gate_o, dot_tn(flat(dg), x[...]))
+    by_line(gate_o, dg)
     out.forward()
     out.finish()
     job.finish()
@@ -1575,7 +1597,7 @@
         line_job.finish()
 
 
-def back_joint(n_line, seqs, d, wd, up, gate, us, gs, wu, wg, x, inner, d1, first, ua, ca, cv, hid, rate):
+def back_joint(n_line, seqs, d, wd, up, gate, rate, wu, wu2, wg, x, inner, d1, first, ua, ca, cv, hid):
     parts, rows, width = first.shape
     columns = wd.shape[1]
     part = jax.ShapeDtypeStruct((8, parts, rows, width), BF)
@@ -1583,10 +1605,10 @@
     by_line = ((n_line, columns // n_line, width), BF)
     wide = lambda a: a.reshape(2, 2, 2, parts * rows, a.shape[-1])
     thin = pltpu.VMEM((2, 2, 2, parts * rows, columns), BF)
-    late = (wd, wide(up), wide(gate), wu, wg, x)
+    late = (wd, wide(up), wide(gate), wu, wu2, wg, x)
     return comm_call(
         functools.partial(back_joint_kernel, n_line), "back_joint", 3,
-        (wide(d), wide(inner), us, gs, d1, first, ua, ca, cv, hid, rate) + late,
+        (wide(d), wide(inner), rate, d1, first, ua, ca, cv, hid) + late,
         [
             (first.shape, F32), ((1, width), F32), ((2, columns), F32),
             ((seqs, 4, parts * rows // seqs, width), BF), by_line, by_line, (down.shape[1:], BF),
@@ -1594,7 +1616,7 @@
         [pltpu.VMEM(part.shape, BF), pltpu.VMEM(first.shape, BF), pltpu.VMEM(down.shape, BF), thin, thin]
         + Late.scratch(late) + PlaneReduce.scratch(part) + UlyGather.sems(parts)
         + line_reduce_scratch(n_line, down),
-        40, VMEM_BYTES, tuple(range(11, 17)),
+        40, VMEM_BYTES, tuple(range(9, 16)),
     )
 
 
@@ -1632,6 +1654,9 @@
     far, core, line, side = place()
     uly = far * 2 + core
 
+    def row(x, wide):
+        return jnp.pad(x, ((0, 0),) * (x.ndim - 1) + ((0, wide - x.shape[-1]),))
+
     pieces = [v.astype(F32) for v in (qk_scale, alpha_attn, alpha_mlp, up_scale, gate_scale)]
     pieces.append(positions.reshape(-1).astype(F32))
     used = sum(v.shape[0] for v in pieces)
@@ -1641,10 +1666,10 @@
         at += v.shape[0]
     small = small.reshape(-1, 128)
 
-    hid_all, small_all, wq_all, wk_all, wv_all, out_cols, down_cols, up_full = entry(
+    hid_all, small_all, wq_all, wk_all, wv_all, out_cols, down_cols, up_first = entry(
         n_line, hidden, small, w_query, w_key, w_value, w_out, w_down, w_up
     )
-    up_full = up_full.reshape(ff_local, width)
+    up_first = up_first.reshape(ff_local, -1)
 
     flat = small_all.reshape(4, n_blk, -1)
     cut = [0, attn_each, 2 * attn_each, 3 * attn_each, 3 * attn_each + ff_each, 3 * attn_each + 2 * ff_each, used]
@@ -1655,6 +1680,10 @@
     mine = lax.dynamic_slice_in_dim(own.reshape(n_line, 2, -1), side, 1, 1)[:, 0]
     up_wide = mine[:, cut[3] : cut[4]].reshape(-1)
     gate_wide = mine[:, cut[4] : cut[5]].reshape(-1)
+    assert ff_local <= width
+    rates = jnp.pad(
+        jnp.stack([attn_rate, mlp_rate, row(up_wide, width), row(gate_wide, width)]), ((0, 4), (0, 0))
+    )
     places = jnp.transpose(
         flat[:, :, cut[5] : cut[6]].reshape(4, n_blk, seqs, rows_each), (2, 1, 0, 3)
     ).reshape(seqs, n_blk, 1, group_rows)
@@ -1665,73 +1694,58 @@
     angles = q_places.reshape(group_tokens, 1) * freqs
     cos = jnp.cos(angles)
     sin = jnp.where(lane < 32, -1.0, 1.0) * jnp.sin(angles)
-    scale_both = jnp.concatenate([scale_wide * HEAD_DIM**0.5, scale_wide], axis=1)[:, None]
+    scale_both = jnp.concatenate([scale_wide * HEAD_DIM**0.5, scale_wide], axis=1)
 
     group_hidden = hid_all.reshape(group_tokens, width)
     wq = wq_all.reshape(heads, HEAD_DIM, width)
     wk = wk_all.reshape(heads, HEAD_DIM, width)
     wv = wv_all.reshape(heads, HEAD_DIM, width)
-    qz, kv, y_both, c_both = heads_forward(group_hidden, wq, wk, wv, cos, sin, scale_both)
-    qz = qz.reshape(seqs, group_rows, heads * 128)
-
-    kv_all, out_all, gate_full, attended, mixed, inverse = attend(
-        n_line, qz, kv.reshape(seqs, group_rows, heads * 128),
-        out_cols, w_gate, q_places, places,
-    )
+    qz, y_both, c_both, kv_all, out_all, gate_full, up_last, attended, mixed, inverse = attend(
+        n_line, seqs, group_hidden, wq, wk, wv, cos, sin, scale_both, out_cols, w_gate, w_up,
+        places,
+    )
+    up_last = up_last.reshape(ff_local, -1)
     gate_full = gate_full.reshape(ff_local, width)
     out_full = out_all.reshape(width, local_width)
 
     fine = (2 * seqs, rows_each // 2, width)
     hidden_fine = hidden.reshape(fine)
     first, unit_att, att_c, first_c, mlp_in, down_full = attn_joint(
-        n_line, mixed, out_full, hidden_fine, attn_rate[None],
+        n_line, mixed, out_full, hidden_fine, rates,
         down_cols.reshape(4, 2 * attn_each, ff_local),
     )
     down_full = down_full.reshape(width, ff_local)
     mlp_in = mlp_in.reshape(plane_tokens, width)
-    inner, up_rows, gate_rows = ff_forward(mlp_in, up_full, gate_full, up_wide[None], gate_wide[None])
+    inner, up_rows, gate_rows = ff_forward(mlp_in, up_first, up_last, gate_full, rates)
     layer_out, grad_first, grad_alpha_mlp, branch_low = ff_joint(
-        inner, down_full, first, mlp_rate[None], cotangent.reshape(fine)
+        inner, down_full, first, rates, cotangent.reshape(fine)
     )
     branch_low = branch_low.reshape(plane_tokens, width)
     grad_residual, grad_alpha_attn, ff_scales, att_low, grad_up, grad_gate, down_own = back_joint(
-        n_line, seqs, branch_low, down_full, up_rows, gate_rows, up_wide[None], gate_wide[None],
-        up_full, gate_full, mlp_in, inner, grad_first, first, unit_att, att_c, first_c, hidden_fine,
-        attn_rate[None],
+        n_line, seqs, branch_low, down_full, up_rows, gate_rows, rates, up_first, up_last, gate_full,
+        mlp_in, inner, grad_first, first, unit_att, att_c, first_c, hidden_fine,
     )
     grad_up_scale, grad_gate_scale = ff_scales[0], ff_scales[1]
     down_own = down_own.reshape(8, attn_each, ff_local)
 
     dq, dkv, out_own, up_own = attend_back(
         n_line, qz, att_low.reshape(seqs, group_rows, width), out_full, mixed, attended, inverse,
-        kv_all, q_places, places, grad_up,
+        kv_all, places, grad_up,
     )
     out_own = out_own.reshape(4, attn_each, local_width)
-    gq, gk, gv, gs, gh = heads_back(
-        group_hidden, dq.reshape(group_tokens, -1), dkv.reshape(group_tokens, -1), y_both, c_both,
-        cos, sin, scale_both, wq, wk, wv,
-    )
-    def row(x, wide):
-        return jnp.pad(x, ((0, 0),) * (x.ndim - 1) + ((0, wide - x.shape[-1]),))
-
     alpha = jnp.concatenate(
         [grad_alpha_attn.reshape(4, n_blk, attn_each), grad_alpha_mlp.reshape(4, n_blk, attn_each)], axis=2
     )
-    grad_scale = gs[:, 0, :HEAD_DIM] + gs[:, 0, HEAD_DIM:]
     ff_sums = jnp.concatenate(
         [grad_up_scale.reshape(n_line, ff_each), grad_gate_scale.reshape(n_line, ff_each)], axis=1
     )
     sides = (jnp.arange(2) == side)[None, :, None]
     ff_sums = jnp.where(sides, ff_sums[:, None], 0.0).reshape(n_blk, 2 * ff_each)
-    rest = jnp.concatenate(
-        [jnp.zeros((n_blk, 128), F32), row(grad_scale.reshape(n_blk, attn_each), 128), row(ff_sums, 384)], axis=1
-    )
+    rest = jnp.concatenate([jnp.zeros((n_blk, 256), F32), row(ff_sums, 384)], axis=1)
     gq, gk, gv, grad_hidden, out_gradient, down_gradient, sums, gate_own = leave(
-        n_line,
-        *(g.reshape(n_blk, attn_each, width) for g in (gq, gk, gv)),
-        gh.reshape(seqs, 4, rows_each, width),
-        grad_residual.reshape(seqs, rows_each, width),
-        out_own, down_own, row(alpha, 128)[:, :, None], rest[:, None], grad_gate,
+        n_line, group_hidden, dq, dkv, y_both, c_both, cos, sin, scale_both, wq, wk, wv,
+        grad_residual.reshape(seqs, rows_each, width), out_own, down_own,
+        row(alpha, 128)[:, :, None], rest[:, None], grad_gate,
     )
     sums = sums[0]
     layer_out, grad_hidden, gq, gk, gv, out_gradient, up_own, gate_own, down_gradient = settle(

time: 467 us -> 452 us (0.968)
  Pallas kernels: 444 us -> 437 us
    pallas_call x5, Pallas kernels: 295 us -> 318 us  [comm_call(): pl.pallas_call(kernel, out_shape=[jax.ShapeDtypeStruct(shape, dtype) for...]
    pallas_call x3 -> x1, Pallas kernels: 78.9 us -> 58.6 us  [leave(): pl.pallas_call(functools.partial(exit_kernel, n_line), out_shape=[jax.Sha...]
    pallas_call x1, Pallas kernels: 57.8 us -> 47.2 us  [entry(): pl.pallas_call(functools.partial(entry_kernel, n_line), out_shape=[out((p...]
where the time goes in v5:
time: 452 us; the launch traced here: 448 us
  Pallas kernels  437 us (97%)
  other arithmetic  6.1 us (1%)
    pallas_call x5, Pallas kernels, comm_call(): pl.pallas_call(kernel, out_shape=[jax.ShapeDtypeStruct(shape, dtype) for...  318 us
    pallas_call x1, Pallas kernels, leave(): pl.pallas_call(functools.partial(exit_kernel, n_line), out_shape=[jax.Sha...  58.6 us
    pallas_call x1, Pallas kernels, entry(): pl.pallas_call(functools.partial(entry_kernel, n_line), out_shape=[out((p...  47.2 us

profile of v5, /device:TPU:0, one launch (start us, length us, event | category | flops | bytes accessed | tf_op | source)
XLA Modules:
  0.0 448.4 jit_solution(11738510467325089204)
XLA Ops:
  0.7 0.1 broadcast_in_dim.49
  0.8 0.7 convert_element_type.39
  1.4 0.1 convert_element_type.40
  1.5 1.4 add_bitcast_fusion.small
  2.9 47.2 %entry.1 = (bf16[2,4,64,1280]{3,2,1,0:T(8,128)(2,1)}, f32[4,8,8,128]{3,2,1,0:T(8,128)}, bf16[8,40,1280]{2,1,0:T(8,128)(2,1)}, bf16[8,40,1280]{2,1,0:T(8,128)(2,1...) custom-call(bf16[2,64,1280]{2,1,0:T(8,128)(2,1)} %hid.1, ...), custom_call_target="tpu_custom_call" | custom-call | bytes 120000000 | tf_op jit(solution)/shard_map/entry/pallas_call | solution.py:956
  50.1 0.9 reshape.168
  51.1 0.1 slice.72
  51.1 0.1 reshape.169
  51.2 0.1 reshape.170.kp_ref
  51.3 0.0 copy-start
  51.4 0.1 reshape.171
  51.5 0.7 pad_maximum_fusion.1.scale_ref.scale
  52.2 0.1 fusion.6
  52.2 0.1 stack_reshape.6
  52.4 0.1 fusion.7
  52.5 0.1 reshape.174
  52.6 0.1 reshape.175
  52.7 0.1 stack_reshape.7
  52.8 0.6 select_maximum_fusion.rate.vec_ref
  53.4 1.8 fusion
  55.2 0.0 copy-done
  55.2 103.7 %attend.1 = (bf16[2,256,640]{2,1,0:T(8,128)(2,1)}, f32[512,640]{1,0:T(8,128)}, f32[512,640]{1,0:T(8,128)}, bf16[8,2,256,640]{3,2,1,0:T(8,128)(2,1)}, bf16[4,8,40...) custom-call(bf16[512,1280]{1,0:T(8,128)(2,1)} %bitcast.46, ...), custom_call_target="tpu_custom_call" | custom-call | bytes 270000000 | tf_op jit(solution)/shard_map/attend/pallas_call | solution.py:1356
  158.9 42.4 %attn_joint.1 = (f32[4,32,1280]{2,1,0:T(8,128)}, f32[4,32,1280]{2,1,0:T(8,128)}, f32[4,32,128]{2,1,0:T(8,128)}, f32[4,32,128]{2,1,0:T(8,128)}, bf16[8,4,32,1280]...) custom-call(bf16[2,256,320]{2,1,0:T(8,128)(2,1)} %get-tuple-element.79.mixed.mixed_ref, bf16[1280,320]{1,0:T(8,128)(2,1)} %bitcast.48, ...), custom_call_target="tpu_custom_call" | custom-call | bytes 75000000 | tf_op jit(solution)/shard_map/attn_joint/pallas_call | solution.py:1356
  201.3 8.8 %ff_forward.1 = (bf16[1024,640]{1,0:T(8,128)(2,1)}, f32[1024,640]{1,0:T(8,128)}, f32[1024,640]{1,0:T(8,128)}) custom-call(bf16[1024,1280]{1,0:T(8,128)(2,1)} %bitcast.58, bf16[640,640]{1,0:T(8,128)(2,1)} %bitcast.66, bf16[640,640]{1,0:T(8,128)(2,1)} %bitcast.68, bf16[640,1280]{1,0:T(8,128)(2,1)} %bitcast.63, f32[8,1280]{1,0:T(8,128)} %select_maximum_fusion.rate.vec_ref), custom_call_target="tpu_custom_call" | custom-call | flops 3355443200 | bytes 9175040 | tf_op jit(solution)/shard_map/ff_forward/pallas_call | solution.py:1312
  210.1 35.8 %ff_joint.1 = (bf16[4,32,1280]{2,1,0:T(8,128)(2,1)}, f32[4,32,1280]{2,1,0:T(8,128)}, f32[1,1280]{1,0:T(1,128)}, bf16[8,4,32,1280]{3,2,1,0:T(8,128)(2,1)}) custom-call(bf16[2,2,2,128,640]{4,3,2,1,0:T(8,128)(2,1)} %bitcast.44, bf16[1280,640]{1,0:T(8,128)(2,1)} %bitcast.42, f32[4,32,1280]{2,1,0:T(8,128)} %get-tuple-element.88.first, ...), custom_call_target="tpu_custom_call" | custom-call | bytes 90000000 | tf_op jit(solution)/shard_map/ff_joint/pallas_call | solution.py:1356
  245.9 47.6 %back_joint.1 = (f32[4,32,1280]{2,1,0:T(8,128)}, f32[1,1280]{1,0:T(1,128)}, f32[2,640]{1,0:T(2,128)}, bf16[2,4,64,1280]{3,2,1,0:T(8,128)(2,1)}, bf16[4,160,1280]...) custom-call(bf16[2,2,2,128,1280]{4,3,2,1,0:T(8,128)(2,1)} %bitcast.62, ...), custom_call_target="tpu_custom_call" | custom-call | bytes 120000000 | tf_op jit(solution)/shard_map/back_joint/pallas_call | solution.py:1356
  293.5 0.0 copy-start.2
  293.5 0.0 copy-start.1
  293.5 0.0 copy-start.3
  293.5 88.4 %attend_back.1 = (bf16[2,256,640]{2,1,0:T(8,128)(2,1)}, bf16[2,256,640]{2,1,0:T(8,128)(2,1)}, bf16[160,320]{1,0:T(8,128)(2,1)}, f32[160,1280]{1,0:T(8,128)}) custom-call(bf16[2,256,640]{2,1,0:T(8,128)(2,1)} %get-tuple-element.90.q_ref, bf16[2,256,1280]{2,1,0:T(8,128)(2,1)} %bitcast.65, bf16[1280,320]{1,0:T(8,128)(2,1)} %bitcast.49, ...), custom_call_target="tpu_custom_call" | custom-call | bytes 225000000 | tf_op jit(solution)/shard_map/attend_back/pallas_call | solution.py:1356
  381.9 0.0 copy-done.2
  381.9 0.0 copy-done.1
  382.0 0.1 reshape.192
  382.1 0.1 reshape.191
  382.1 0.7 select_maximum_fusion.3
  382.8 0.0 copy-done.3
  382.8 0.1 reshape_squeeze.11
  382.9 0.1 reshape_squeeze.12
  383.0 0.1 pad_maximum_fusion
  383.1 0.1 broadcast_select_fusion
  383.2 0.6 broadcast_in_dim.54.rest
  383.8 58.6 %leave.1 = (f32[40,1280]{1,0:T(8,128)}, f32[40,1280]{1,0:T(8,128)}, f32[40,1280]{1,0:T(8,128)}, f32[2,64,1280]{2,1,0:T(8,128)}, f32[40,1280]{1,0:T(8,128)}, /*in...) custom-call(bf16[512,1280]{1,0:T(8,128)(2,1)} %bitcast.47, bf16[2,256,640]{2,1,0:T(8,128)(2,1)} %get-tuple-element.103.dq, ...), custom_call_target="tpu_custom_call" | custom-call | tf_op jit(solution)/shard_map/leave/pallas_call | solution.py:853
  442.4 0.0 copy-start.4
  442.4 4.3 settle.1
  446.7 0.0 copy-done.4
  446.7 0.6 slice_bitcast_fusion
  447.3 0.6 fusion.8
  (22 shorter events, 0.2 us)
Async XLA Ops:
  51.3 3.9 copy-start
  293.5 88.4 %copy-start.2 = (f32[1,1280]{1,0:T(1,128)S(1)}, f32[1,1280]{1,0:T(1,128)}, u32[]{:S(2)}) copy-start(f32[1,1280]{1,0:T(1,128)} %get-tuple-element.110) | copy-start | bytes 15364
  293.5 88.4 %copy-start.1 = (f32[1,1280]{1,0:T(1,128)S(1)}, f32[1,1280]{1,0:T(1,128)}, u32[]{:S(2)}) copy-start(f32[1,1280]{1,0:T(1,128)} %get-tuple-element.111) | copy-start | bytes 15364
  293.5 89.3 %copy-start.3 = (f32[2,640]{1,0:T(2,128)S(1)}, f32[2,640]{1,0:T(2,128)}, u32[]{:S(2)}) copy-start(f32[2,640]{1,0:T(2,128)} %get-tuple-element.112) | copy-start | bytes 15364
  442.4 4.4 copy-start.4

commit v6 on v5

--- a/solution.py
+++ b/solution.py
@@ -256,21 +256,17 @@
         self.near[k][i].wait_recv()
         return add_low(self.x[plane_index(sy, self.c, ss), i], self.near_ref[k, i])
 
-    def start(self):
-        for spot in self.near:
-            for copy in spot:
-                copy.start()
-
-    def middle(self):
+    def middle(self, far):
         for i in self.parts:
-            self.out_d[i] = self.pair(0, i).astype(BF)
-            self.corner[i].start()
-            if i % 2 == 0:
+            if far:
+                self.out_d[i] = self.pair(0, i).astype(BF)
+                self.corner[i].start()
+                if i % 2 == 1:
+                    self.out_y[i] = self.pair(2, i).astype(BF)
+                    self.by_y[i].start()
+            elif i % 2 == 0:
                 self.out_x[i] = self.pair(1, i).astype(BF)
                 self.by_x[i].start()
-            else:
-                self.out_y[i] = self.pair(2, i).astype(BF)
-                self.by_y[i].start()
 
     def last(self):
         for i in self.parts:
@@ -677,8 +673,42 @@
     return scratch
 
 
+def comm_call(
+    kernel, name, collective_id, args, outs, scratch, micros, room=VMEM_BYTES, far_args=(), far_outs=(), late=()
+):
+    vmem, anyway = pl.BlockSpec(memory_space=pltpu.VMEM), pl.BlockSpec(memory_space=pl.ANY)
+    held = [pltpu.VMEM(args[i].shape, args[i].dtype) for i in late]
+    held += [pltpu.SemaphoreType.DMA((len(late),))] * (len(late) > 0)
+
+    def whole(*refs):
+        refs = list(refs)
+        mine, copies = refs[len(refs) - len(held) :], []
+        refs = refs[: len(refs) - len(held)]
+        for j, i in enumerate(late):
+            copies.append(pltpu.make_async_copy(refs[i], mine[j], mine[-1].at[j]))
+            copies[-1].start()
+            refs[i] = mine[j]
+
+        def ready():
+            for copy in copies:
+                copy.wait()
+
+        kernel(ready, *refs)
+
+    return pl.pallas_call(
+        whole,
+        out_shape=[jax.ShapeDtypeStruct(shape, dtype) for shape, dtype in outs],
+        in_specs=[anyway if i in far_args or i in late else vmem for i in range(len(args))],
+        out_specs=[anyway if i in far_outs else vmem for i in range(len(outs))],
+        scratch_shapes=list(scratch) + held,
+        compiler_params=params(collective_id, room),
+        cost_estimate=pl.CostEstimate(flops=0, bytes_accessed=micros * 3_000_000, transcendentals=0),
+        name=name,
+    )(*args)
+
+
 def exit_kernel(
-    n_line, x, dq, dkv, yy_ref, cc_ref, cos, sin, scale, wq, wk, wv, res, oc, dc, alpha, rest, gg,
+    n_line, ready, x, dq, dkv, yy_ref, cc_ref, cos, sin, scale, wq, wk, wv, res, oc, dc, alpha, rest, gg,
     gq_o, gk_o, gv_o, gh_o, go_o, gd_o, sum_o, gg_o, oc_o, dc_o,
     flat, acc, gq, gk, gv, gh, scale_s,
     alpha_in, line_out, line_all, oc_s, oc_r, dc_s, dc_r, al_s, al_r, su_s, su_r, keep, *scratch,
@@ -709,6 +739,7 @@
         job.start()
     for job, _ in gates:
         job.step(n_line - 1)
+    ready()
     rows_all = x[...]
     seqs, group_rows, wide = dq.shape
     heads = wide // 128
@@ -850,15 +881,10 @@
     outs = [grad.shape[1:]] * 3 + [
         res.shape, (oc.shape[1], 4 * oc.shape[2]), (dc.shape[1], 8 * dc.shape[2]), rest.shape[1:], gg.shape[1:]
     ]
-    return pl.pallas_call(
-        functools.partial(exit_kernel, n_line),
-        out_shape=[jax.ShapeDtypeStruct(shape, F32) for shape in outs],
-        in_specs=[vmem] * len(args),
-        out_specs=[vmem] * len(outs),
-        scratch_shapes=scratch,
-        compiler_params=params(8),
-        name="leave",
-    )(*args)
+    return comm_call(
+        functools.partial(exit_kernel, n_line), "leave", 8, args, [(shape, F32) for shape in outs], scratch,
+        60, late=tuple(range(11)),
+    )
 
 
 def entry_kernel(
@@ -1026,7 +1052,7 @@
 
 
 def attend_kernel(
-    n_line, x_ref, wq_ref, wk_ref, wv_ref, cos_ref, sin_ref, scale_ref, oc_ref, wg_ref, wu_ref, kp_ref,
+    n_line, ready, x_ref, wq_ref, wk_ref, wv_ref, cos_ref, sin_ref, scale_ref, oc_ref, wg_ref, wu_ref, kp_ref,
     q_ref, y_ref, c_ref, kv_o, oc_o, wg_o, wu_o, o_ref, mixed_ref, inv_ref, kv_ref, acc, total, place_q, *sems,
 ):
     y, c, z, s = place()
@@ -1039,28 +1065,8 @@
         n_line, lambda: wu_ref.at[:, slice(cut, wu_ref.shape[-1])], lambda zz: wu_o.at[zz], *sems[-4:]
     )
     up.start()
-    x = x_ref[...]
-
-    def make(h, carry):
-        lanes = pl.ds(pl.multiple_of(h * 128, 128), 128)
-        wv = wv_ref[h]
-        got = dot_nt(x, jnp.concatenate([wq_ref[h], wk_ref[h], jnp.zeros_like(wv), wv], axis=0))
-        raw, value = got[:, :128], got[:, 128:]
-        low = lanes_of(raw.shape) < HEAD_DIM
-        turned = raw * cos_ref[...] + turn(raw) * sin_ref[...]
-        norm = lax.rsqrt(halves(turned * turned) + HEAD_DIM * tiny_eps)
-        unit = turned * norm
-        both = unit * scale_ref[pl.ds(h, 1)]
-        query = jnp.where(low, both, 0.0).astype(BF)
-        kv = jnp.where(low, pltpu.roll(both, HEAD_DIM, 1), value).astype(BF)
-        for i in range(seqs):
-            q_ref[i, :, lanes] = query[i * rows : (i + 1) * rows]
-            kv_ref[i, :, lanes] = kv[i * rows : (i + 1) * rows]
-        y_ref[:, lanes] = unit
-        c_ref[:, lanes] = norm
-        return carry
-
-    lax.fori_loop(0, heads, make, 0)
+    ready()
+
     each = len(BlkGather.sems(n_line))
     picks = [
         (lambda i=i: kv_ref.at[i], lambda block, i=i: kv_o.at[block, i]) for i in range(seqs)
@@ -1068,11 +1074,32 @@
     jobs = [
         BlkGather(n_line, *pick, *sems[each * i : each * (i + 1)]) for i, pick in enumerate(picks)
     ]
+
+    def make(t, carry):
+        i, h = t // heads, lax.rem(t, heads)
+        lanes = pl.ds(pl.multiple_of(h * 128, 128), 128)
+        mine = pl.ds(pl.multiple_of(i * rows, rows), rows)
+        wv = wv_ref[h]
+        got = dot_nt(x_ref[mine], jnp.concatenate([wq_ref[h], wk_ref[h], jnp.zeros_like(wv), wv], axis=0))
+        raw, value = got[:, :128], got[:, 128:]
+        low = lanes_of(raw.shape) < HEAD_DIM
+        turned = raw * cos_ref[mine] + turn(raw) * sin_ref[mine]
+        norm = lax.rsqrt(halves(turned * turned) + HEAD_DIM * tiny_eps)
+        unit = turned * norm
+        both = unit * scale_ref[pl.ds(h, 1)]
+        q_ref[i, :, lanes] = jnp.where(low, both, 0.0).astype(BF)
+        kv_ref[i, :, lanes] = jnp.where(low, pltpu.roll(both, HEAD_DIM, 1), value).astype(BF)
+        y_ref[mine, lanes] = unit
+        c_ref[mine, lanes] = norm
+        for j in range(seqs):
+            pl.when(t == heads * (j + 1) - 1)(jobs[j].start)
+        return carry
+
+    lax.fori_loop(0, seqs * heads, make, 0)
     gates = line_gathers(
         n_line, wg_ref, lambda z: wg_o.at[z], sems[each * (seqs + 1) : each * (seqs + 1) + chunk]
     )
-    for job in jobs:
-        job.start()
+    jobs[-1].start()
     for job in gates:
         job.keep().start()
     acc[...] = jnp.zeros_like(acc)
@@ -1117,8 +1144,12 @@
                         pl.when(job.goes(w))(lambda: job.own(w).start())
             zz = jnp.where(way == 0, z - k, z + k)
             block = zz * 2 + jnp.where(stage == 0, s, 1 - s)
-            for i in range(seqs):
+
+            def one(i, carry):
                 attend_to(i, block, lambda lanes: kv_o[block, i, :, lanes])
+                return carry
+
+            lax.fori_loop(0, seqs, one, 0)
 
     arrivals(n_line, body)
     low = lanes_of((rows, 128)) < HEAD_DIM
@@ -1158,18 +1189,23 @@
         ],
         [pltpu.VMEM(wide, BF), pltpu.VMEM(head, F32), pltpu.VMEM(head, F32), pltpu.VMEM((seqs, rows, rows), F32)]
         + BlkGather.sems(n_line) * (seqs + 1) + line_gather_sems(n_line) + LineGather.sems(n_line),
-        90, far_outs=(4, 5, 6),
+        90, far_outs=(4, 5, 6), late=(0, 1, 2, 3, 4, 5),
     )
 
 
 def attend_back_kernel(
-    n_line, fits, q_ref, low_ref, w_ref, mixed_ref, o_ref, inv_ref, kv_ref, kp_ref, gu_ref,
+    n_line, fits, ready, q_ref, low_ref, w_ref, mixed_ref, o_ref, inv_ref, kv_ref, kp_ref, gu_ref,
     dq_ref, dkv_ref, oc_ref, gu_o, dz, delta, dq, parts, oparts, key_s, key_sem, *scratch,
 ):
     y, c, z, s = place()
     blk_greet(n_line)
     seqs, rows, wide = q_ref.shape
     heads, width = wide // 128, low_ref.shape[-1]
+    each = 6
+    ups = line_reduces(n_line, gu_ref, scratch[each * (seqs + 1) :])
+    for line_job, _ in ups:
+        line_job.step(n_line - 1)
+    ready()
     low_rows = low_ref[...].reshape(seqs * rows, width)
     grad = dot_tn(low_rows, mixed_ref[...].reshape(seqs * rows, mixed_ref.shape[-1])).astype(BF)
     n_blk, each_out = 2 * n_line, width // (8 * n_line)
@@ -1180,7 +1216,6 @@
     each = 6
     jobs = [BlkReduce(n_line, parts.at[:, i], *scratch[each * i : each * (i + 1)]) for i in range(seqs)]
     out_job = BlkReduce(n_line, oparts, *scratch[each * seqs : each * (seqs + 1)])
-    ups = line_reduces(n_line, gu_ref, scratch[each * (seqs + 1) :])
     for k in range(n_line - 1, -1, -1):
         out_job.start(k)
     low = lanes_of((rows, 128)) < HEAD_DIM
@@ -1208,7 +1243,7 @@
             copy = pltpu.make_async_copy(kv_ref.at[block], key_s, key_sem.at[0])
             copy.start()
             copy.wait()
-        for i in range(seqs):
+        def one(i, carry):
             allowed = down_columns(kp_ref[i, block]) <= kp_ref[i, z * 2 + s]
             for h in range(heads):
                 lanes = slice(h * 128, (h + 1) * 128)
@@ -1221,12 +1256,15 @@
                     jnp.concatenate([ds, p.astype(BF)], axis=1), pair
                 ).astype(BF)
                 dq[i, h] = dq[i, h] + dot_tn(ds, kv)
+            return carry
+
+        lax.fori_loop(0, seqs, one, 0)
 
     def step(t, carry):
         k, r = n_line - 1 - t // 4, lax.rem(t, 4)
         way, stays = r // 2, lax.rem(r, 2)
 
-        @pl.when((r == 0) & (k > 0))
+        @pl.when((r == 0) & (k > 0) & (k < n_line - 1))
         def _():
             for line_job, _ in ups:
                 line_job.step(k)
@@ -1286,42 +1324,8 @@
         ]
         + BlkReduce.scratch(n_line, one) * seqs + BlkReduce.scratch(n_line, out_one)
         + line_reduce_scratch(n_line, gu),
-        75, 67_000_000, () if fits else (6,),
-    )
-
-
-def ff_kernel(x_ref, wu_ref, wu2_ref, wg_ref, vec_ref, inner_ref, up_ref, gate_ref):
-    x = x_ref[...]
-    cut = wu_ref.shape[1]
-    up = dot_nt(x[:, :cut], wu_ref[...]) + dot_nt(x[:, cut:], wu2_ref[...])
-    gate = dot_nt(x, wg_ref[...])
-    columns = up.shape[1]
-    z = gate * vec_ref[3:4, :columns] * D**0.5
-    inner_ref[...] = (z / (1.0 + jnp.exp(-z)) * (up * vec_ref[2:3, :columns])).astype(BF)
-    up_ref[...] = up
-    gate_ref[...] = gate
-
-
-def ff_forward(x, wu, wu2, wg, vec):
-    rows, width = x.shape
-    columns = wu.shape[0]
-    block = rows // 4
-    whole = lambda a: pl.BlockSpec(a.shape, lambda i: (0, 0))
-    part = lambda n: pl.BlockSpec((block, n), lambda i: (i, 0))
-    out = lambda dtype: jax.ShapeDtypeStruct((rows, columns), dtype)
-    return pl.pallas_call(
-        ff_kernel,
-        grid=(4,),
-        out_shape=[out(BF), out(F32), out(F32)],
-        in_specs=[part(width)] + [whole(a) for a in (wu, wu2, wg, vec)],
-        out_specs=[part(columns)] * 3,
-        compiler_params=pltpu.CompilerParams(vmem_limit_bytes=VMEM_BYTES),
-        cost_estimate=pl.CostEstimate(
-            flops=4 * rows * width * columns, bytes_accessed=2 * rows * width + 10 * rows * columns,
-            transcendentals=rows * columns,
-        ),
-        name="ff_forward",
-    )(x, wu, wu2, wg, vec)
+        75, 67_000_000, () if fits else (6,), late=(0, 1, 2, 3, 4) + (6,) * fits,
+    )
 
 
 def unit_of(x):
@@ -1351,25 +1355,12 @@
         return self.bufs[i]
 
 
-def comm_call(kernel, name, collective_id, args, outs, scratch, micros, room=VMEM_BYTES, far_args=(), far_outs=()):
-    vmem, anyway = pl.BlockSpec(memory_space=pltpu.VMEM), pl.BlockSpec(memory_space=pl.ANY)
-    return pl.pallas_call(
-        kernel,
-        out_shape=[jax.ShapeDtypeStruct(shape, dtype) for shape, dtype in outs],
-        in_specs=[anyway if i in far_args else vmem for i in range(len(args))],
-        out_specs=[anyway if i in far_outs else vmem for i in range(len(outs))],
-        scratch_shapes=scratch,
-        compiler_params=params(collective_id, room),
-        cost_estimate=pl.CostEstimate(flops=0, bytes_accessed=micros * 3_000_000, transcendentals=0),
-        name=name,
-    )(*args)
-
-
 def attn_joint_kernel(
-    n_line, mixed, w, hid, rate, dc, first_o, ua_o, ca_o, cv_o, all_o, down_o, part, low, *scratch
+    n_line, ready, mixed, w, hid, rate, dc, first_o, ua_o, ca_o, cv_o, all_o, down_o, part, low, *scratch
 ):
     ends = line_ends(n_line)
     greet(plane_peers(), ends[:2])
+    ready()
     split = len(UlyReduce.scratch(part))
     job = UlyReduce(part, *scratch[:split])
     out = PlaneGather(low, all_o, *scratch[split : split + 3])
@@ -1426,37 +1417,65 @@
         ],
         [pltpu.VMEM(part.shape, BF), pltpu.VMEM(hid.shape, BF)]
         + UlyReduce.scratch(part) + PlaneGather.sems(parts) + line_gather_sems(n_line),
-        25, far_outs=(5,),
-    )
-
-
-def plane_products(job, part, c, product, between=lambda: None):
+        25, far_outs=(5,), late=(0, 1, 2, 4),
+    )
+
+
+def plane_products(job, part, y, c, prepare, product):
     _, parts, rows, width = part.shape
-    for cc, first in ((1 - c, True), (c, False)):
-        def one(yy, carry):
+    for yy, spots in ((1 - y, (0, 2)), (y, (1, 3))):
+        def one(j, carry):
+            cc = jnp.where(j == 0, 1 - c, c)
+            prepare(yy, cc)
             got = product(yy, cc).astype(BF).reshape(2, parts, rows, width)
             for ss in (0, 1):
                 part[plane_index(yy, cc, ss)] = got[ss]
+
+            @pl.when(j == 0)
+            def _():
+                for k in spots:
+                    for copy in job.near[k]:
+                        copy.start()
+
             return carry
 
         lax.fori_loop(0, 2, one, 0)
-        if first:
-            job.start()
-            between()
-
-
-def ff_joint_kernel(inner, w, first, rate, cot, out_o, d1_o, sum_o, all_o, part, low, *scratch):
+        job.middle(spots[0] == 0)
+
+
+def ff_joint_kernel(
+    ready, x, wu, wu2, wg, rate, w, first, cot, out_o, d1_o, sum_o, all_o, inner_h, up_h, gate_h,
+    part, low, inner, up_s, gate_s, kept, *scratch,
+):
     y, c, z, s = place()
     greet(plane_peers())
     split = len(PlaneReduce.scratch(part))
     job = PlaneReduce(part, *scratch[:split])
     out = PlaneGather(low, all_o, *scratch[split:])
     _, seqs, rows, width = part.shape
-    columns = inner.shape[-1]
+    columns, tokens = inner.shape[-1], 2 * seqs * rows
+    cut = wu.shape[1]
+
+    def forward(yy, cc):
+        block = x[yy, cc].reshape(tokens, width)
+        up = dot_nt(block[:, :cut], wu[...]) + dot_nt(block[:, cut:], wu2[...])
+        gate = dot_nt(block, wg[...])
+        gz = gate * rate[3:4, :columns] * D**0.5
+        got = gz / (1.0 + jnp.exp(-gz)) * (up * rate[2:3, :columns])
+        inner[yy, cc] = got.astype(BF).reshape(inner.shape[2:])
+        up_s[yy, cc] = up.reshape(up_s.shape[2:])
+        gate_s[yy, cc] = gate.reshape(gate_s.shape[2:])
+
+    ready()
     plane_products(
-        job, part, c, lambda yy, cc: dot_nt(inner[yy, cc].reshape(2 * seqs * rows, columns), w[...])
-    )
-    job.middle()
+        job, part, y, c, forward, lambda yy, cc: dot_nt(inner[yy, cc].reshape(tokens, columns), w[...])
+    )
+    keeps = [
+        pltpu.make_async_copy(a, o, kept.at[i])
+        for i, (a, o) in enumerate(((inner, inner_h), (up_s, up_h), (gate_s, gate_h)))
+    ]
+    for copy in keeps:
+        copy.start()
     job.last()
     for i in range(seqs):
         ub, cb = unit_of(job.result(i))
@@ -1475,28 +1494,40 @@
     out.forward_part(seqs - 1)
     out.finish()
     job.finish()
-
-
-def ff_joint(inner, w, first, rate, cot):
+    for copy in keeps:
+        copy.wait()
+
+
+def ff_joint(x, wu, wu2, wg, rate, w, first, cot):
     seqs, rows, width = first.shape
     part = jax.ShapeDtypeStruct((8, seqs, rows, width), BF)
+    columns = wg.shape[0]
+    wide = (2, 2, 2, seqs * rows, columns)
     return comm_call(
         ff_joint_kernel, "ff_joint", 2,
-        (inner.reshape(2, 2, 2, seqs * rows, inner.shape[-1]), w, first, rate, cot),
-        [(first.shape, BF), (first.shape, F32), ((1, width), F32), (part.shape, BF)],
-        [pltpu.VMEM(part.shape, BF), pltpu.VMEM(first.shape, BF)] + PlaneReduce.scratch(part) + PlaneGather.sems(seqs),
-        30,
+        (x.reshape(wide[:4] + (width,)), wu, wu2, wg, rate, w, first, cot),
+        [
+            (first.shape, BF), (first.shape, F32), ((1, width), F32), (part.shape, BF),
+            (wide, BF), (wide, F32), (wide, F32),
+        ],
+        [
+            pltpu.VMEM(part.shape, BF), pltpu.VMEM(first.shape, BF), pltpu.VMEM(wide, BF),
+            pltpu.VMEM(wide, F32), pltpu.VMEM(wide, F32), pltpu.SemaphoreType.DMA((3,)),
+        ]
+        + PlaneReduce.scratch(part) + PlaneGather.sems(seqs),
+        35, far_outs=(4, 5, 6), late=(0, 1, 2, 3, 5),
     )
 
 
 def back_joint_kernel(
-    n_line, d, inner, rate, d1, first, ua, ca, cv, hid, wd_h, up_h, gate_h, wu_h, wu2_h, wg_h, x_h,
+    n_line, ready, d, inner, rate, d1, first, ua, ca, cv, hid, wd_h, up_h, gate_h, wu_h, wu2_h, wg_h, x_h,
     res_o, sum_o, ff_sum_o, all_o, up_o, gate_o, down_o, part, low, down_s, du, dg, *scratch,
 ):
     y, c, z, s = place()
     late = Late((wd_h, up_h, gate_h, wu_h, wu2_h, wg_h, x_h), scratch[:8])
     scratch = scratch[8:]
     greet(plane_peers(), line_ends(n_line)[:2])
+    ready()
     split = len(PlaneReduce.scratch(part))
     job = PlaneReduce(part, *scratch[:split])
     _, parts, rows, width = part.shape
@@ -1531,23 +1562,18 @@
 
     ff_sum_o[...] = jnp.zeros_like(ff_sum_o)
 
-    def gated_back(cc):
-        def one(yy, carry):
-            got = dot_nn(d[yy, cc].reshape(tokens // 4, width), wd[...])
-            up, gate = up_ref[yy, cc].reshape(got.shape), gate_ref[yy, cc].reshape(got.shape)
-            gz = gate * g_scale
-            sig = 1.0 / (1.0 + jnp.exp(-gz))
-            d_up = got * (gz * sig)
-            d_gate = got * (up * u_scale) * sig * (1.0 + gz * (1.0 - sig))
-            du[yy, cc] = (d_up * u_scale).astype(BF).reshape(du.shape[2:])
-            dg[yy, cc] = (d_gate * g_scale).astype(BF).reshape(dg.shape[2:])
-            ff_sum_o[0:1] = ff_sum_o[0:1] + jnp.sum(d_up * up, axis=0, keepdims=True)
-            ff_sum_o[1:2] = ff_sum_o[1:2] + jnp.sum(d_gate * gate, axis=0, keepdims=True) * D**0.5
-            return carry
-
-        lax.fori_loop(0, 2, one, 0)
-
-    gated_back(1 - c)
+    def gated_back(yy, cc):
+        got = dot_nn(d[yy, cc].reshape(tokens // 4, width), wd[...])
+        up, gate = up_ref[yy, cc].reshape(got.shape), gate_ref[yy, cc].reshape(got.shape)
+        gz = gate * g_scale
+        sig = 1.0 / (1.0 + jnp.exp(-gz))
+        d_up = got * (gz * sig)
+        d_gate = got * (up * u_scale) * sig * (1.0 + gz * (1.0 - sig))
+        du[yy, cc] = (d_up * u_scale).astype(BF).reshape(du.shape[2:])
+        dg[yy, cc] = (d_gate * g_scale).astype(BF).reshape(dg.shape[2:])
+        ff_sum_o[0:1] = ff_sum_o[0:1] + jnp.sum(d_up * up, axis=0, keepdims=True)
+        ff_sum_o[1:2] = ff_sum_o[1:2] + jnp.sum(d_gate * gate, axis=0, keepdims=True) * D**0.5
+
     wu, wu2, wg = late(3), late(4), late(5)
 
     def product(yy, cc):
@@ -1555,8 +1581,7 @@
         got = jnp.concatenate([dot_nn(u, wu[...]), dot_nn(u, wu2[...])], axis=1)
         return got + dot_nn(g, wg[...])
 
-    plane_products(job, part, c, product, lambda: gated_back(c))
-    job.middle()
+    plane_products(job, part, y, c, gated_back, product)
     steps = [(k, line_job) for k in range(n_line - 2, 0, -1) for line_job, _ in downs]
     job.last()
     x = late(6)
@@ -1616,7 +1641,7 @@
         [pltpu.VMEM(part.shape, BF), pltpu.VMEM(first.shape, BF), pltpu.VMEM(down.shape, BF), thin, thin]
         + Late.scratch(late) + PlaneReduce.scratch(part) + UlyGather.sems(parts)
         + line_reduce_scratch(n_line, down),
-        40, VMEM_BYTES, tuple(range(9, 16)),
+        40, VMEM_BYTES, tuple(range(9, 16)), late=(0, 1),
     )
 
 
@@ -1716,9 +1741,8 @@
     )
     down_full = down_full.reshape(width, ff_local)
     mlp_in = mlp_in.reshape(plane_tokens, width)
-    inner, up_rows, gate_rows = ff_forward(mlp_in, up_first, up_last, gate_full, rates)
-    layer_out, grad_first, grad_alpha_mlp, branch_low = ff_joint(
-        inner, down_full, first, rates, cotangent.reshape(fine)
+    layer_out, grad_first, grad_alpha_mlp, branch_low, inner, up_rows, gate_rows = ff_joint(
+        mlp_in, up_first, up_last, gate_full, rates, down_full, first, cotangent.reshape(fine)
     )
     branch_low = branch_low.reshape(plane_tokens, width)
     grad_residual, grad_alpha_attn, ff_scales, att_low, grad_up, grad_gate, down_own = back_joint(

time: 452 us -> 429 us (0.949)
  Pallas kernels: 437 us -> 416 us
    pallas_call x7 -> x6, Pallas kernels: 385 us -> 364 us  [comm_call(): pl.pallas_call(whole, out_shape=[jax.ShapeDtypeStruct(shape, dtype) for s...]
where the time goes in v6:
time: 429 us; the launch traced here: 427 us
  Pallas kernels  416 us (97%)
  other arithmetic  6.1 us (1%)
  local copies, waits for them, and re-layouts  4.29 us (1%)
    pallas_call x6, Pallas kernels, comm_call(): pl.pallas_call(whole, out_shape=[jax.ShapeDtypeStruct(shape, dtype) for s...  364 us
    pallas_call x1, Pallas kernels, entry(): pl.pallas_call(functools.partial(entry_kernel, n_line), out_shape=[out((p...  47.2 us

profile of v6, /device:TPU:0, one launch (start us, length us, event | category | flops | bytes accessed | tf_op | source)
XLA Modules:
  0.0 427.0 jit_solution(15278606075064062785)
XLA Ops:
  0.7 0.1 broadcast_in_dim.49
  0.8 0.7 convert_element_type.39
  1.4 0.1 convert_element_type.40
  1.5 1.4 add_bitcast_fusion.small
  2.9 47.2 %entry.1 = (bf16[2,4,64,1280]{3,2,1,0:T(8,128)(2,1)}, f32[4,8,8,128]{3,2,1,0:T(8,128)}, bf16[8,40,1280]{2,1,0:T(8,128)(2,1)}, bf16[8,40,1280]{2,1,0:T(8,128)(2,1...) custom-call(bf16[2,64,1280]{2,1,0:T(8,128)(2,1)} %hid.1, ...), custom_call_target="tpu_custom_call" | custom-call | bytes 120000000 | tf_op jit(solution)/shard_map/entry/pallas_call | solution.py:982
  50.1 0.9 reshape.158
  51.1 0.1 slice.72
  51.2 0.1 reshape.159
  51.3 0.1 reshape.160.refs_10_.refs_7_
  51.4 0.0 copy-start
  51.4 0.1 reshape.161
  51.5 0.7 pad_maximum_fusion.1.refs_6_.refs_7_
  52.2 0.1 fusion.6
  52.3 0.1 stack_reshape.6
  52.4 0.1 fusion.7
  52.5 0.1 reshape.164
  52.6 0.1 reshape.165
  52.7 0.1 stack_reshape.7
  52.8 0.6 select_maximum_fusion.refs_3_.refs_4_.refs_2_
  53.4 1.8 fusion
  55.2 0.0 copy-done
  55.2 104.5 %attend.1 = (bf16[2,256,640]{2,1,0:T(8,128)(2,1)}, f32[512,640]{1,0:T(8,128)}, f32[512,640]{1,0:T(8,128)}, bf16[8,2,256,640]{3,2,1,0:T(8,128)(2,1)}, bf16[4,8,40...) custom-call(bf16[512,1280]{1,0:T(8,128)(2,1)} %bitcast.46, ...), custom_call_target="tpu_custom_call" | custom-call | bytes 270000000 | tf_op jit(solution)/shard_map/attend/pallas_call | solution.py:698
  159.7 31.6 %attn_joint.1 = (f32[4,32,1280]{2,1,0:T(8,128)}, f32[4,32,1280]{2,1,0:T(8,128)}, f32[4,32,128]{2,1,0:T(8,128)}, f32[4,32,128]{2,1,0:T(8,128)}, bf16[8,4,32,1280]...) custom-call(bf16[2,256,320]{2,1,0:T(8,128)(2,1)} %get-tuple-element.79.refs_0_.refs_3_, bf16[1280,320]{1,0:T(8,128)(2,1)} %bitcast.48, ...), custom_call_target="tpu_custom_call" | custom-call | bytes 75000000 | tf_op jit(solution)/shard_map/attn_joint/pallas_call | solution.py:698
  191.3 38.8 %ff_joint.1 = (bf16[4,32,1280]{2,1,0:T(8,128)(2,1)}, f32[4,32,1280]{2,1,0:T(8,128)}, f32[1,1280]{1,0:T(1,128)}, bf16[8,4,32,1280]{3,2,1,0:T(8,128)(2,1)}, bf16[2...) custom-call(bf16[2,2,2,128,1280]{4,3,2,1,0:T(8,128)(2,1)} %bitcast.40, ...), custom_call_target="tpu_custom_call" | custom-call | bytes 105000000 | tf_op jit(solution)/shard_map/ff_joint/pallas_call | solution.py:698
  230.1 46.5 %back_joint.1 = (f32[4,32,1280]{2,1,0:T(8,128)}, f32[1,1280]{1,0:T(1,128)}, f32[2,640]{1,0:T(2,128)}, bf16[2,4,64,1280]{3,2,1,0:T(8,128)(2,1)}, bf16[4,160,1280]...) custom-call(bf16[2,2,2,128,1280]{4,3,2,1,0:T(8,128)(2,1)} %bitcast.62, ...), custom_call_target="tpu_custom_call" | custom-call | bytes 120000000 | tf_op jit(solution)/shard_map/back_joint/pallas_call | solution.py:698
  276.6 0.0 copy-start.2
  276.6 0.0 copy-start.1
  276.6 0.0 copy-start.3
  276.6 86.4 %attend_back.1 = (bf16[2,256,640]{2,1,0:T(8,128)(2,1)}, bf16[2,256,640]{2,1,0:T(8,128)(2,1)}, bf16[160,320]{1,0:T(8,128)(2,1)}, f32[160,1280]{1,0:T(8,128)}) custom-call(bf16[2,256,640]{2,1,0:T(8,128)(2,1)} %get-tuple-element.89.refs_0_, bf16[2,256,1280]{2,1,0:T(8,128)(2,1)} %bitcast.63, bf16[1280,320]{1,0:T(8,128)(2,1)} %bitcast.49, ...), custom_call_target="tpu_custom_call" | custom-call | bytes 225000000 | tf_op jit(solution)/shard_map/attend_back/pallas_call | solution.py:698
  363.0 0.0 copy-done.2
  363.0 0.0 copy-done.1
  363.1 0.1 reshape.179
  363.2 0.1 reshape.178
  363.2 0.7 select_maximum_fusion.3
  363.9 0.0 copy-done.3
  364.0 0.1 reshape_squeeze.11
  364.0 0.1 reshape_squeeze.12
  364.1 0.1 pad_maximum_fusion
  364.2 0.1 broadcast_select_fusion
  364.3 0.6 broadcast_in_dim.54.refs_15_
  364.9 56.5 %leave.1 = (f32[40,1280]{1,0:T(8,128)}, f32[40,1280]{1,0:T(8,128)}, f32[40,1280]{1,0:T(8,128)}, f32[2,64,1280]{2,1,0:T(8,128)}, f32[40,1280]{1,0:T(8,128)}, /*in...) custom-call(bf16[512,1280]{1,0:T(8,128)(2,1)} %bitcast.47, ...), custom_call_target="tpu_custom_call" | custom-call | bytes 180000000 | tf_op jit(solution)/shard_map/leave/pallas_call | solution.py:698
  421.4 0.0 copy-start.4
  421.4 4.3 %settle.1 = (bf16[2,64,1280]{2,1,0:T(8,128)(2,1)}, f32[2,64,1280]{2,1,0:T(8,128)}, f32[40,1280]{1,0:T(8,128)}, f32[40,1280]{1,0:T(8,128)}, f32[40,1280]{1,0:T(8,...) custom-call(bf16[2,64,1280]{2,1,0:T(8,128)(2,1)} %bitcast.68, ...), custom_call_target="tpu_custom_call" | custom-call | tf_op jit(solution)/shard_map/settle/pallas_call | solution.py:1656
  425.8 0.0 copy-done.4
  425.8 0.6 slice_bitcast_fusion
  426.4 0.6 fusion.8
  (22 shorter events, 0.2 us)
Async XLA Ops:
  51.4 3.9 copy-start
  276.6 86.5 %copy-start.2 = (f32[1,1280]{1,0:T(1,128)S(1)}, f32[1,1280]{1,0:T(1,128)}, u32[]{:S(2)}) copy-start(f32[1,1280]{1,0:T(1,128)} %get-tuple-element.110) | copy-start | bytes 15364
  276.6 86.5 %copy-start.1 = (f32[1,1280]{1,0:T(1,128)S(1)}, f32[1,1280]{1,0:T(1,128)}, u32[]{:S(2)}) copy-start(f32[1,1280]{1,0:T(1,128)} %get-tuple-element.111) | copy-start | bytes 15364
  276.6 87.4 %copy-start.3 = (f32[2,640]{1,0:T(2,128)S(1)}, f32[2,640]{1,0:T(2,128)}, u32[]{:S(2)}) copy-start(f32[2,640]{1,0:T(2,128)} %get-tuple-element.112) | copy-start | bytes 15364
  421.4 4.4 %copy-start.4 = (f32[1,640]{1,0:T(1,128)S(1)}, f32[1,640]{1,0:T(1,128)}, u32[]{:S(2)}) copy-start(f32[1,640]{1,0:T(1,128)} %get-tuple-element.131) | copy-start | bytes 7684

commit v7 on v6

--- a/solution.py
+++ b/solution.py
@@ -708,9 +708,9 @@
 
 
 def exit_kernel(
-    n_line, ready, x, dq, dkv, yy_ref, cc_ref, cos, sin, scale, wq, wk, wv, res, oc, dc, alpha, rest, gg,
+    n_line, ready, x, dq, dkv, yy_ref, cc_ref, cos, sin, scale, wq, wk, wv, res, oc, dc, a_sum, m_sum, ff_sum, gg,
     gq_o, gk_o, gv_o, gh_o, go_o, gd_o, sum_o, gg_o, oc_o, dc_o,
-    flat, acc, gq, gk, gv, gh, scale_s,
+    flat, acc, gq, gk, gv, gh, scale_s, alpha,
     alpha_in, line_out, line_all, oc_s, oc_r, dc_s, dc_r, al_s, al_r, su_s, su_r, keep, *scratch,
 ):
     y, c, z, s = place()
@@ -735,10 +735,18 @@
         if k < 3:
             cols.append(remote(oc.at[yy * 2 + cc], oc_o.at[u], oc_s.at[k], oc_r.at[k], target))
             small.append(remote(alpha.at[yy * 2 + cc], alpha_in.at[k], al_s.at[k], al_r.at[k], target))
+    for job, _ in gates:
+        job.step(n_line - 1)
+    for job in cols:
+        job.start()
+    each_rows = gq.shape[1]
+    for v in range(4):
+        for k in range(n_blk):
+            at = (v * n_blk + k) * each_rows
+            alpha[v, k, :, :each_rows] = a_sum[:, at : at + each_rows]
+            alpha[v, k, :, each_rows : 2 * each_rows] = m_sum[:, at : at + each_rows]
     for job in small:
         job.start()
-    for job, _ in gates:
-        job.step(n_line - 1)
     ready()
     rows_all = x[...]
     seqs, group_rows, wide = dq.shape
@@ -782,7 +790,6 @@
         return carry
 
     lax.fori_loop(0, heads, head, 0)
-    each_rows = gq.shape[1]
     for i, g in enumerate((gq, gk, gv)):
         for k in range(n_blk):
             g[k] = flat[i, k * each_rows : (k + 1) * each_rows]
@@ -799,11 +806,15 @@
     for job in mine:
         job.start()
     hid.middle()
-    for job in cols:
-        job.start()
     for job in small:
         job.wait_recv()
-    line_out[...] = rest[...]
+    line_out[...] = jnp.zeros_like(line_out)
+    ff_each = ff_sum.shape[1] // n_line
+    for k in range(n_line):
+        for j in (0, 1):
+            line_out[k * 2 + s, :, 256 + j * ff_each : 256 + (j + 1) * ff_each] = ff_sum[
+                j : j + 1, k * ff_each : (k + 1) * ff_each
+            ]
     line_out[:, :, :128] = alpha[u] + alpha_in[0] + alpha_in[1] + alpha_in[2]
     scales = jnp.concatenate(
         [scale_s[h][:, :HEAD_DIM] + scale_s[h][:, HEAD_DIM:] for h in range(heads)], axis=1
@@ -853,7 +864,7 @@
         job.wait_send()
 
 
-def leave(n_line, x, dq, dkv, y, c, cos, sin, scale, wq, wk, wv, res, oc, dc, alpha, rest, gg):
+def leave(n_line, x, dq, dkv, y, c, cos, sin, scale, wq, wk, wv, res, oc, dc, a_sum, m_sum, ff_sum, gg):
     n_blk = 2 * n_line
     heads, _, width = wq.shape
     seqs, rows, _ = res.shape
@@ -869,17 +880,18 @@
         pltpu.VMEM(grad.shape, BF), pltpu.VMEM(grad.shape, BF), pltpu.VMEM(grad.shape, BF),
         pltpu.VMEM(gh.shape, BF),
         pltpu.VMEM((heads, 1, 128), F32),
-        pltpu.VMEM((3,) + alpha.shape[1:], F32),
-        pltpu.VMEM(rest.shape, F32),
-        pltpu.VMEM((n_blk - 1,) + rest.shape[1:], F32),
+        pltpu.VMEM((4, n_blk, 1, 128), F32),
+        pltpu.VMEM((3, n_blk, 1, 128), F32),
+        pltpu.VMEM((n_blk, 1, 640), F32),
+        pltpu.VMEM((n_blk - 1, 1, 640), F32),
         dma((3,)), dma((3,)), dma((7,)), dma((7,)), dma((3,)), dma((3,)),
         dma((n_blk - 1,)), dma((n_blk - 1,)), dma((2,)),
     ]
     scratch += BlkReduce.scratch(n_line, grad) * 3
     scratch += UlyReduce.scratch(gh) + line_reduce_scratch(n_line, gg)
-    args = (x, dq, dkv, y, c, cos, sin, scale, wq, wk, wv, res, oc, dc, alpha, rest, gg)
+    args = (x, dq, dkv, y, c, cos, sin, scale, wq, wk, wv, res, oc, dc, a_sum, m_sum, ff_sum, gg)
     outs = [grad.shape[1:]] * 3 + [
-        res.shape, (oc.shape[1], 4 * oc.shape[2]), (dc.shape[1], 8 * dc.shape[2]), rest.shape[1:], gg.shape[1:]
+        res.shape, (oc.shape[1], 4 * oc.shape[2]), (dc.shape[1], 8 * dc.shape[2]), (1, 640), gg.shape[1:]
     ]
     return comm_call(
         functools.partial(exit_kernel, n_line), "leave", 8, args, [(shape, F32) for shape in outs], scratch,
@@ -1053,7 +1065,8 @@
 
 def attend_kernel(
     n_line, ready, x_ref, wq_ref, wk_ref, wv_ref, cos_ref, sin_ref, scale_ref, oc_ref, wg_ref, wu_ref, kp_ref,
-    q_ref, y_ref, c_ref, kv_o, oc_o, wg_o, wu_o, o_ref, mixed_ref, inv_ref, kv_ref, acc, total, place_q, *sems,
+    q_h, y_h, c_h, kv_h, oc_o, wg_o, wu_o, o_ref, mixed_ref, inv_ref,
+    kv_ref, acc, total, place_q, q_ref, y_ref, c_ref, kv_o, kept, *sems,
 ):
     y, c, z, s = place()
     blk_greet(n_line)
@@ -1102,6 +1115,17 @@
     jobs[-1].start()
     for job in gates:
         job.keep().start()
+    n_blk = 2 * n_line
+    keeps = [
+        pltpu.make_async_copy(a, o, kept.at[n_blk + i])
+        for i, (a, o) in enumerate(((q_ref, q_h), (y_ref, y_h), (c_ref, c_h)))
+    ]
+    for copy in keeps:
+        copy.start()
+
+    def keep_keys(block):
+        return pltpu.make_async_copy(kv_o.at[block], kv_h.at[block], kept.at[block])
+
     acc[...] = jnp.zeros_like(acc)
     total[...] = jnp.zeros_like(total)
     for i in range(seqs):
@@ -1127,23 +1151,29 @@
             for job in gates + [up]:
                 job.step(ahead)
 
+        @pl.when((stage == 0) & (k > 0) & (way == 0))
+        def _():
+            for job in jobs:
+                job.step(k)
+
+        for w, last in ((0, z), (1, n_line - 1 - z)):
+            @pl.when((stage == 0) & (k == last) & ((k == 0) | (way == 0)))
+            def _():
+                for job in gates:
+                    pl.when(job.goes(w))(lambda: job.own(w).start())
+
         there = (k == 0) | jnp.where(way == 0, z >= k, z + k < n_line)
 
         @pl.when(there)
         def _():
             for job in jobs:
                 for w in (0, 1):
-                    pl.when((stage == 0) & (k > 0) & (way == w))(lambda: job.take(w, k))
                     pl.when((stage == 1) & (k > 0) & (way == w))(lambda: job.over(w, k).wait_recv())
                 pl.when((stage == 1) & (k == 0))(lambda: job.own(2).wait_recv())
                 pl.when((stage == 0) & (k == 0))(lambda: job.keep().wait())
-            for w, last in ((0, z), (1, n_line - 1 - z)):
-                @pl.when((stage == 0) & (k == last) & ((k == 0) | (way == w)))
-                def _():
-                    for job in gates:
-                        pl.when(job.goes(w))(lambda: job.own(w).start())
             zz = jnp.where(way == 0, z - k, z + k)
             block = zz * 2 + jnp.where(stage == 0, s, 1 - s)
+            keep_keys(block).start()
 
             def one(i, carry):
                 attend_to(i, block, lambda lanes: kv_o[block, i, :, lanes])
@@ -1171,6 +1201,8 @@
         job.finish_sends()
     for job in gates + [up]:
         job.finish()
+    for copy in keeps + [keep_keys(block) for block in range(n_blk)]:
+        copy.wait()
 
 
 def attend(n_line, seqs, x, wq, wk, wv, cos, sin, scale, oc, wg, wu, k_places):
@@ -1187,9 +1219,13 @@
             ((n_line,) + wg.shape, BF), ((n_line, wu.shape[0], width - first), BF), (head, F32),
             ((seqs, rows, heads * HEAD_DIM), BF), ((seqs, heads, 8, rows), F32),
         ],
-        [pltpu.VMEM(wide, BF), pltpu.VMEM(head, F32), pltpu.VMEM(head, F32), pltpu.VMEM((seqs, rows, rows), F32)]
+        [
+            pltpu.VMEM(wide, BF), pltpu.VMEM(head, F32), pltpu.VMEM(head, F32), pltpu.VMEM((seqs, rows, rows), F32),
+            pltpu.VMEM(wide, BF), pltpu.VMEM(*flat), pltpu.VMEM(*flat), pltpu.VMEM((n_blk,) + wide, BF),
+            pltpu.SemaphoreType.DMA((n_blk + 3,)),
+        ]
         + BlkGather.sems(n_line) * (seqs + 1) + line_gather_sems(n_line) + LineGather.sems(n_line),
-        90, far_outs=(4, 5, 6), late=(0, 1, 2, 3, 4, 5),
+        90, far_outs=(0, 1, 2, 3, 4, 5, 6), late=(0, 1, 2, 3, 4, 5),
     )
 
 
@@ -1417,7 +1453,7 @@
         ],
         [pltpu.VMEM(part.shape, BF), pltpu.VMEM(hid.shape, BF)]
         + UlyReduce.scratch(part) + PlaneGather.sems(parts) + line_gather_sems(n_line),
-        25, far_outs=(5,), late=(0, 1, 2, 4),
+        25, far_outs=(4, 5), late=(0, 1, 2, 4),
     )
 
 
@@ -1515,7 +1551,7 @@
             pltpu.VMEM(wide, F32), pltpu.VMEM(wide, F32), pltpu.SemaphoreType.DMA((3,)),
         ]
         + PlaneReduce.scratch(part) + PlaneGather.sems(seqs),
-        35, far_outs=(4, 5, 6), late=(0, 1, 2, 3, 5),
+        35, far_outs=(3, 4, 5, 6), late=(0, 1, 2, 3, 5),
     )
 
 
@@ -1641,26 +1677,39 @@
         [pltpu.VMEM(part.shape, BF), pltpu.VMEM(first.shape, BF), pltpu.VMEM(down.shape, BF), thin, thin]
         + Late.scratch(late) + PlaneReduce.scratch(part) + UlyGather.sems(parts)
         + line_reduce_scratch(n_line, down),
-        40, VMEM_BYTES, tuple(range(9, 16)), late=(0, 1),
-    )
-
-
-def settle_kernel(*refs):
-    count = len(refs) // 2
-    for x, o in zip(refs[:count], refs[count:]):
-        o[...] = x[...]
+        40, VMEM_BYTES, tuple(range(9, 16)), far_outs=(3,), late=(0, 1),
+    )
+
+
+def settle_kernel(count, *refs):
+    ins, outs, bufs = refs[:count], refs[count : 2 * count], refs[2 * count : 3 * count]
+    come, go = refs[3 * count :]
+    into = [pltpu.make_async_copy(x, b, come.at[i]) for i, (x, b) in enumerate(zip(ins, bufs))]
+    out = [pltpu.make_async_copy(b, o, go.at[i]) for i, (b, o) in enumerate(zip(bufs, outs))]
+    for copy in into:
+        copy.start()
+    for a, b in zip(into, out):
+        a.wait()
+        b.start()
+    for copy in out:
+        copy.wait()
 
 
 def settle(*arrays):
-    vmem = pl.BlockSpec(memory_space=pltpu.VMEM)
+    count = len(arrays)
+    anyway = pl.BlockSpec(memory_space=pl.ANY)
     return pl.pallas_call(
-        settle_kernel,
+        functools.partial(settle_kernel, count),
         out_shape=[jax.ShapeDtypeStruct(a.shape, a.dtype) for a in arrays],
-        in_specs=[vmem] * len(arrays),
-        out_specs=[vmem] * len(arrays),
+        in_specs=[anyway] * count,
+        out_specs=[anyway] * count,
+        scratch_shapes=[pltpu.VMEM(a.shape, a.dtype) for a in arrays]
+        + [pltpu.SemaphoreType.DMA((count,))] * 2,
         compiler_params=pltpu.CompilerParams(vmem_limit_bytes=VMEM_BYTES),
         name="settle",
     )(*arrays)
+
+
 def local(
     hidden, positions, w_query, w_key, w_value, w_out, w_up, w_gate, w_down,
     qk_scale, alpha_attn, alpha_mlp, up_scale, gate_scale, cotangent,
@@ -1684,33 +1733,37 @@
 
     pieces = [v.astype(F32) for v in (qk_scale, alpha_attn, alpha_mlp, up_scale, gate_scale)]
     pieces.append(positions.reshape(-1).astype(F32))
-    used = sum(v.shape[0] for v in pieces)
-    room, at, small = used + -used % 1024, 0, 0.0
-    for v in pieces:
-        small = small + jnp.pad(v, (at, room - at - v.shape[0]))
-        at += v.shape[0]
-    small = small.reshape(-1, 128)
+    rows_of = [-(-v.shape[0] // 128) for v in pieces]
+    starts = [sum(rows_of[:i]) for i in range(len(pieces) + 1)]
+    tall = starts[-1] + -starts[-1] % 8
+    small = 0.0
+    for v, start in zip(pieces, starts):
+        small = small + jnp.pad(v, (start * 128, (tall - start) * 128 - v.shape[0]))
+    small = small.reshape(tall, 128)
 
     hid_all, small_all, wq_all, wk_all, wv_all, out_cols, down_cols, up_first = entry(
         n_line, hidden, small, w_query, w_key, w_value, w_out, w_down, w_up
     )
     up_first = up_first.reshape(ff_local, -1)
 
-    flat = small_all.reshape(4, n_blk, -1)
-    cut = [0, attn_each, 2 * attn_each, 3 * attn_each, 3 * attn_each + ff_each, 3 * attn_each + 2 * ff_each, used]
+    flat = small_all.reshape(4, n_blk, tall * 128)
+
+    def piece(rows, i):
+        return rows[..., starts[i] * 128 : starts[i] * 128 + pieces[i].shape[0]]
+
     own = lax.dynamic_slice_in_dim(flat, uly, 1, 0)[0]
-    scale_wide = own[:, : cut[1]].reshape(heads, HEAD_DIM)
-    attn_rate = flat[:, :, cut[1] : cut[2]].reshape(-1)
-    mlp_rate = flat[:, :, cut[2] : cut[3]].reshape(-1)
+    scale_wide = piece(own, 0).reshape(heads, HEAD_DIM)
+    attn_rate = piece(flat, 1).reshape(-1)
+    mlp_rate = piece(flat, 2).reshape(-1)
     mine = lax.dynamic_slice_in_dim(own.reshape(n_line, 2, -1), side, 1, 1)[:, 0]
-    up_wide = mine[:, cut[3] : cut[4]].reshape(-1)
-    gate_wide = mine[:, cut[4] : cut[5]].reshape(-1)
+    up_wide = piece(mine, 3).reshape(-1)
+    gate_wide = piece(mine, 4).reshape(-1)
     assert ff_local <= width
     rates = jnp.pad(
         jnp.stack([attn_rate, mlp_rate, row(up_wide, width), row(gate_wide, width)]), ((0, 4), (0, 0))
     )
     places = jnp.transpose(
-        flat[:, :, cut[5] : cut[6]].reshape(4, n_blk, seqs, rows_each), (2, 1, 0, 3)
+        piece(flat, 5).reshape(4, n_blk, seqs, rows_each), (2, 1, 0, 3)
     ).reshape(seqs, n_blk, 1, group_rows)
     q_places = lax.dynamic_slice_in_dim(places, line * 2 + side, 1, 1)[:, 0]
 
@@ -1749,7 +1802,6 @@
         n_line, seqs, branch_low, down_full, up_rows, gate_rows, rates, up_first, up_last, gate_full,
         mlp_in, inner, grad_first, first, unit_att, att_c, first_c, hidden_fine,
     )
-    grad_up_scale, grad_gate_scale = ff_scales[0], ff_scales[1]
     down_own = down_own.reshape(8, attn_each, ff_local)
 
     dq, dkv, out_own, up_own = attend_back(
@@ -1757,19 +1809,10 @@
         kv_all, places, grad_up,
     )
     out_own = out_own.reshape(4, attn_each, local_width)
-    alpha = jnp.concatenate(
-        [grad_alpha_attn.reshape(4, n_blk, attn_each), grad_alpha_mlp.reshape(4, n_blk, attn_each)], axis=2
-    )
-    ff_sums = jnp.concatenate(
-        [grad_up_scale.reshape(n_line, ff_each), grad_gate_scale.reshape(n_line, ff_each)], axis=1
-    )
-    sides = (jnp.arange(2) == side)[None, :, None]
-    ff_sums = jnp.where(sides, ff_sums[:, None], 0.0).reshape(n_blk, 2 * ff_each)
-    rest = jnp.concatenate([jnp.zeros((n_blk, 256), F32), row(ff_sums, 384)], axis=1)
     gq, gk, gv, grad_hidden, out_gradient, down_gradient, sums, gate_own = leave(
         n_line, group_hidden, dq, dkv, y_both, c_both, cos, sin, scale_both, wq, wk, wv,
         grad_residual.reshape(seqs, rows_each, width), out_own, down_own,
-        row(alpha, 128)[:, :, None], rest[:, None], grad_gate,
+        grad_alpha_attn, grad_alpha_mlp, ff_scales, grad_gate,
     )
     sums = sums[0]
     layer_out, grad_hidden, gq, gk, gv, out_gradient, up_own, gate_own, down_gradient = settle(

time: 429 us -> 419 us (0.977)
  Pallas kernels: 416 us -> 410 us
    pallas_call x6, Pallas kernels: 364 us -> 359 us  [comm_call(): pl.pallas_call(whole, out_shape=[jax.ShapeDtypeStruct(shape, dtype) for s...]
where the time goes in v7:
time: 419 us
  Pallas kernels  410 us (98%)
  other arithmetic  5.14 us (1%)
    pallas_call x6, Pallas kernels, comm_call(): pl.pallas_call(whole, out_shape=[jax.ShapeDtypeStruct(shape, dtype) for s...  359 us
    pallas_call x1, Pallas kernels, entry(): pl.pallas_call(functools.partial(entry_kernel, n_line), out_shape=[out((p...  47.2 us

profile of v7, /device:TPU:0, one launch (start us, length us, event | category | flops | bytes accessed | tf_op | source)
XLA Modules:
  0.0 418.9 jit_solution(6140765895082562863)
XLA Ops:
  0.7 0.7 convert_element_type.35
  1.3 0.1 convert_element_type.36
  1.4 1.3 add_bitcast_fusion.small
  2.8 47.2 %entry.1 = (bf16[2,4,64,1280]{3,2,1,0:T(8,128)(2,1)}, f32[4,8,8,128]{3,2,1,0:T(8,128)}, bf16[8,40,1280]{2,1,0:T(8,128)(2,1)}, bf16[8,40,1280]{2,1,0:T(8,128)(2,1...) custom-call(bf16[2,64,1280]{2,1,0:T(8,128)(2,1)} %hid.1, ...), custom_call_target="tpu_custom_call" | custom-call | bytes 120000000 | tf_op jit(solution)/shard_map/entry/pallas_call | solution.py:994
  49.9 0.9 reshape.144
  50.9 0.1 reshape.145
  51.0 0.1 reshape.146.refs_10_.refs_7_
  51.1 0.0 copy-start
  51.2 0.1 reshape.147
  51.2 0.7 pad_maximum_fusion.refs_6_.refs_7_
  51.9 0.1 stack_reshape.6
  52.1 0.1 reshape.150
  52.2 0.1 reshape.151
  52.3 0.1 stack_reshape.7
  52.4 0.6 select_maximum_fusion.refs_3_.refs_4_.refs_2_
  53.0 1.8 fusion
  54.8 0.0 copy-done
  54.8 99.4 %attend.1 = (bf16[2,256,640]{2,1,0:T(8,128)(2,1)}, f32[512,640]{1,0:T(8,128)}, f32[512,640]{1,0:T(8,128)}, bf16[8,2,256,640]{3,2,1,0:T(8,128)(2,1)}, bf16[4,8,40...) custom-call(bf16[512,1280]{1,0:T(8,128)(2,1)} %bitcast.45, ...), custom_call_target="tpu_custom_call" | custom-call | bytes 270000000 | tf_op jit(solution)/shard_map/attend/pallas_call | solution.py:698
  154.3 32.1 %attn_joint.1 = (f32[4,32,1280]{2,1,0:T(8,128)}, f32[4,32,1280]{2,1,0:T(8,128)}, f32[4,32,128]{2,1,0:T(8,128)}, f32[4,32,128]{2,1,0:T(8,128)}, bf16[8,4,32,1280]...) custom-call(bf16[2,256,320]{2,1,0:T(8,128)(2,1)} %get-tuple-element.79.refs_0_.refs_3_, bf16[1280,320]{1,0:T(8,128)(2,1)} %bitcast.47, ...), custom_call_target="tpu_custom_call" | custom-call | bytes 75000000 | tf_op jit(solution)/shard_map/attn_joint/pallas_call | solution.py:698
  186.4 39.5 %ff_joint.1 = (bf16[4,32,1280]{2,1,0:T(8,128)(2,1)}, f32[4,32,1280]{2,1,0:T(8,128)}, f32[1,1280]{1,0:T(1,128)}, bf16[8,4,32,1280]{3,2,1,0:T(8,128)(2,1)}, bf16[2...) custom-call(bf16[2,2,2,128,1280]{4,3,2,1,0:T(8,128)(2,1)} %bitcast.39, ...), custom_call_target="tpu_custom_call" | custom-call | bytes 105000000 | tf_op jit(solution)/shard_map/ff_joint/pallas_call | solution.py:698
  225.8 46.5 %back_joint.1 = (f32[4,32,1280]{2,1,0:T(8,128)}, f32[1,1280]{1,0:T(1,128)}, f32[2,640]{1,0:T(2,128)}, bf16[2,4,64,1280]{3,2,1,0:T(8,128)(2,1)}, bf16[4,160,1280]...) custom-call(bf16[2,2,2,128,1280]{4,3,2,1,0:T(8,128)(2,1)} %bitcast.61, ...), custom_call_target="tpu_custom_call" | custom-call | bytes 120000000 | tf_op jit(solution)/shard_map/back_joint/pallas_call | solution.py:698
  272.3 85.6 %attend_back.1 = (bf16[2,256,640]{2,1,0:T(8,128)(2,1)}, bf16[2,256,640]{2,1,0:T(8,128)(2,1)}, bf16[160,320]{1,0:T(8,128)(2,1)}, f32[160,1280]{1,0:T(8,128)}) custom-call(bf16[2,256,640]{2,1,0:T(8,128)(2,1)} %get-tuple-element.89.refs_0_, bf16[2,256,1280]{2,1,0:T(8,128)(2,1)} %bitcast.62, bf16[1280,320]{1,0:T(8,128)(2,1)} %bitcast.48, ...), custom_call_target="tpu_custom_call" | custom-call | bytes 225000000 | tf_op jit(solution)/shard_map/attend_back/pallas_call | solution.py:698
  357.9 55.9 %leave.1 = (f32[40,1280]{1,0:T(8,128)}, f32[40,1280]{1,0:T(8,128)}, f32[40,1280]{1,0:T(8,128)}, f32[2,64,1280]{2,1,0:T(8,128)}, f32[40,1280]{1,0:T(8,128)}, /*in...) custom-call(bf16[512,1280]{1,0:T(8,128)(2,1)} %bitcast.46, ...), custom_call_target="tpu_custom_call" | custom-call | bytes 180000000 | tf_op jit(solution)/shard_map/leave/pallas_call | solution.py:698
  413.8 0.0 copy-start.1
  413.8 3.8 settle.1
  417.7 0.0 copy-done.1
  417.7 0.6 slice_bitcast_fusion
  418.2 0.6 fusion.8
  (17 shorter events, 0.1 us)
Async XLA Ops:
  51.1 3.7 copy-start
  413.8 3.9 copy-start.1

commit v8 on v7

--- a/solution.py
+++ b/solution.py
@@ -1,4 +1,5 @@
 import functools
+import math
 
 import jax
 import jax.numpy as jnp
@@ -899,9 +900,47 @@
     )
 
 
+def tables(n_line, starts, sizes, small, places, cos, sin, scale, rates):
+    y, c, z, s = place()
+    u, b, n_blk = y * 2 + c, z * 2 + s, 2 * n_line
+    seqs, rows_each = places.shape[0], places.shape[-1] // 4
+    for v in range(4):
+        for k in range(n_blk):
+            row = small[v, k, starts[5] : starts[5] + 1]
+            for i in range(seqs):
+                places[i, k, :, v * rows_each : (v + 1) * rows_each] = row[:, i * rows_each : (i + 1) * rows_each]
+    lane = lanes_of((1, 128)) % HEAD_DIM
+    freqs = jnp.exp((lane % 32).astype(F32) * (-math.log(rotary_base) * 2.0 / HEAD_DIM))
+    turns = jnp.where(lane < 32, -1.0, 1.0)
+    for i in range(seqs):
+        spot = places[i, b]
+        group = spot.shape[1]
+        angles = jnp.transpose(jnp.broadcast_to(spot, (128, group))) * freqs
+        cos[i * group : (i + 1) * group] = jnp.cos(angles)
+        sin[i * group : (i + 1) * group] = jnp.sin(angles) * turns
+    each = sizes[0]
+    flat = jnp.concatenate([small[u, k, 0:1, :each] for k in range(n_blk)], axis=1)
+    scale[...] = jnp.zeros_like(scale)
+    for h in range(flat.shape[1] // HEAD_DIM):
+        piece = flat[:, h * HEAD_DIM : (h + 1) * HEAD_DIM]
+        scale[h : h + 1] = jnp.concatenate([piece * HEAD_DIM**0.5, piece], axis=1)
+    rates[...] = jnp.zeros_like(rates)
+    for j in (1, 2):
+        for v in range(4):
+            for k in range(n_blk):
+                at = (v * n_blk + k) * each
+                rates[j - 1 : j, at : at + each] = small[v, k, starts[j] : starts[j] + 1, :each]
+    for j in (3, 4):
+        for k in range(n_line):
+            for r in range(starts[j + 1] - starts[j]):
+                wide = min(128, sizes[j] - 128 * r)
+                at = k * sizes[j] + 128 * r
+                rates[j - 1 : j, at : at + wide] = small[u, k * 2 + s, starts[j] + r : starts[j] + r + 1, :wide]
+
+
 def entry_kernel(
-    n_line, hid, small, wq, wk, wv, wo, wd, wu,
-    hid_o, small_o, wq_o, wk_o, wv_o, oc_o, dc_o, wu_o, oc, dc, *sems
+    n_line, starts, sizes, hid, small, wq, wk, wv, wo, wd, wu,
+    hid_o, places_o, cos_o, sin_o, scale_o, rates_o, wq_o, wk_o, wv_o, oc_o, dc_o, wu_o, small_o, oc, dc, *sems
 ):
     y, c, z, s = place()
     u, p = y * 2 + c, plane_index(y, c, s)
@@ -968,12 +1007,17 @@
     for k in range(1, n_line):
         for job in up_jobs:
             job.step(k)
+    for job in small_jobs:
+        job.wait_recv()
+    tables(n_line, starts, sizes, small_o, places_o, cos_o, sin_o, scale_o, rates_o)
     for job in jobs[1:]:
         job.finish_arrivals()
     hid_job.finish()
     for job in up_jobs:
         job.finish()
-    for job in small_jobs + col_jobs:
+    for job in small_jobs:
+        job.wait_send()
+    for job in col_jobs:
         job.wait()
     for job in mine:
         job.wait()
@@ -981,7 +1025,7 @@
         job.finish_sends()
 
 
-def entry(n_line, hid, small, wq, wk, wv, wo, wd, wu):
+def entry(n_line, starts, sizes, hid, small, wq, wk, wv, wo, wd, wu):
     n_blk = 2 * n_line
     oc = jax.ShapeDtypeStruct((4, wo.shape[0], wo.shape[1] // 4), wo.dtype)
     dc = jax.ShapeDtypeStruct((8, wd.shape[0], wd.shape[1] // 8), wd.dtype)
@@ -992,10 +1036,14 @@
         return jax.ShapeDtypeStruct(shape, like.dtype)
 
     return pl.pallas_call(
-        functools.partial(entry_kernel, n_line),
+        functools.partial(entry_kernel, n_line, starts, sizes),
         out_shape=[
             out((parts, 4) + hid.shape[1:], hid),
-            out((4, n_blk) + small.shape, small),
+            out((parts, n_blk, 1, 4 * hid.shape[1]), small),
+            out((parts * 4 * hid.shape[1], 128), small),
+            out((parts * 4 * hid.shape[1], 128), small),
+            out((8, 128), small),
+            out((8, hid.shape[2]), small),
             out((n_blk,) + wq.shape, wq),
             out((n_blk,) + wk.shape, wk),
             out((n_blk,) + wv.shape, wv),
@@ -1004,8 +1052,12 @@
             out((n_line, wu.shape[0], lane_chunks(wu.shape[1])[0].stop), wu),
         ],
         in_specs=[vmem] * 8,
-        out_specs=[vmem, vmem, anyway, anyway, anyway, vmem, vmem, anyway],
-        scratch_shapes=[pltpu.VMEM(oc.shape, oc.dtype), pltpu.VMEM(dc.shape, dc.dtype)]
+        out_specs=[vmem] * 6 + [anyway, anyway, anyway, vmem, vmem, anyway],
+        scratch_shapes=[
+            pltpu.VMEM((4, n_blk) + small.shape, small.dtype),
+            pltpu.VMEM(oc.shape, oc.dtype),
+            pltpu.VMEM(dc.shape, dc.dtype),
+        ]
         + UlyGather.sems(parts)
         + BlkGather.sems(n_line) * 4
         + LineGather.sems(n_line)
@@ -1741,38 +1793,14 @@
         small = small + jnp.pad(v, (start * 128, (tall - start) * 128 - v.shape[0]))
     small = small.reshape(tall, 128)
 
-    hid_all, small_all, wq_all, wk_all, wv_all, out_cols, down_cols, up_first = entry(
-        n_line, hidden, small, w_query, w_key, w_value, w_out, w_down, w_up
+    sizes = tuple(v.shape[0] for v in pieces)
+    assert ff_local <= width and tokens <= 128 and attn_each <= 64
+    (
+        hid_all, places, cos, sin, scale_both, rates, wq_all, wk_all, wv_all, out_cols, down_cols, up_first
+    ) = entry(
+        n_line, tuple(starts), sizes, hidden, small, w_query, w_key, w_value, w_out, w_down, w_up
     )
     up_first = up_first.reshape(ff_local, -1)
-
-    flat = small_all.reshape(4, n_blk, tall * 128)
-
-    def piece(rows, i):
-        return rows[..., starts[i] * 128 : starts[i] * 128 + pieces[i].shape[0]]
-
-    own = lax.dynamic_slice_in_dim(flat, uly, 1, 0)[0]
-    scale_wide = piece(own, 0).reshape(heads, HEAD_DIM)
-    attn_rate = piece(flat, 1).reshape(-1)
-    mlp_rate = piece(flat, 2).reshape(-1)
-    mine = lax.dynamic_slice_in_dim(own.reshape(n_line, 2, -1), side, 1, 1)[:, 0]
-    up_wide = piece(mine, 3).reshape(-1)
-    gate_wide = piece(mine, 4).reshape(-1)
-    assert ff_local <= width
-    rates = jnp.pad(
-        jnp.stack([attn_rate, mlp_rate, row(up_wide, width), row(gate_wide, width)]), ((0, 4), (0, 0))
-    )
-    places = jnp.transpose(
-        piece(flat, 5).reshape(4, n_blk, seqs, rows_each), (2, 1, 0, 3)
-    ).reshape(seqs, n_blk, 1, group_rows)
-    q_places = lax.dynamic_slice_in_dim(places, line * 2 + side, 1, 1)[:, 0]
-
-    lane = jnp.arange(128) % HEAD_DIM
-    freqs = rotary_base ** (-((lane % 32).astype(F32) * (2.0 / HEAD_DIM)))
-    angles = q_places.reshape(group_tokens, 1) * freqs
-    cos = jnp.cos(angles)
-    sin = jnp.where(lane < 32, -1.0, 1.0) * jnp.sin(angles)
-    scale_both = jnp.concatenate([scale_wide * HEAD_DIM**0.5, scale_wide], axis=1)
 
     group_hidden = hid_all.reshape(group_tokens, width)
     wq = wq_all.reshape(heads, HEAD_DIM, width)

time: 419 us -> 416 us (level)
  no operation moved by 1% of the time
where the time goes in v8:
time: 416 us; the launch traced here: 415 us
  Pallas kernels  411 us (99%)
    pallas_call x6, Pallas kernels, comm_call(): pl.pallas_call(whole, out_shape=[jax.ShapeDtypeStruct(shape, dtype) for s...  359 us
    pallas_call x1, Pallas kernels, entry(): pl.pallas_call(functools.partial(entry_kernel, n_line, starts, sizes), ou...  48.5 us

profile of v8, /device:TPU:0, one launch (start us, length us, event | category | flops | bytes accessed | tf_op | source)
XLA Modules:
  0.0 415.3 jit_solution(8987136384500855483)
XLA Ops:
  0.6 0.7 convert_element_type.16
  1.3 0.1 convert_element_type.24
  1.4 1.3 add_bitcast_fusion.small
  2.7 48.5 %entry.1 = (bf16[2,4,64,1280]{3,2,1,0:T(8,128)(2,1)}, f32[2,8,1,256]{3,2,1,0:T(1,128)}, f32[512,128]{1,0:T(8,128)}, f32[512,128]{1,0:T(8,128)}, f32[8,128]{1,0:T...) custom-call(bf16[2,64,1280]{2,1,0:T(8,128)(2,1)} %hid.1, ...), custom_call_target="tpu_custom_call" | custom-call | bytes 120000000 | tf_op jit(solution)/shard_map/entry/pallas_call | solution.py:1038
  51.3 99.5 %attend.1 = (bf16[2,256,640]{2,1,0:T(8,128)(2,1)}, f32[512,640]{1,0:T(8,128)}, f32[512,640]{1,0:T(8,128)}, bf16[8,2,256,640]{3,2,1,0:T(8,128)(2,1)}, bf16[4,8,40...) custom-call(bf16[512,1280]{1,0:T(8,128)(2,1)} %bitcast.36, ...), custom_call_target="tpu_custom_call" | custom-call | bytes 270000000 | tf_op jit(solution)/shard_map/attend/pallas_call | solution.py:699
  150.7 31.9 %attn_joint.1 = (f32[4,32,1280]{2,1,0:T(8,128)}, f32[4,32,1280]{2,1,0:T(8,128)}, f32[4,32,128]{2,1,0:T(8,128)}, f32[4,32,128]{2,1,0:T(8,128)}, bf16[8,4,32,1280]...) custom-call(bf16[2,256,320]{2,1,0:T(8,128)(2,1)} %get-tuple-element.86.refs_0_.refs_3_, bf16[1280,320]{1,0:T(8,128)(2,1)} %bitcast.38, ...), custom_call_target="tpu_custom_call" | custom-call | bytes 75000000 | tf_op jit(solution)/shard_map/attn_joint/pallas_call | solution.py:699
  182.6 39.6 %ff_joint.1 = (bf16[4,32,1280]{2,1,0:T(8,128)(2,1)}, f32[4,32,1280]{2,1,0:T(8,128)}, f32[1,1280]{1,0:T(1,128)}, bf16[8,4,32,1280]{3,2,1,0:T(8,128)(2,1)}, bf16[2...) custom-call(bf16[2,2,2,128,1280]{4,3,2,1,0:T(8,128)(2,1)} %bitcast.30, ...), custom_call_target="tpu_custom_call" | custom-call | bytes 105000000 | tf_op jit(solution)/shard_map/ff_joint/pallas_call | solution.py:699
  222.3 46.4 %back_joint.1 = (f32[4,32,1280]{2,1,0:T(8,128)}, f32[1,1280]{1,0:T(1,128)}, f32[2,640]{1,0:T(2,128)}, bf16[2,4,64,1280]{3,2,1,0:T(8,128)(2,1)}, bf16[4,160,1280]...) custom-call(bf16[2,2,2,128,1280]{4,3,2,1,0:T(8,128)(2,1)} %bitcast.52, ...), custom_call_target="tpu_custom_call" | custom-call | bytes 120000000 | tf_op jit(solution)/shard_map/back_joint/pallas_call | solution.py:699
  268.7 85.6 %attend_back.1 = (bf16[2,256,640]{2,1,0:T(8,128)(2,1)}, bf16[2,256,640]{2,1,0:T(8,128)(2,1)}, bf16[160,320]{1,0:T(8,128)(2,1)}, f32[160,1280]{1,0:T(8,128)}) custom-call(bf16[2,256,640]{2,1,0:T(8,128)(2,1)} %get-tuple-element.97.refs_0_, bf16[2,256,1280]{2,1,0:T(8,128)(2,1)} %bitcast.53, bf16[1280,320]{1,0:T(8,128)(2,1)} %bitcast.39, ...), custom_call_target="tpu_custom_call" | custom-call | bytes 225000000 | tf_op jit(solution)/shard_map/attend_back/pallas_call | solution.py:699
  354.4 55.9 %leave.1 = (f32[40,1280]{1,0:T(8,128)}, f32[40,1280]{1,0:T(8,128)}, f32[40,1280]{1,0:T(8,128)}, f32[2,64,1280]{2,1,0:T(8,128)}, f32[40,1280]{1,0:T(8,128)}, /*in...) custom-call(bf16[512,1280]{1,0:T(8,128)(2,1)} %bitcast.37, ...), custom_call_target="tpu_custom_call" | custom-call | bytes 180000000 | tf_op jit(solution)/shard_map/leave/pallas_call | solution.py:699
  410.2 0.0 copy-start
  410.2 3.8 settle.1
  414.1 0.0 copy-done
  414.1 0.6 slice_bitcast_fusion
  414.7 0.6 fusion
Async XLA Ops:
  410.2 3.9 copy-start

commit v9 on v8

--- a/solution.py
+++ b/solution.py
@@ -1007,9 +1007,10 @@
     for k in range(1, n_line):
         for job in up_jobs:
             job.step(k)
-    for job in small_jobs:
-        job.wait_recv()
-    tables(n_line, starts, sizes, small_o, places_o, cos_o, sin_o, scale_o, rates_o)
+        if k == 1:
+            for job in small_jobs:
+                job.wait_recv()
+            tables(n_line, starts, sizes, small_o, places_o, cos_o, sin_o, scale_o, rates_o)
     for job in jobs[1:]:
         job.finish_arrivals()
     hid_job.finish()
@@ -1733,13 +1734,16 @@
     )
 
 
-def settle_kernel(count, *refs):
-    ins, outs, bufs = refs[:count], refs[count : 2 * count], refs[2 * count : 3 * count]
-    come, go = refs[3 * count :]
+def settle_kernel(count, cuts, *refs):
+    ins, sums = refs[:count], refs[count]
+    outs, pieces = refs[count + 1 : 2 * count + 1], refs[2 * count + 1 : 2 * count + 1 + len(cuts)]
+    *bufs, come, go = refs[2 * count + 1 + len(cuts) :]
     into = [pltpu.make_async_copy(x, b, come.at[i]) for i, (x, b) in enumerate(zip(ins, bufs))]
     out = [pltpu.make_async_copy(b, o, go.at[i]) for i, (b, o) in enumerate(zip(bufs, outs))]
     for copy in into:
         copy.start()
+    for piece, (at, wide) in zip(pieces, cuts):
+        piece[...] = sums[:, at : at + wide]
     for a, b in zip(into, out):
         a.wait()
         b.start()
@@ -1747,19 +1751,20 @@
         copy.wait()
 
 
-def settle(*arrays):
+def settle(sums, cuts, *arrays):
     count = len(arrays)
-    anyway = pl.BlockSpec(memory_space=pl.ANY)
+    anyway, vmem = pl.BlockSpec(memory_space=pl.ANY), pl.BlockSpec(memory_space=pltpu.VMEM)
     return pl.pallas_call(
-        functools.partial(settle_kernel, count),
-        out_shape=[jax.ShapeDtypeStruct(a.shape, a.dtype) for a in arrays],
-        in_specs=[anyway] * count,
-        out_specs=[anyway] * count,
+        functools.partial(settle_kernel, count, cuts),
+        out_shape=[jax.ShapeDtypeStruct(a.shape, a.dtype) for a in arrays]
+        + [jax.ShapeDtypeStruct((1, wide), F32) for _, wide in cuts],
+        in_specs=[anyway] * count + [vmem],
+        out_specs=[anyway] * count + [vmem] * len(cuts),
         scratch_shapes=[pltpu.VMEM(a.shape, a.dtype) for a in arrays]
         + [pltpu.SemaphoreType.DMA((count,))] * 2,
         compiler_params=pltpu.CompilerParams(vmem_limit_bytes=VMEM_BYTES),
         name="settle",
-    )(*arrays)
+    )(*arrays, sums)
 
 
 def local(
@@ -1842,27 +1847,15 @@
         grad_residual.reshape(seqs, rows_each, width), out_own, down_own,
         grad_alpha_attn, grad_alpha_mlp, ff_scales, grad_gate,
     )
-    sums = sums[0]
-    layer_out, grad_hidden, gq, gk, gv, out_gradient, up_own, gate_own, down_gradient = settle(
+    cuts = (
+        (128, attn_each), (0, attn_each), (attn_each, attn_each), (256, ff_each), (256 + ff_each, ff_each)
+    )
+    settled = settle(
+        sums, cuts,
         layer_out.reshape(hidden.shape), grad_hidden, gq, gk, gv, out_gradient, up_own, gate_own,
         down_gradient,
     )
-    return (
-        layer_out,
-        grad_hidden,
-        gq,
-        gk,
-        gv,
-        out_gradient,
-        up_own,
-        gate_own,
-        down_gradient,
-        sums[128 : 128 + attn_each],
-        sums[:attn_each],
-        sums[attn_each : 2 * attn_each],
-        sums[256 : 256 + ff_each],
-        sums[256 + ff_each : 256 + 2 * ff_each],
-    )
+    return tuple(settled[:9]) + tuple(piece.reshape(-1) for piece in settled[9:])
 
 
 def solution(mesh):

time: 416 us -> 414 us (level)
  no operation moved by 1% of the time
where the time goes in v9:
time: 414 us
  Pallas kernels  411 us (99%)
    pallas_call x6, Pallas kernels, comm_call(): pl.pallas_call(whole, out_shape=[jax.ShapeDtypeStruct(shape, dtype) for s...  358 us
    pallas_call x1, Pallas kernels, entry(): pl.pallas_call(functools.partial(entry_kernel, n_line, starts, sizes), ou...  47.8 us

profile of v9, /device:TPU:0, one launch (start us, length us, event | category | flops | bytes accessed | tf_op | source)
XLA Modules:
  0.0 413.9 jit_solution(15666648265883108395)
XLA Ops:
  0.6 0.7 convert_element_type.16
  1.3 0.1 convert_element_type.24
  1.4 1.3 add_bitcast_fusion.small
  2.7 47.8 %entry.1 = (bf16[2,4,64,1280]{3,2,1,0:T(8,128)(2,1)}, f32[2,8,1,256]{3,2,1,0:T(1,128)}, f32[512,128]{1,0:T(8,128)}, f32[512,128]{1,0:T(8,128)}, f32[8,128]{1,0:T...) custom-call(bf16[2,64,1280]{2,1,0:T(8,128)(2,1)} %hid.1, ...), custom_call_target="tpu_custom_call" | custom-call | bytes 120000000 | tf_op jit(solution)/shard_map/entry/pallas_call | solution.py:1039
  50.6 99.5 %attend.1 = (bf16[2,256,640]{2,1,0:T(8,128)(2,1)}, f32[512,640]{1,0:T(8,128)}, f32[512,640]{1,0:T(8,128)}, bf16[8,2,256,640]{3,2,1,0:T(8,128)(2,1)}, bf16[4,8,40...) custom-call(bf16[512,1280]{1,0:T(8,128)(2,1)} %bitcast.33, ...), custom_call_target="tpu_custom_call" | custom-call | bytes 270000000 | tf_op jit(solution)/shard_map/attend/pallas_call | solution.py:699
  150.0 32.3 %attn_joint.1 = (f32[4,32,1280]{2,1,0:T(8,128)}, f32[4,32,1280]{2,1,0:T(8,128)}, f32[4,32,128]{2,1,0:T(8,128)}, f32[4,32,128]{2,1,0:T(8,128)}, bf16[8,4,32,1280]...) custom-call(bf16[2,256,320]{2,1,0:T(8,128)(2,1)} %get-tuple-element.91.refs_0_.refs_3_, bf16[1280,320]{1,0:T(8,128)(2,1)} %bitcast.35, ...), custom_call_target="tpu_custom_call" | custom-call | bytes 75000000 | tf_op jit(solution)/shard_map/attn_joint/pallas_call | solution.py:699
  182.4 38.9 %ff_joint.1 = (bf16[4,32,1280]{2,1,0:T(8,128)(2,1)}, f32[4,32,1280]{2,1,0:T(8,128)}, f32[1,1280]{1,0:T(1,128)}, bf16[8,4,32,1280]{3,2,1,0:T(8,128)(2,1)}, bf16[2...) custom-call(bf16[2,2,2,128,1280]{4,3,2,1,0:T(8,128)(2,1)} %bitcast.27, ...), custom_call_target="tpu_custom_call" | custom-call | bytes 105000000 | tf_op jit(solution)/shard_map/ff_joint/pallas_call | solution.py:699
  221.3 46.2 %back_joint.1 = (f32[4,32,1280]{2,1,0:T(8,128)}, f32[1,1280]{1,0:T(1,128)}, f32[2,640]{1,0:T(2,128)}, bf16[2,4,64,1280]{3,2,1,0:T(8,128)(2,1)}, bf16[4,160,1280]...) custom-call(bf16[2,2,2,128,1280]{4,3,2,1,0:T(8,128)(2,1)} %bitcast.49, ...), custom_call_target="tpu_custom_call" | custom-call | bytes 120000000 | tf_op jit(solution)/shard_map/back_joint/pallas_call | solution.py:699
  267.5 85.9 %attend_back.1 = (bf16[2,256,640]{2,1,0:T(8,128)(2,1)}, bf16[2,256,640]{2,1,0:T(8,128)(2,1)}, bf16[160,320]{1,0:T(8,128)(2,1)}, f32[160,1280]{1,0:T(8,128)}) custom-call(bf16[2,256,640]{2,1,0:T(8,128)(2,1)} %get-tuple-element.102.refs_0_, bf16[2,256,1280]{2,1,0:T(8,128)(2,1)} %bitcast.50, bf16[1280,320]{1,0:T(8,128)(2,1)} %bitcast.36, ...), custom_call_target="tpu_custom_call" | custom-call | bytes 225000000 | tf_op jit(solution)/shard_map/attend_back/pallas_call | solution.py:699
  353.4 55.3 %leave.1 = (f32[40,1280]{1,0:T(8,128)}, f32[40,1280]{1,0:T(8,128)}, f32[40,1280]{1,0:T(8,128)}, f32[2,64,1280]{2,1,0:T(8,128)}, f32[40,1280]{1,0:T(8,128)}, /*in...) custom-call(bf16[512,1280]{1,0:T(8,128)(2,1)} %bitcast.34, ...), custom_call_target="tpu_custom_call" | custom-call | bytes 180000000 | tf_op jit(solution)/shard_map/leave/pallas_call | solution.py:699
  408.7 5.1 %settle.1 = (bf16[2,64,1280]{2,1,0:T(8,128)(2,1)}, f32[2,64,1280]{2,1,0:T(8,128)}, f32[40,1280]{1,0:T(8,128)}, f32[40,1280]{1,0:T(8,128)}, f32[40,1280]{1,0:T(8,...) custom-call(bf16[2,64,1280]{2,1,0:T(8,128)(2,1)} %bitcast.55, ...), custom_call_target="tpu_custom_call" | custom-call | tf_op jit(solution)/shard_map/settle/pallas_call | solution.py:1757

commit v10 on v9

--- a/solution.py
+++ b/solution.py
@@ -1228,11 +1228,8 @@
             block = zz * 2 + jnp.where(stage == 0, s, 1 - s)
             keep_keys(block).start()
 
-            def one(i, carry):
+            for i in range(seqs):
                 attend_to(i, block, lambda lanes: kv_o[block, i, :, lanes])
-                return carry
-
-            lax.fori_loop(0, seqs, one, 0)
 
     arrivals(n_line, body)
     low = lanes_of((rows, 128)) < HEAD_DIM

time: 414 us -> 414 us (level)
  no operation moved by 1% of the time
where the time goes in v10:
time: 414 us
  Pallas kernels  411 us (99%)
    pallas_call x6, Pallas kernels, comm_call(): pl.pallas_call(whole, out_shape=[jax.ShapeDtypeStruct(shape, dtype) for s...  358 us
    pallas_call x1, Pallas kernels, entry(): pl.pallas_call(functools.partial(entry_kernel, n_line, starts, sizes), ou...  47.8 us

profile of v10, /device:TPU:0, one launch (start us, length us, event | category | flops | bytes accessed | tf_op | source)
XLA Modules:
  0.0 413.5 jit_solution(1973250364110836757)
XLA Ops:
  0.6 0.7 convert_element_type.16
  1.3 0.1 convert_element_type.24
  1.4 1.3 add_bitcast_fusion.small
  2.7 47.8 %entry.1 = (bf16[2,4,64,1280]{3,2,1,0:T(8,128)(2,1)}, f32[2,8,1,256]{3,2,1,0:T(1,128)}, f32[512,128]{1,0:T(8,128)}, f32[512,128]{1,0:T(8,128)}, f32[8,128]{1,0:T...) custom-call(bf16[2,64,1280]{2,1,0:T(8,128)(2,1)} %hid.1, ...), custom_call_target="tpu_custom_call" | custom-call | bytes 120000000 | tf_op jit(solution)/shard_map/entry/pallas_call | solution.py:1039
  50.6 98.7 %attend.1 = (bf16[2,256,640]{2,1,0:T(8,128)(2,1)}, f32[512,640]{1,0:T(8,128)}, f32[512,640]{1,0:T(8,128)}, bf16[8,2,256,640]{3,2,1,0:T(8,128)(2,1)}, bf16[4,8,40...) custom-call(bf16[512,1280]{1,0:T(8,128)(2,1)} %bitcast.33, ...), custom_call_target="tpu_custom_call" | custom-call | bytes 270000000 | tf_op jit(solution)/shard_map/attend/pallas_call | solution.py:699
  149.2 32.5 %attn_joint.1 = (f32[4,32,1280]{2,1,0:T(8,128)}, f32[4,32,1280]{2,1,0:T(8,128)}, f32[4,32,128]{2,1,0:T(8,128)}, f32[4,32,128]{2,1,0:T(8,128)}, bf16[8,4,32,1280]...) custom-call(bf16[2,256,320]{2,1,0:T(8,128)(2,1)} %get-tuple-element.91.refs_0_.refs_3_, bf16[1280,320]{1,0:T(8,128)(2,1)} %bitcast.35, ...), custom_call_target="tpu_custom_call" | custom-call | bytes 75000000 | tf_op jit(solution)/shard_map/attn_joint/pallas_call | solution.py:699
  181.7 38.8 %ff_joint.1 = (bf16[4,32,1280]{2,1,0:T(8,128)(2,1)}, f32[4,32,1280]{2,1,0:T(8,128)}, f32[1,1280]{1,0:T(1,128)}, bf16[8,4,32,1280]{3,2,1,0:T(8,128)(2,1)}, bf16[2...) custom-call(bf16[2,2,2,128,1280]{4,3,2,1,0:T(8,128)(2,1)} %bitcast.27, ...), custom_call_target="tpu_custom_call" | custom-call | bytes 105000000 | tf_op jit(solution)/shard_map/ff_joint/pallas_call | solution.py:699
  220.5 46.1 %back_joint.1 = (f32[4,32,1280]{2,1,0:T(8,128)}, f32[1,1280]{1,0:T(1,128)}, f32[2,640]{1,0:T(2,128)}, bf16[2,4,64,1280]{3,2,1,0:T(8,128)(2,1)}, bf16[4,160,1280]...) custom-call(bf16[2,2,2,128,1280]{4,3,2,1,0:T(8,128)(2,1)} %bitcast.49, ...), custom_call_target="tpu_custom_call" | custom-call | bytes 120000000 | tf_op jit(solution)/shard_map/back_joint/pallas_call | solution.py:699
  266.7 86.0 %attend_back.1 = (bf16[2,256,640]{2,1,0:T(8,128)(2,1)}, bf16[2,256,640]{2,1,0:T(8,128)(2,1)}, bf16[160,320]{1,0:T(8,128)(2,1)}, f32[160,1280]{1,0:T(8,128)}) custom-call(bf16[2,256,640]{2,1,0:T(8,128)(2,1)} %get-tuple-element.102.refs_0_, bf16[2,256,1280]{2,1,0:T(8,128)(2,1)} %bitcast.50, bf16[1280,320]{1,0:T(8,128)(2,1)} %bitcast.36, ...), custom_call_target="tpu_custom_call" | custom-call | bytes 225000000 | tf_op jit(solution)/shard_map/attend_back/pallas_call | solution.py:699
  352.7 55.6 %leave.1 = (f32[40,1280]{1,0:T(8,128)}, f32[40,1280]{1,0:T(8,128)}, f32[40,1280]{1,0:T(8,128)}, f32[2,64,1280]{2,1,0:T(8,128)}, f32[40,1280]{1,0:T(8,128)}, /*in...) custom-call(bf16[512,1280]{1,0:T(8,128)(2,1)} %bitcast.34, ...), custom_call_target="tpu_custom_call" | custom-call | bytes 180000000 | tf_op jit(solution)/shard_map/leave/pallas_call | solution.py:699
  408.3 5.1 %settle.1 = (bf16[2,64,1280]{2,1,0:T(8,128)(2,1)}, f32[2,64,1280]{2,1,0:T(8,128)}, f32[40,1280]{1,0:T(8,128)}, f32[40,1280]{1,0:T(8,128)}, f32[40,1280]{1,0:T(8,...) custom-call(bf16[2,64,1280]{2,1,0:T(8,128)(2,1)} %bitcast.55, ...), custom_call_target="tpu_custom_call" | custom-call | tf_op jit(solution)/shard_map/settle/pallas_call | solution.py:1754
